TPU v7x, 32 devices: a whole 2x2x4 slice. The times are simulated.
32 devices in a mesh: seq: 8 (over y, x, core), head: 4 (over z).
Axes of the slice: x: 2, y: 2, z: 4, core: 2. Of those that a mesh axis runs over, the one named last changes fastest.
Arguments:
- dna: bfloat16 [6144, 768], P('seq')
- conv_in: bfloat16 [5, 1536, 768], P(None, 'head')
- dilated_kernel_weight: bfloat16 [3, 1536, 1536], P(None, 'head'), may hold values from -0.09375 to 0.09375
- w_query: bfloat16 [1536, 1536], P('head')
- w_key: bfloat16 [1536, 1536], P('head')
- w_value: bfloat16 [1536, 1536], P('head'), may hold values from -0.15625 to 0.15625
- w_out: bfloat16 [1536, 1536], P('head'), may hold values from -0.21875 to 0.21875
Outputs:
- encoded: bfloat16 [3072, 1536], P('seq', 'head')
All inputs are finite; a program needn't handle non-finite values.
Results may differ from a plain program's by a relative error of at most 0.007.
Values may be sent and summed in bfloat16 or wider, within the bound.
No kernel may reach another device: no remote copies, remote signals or barrier semaphores. Data moves between devices by JAX's collectives and lax.ppermute only.
A program may use at most 64 MiB of HBM per device.

v0:
```python
import math

import jax
import jax.numpy as jnp
from jax import lax
from jax.sharding import PartitionSpec as P

C = 1536
HEAD_DIM = 64
KW = 5
DILATION_STEP = 4


def padded_2(block, sides, width):
    for axis, dim in sides:
        count = lax.axis_size(axis)
        forward = [(i, i + 1) for i in range(count - 1)]
        backward = [(target, source) for source, target in forward]
        low = lax.ppermute(
            lax.slice_in_dim(block, block.shape[dim] - width, None, axis=dim), axis, forward
        )
        high = lax.ppermute(lax.slice_in_dim(block, 0, width, axis=dim), axis, backward)
        block = jnp.concatenate([low, block, high], axis=dim)
    return block


def row_scale(hidden):
    squares = lax.psum(jnp.sum(hidden * hidden, axis=1), "head")
    return hidden * lax.rsqrt(squares / C + 1e-06)[:, None]


def reduce_operands(left, right):
    return lax.dot_general(
        left, right, (((1,), (1,)), ((), ())), preferred_element_type=jnp.float32
    )


def on_device(dna, conv_in, dilated_kernel_weight, w_query, w_key, w_value, w_out):
    local_row_count = dna.shape[0] // 2
    half = (KW - 1) // 2
    padded = padded_2(dna, (("seq", 0),), half)
    h1 = jnp.zeros((local_row_count, conv_in.shape[1]), jnp.float32)
    for kernel_offset in range(KW):
        rows = lax.slice(
            padded,
            (kernel_offset, 0),
            (kernel_offset + 2 * local_row_count - 1, padded.shape[1]),
            (2, 1),
        )
        h1 = h1 + reduce_operands(rows, conv_in[kernel_offset])
    gelu_output = jax.nn.gelu(row_scale(h1), approximate=True).astype(jnp.bfloat16)
    complete_output = lax.all_gather(gelu_output, "head", axis=1, tiled=True)
    broad_input = padded_2(complete_output, (("seq", 0),), DILATION_STEP)
    second_hidden = h1
    for kernel_offset in range(3):
        second_hidden = second_hidden + reduce_operands(
            broad_input[
                DILATION_STEP * kernel_offset : DILATION_STEP * kernel_offset + local_row_count
            ],
            dilated_kernel_weight[kernel_offset],
        )
    normed = row_scale(second_hidden).astype(jnp.bfloat16)
    local_width = w_query.shape[0]
    heads_here = local_width // HEAD_DIM
    empty = jnp.zeros((local_row_count, local_width), jnp.float32)
    totals = (empty, empty, empty)
    piece = lax.all_gather(normed, "head", axis=1, tiled=True)
    count = piece.shape[1]
    outs = []
    for total, weight in zip(totals, (w_query, w_key, w_value)):
        block = lax.slice_in_dim(weight, 0, count, axis=1)
        outs.append(total + reduce_operands(piece, block))
    q_acc, k_acc, v_acc = tuple(outs)
    query = q_acc.astype(jnp.bfloat16).reshape(local_row_count, heads_here, HEAD_DIM)
    keys = k_acc.astype(jnp.bfloat16)
    values = v_acc.astype(jnp.bfloat16)
    scale = 1.0 / math.sqrt(HEAD_DIM)
    start_state = (
        jnp.full((heads_here, local_row_count), -1e30, jnp.float32),
        jnp.zeros((heads_here, local_row_count), jnp.float32),
        jnp.zeros((local_row_count, heads_here, HEAD_DIM), jnp.float32),
    )
    key_rows = lax.all_gather(keys, "seq", axis=0, tiled=True)
    value_rows = lax.all_gather(values, "seq", axis=0, tiled=True)
    count = key_rows.shape[0]
    width = 512 if count % 512 == 0 else count
    blocks = count // width
    key_blocks = key_rows.reshape(blocks, width, heads_here, HEAD_DIM)
    value_blocks = value_rows.reshape(blocks, width, heads_here, HEAD_DIM)

    def step(state, operands):
        running, total, acc = state
        key_block, value_block = operands
        scores = (
            jnp.einsum("qhd,khd->hqk", query, key_block, preferred_element_type=jnp.float32) * scale
        )
        newest = jnp.maximum(running, jnp.max(scores, axis=2))
        factor = jnp.exp(running - newest)
        weights = jnp.exp(scores - newest[:, :, None])
        total = total * factor + jnp.sum(weights, axis=2)
        update = jnp.einsum(
            "hqk,khd->qhd",
            weights.astype(jnp.bfloat16),
            value_block,
            preferred_element_type=jnp.float32,
        )
        acc = acc * jnp.transpose(factor)[:, :, None] + update
        return ((newest, total, acc), None)

    state, _ = lax.scan(step, start_state, (key_blocks, value_blocks))
    running, total, acc = state
    attended = (
        (acc / jnp.transpose(total)[:, :, None])
        .reshape(local_row_count, local_width)
        .astype(jnp.bfloat16)
    )
    partial_out = jnp.dot(attended, w_out, preferred_element_type=jnp.float32)
    mixed = lax.psum_scatter(
        partial_out.astype(jnp.bfloat16), "head", scatter_dimension=1, tiled=True
    ).astype(jnp.float32)
    return (second_hidden + mixed).astype(jnp.bfloat16)


def solution(mesh):
    in_specs = (
        P("seq", None),
        P(None, "head", None),
        P(None, "head", None),
        P("head", None),
        P("head", None),
        P("head", None),
        P("head", None),
    )
    out_specs = P("seq", "head")
    return jax.shard_map(
        on_device, mesh=mesh, in_specs=in_specs, out_specs=out_specs, check_vma=False
    )
```

profile of v0, /device:TPU:0, one launch (start us, length us, event | category | flops | bytes accessed | tf_op | source)
XLA Modules:
  0.0 285.1 jit_solution(8050887976854538106)
XLA Ops:
  7.4 2.3 collective-permute-start
  11.1 5.0 %slice.65 = bf16[384,768]{1,0:T(8,128)(2,1)S(1)} slice(bf16[768,768]{1,0:T(8,128)(2,1)} %param.9), slice={[0:767:2], [0:768:1]} | slice | bytes 1179648 | tf_op jit(solution)/shard_map/slice | solution.py:44
  16.1 2.4 fusion.44
  18.5 3.5 %slice.67 = bf16[384,768]{1,0:T(8,128)(2,1)} slice(bf16[768,768]{1,0:T(8,128)(2,1)S(1)} %copy-done.1), slice={[1:768:2], [0:768:1]} | slice | bytes 1179648 | tf_op jit(solution)/shard_map/slice | solution.py:44
  23.0 3.7 %slice.69 = bf16[384,768]{1,0:T(8,128)(2,1)} slice(bf16[772,768]{1,0:T(8,128)(2,1)S(1)} %pad_maximum_fusion), slice={[4:771:2], [0:768:1]} | slice | bytes 1179648 | tf_op jit(solution)/shard_map/slice | solution.py:44
  27.8 3.6 %slice.61 = bf16[384,768]{1,0:T(8,128)(2,1)} slice(bf16[772,768]{1,0:T(8,128)(2,1)S(1)} %pad_maximum_fusion), slice={[0:767:2], [0:768:1]} | slice | bytes 1179648 | tf_op jit(solution)/shard_map/slice | solution.py:44
  38.0 12.8 %psum.14 = f32[384]{0:T(512)S(1)} all-reduce(f32[384]{0:T(512)S(1)} %get-tuple-element.105), channel_id=1, replica_groups=mesh['seq'=8,'head'=4] {'head'}, use_global_device_ids=true, to_apply=%region_1.0 | all-reduce | flops 384 | bytes 3072 | tf_op jit(solution)/shard_map/psum | solution.py:28
  51.8 31.3 %all-gather.5.cloned.1.call-done = bf16[384,1536]{0,1:T(8,128)(2,1)} async-done(((bf16[384,384]{0,1:T(8,128)(2,1)}), bf16[384,1536]{0,1:T(8,128)(2,1)}) %all-gather.5.cloned.1.call-update) | async-done | bytes 1179664 | tf_op jit(solution)/shard_map/all_gather | solution.py:52
  86.0 3.1 %collective-permute-start.2 = (bf16[4,1536]{0,1:T(8,128)(2,1)S(1)}, bf16[4,1536]{0,1:T(8,128)(2,1)S(1)}, u32[]{:S(2)}, u32[]{:S(2)}) collective-permute-start(bf16[4,1536]{0,1:T(8,128)(2,1)S(1)} %get-tuple-element.102), channel_id=1, source_target_pairs={{0,4},{4,8},{8,12},{12,16},{16,20},{20,24},{24,28},{1,5},{5,9},{9,... | collective-permute-start | bytes 36872 | tf_op jit(solution)/shard_map/ppermute | solution.py:19
  89.1 2.4 fusion.28
  93.3 9.9 %psum.15 = f32[384]{0:T(512)S(1)} all-reduce(f32[384]{0:T(512)S(1)} %get-tuple-element.107), channel_id=1, replica_groups=mesh['seq'=8,'head'=4] {'head'}, use_global_device_ids=true, to_apply=%region_3.0 | all-reduce | flops 384 | bytes 3072 | tf_op jit(solution)/shard_map/psum | solution.py:28
  104.1 35.4 %all-gather.7.cloned.1.call-done = bf16[384,1536]{0,1:T(8,128)(2,1)} async-done(((bf16[384,384]{0,1:T(8,128)(2,1)}), bf16[384,1536]{0,1:T(8,128)(2,1)}) %all-gather.7.cloned.1.call-update) | async-done | bytes 1179664 | tf_op jit(solution)/shard_map/all_gather | solution.py:67
  139.4 3.2 %convolution_convert_fusion.3 = bf16[384,384]{1,0:T(8,128)(2,1)} fusion(bf16[384,1536]{0,1:T(8,128)(2,1)} %all-gather.7.cloned.1.call-done, bf16[384,1536]{1,0:T(8,128)(2,1)} %param.13), kind=kOutput, calls=%fused_computation.34 | convolution fusion | flops 453132288 | bytes 2654208 | tf_op jit(solution)/shard_map/dot_general | solution.py:33
  142.7 3.2 %convolution_convert_fusion.2 = bf16[384,384]{1,0:T(8,128)(2,1)} fusion(bf16[384,1536]{0,1:T(8,128)(2,1)} %all-gather.7.cloned.1.call-done, bf16[384,1536]{1,0:T(8,128)(2,1)} %param.14), kind=kOutput, calls=%fused_computation.33 | convolution fusion | flops 453132288 | bytes 2654208 | tf_op jit(solution)/shard_map/dot_general | solution.py:33
  146.1 2.4 convolution_convert_fusion.1
  148.5 22.4 %all-gather.9.cloned.1.call-done = bf16[3072,384]{1,0:T(8,128)(2,1)} async-done(((bf16[384,384]{1,0:T(8,128)(2,1)}), bf16[3072,384]{1,0:T(8,128)(2,1)}) %all-gather.9.cloned.1.call-update) | async-done | bytes 2359312 | tf_op jit(solution)/shard_map/all_gather | solution.py:83
  170.9 8.1 %reshape.19 = bf16[6,512,6,64]{3,2,1,0:T(8,128)(2,1)} reshape(bf16[3072,384]{1,0:T(8,128)(2,1)} %all-gather.9.cloned.1.call-done) | data formatting | bytes 4718592 | tf_op jit(solution)/shard_map/reshape | solution.py:88
  179.0 7.2 %copy.16 = bf16[6,512,6,64]{1,3,2,0:T(8,128)(2,1)} copy(bf16[6,512,6,64]{3,2,1,0:T(8,128)(2,1)} %reshape.19) | data formatting | bytes 4718592
  186.2 15.4 %all-gather.11.cloned.1.call-done = bf16[3072,384]{1,0:T(8,128)(2,1)} async-done(((bf16[384,384]{1,0:T(8,128)(2,1)}), bf16[3072,384]{1,0:T(8,128)(2,1)}) %all-gather.11.cloned.1.call-update) | async-done | bytes 2359312 | tf_op jit(solution)/shard_map/all_gather | solution.py:84
  201.7 8.1 %reshape.20 = bf16[6,512,6,64]{3,2,1,0:T(8,128)(2,1)} reshape(bf16[3072,384]{1,0:T(8,128)(2,1)} %all-gather.11.cloned.1.call-done) | data formatting | bytes 4718592 | tf_op jit(solution)/shard_map/reshape | solution.py:89
  209.8 7.1 %copy.17 = bf16[6,512,6,64]{1,3,2,0:T(8,128)(2,1)} copy(bf16[6,512,6,64]{3,2,1,0:T(8,128)(2,1)} %reshape.20) | data formatting | bytes 4718592
  216.9 28.4 %while.15 = (s32[]{:T(128)}, f32[6,384]{1,0:T(8,128)S(1)}, f32[6,384]{1,0:T(8,128)S(1)}, f32[384,6,64]{0,2,1:T(8,128)S(1)}, bf16[6,512,6,64]{1,3,2,0:T(8,128)(2,...) while((s32[]{:T(128)}, f32[6,384]{1,0:T(8,128)S(1)}, ...), condition=%wide.region_7.8_spmd.clone, body=%wide.region_4.7_spmd.clone.sunk | while | flops 311883264 | bytes 16564345 | solution.py:110
  219.6 2.0 fusion.86
  247.4 29.3 %reduce-scatter.2.cloned.1.call-done = bf16[384,384]{0,1:T(8,128)(2,1)} async-done(((bf16[384,1536]{0,1:T(8,128)(2,1)}), bf16[384,384]{0,1:T(8,128)(2,1)}) %reduce-scatter.2.cloned.1.call-update) | async-done | bytes 294928 | tf_op jit(solution)/shard_map/reduce_scatter | solution.py:118
  (86 shorter events, 47.6 us)
Async XLA Ops:
  6.5 238.8 %copy-start = (bf16[384,1536]{1,0:T(8,128)(2,1)S(1)}, bf16[384,1536]{1,0:T(8,128)(2,1)}, u32[]{:S(2)}) copy-start(bf16[384,1536]{1,0:T(8,128)(2,1)} %param.15) | copy-start | bytes 3538948
  6.5 12.0 %copy-start.1 = (bf16[768,768]{1,0:T(8,128)(2,1)S(1)}, bf16[768,768]{1,0:T(8,128)(2,1)}, u32[]{:S(2)}) copy-start(bf16[768,768]{1,0:T(8,128)(2,1)} %param.9) | copy-start | bytes 3538948
  6.5 76.6 %all-gather.5.cloned.1.call-start = ((), (), s32[]{:S(2)}) async-start(), calls=%async_computation.1 | async-start | bytes 1474560 | tf_op jit(solution)/shard_map/all_gather | solution.py:52
  7.4 14.6 %collective-permute-start = (bf16[2,768]{1,0:T(2,128)(2,1)S(1)}, bf16[2,768]{1,0:T(2,128)(2,1)S(1)}, u32[]{:S(2)}, u32[]{:S(2)}) collective-permute-start(bf16[2,768]{1,0:T(2,128)(2,1)S(1)} %get-tuple-element.103), channel_id=1, source_target_pairs={{0,4},{4,8},{8,12},{12,16},{16,20},{20,24},{24,28},{1,5},{5,9},{9,... | collective-permute-start | bytes 9224 | tf_op jit(solution)/shard_map/ppermute | solution.py:19
  9.8 12.3 %collective-permute-start.1 = (bf16[2,768]{1,0:T(2,128)(2,1)S(1)}, bf16[2,768]{1,0:T(2,128)(2,1)}, u32[]{:S(2)}, u32[]{:S(2)}) collective-permute-start(bf16[2,768]{1,0:T(2,128)(2,1)S(1)} %get-tuple-element.104), channel_id=1, source_target_pairs={{4,0},{8,4},{12,8},{16,12},{20,16},{24,20},{28,24},{5,1},{9,5},{13... | collective-permute-start | bytes 9224 | tf_op jit(solution)/shard_map/ppermute | solution.py:22
  26.7 6.3 %copy-start.2 = (f32[384,384]{0,1:T(8,128)S(1)}, f32[384,384]{0,1:T(8,128)}, u32[]{:S(2)}) copy-start(f32[384,384]{0,1:T(8,128)} %fusion.44) | copy-start | bytes 1769476
  31.4 3.5 %copy-start.3 = (bf16[384,768]{1,0:T(8,128)(2,1)S(1)}, bf16[384,768]{1,0:T(8,128)(2,1)}, u32[]{:S(2)}) copy-start(bf16[384,768]{1,0:T(8,128)(2,1)} %slice.67) | copy-start | bytes 1769476
  33.0 3.4 %copy-start.4 = (bf16[384,768]{1,0:T(8,128)(2,1)S(1)}, bf16[384,768]{1,0:T(8,128)(2,1)}, u32[]{:S(2)}) copy-start(bf16[384,768]{1,0:T(8,128)(2,1)} %slice.69) | copy-start | bytes 1769476
  51.8 87.7 %all-gather.7.cloned.1.call-start = ((), (), s32[]{:S(2)}) async-start(), calls=%async_computation.2 | async-start | bytes 1474560 | tf_op jit(solution)/shard_map/all_gather | solution.py:67
  83.1 8.4 %copy-start.5 = (bf16[384,1536]{0,1:T(8,128)(2,1)S(1)}, bf16[384,1536]{0,1:T(8,128)(2,1)}, u32[]{:S(2)}) copy-start(bf16[384,1536]{0,1:T(8,128)(2,1)} %all-gather.5.cloned.1.call-done) | copy-start | bytes 3538948
  83.1 8.4 %copy-start.6 = (bf16[3,384,1536]{2,1,0:T(8,128)(2,1)S(1)}, bf16[3,384,1536]{2,1,0:T(8,128)(2,1)}, u32[]{:S(2)}) copy-start(bf16[3,384,1536]{2,1,0:T(8,128)(2,1)} %param.11) | copy-start | bytes 10616836
  84.6 7.8 %collective-permute-start.3 = (bf16[4,1536]{0,1:T(8,128)(2,1)S(1)}, bf16[4,1536]{0,1:T(8,128)(2,1)S(1)}, u32[]{:S(2)}, u32[]{:S(2)}) collective-permute-start(bf16[4,1536]{0,1:T(8,128)(2,1)S(1)} %get-tuple-element.101), channel_id=1, source_target_pairs={{4,0},{8,4},{12,8},{16,12},{20,16},{24,20},{28,24},{5,1},{9,5},{13... | collective-permute-start | bytes 36872 | tf_op jit(solution)/shard_map/ppermute | solution.py:22
  86.0 5.5 %collective-permute-start.2 = (bf16[4,1536]{0,1:T(8,128)(2,1)S(1)}, bf16[4,1536]{0,1:T(8,128)(2,1)S(1)}, u32[]{:S(2)}, u32[]{:S(2)}) collective-permute-start(bf16[4,1536]{0,1:T(8,128)(2,1)S(1)} %get-tuple-element.102), channel_id=1, source_target_pairs={{0,4},{4,8},{8,12},{12,16},{16,20},{20,24},{24,28},{1,5},{5,9},{9,... | collective-permute-start | bytes 36872 | tf_op jit(solution)/shard_map/ppermute | solution.py:19
  104.0 66.9 %all-gather.9.cloned.1.call-start = ((), (), s32[]{:S(2)}) async-start(), calls=%async_computation.3 | async-start | bytes 2654208 | tf_op jit(solution)/shard_map/all_gather | solution.py:83
  142.6 59.1 %all-gather.11.cloned.1.call-start = ((), (), s32[]{:S(2)}) async-start(), calls=%async_computation.4 | async-start | bytes 2654208 | tf_op jit(solution)/shard_map/all_gather | solution.py:84
  145.9 130.8 %reduce-scatter.2.cloned.1.call-start = ((), (), s32[]{:S(2)}) async-start(), calls=%async_computation.5 | async-start | bytes 1474560 | tf_op jit(solution)/shard_map/reduce_scatter | solution.py:118
Sparse Core Ops, SparseCore 0:
  51.9 31.1 all-gather.4
  104.1 35.2 all-gather.6
  142.7 28.1 all-gather.8
  172.6 29.0 all-gather.10
  247.5 29.1 reduce-scatter.1
where the time goes:
time: 287 us; the launch traced here: 285 us
  waiting for transfers between devices  134 us (47%)
  local copies, waits for them, and re-layouts  50.8 us (18%)
  matrix products  47 us (16%)
  blocking collectives  22.7 us (8%)
  between operations  13.4 us (5%)
  other arithmetic  8.58 us (3%)
  starting transfers between devices  8.47 us (3%)
    all_gather x1, waiting for transfers between devices, on_device(): piece = lax.all_gather(normed, 'head', axis=1, tiled=True)  35.4 us
    all_gather x1, waiting for transfers between devices, on_device(): complete_output = lax.all_gather(gelu_output, 'head', axis=1, tiled=True)  31.3 us
    reduce_scatter x1, waiting for transfers between devices, on_device(): lax.psum_scatter(partial_out.astype(jnp.bfloat16), 'head', scatter_dimens...  29.3 us
    psum x2, blocking collectives, row_scale(): squares = lax.psum(jnp.sum(hidden * hidden, axis=1), 'head')  22.7 us
    all_gather x1, waiting for transfers between devices, on_device(): key_rows = lax.all_gather(keys, 'seq', axis=0, tiled=True)  22.4 us
    dot_general x11, matrix products, reduce_operands(): lax.dot_general(left, right, (((1,), (1,)), ((), ())), preferred_element_...  21.8 us
    slice x5, local copies, waits for them, and re-layouts, on_device(): lax.slice(padded, (kernel_offset, 0), (kernel_offset + 2 * local_row_coun...  17 us
    all_gather x1, waiting for transfers between devices, on_device(): value_rows = lax.all_gather(values, 'seq', axis=0, tiled=True)  15.4 us
  transfers between devices with their start and end apart: 9, of which 5 were waited for; matrix products, arithmetic and copies ran while one was open for 12% of the time, Pallas kernels for 0%

commit v1 on v0

--- a/solution.py
+++ b/solution.py
@@ -1,14 +1,21 @@
+import functools
 import math
 
 import jax
 import jax.numpy as jnp
 from jax import lax
+from jax.experimental import pallas as pl
+from jax.experimental.pallas import tpu as pltpu
 from jax.sharding import PartitionSpec as P
 
 C = 1536
 HEAD_DIM = 64
 KW = 5
 DILATION_STEP = 4
+EPS = 1e-06
+EDGE = 16
+LOG2E = math.log2(math.e)
+MIB = 1 << 20
 
 
 def padded_2(block, sides, width):
@@ -26,7 +33,7 @@
 
 def row_scale(hidden):
     squares = lax.psum(jnp.sum(hidden * hidden, axis=1), "head")
-    return hidden * lax.rsqrt(squares / C + 1e-06)[:, None]
+    return hidden * lax.rsqrt(squares / C + EPS)[:, None]
 
 
 def reduce_operands(left, right):
@@ -35,7 +42,7 @@
     )
 
 
-def on_device(dna, conv_in, dilated_kernel_weight, w_query, w_key, w_value, w_out):
+def general_form(dna, conv_in, dilated_kernel_weight, w_query, w_key, w_value, w_out):
     local_row_count = dna.shape[0] // 2
     half = (KW - 1) // 2
     padded = padded_2(dna, (("seq", 0),), half)
@@ -62,15 +69,8 @@
     normed = row_scale(second_hidden).astype(jnp.bfloat16)
     local_width = w_query.shape[0]
     heads_here = local_width // HEAD_DIM
-    empty = jnp.zeros((local_row_count, local_width), jnp.float32)
-    totals = (empty, empty, empty)
     piece = lax.all_gather(normed, "head", axis=1, tiled=True)
-    count = piece.shape[1]
-    outs = []
-    for total, weight in zip(totals, (w_query, w_key, w_value)):
-        block = lax.slice_in_dim(weight, 0, count, axis=1)
-        outs.append(total + reduce_operands(piece, block))
-    q_acc, k_acc, v_acc = tuple(outs)
+    q_acc, k_acc, v_acc = (reduce_operands(piece, w) for w in (w_query, w_key, w_value))
     query = q_acc.astype(jnp.bfloat16).reshape(local_row_count, heads_here, HEAD_DIM)
     keys = k_acc.astype(jnp.bfloat16)
     values = v_acc.astype(jnp.bfloat16)
@@ -121,6 +121,257 @@
     return (second_hidden + mixed).astype(jnp.bfloat16)
 
 
+def whole(shape):
+    return pl.BlockSpec(shape, lambda *_: (0,) * len(shape))
+
+
+def nbytes(*arrays):
+    return sum(math.prod(a.shape) * jnp.dtype(a.dtype).itemsize for a in arrays)
+
+
+def cost(flops, arrays, transcendentals=0):
+    return pl.CostEstimate(
+        flops=int(flops), bytes_accessed=int(nbytes(*arrays)), transcendentals=int(transcendentals)
+    )
+
+
+def rotate(offset):
+    count = lax.axis_size("head")
+    return [(i, (i + offset) % count) for i in range(count)]
+
+
+def shared(block):
+    count = lax.axis_size("head")
+    return [block] + [lax.ppermute(block, "head", rotate(k)) for k in (1, count - 1, 2)]
+
+
+def owner(k):
+    count = lax.axis_size("head")
+    return lax.rem(lax.axis_index("head") + count - k, count)
+
+
+SHIFTS = (0, 1, 3, 2)
+
+
+def conv_kernel(dna_ref, low_ref, high_ref, weight_ref, h1_ref, sent_ref, wide):
+    rows = dna_ref.shape[0]
+    tiles = wide.shape[0]
+    for j in range(tiles):
+        lanes = pl.ds(128 * j, 128)
+        wide[j, pl.ds(0, EDGE), :] = low_ref[:, lanes].astype(jnp.float32)
+        wide[j, pl.ds(EDGE, rows), :] = dna_ref[:, lanes].astype(jnp.float32)
+        wide[j, pl.ds(EDGE + rows, EDGE), :] = high_ref[:, lanes].astype(jnp.float32)
+    count = sent_ref.shape[0]
+    first = EDGE - 2 * DILATION_STEP - KW // 2
+    total = None
+    for tap in range(KW):
+        picked = [wide[j, pl.ds(first + tap, count, stride=2), :] for j in range(tiles)]
+        taken = jnp.concatenate(picked, axis=1).astype(jnp.bfloat16)
+        term = reduce_operands(taken, weight_ref[tap])
+        total = term if total is None else total + term
+    sent_ref[...] = total.astype(jnp.bfloat16)
+    h1_ref[...] = total[DILATION_STEP : DILATION_STEP + rows // 2]
+
+
+def first_conv(dna, low, high, weight):
+    rows, width = dna.shape
+    out = weight.shape[1]
+    kept = jax.ShapeDtypeStruct((rows // 2, out), jnp.float32)
+    sent = jax.ShapeDtypeStruct((rows // 2 + 2 * DILATION_STEP, out), jnp.bfloat16)
+    return pl.pallas_call(
+        conv_kernel,
+        out_shape=(kept, sent),
+        scratch_shapes=[pltpu.VMEM((width // 128, rows + 2 * EDGE, 128), jnp.float32)],
+        compiler_params=pltpu.CompilerParams(vmem_limit_bytes=32 * MIB),
+        cost_estimate=cost(
+            2 * sent.shape[0] * out * width * KW, (dna, low, high, weight, kept, sent)
+        ),
+        name="first_conv",
+    )(dna, low, high, weight)
+
+
+def dilated_kernel(a0, a1, a2, a3, h1_ref, weight_ref, h2_ref, sent_ref, act):
+    parts = (a0, a1, a2, a3)
+    count, width = a0.shape
+    rows = h1_ref.shape[0]
+    squares = None
+    for part in parts:
+        block = part[...].astype(jnp.float32)
+        term = jnp.sum(block * block, axis=1, keepdims=True)
+        squares = term if squares is None else squares + term
+    inverse = lax.rsqrt(squares / C + EPS)
+    position = lax.axis_index("seq") * rows - DILATION_STEP + lax.broadcasted_iota(
+        jnp.int32, (count, 1), 0
+    )
+    inside = (position >= 0) & (position < rows * lax.axis_size("seq"))
+    inverse = jnp.where(inside, inverse, 0.0)
+    total = h1_ref[...]
+    for part, shift in zip(parts, SHIFTS):
+        act[...] = jax.nn.gelu(part[...].astype(jnp.float32) * inverse, approximate=True)
+        columns = pl.ds(pl.multiple_of(owner(shift) * width, 128), width)
+        for tap in range(3):
+            taken = act[pl.ds(tap * DILATION_STEP, rows), :].astype(jnp.bfloat16)
+            total = total + reduce_operands(taken, weight_ref[tap, :, columns])
+    h2_ref[...] = total
+    sent_ref[...] = total.astype(jnp.bfloat16)
+
+
+def second_conv(parts, h1, weight):
+    count, width = parts[0].shape
+    rows, out = h1.shape
+    kept = jax.ShapeDtypeStruct((rows, out), jnp.float32)
+    sent = jax.ShapeDtypeStruct((rows, out), jnp.bfloat16)
+    return pl.pallas_call(
+        dilated_kernel,
+        out_shape=(kept, sent),
+        scratch_shapes=[pltpu.VMEM((count, width), jnp.float32)],
+        compiler_params=pltpu.CompilerParams(vmem_limit_bytes=32 * MIB),
+        cost_estimate=cost(
+            2 * rows * out * weight.shape[2] * 3,
+            (*parts, h1, weight, kept, sent),
+            count * weight.shape[2],
+        ),
+        name="second_conv",
+    )(*parts, h1, weight)
+
+
+def project_kernel(a0, a1, a2, a3, wq, wk, wv, q_ref, kv_ref):
+    parts = (a0, a1, a2, a3)
+    width = a0.shape[1]
+    squares = None
+    for part in parts:
+        block = part[...].astype(jnp.float32)
+        term = jnp.sum(block * block, axis=1, keepdims=True)
+        squares = term if squares is None else squares + term
+    inverse = lax.rsqrt(squares / C + EPS)
+
+    def product(weight_ref):
+        total = None
+        for part, shift in zip(parts, SHIFTS):
+            columns = pl.ds(pl.multiple_of(owner(shift) * width, 128), width)
+            term = reduce_operands(part[...], weight_ref[:, columns])
+            total = term if total is None else total + term
+        return total
+
+    out = wq.shape[0]
+    kv_ref[:, :out] = (product(wk) * inverse).astype(jnp.bfloat16)
+    kv_ref[:, out:] = (product(wv) * inverse).astype(jnp.bfloat16)
+    scale = LOG2E / math.sqrt(HEAD_DIM)
+    q_ref[...] = (product(wq) * (inverse * scale)).astype(jnp.bfloat16)
+
+
+def project(parts, wq, wk, wv):
+    rows = parts[0].shape[0]
+    out = wq.shape[0]
+    q = jax.ShapeDtypeStruct((rows, out), jnp.bfloat16)
+    kv = jax.ShapeDtypeStruct((rows, 2 * out), jnp.bfloat16)
+    return pl.pallas_call(
+        project_kernel,
+        out_shape=(q, kv),
+        compiler_params=pltpu.CompilerParams(vmem_limit_bytes=32 * MIB),
+        cost_estimate=cost(6 * rows * out * wq.shape[1], (*parts, wq, wk, wv, q, kv)),
+        name="project",
+    )(*parts, wq, wk, wv)
+
+
+def attend_kernel(count, q_ref, *refs):
+    keys, values = refs[:count], refs[count : 2 * count]
+    w_ref, h2_ref, own_ref, p1, p2, p3, acc = refs[2 * count :]
+    step = pl.program_id(0)
+    rows, width = own_ref.shape
+    tile = 128
+    lane = lax.broadcasted_iota(jnp.int32, (tile, 2 * HEAD_DIM), 1)
+    pieces = []
+    for start in range(0, rows, tile):
+        query = q_ref[pl.ds(start, tile), :]
+        results = []
+        for head in range(2):
+            mine = (lane // HEAD_DIM) == head
+            one = jnp.where(mine, query, jnp.zeros_like(query))
+            scores = [reduce_operands(one, key[...]) for key in keys]
+            top = functools.reduce(jnp.maximum, scores)
+            top = jnp.max(top, axis=1, keepdims=True)
+            total, out = None, None
+            for score, value in zip(scores, values):
+                weights = jnp.exp2(score - top)
+                total = weights if total is None else total + weights
+                term = jnp.dot(
+                    weights.astype(jnp.bfloat16), value[...], preferred_element_type=jnp.float32
+                )
+                out = term if out is None else out + term
+            results.append(out / jnp.sum(total, axis=1, keepdims=True))
+        pieces.append(jnp.where(lane < HEAD_DIM, results[0], results[1]).astype(jnp.bfloat16))
+    attended = jnp.concatenate(pieces, axis=0)
+    product = jnp.dot(attended, w_ref[...], preferred_element_type=jnp.float32)
+
+    @pl.when(step == 0)
+    def _():
+        acc[...] = product
+
+    @pl.when(step > 0)
+    def _():
+        acc[...] += product
+
+    @pl.when(step == pl.num_programs(0) - 1)
+    def _():
+        def block(shift):
+            return acc[:, pl.ds(pl.multiple_of(owner(shift) * width, 128), width)]
+
+        own_ref[...] = block(0) + h2_ref[...]
+        for ref, shift in ((p1, 3), (p2, 1), (p3, 2)):
+            ref[...] = block(shift).astype(jnp.bfloat16)
+
+
+def attend(q, blocks, w_out, h2):
+    rows, width = h2.shape
+    pairs = width // (2 * HEAD_DIM)
+    count = len(blocks)
+    seen = blocks[0].shape[0]
+    own = jax.ShapeDtypeStruct((rows, width), jnp.float32)
+    part = jax.ShapeDtypeStruct((rows, width), jnp.bfloat16)
+    lanes = 2 * HEAD_DIM
+    return pl.pallas_call(
+        functools.partial(attend_kernel, count),
+        grid=(pairs,),
+        out_shape=(own, part, part, part),
+        in_specs=[pl.BlockSpec((rows, lanes), lambda g: (0, g))]
+        + [pl.BlockSpec((seen, lanes), lambda g: (0, g))] * count
+        + [pl.BlockSpec((seen, lanes), lambda g: (0, g + pairs))] * count
+        + [pl.BlockSpec((lanes, w_out.shape[1]), lambda g: (g, 0)), whole(h2.shape)],
+        out_specs=[whole((rows, width))] * 4,
+        scratch_shapes=[pltpu.VMEM((rows, w_out.shape[1]), jnp.float32)],
+        compiler_params=pltpu.CompilerParams(vmem_limit_bytes=40 * MIB),
+        cost_estimate=cost(
+            4 * rows * width * seen * count + 2 * rows * width * w_out.shape[1],
+            (q, *blocks, w_out, h2, own, part, part, part),
+            rows * seen * count * width // HEAD_DIM,
+        ),
+        name="attend",
+    )(q, *blocks, *blocks, w_out, h2)
+
+
+def exchanged(block, mask):
+    count = lax.axis_size("seq")
+    return lax.ppermute(block, "seq", [(i, i ^ mask) for i in range(count)])
+
+
+def on_device(dna, conv_in, dilated_kernel_weight, w_query, w_key, w_value, w_out):
+    count = lax.axis_size("seq")
+    low = lax.ppermute(dna[-EDGE:], "seq", [(i, i + 1) for i in range(count - 1)])
+    high = lax.ppermute(dna[:EDGE], "seq", [(i + 1, i) for i in range(count - 1)])
+    h1, sent = first_conv(dna, low, high, conv_in)
+    h2, sent = second_conv(shared(sent), h1, dilated_kernel_weight)
+    q, kv = project(shared(sent), w_query, w_key, w_value)
+    far = [exchanged(kv, mask) for mask in range(2, count, 2)]
+    near = [kv] + far
+    blocks = near + [exchanged(block, 1) for block in near]
+    own, p1, p2, p3 = attend(q, blocks, w_out, h2)
+    total = own
+    for part, shift in ((p1, 1), (p2, 3), (p3, 2)):
+        total = total + lax.ppermute(part, "head", rotate(shift)).astype(jnp.float32)
+    return total.astype(jnp.bfloat16)
+
+
 def solution(mesh):
     in_specs = (
         P("seq", None),
@@ -132,6 +383,7 @@
         P("head", None),
     )
     out_specs = P("seq", "head")
-    return jax.shard_map(
-        on_device, mesh=mesh, in_specs=in_specs, out_specs=out_specs, check_vma=False
-    )
+    seq, head = mesh.shape["seq"], mesh.shape["head"]
+    aligned = (C // head) % 128 == 0
+    body = on_device if head == 4 and seq & (seq - 1) == 0 and aligned else general_form
+    return jax.shard_map(body, mesh=mesh, in_specs=in_specs, out_specs=out_specs, check_vma=False)

time: 287 us -> 152 us (0.53)
  waiting for transfers between devices: 134 us -> 86.6 us
  matrix products: 47 us -> 0 us
  local copies, waits for them, and re-layouts: 50.8 us -> 3.89 us
  starting transfers between devices: 8.47 us -> 34.3 us
  Pallas kernels: 0 us -> 24.6 us
  blocking collectives: 22.7 us -> 0 us
  between operations: 13.4 us -> 0.11 us
  other arithmetic: 8.58 us -> 0.84 us
    all_gather x4 -> x0, waiting for transfers between devices: 105 us -> none  [the longest x1 35.4 us: on_device(): piece = lax.all_gather(normed, 'head', axis=1, tiled=True)]
    ppermute x4 -> x18, waiting for transfers between devices: 0.01 us -> 86.6 us  [the longest x6 39.2 us: shared(): lax.ppermute(block, 'head', rotate(k))]
    dot_general x24 -> x0, matrix products: 47 us -> none  [the longest x11 21.8 us: reduce_operands(): lax.dot_general(left, right, (((1,), (1,)), ((), ())), preferred_element_...]
    reduce_scatter x1 -> x0, waiting for transfers between devices: 29.3 us -> none  [on_device(): lax.psum_scatter(partial_out.astype(jnp.bfloat16), 'head', scatter_dimens...]
    ppermute x4 -> x18, starting transfers between devices: 8.12 us -> 34.3 us  [the longest x6 16.4 us: shared(): lax.ppermute(block, 'head', rotate(k))]
    pallas_call x0 -> x4, Pallas kernels: none -> 24.6 us  [the longest x1 17.4 us: attend(): pl.pallas_call(functools.partial(attend_kernel, count), grid=(pairs,), ou...]
    psum x2 -> x0, blocking collectives: 22.7 us -> none  [row_scale(): squares = lax.psum(jnp.sum(hidden * hidden, axis=1), 'head')]
    slice x7 -> x1, local copies, waits for them, and re-layouts: 19.3 us -> 0.76 us  [on_device(): dna[:EDGE]]
  transfers between devices with their start and end apart: 9 -> 18, of which waited for: 5 -> 13; matrix products, arithmetic and copies ran while one was open for 12% -> 0% of each run, Pallas kernels for 0% -> 0%
where the time goes in v1:
time: 152 us; the launch traced here: 150 us
  waiting for transfers between devices  86.6 us (57%)
  starting transfers between devices  34.3 us (23%)
  Pallas kernels  24.6 us (16%)
  local copies, waits for them, and re-layouts  3.89 us (3%)
    ppermute x6, waiting for transfers between devices, shared(): lax.ppermute(block, 'head', rotate(k))  39.2 us
    ppermute x7, waiting for transfers between devices, exchanged(): return lax.ppermute(block, 'seq', [(i, i ^ mask) for i in range(count)])  25.5 us
    ppermute x3, waiting for transfers between devices, on_device(): lax.ppermute(part, 'head', rotate(shift)).astype(jnp.float32)  21.1 us
    pallas_call x1, Pallas kernels, attend(): pl.pallas_call(functools.partial(attend_kernel, count), grid=(pairs,), ou...  17.4 us
    ppermute x6, starting transfers between devices, shared(): lax.ppermute(block, 'head', rotate(k))  16.4 us
    ppermute x3, starting transfers between devices, on_device(): lax.ppermute(part, 'head', rotate(shift)).astype(jnp.float32)  8.73 us
    ppermute x7, starting transfers between devices, exchanged(): return lax.ppermute(block, 'seq', [(i, i ^ mask) for i in range(count)])  4.61 us
    ppermute x1, starting transfers between devices, on_device(): lax.ppermute(dna[-EDGE:], 'seq', [(i, i + 1) for i in range(count - 1)])  3.29 us
  transfers between devices with their start and end apart: 18, of which 13 were waited for; matrix products, arithmetic and copies ran while one was open for 0% of the time, Pallas kernels for 0%

profile of v1, /device:TPU:0, one launch (start us, length us, event | category | flops | bytes accessed | tf_op | source)
XLA Modules:
  0.0 150.3 jit_solution(12454450005872219666)
XLA Ops:
  2.1 3.3 %collective-permute-start = (bf16[16,768]{1,0:T(8,128)(2,1)S(1)}, bf16[16,768]{1,0:T(8,128)(2,1)S(1)}, u32[]{:S(2)}, u32[]{:S(2)}) collective-permute-start(bf16[16,768]{1,0:T(8,128)(2,1)S(1)} %get-tuple-element.26), channel_id=1, source_target_pairs={{0,4},{4,8},{8,12},{12,16},{16,20},{20,24},{24,28},{1,5},{5,9},{9,... | collective-permute-start | bytes 73736 | tf_op jit(solution)/shard_map/ppermute | solution.py:360
  7.5 1.8 %copy-done.2 = bf16[5,384,768]{2,1,0:T(8,128)(2,1)S(1)} copy-done((bf16[5,384,768]{2,1,0:T(8,128)(2,1)S(1)}, bf16[5,384,768]{2,1,0:T(8,128)(2,1)}, u32[]{:S(2)}) %copy-start.2) | copy-done | bytes 2949144
  9.3 1.8 %first_conv.1 = (f32[384,384]{1,0:T(8,128)S(1)}, bf16[392,384]{1,0:T(8,128)(2,1)S(1)}) custom-call(bf16[768,768]{1,0:T(8,128)(2,1)S(1)} %copy-done.1, bf16[16,768]{1,0:T(8,128)(2,1)S(1)} %collective-permute-done.low_ref, bf16[16,768]{1,0:T(8,128)(2,1)S(1)} %collective-permute-done.1.high_ref, bf16[5,384,768]{2,1,0:T(8,128)(2,1)S(1)} %copy-done.2), custom_call_target="tpu_custom_call" | custom-call | flops 1156055040 | bytes 5068800 | tf_op jit(solution)/shard_map/first_conv/pallas_call | solution.py:181
  11.1 4.1 %collective-permute-start.4 = (bf16[392,384]{1,0:T(8,128)(2,1)S(1)}, bf16[392,384]{1,0:T(8,128)(2,1)S(1)}, u32[]{:S(2)}, u32[]{:S(2)}) collective-permute-start(bf16[392,384]{1,0:T(8,128)(2,1)S(1)} %get-tuple-element.15.a0), channel_id=1, source_target_pairs={{0,2},{1,3},{2,0},{3,1},{4,6},{5,7},{6,4},{7,5},{8,10},{9,11},{10,... | collective-permute-start | bytes 903176 | tf_op jit(solution)/shard_map/ppermute | solution.py:145
  15.2 1.3 collective-permute-start.3
  17.2 12.0 %collective-permute-done.4.a3 = bf16[392,384]{1,0:T(8,128)(2,1)S(1)} collective-permute-done((bf16[392,384]{1,0:T(8,128)(2,1)S(1)}, bf16[392,384]{1,0:T(8,128)(2,1)S(1)}, u32[]{:S(2)}, u32[]{:S(2)}) %collective-permute-start.4) | collective-permute-done | bytes 301088 | tf_op jit(solution)/shard_map/ppermute | solution.py:145
  30.2 7.2 %collective-permute-done.2.a1 = bf16[392,384]{1,0:T(8,128)(2,1)S(1)} collective-permute-done((bf16[392,384]{1,0:T(8,128)(2,1)S(1)}, bf16[392,384]{1,0:T(8,128)(2,1)S(1)}, u32[]{:S(2)}, u32[]{:S(2)}) %collective-permute-start.2) | collective-permute-done | bytes 301088 | tf_op jit(solution)/shard_map/ppermute | solution.py:145
  37.3 2.9 %second_conv.1 = (f32[384,384]{1,0:T(8,128)S(1)}, bf16[384,384]{1,0:T(8,128)(2,1)S(1)}) custom-call(bf16[392,384]{1,0:T(8,128)(2,1)S(1)} %get-tuple-element.15.a0, bf16[392,384]{1,0:T(8,128)(2,1)S(1)} %collective-permute-done.2.a1, bf16[392,384]{1,0:T(8,128)(2,1)S(1)} %collective-permute-done.3.a2, bf16[392,384]{1,0:T(8,128)(2,1)S(1)} %collective-permute-done.4.a3, ...), custom_call_target="tpu_custom_call" | custom-call | flops 1358954496 | bytes 6217728 | tf_op jit(solution)/shard_map/second_conv/pallas_call | solution.py:224
  40.3 8.2 %collective-permute-start.7 = (bf16[384,384]{1,0:T(8,128)(2,1)S(1)}, bf16[384,384]{1,0:T(8,128)(2,1)S(1)}, u32[]{:S(2)}, u32[]{:S(2)}) collective-permute-start(bf16[384,384]{1,0:T(8,128)(2,1)S(1)} %get-tuple-element.17.a0), channel_id=1, source_target_pairs={{0,2},{1,3},{2,0},{3,1},{4,6},{5,7},{6,4},{7,5},{8,10},{9,11},{10,... | collective-permute-start | bytes 884744 | tf_op jit(solution)/shard_map/ppermute | solution.py:145
  48.9 1.6 %collective-permute-start.5 = (bf16[384,384]{1,0:T(8,128)(2,1)S(1)}, bf16[384,384]{1,0:T(8,128)(2,1)S(1)}, u32[]{:S(2)}, u32[]{:S(2)}) collective-permute-start(bf16[384,384]{1,0:T(8,128)(2,1)S(1)} %get-tuple-element.17.a0), channel_id=1, source_target_pairs={{0,1},{1,2},{2,3},{3,0},{4,5},{5,6},{6,7},{7,4},{8,9},{9,10},{10,1... | collective-permute-start | bytes 884744 | tf_op jit(solution)/shard_map/ppermute | solution.py:145
  50.5 12.7 %collective-permute-done.7.a3 = bf16[384,384]{1,0:T(8,128)(2,1)S(1)} collective-permute-done((bf16[384,384]{1,0:T(8,128)(2,1)S(1)}, bf16[384,384]{1,0:T(8,128)(2,1)S(1)}, u32[]{:S(2)}, u32[]{:S(2)}) %collective-permute-start.7) | collective-permute-done | bytes 294944 | tf_op jit(solution)/shard_map/ppermute | solution.py:145
  63.2 6.4 %collective-permute-done.6.a2 = bf16[384,384]{1,0:T(8,128)(2,1)S(1)} collective-permute-done((bf16[384,384]{1,0:T(8,128)(2,1)S(1)}, bf16[384,384]{1,0:T(8,128)(2,1)S(1)}, u32[]{:S(2)}, u32[]{:S(2)}) %collective-permute-start.6) | collective-permute-done | bytes 294944 | tf_op jit(solution)/shard_map/ppermute | solution.py:145
  69.6 2.5 %project.1 = (bf16[384,384]{1,0:T(8,128)(2,1)S(1)}, bf16[384,768]{1,0:T(8,128)(2,1)S(1)}) custom-call(bf16[384,384]{1,0:T(8,128)(2,1)S(1)} %get-tuple-element.17.a0, bf16[384,384]{1,0:T(8,128)(2,1)S(1)} %collective-permute-done.5.a1, bf16[384,384]{1,0:T(8,128)(2,1)S(1)} %collective-permute-done.6.a2, bf16[384,384]{1,0:T(8,128)(2,1)S(1)} %collective-permute-done.7.a3, ...), custom_call_target="tpu_custom_call" | custom-call | flops 1358954496 | bytes 5603328 | tf_op jit(solution)/shard_map/project/pallas_call | solution.py:268
  72.1 1.8 %collective-permute-start.10 = (bf16[384,768]{1,0:T(8,128)(2,1)S(1)}, bf16[384,768]{1,0:T(8,128)(2,1)S(1)}, u32[]{:S(2)}, u32[]{:S(2)}) collective-permute-start(bf16[384,768]{1,0:T(8,128)(2,1)S(1)} %get-tuple-element.19.refs_0_.refs_8_), channel_id=1, source_target_pairs={{0,24},{4,28},{8,16},{12,20},{16,8},{20,12},{24,0},{28,4},{1,25},{... | collective-permute-start | bytes 1769480 | tf_op jit(solution)/shard_map/ppermute | solution.py:355
  73.9 2.2 %collective-permute-start.9 = (bf16[384,768]{1,0:T(8,128)(2,1)S(1)}, bf16[384,768]{1,0:T(8,128)(2,1)S(1)}, u32[]{:S(2)}, u32[]{:S(2)}) collective-permute-start(bf16[384,768]{1,0:T(8,128)(2,1)S(1)} %get-tuple-element.19.refs_0_.refs_8_), channel_id=1, source_target_pairs={{0,16},{4,20},{8,24},{12,28},{16,0},{20,4},{24,8},{28,12},{1,17},{... | collective-permute-start | bytes 1769480 | tf_op jit(solution)/shard_map/ppermute | solution.py:355
  76.2 13.2 %collective-permute-done.10.refs_3_.refs_11_ = bf16[384,768]{1,0:T(8,128)(2,1)S(1)} collective-permute-done((bf16[384,768]{1,0:T(8,128)(2,1)S(1)}, bf16[384,768]{1,0:T(8,128)(2,1)S(1)}, u32[]{:S(2)}, u32[]{:S(2)}) %collective-permute-start.10) | collective-permute-done | bytes 589856 | tf_op jit(solution)/shard_map/ppermute | solution.py:355
  89.3 10.0 %collective-permute-done.9.refs_2_.refs_10_ = bf16[384,768]{1,0:T(8,128)(2,1)S(1)} collective-permute-done((bf16[384,768]{1,0:T(8,128)(2,1)S(1)}, bf16[384,768]{1,0:T(8,128)(2,1)S(1)}, u32[]{:S(2)}, u32[]{:S(2)}) %collective-permute-start.9) | collective-permute-done | bytes 589856 | tf_op jit(solution)/shard_map/ppermute | solution.py:355
  99.8 1.5 collective-permute-done.13.refs_6_.refs_14_
  102.2 17.4 %attend.1 = (f32[384,384]{1,0:T(8,128)S(1)}, bf16[384,384]{1,0:T(8,128)(2,1)S(1)}, bf16[384,384]{1,0:T(8,128)(2,1)S(1)}, bf16[384,384]{1,0:T(8,128)(2,1)S(1)}) custom-call(bf16[384,384]{1,0:T(8,128)(2,1)S(1)} %get-tuple-element.18.q_ref, bf16[384,768]{1,0:T(8,128)(2,1)S(1)} %get-tuple-element.19.refs_0_.refs_8_, ...), custom_call_target="tpu_custom_call" | custom-call | flops 2264924160 | bytes 8257536 | tf_op jit(solution)/shard_map/attend/pallas_call | solution.py:333
  119.6 7.2 %collective-permute-start.15 = (bf16[384,384]{1,0:T(8,128)(2,1)S(1)}, bf16[384,384]{1,0:T(8,128)(2,1)S(1)}, u32[]{:S(2)}, u32[]{:S(2)}) collective-permute-start(bf16[384,384]{1,0:T(8,128)(2,1)S(1)} %get-tuple-element.22), channel_id=1, source_target_pairs={{0,1},{1,2},{2,3},{3,0},{4,5},{5,6},{6,7},{7,4},{8,9},{9,10},{10,1... | collective-permute-start | bytes 884744 | tf_op jit(solution)/shard_map/ppermute | solution.py:371
  126.8 1.5 %collective-permute-start.17 = (bf16[384,384]{1,0:T(8,128)(2,1)S(1)}, bf16[384,384]{1,0:T(8,128)(2,1)S(1)}, u32[]{:S(2)}, u32[]{:S(2)}) collective-permute-start(bf16[384,384]{1,0:T(8,128)(2,1)S(1)} %get-tuple-element.24), channel_id=1, source_target_pairs={{0,2},{1,3},{2,0},{3,1},{4,6},{5,7},{6,4},{7,5},{8,10},{9,11},{10,... | collective-permute-start | bytes 884744 | tf_op jit(solution)/shard_map/ppermute | solution.py:371
  128.3 5.8 %collective-permute-done.15 = bf16[384,384]{1,0:T(8,128)(2,1)S(1)} collective-permute-done((bf16[384,384]{1,0:T(8,128)(2,1)S(1)}, bf16[384,384]{1,0:T(8,128)(2,1)S(1)}, u32[]{:S(2)}, u32[]{:S(2)}) %collective-permute-start.15) | collective-permute-done | bytes 294944 | tf_op jit(solution)/shard_map/ppermute | solution.py:371
  134.2 6.4 %collective-permute-done.16 = bf16[384,384]{1,0:T(8,128)(2,1)S(1)} collective-permute-done((bf16[384,384]{1,0:T(8,128)(2,1)S(1)}, bf16[384,384]{1,0:T(8,128)(2,1)S(1)}, u32[]{:S(2)}, u32[]{:S(2)}) %collective-permute-start.16) | collective-permute-done | bytes 294944 | tf_op jit(solution)/shard_map/ppermute | solution.py:371
  140.5 8.9 %collective-permute-done.17 = bf16[384,384]{1,0:T(8,128)(2,1)S(1)} collective-permute-done((bf16[384,384]{1,0:T(8,128)(2,1)S(1)}, bf16[384,384]{1,0:T(8,128)(2,1)S(1)}, u32[]{:S(2)}, u32[]{:S(2)}) %collective-permute-start.17) | collective-permute-done | bytes 294944 | tf_op jit(solution)/shard_map/ppermute | solution.py:371
  (32 shorter events, 8.4 us)
Async XLA Ops:
  0.8 4.6 %collective-permute-start.1 = (bf16[16,768]{1,0:T(8,128)(2,1)S(1)}, bf16[16,768]{1,0:T(8,128)(2,1)S(1)}, u32[]{:S(2)}, u32[]{:S(2)}) collective-permute-start(bf16[16,768]{1,0:T(8,128)(2,1)S(1)} %get-tuple-element.25), channel_id=1, source_target_pairs={{4,0},{8,4},{12,8},{16,12},{20,16},{24,20},{28,24},{5,1},{9,5},{13... | collective-permute-start | bytes 73736 | tf_op jit(solution)/shard_map/ppermute | solution.py:361
  2.0 35.3 %copy-start = (bf16[3,384,1536]{2,1,0:T(8,128)(2,1)S(1)}, bf16[3,384,1536]{2,1,0:T(8,128)(2,1)}, u32[]{:S(2)}) copy-start(bf16[3,384,1536]{2,1,0:T(8,128)(2,1)} %weight_ref.3) | copy-start | bytes 10616836
  2.1 4.1 %collective-permute-start = (bf16[16,768]{1,0:T(8,128)(2,1)S(1)}, bf16[16,768]{1,0:T(8,128)(2,1)S(1)}, u32[]{:S(2)}, u32[]{:S(2)}) collective-permute-start(bf16[16,768]{1,0:T(8,128)(2,1)S(1)} %get-tuple-element.26), channel_id=1, source_target_pairs={{0,4},{4,8},{8,12},{12,16},{16,20},{20,24},{24,28},{1,5},{5,9},{9,... | collective-permute-start | bytes 73736 | tf_op jit(solution)/shard_map/ppermute | solution.py:360
  7.5 1.8 %copy-start.2 = (bf16[5,384,768]{2,1,0:T(8,128)(2,1)S(1)}, bf16[5,384,768]{2,1,0:T(8,128)(2,1)}, u32[]{:S(2)}) copy-start(bf16[5,384,768]{2,1,0:T(8,128)(2,1)} %weight_ref.2) | copy-start | bytes 8847364
  11.1 18.1 %collective-permute-start.4 = (bf16[392,384]{1,0:T(8,128)(2,1)S(1)}, bf16[392,384]{1,0:T(8,128)(2,1)S(1)}, u32[]{:S(2)}, u32[]{:S(2)}) collective-permute-start(bf16[392,384]{1,0:T(8,128)(2,1)S(1)} %get-tuple-element.15.a0), channel_id=1, source_target_pairs={{0,2},{1,3},{2,0},{3,1},{4,6},{5,7},{6,4},{7,5},{8,10},{9,11},{10,... | collective-permute-start | bytes 903176 | tf_op jit(solution)/shard_map/ppermute | solution.py:145
  15.2 15.0 %collective-permute-start.3 = (bf16[392,384]{1,0:T(8,128)(2,1)S(1)}, bf16[392,384]{1,0:T(8,128)(2,1)S(1)}, u32[]{:S(2)}, u32[]{:S(2)}) collective-permute-start(bf16[392,384]{1,0:T(8,128)(2,1)S(1)} %get-tuple-element.15.a0), channel_id=1, source_target_pairs={{0,3},{1,0},{2,1},{3,2},{4,7},{5,4},{6,5},{7,6},{8,11},{9,8},{10,9... | collective-permute-start | bytes 903176 | tf_op jit(solution)/shard_map/ppermute | solution.py:145
  16.5 20.8 %collective-permute-start.2 = (bf16[392,384]{1,0:T(8,128)(2,1)S(1)}, bf16[392,384]{1,0:T(8,128)(2,1)S(1)}, u32[]{:S(2)}, u32[]{:S(2)}) collective-permute-start(bf16[392,384]{1,0:T(8,128)(2,1)S(1)} %get-tuple-element.15.a0), channel_id=1, source_target_pairs={{0,1},{1,2},{2,3},{3,0},{4,5},{5,6},{6,7},{7,4},{8,9},{9,10},{10,1... | collective-permute-start | bytes 903176 | tf_op jit(solution)/shard_map/ppermute | solution.py:145
  37.3 32.3 %copy-start.3 = (bf16[384,1536]{1,0:T(8,128)(2,1)S(1)}, bf16[384,1536]{1,0:T(8,128)(2,1)}, u32[]{:S(2)}) copy-start(bf16[384,1536]{1,0:T(8,128)(2,1)} %wq.1) | copy-start | bytes 3538948
  37.3 32.3 %copy-start.4 = (bf16[384,1536]{1,0:T(8,128)(2,1)S(1)}, bf16[384,1536]{1,0:T(8,128)(2,1)}, u32[]{:S(2)}) copy-start(bf16[384,1536]{1,0:T(8,128)(2,1)} %wk.1) | copy-start | bytes 3538948
  37.3 32.3 %copy-start.5 = (bf16[384,1536]{1,0:T(8,128)(2,1)S(1)}, bf16[384,1536]{1,0:T(8,128)(2,1)}, u32[]{:S(2)}) copy-start(bf16[384,1536]{1,0:T(8,128)(2,1)} %wv.1) | copy-start | bytes 3538948
  40.2 61.9 %copy-start.6 = (bf16[384,1536]{1,0:T(8,128)(2,1)S(1)}, bf16[384,1536]{1,0:T(8,128)(2,1)}, u32[]{:S(2)}) copy-start(bf16[384,1536]{1,0:T(8,128)(2,1)} %refs_16_.1) | copy-start | bytes 3538948
  40.3 22.9 %collective-permute-start.7 = (bf16[384,384]{1,0:T(8,128)(2,1)S(1)}, bf16[384,384]{1,0:T(8,128)(2,1)S(1)}, u32[]{:S(2)}, u32[]{:S(2)}) collective-permute-start(bf16[384,384]{1,0:T(8,128)(2,1)S(1)} %get-tuple-element.17.a0), channel_id=1, source_target_pairs={{0,2},{1,3},{2,0},{3,1},{4,6},{5,7},{6,4},{7,5},{8,10},{9,11},{10,... | collective-permute-start | bytes 884744 | tf_op jit(solution)/shard_map/ppermute | solution.py:145
  48.5 21.1 %collective-permute-start.6 = (bf16[384,384]{1,0:T(8,128)(2,1)S(1)}, bf16[384,384]{1,0:T(8,128)(2,1)S(1)}, u32[]{:S(2)}, u32[]{:S(2)}) collective-permute-start(bf16[384,384]{1,0:T(8,128)(2,1)S(1)} %get-tuple-element.17.a0), channel_id=1, source_target_pairs={{0,3},{1,0},{2,1},{3,2},{4,7},{5,4},{6,5},{7,6},{8,11},{9,8},{10,9... | collective-permute-start | bytes 884744 | tf_op jit(solution)/shard_map/ppermute | solution.py:145
  48.9 20.7 %collective-permute-start.5 = (bf16[384,384]{1,0:T(8,128)(2,1)S(1)}, bf16[384,384]{1,0:T(8,128)(2,1)S(1)}, u32[]{:S(2)}, u32[]{:S(2)}) collective-permute-start(bf16[384,384]{1,0:T(8,128)(2,1)S(1)} %get-tuple-element.17.a0), channel_id=1, source_target_pairs={{0,1},{1,2},{2,3},{3,0},{4,5},{5,6},{6,7},{7,4},{8,9},{9,10},{10,1... | collective-permute-start | bytes 884744 | tf_op jit(solution)/shard_map/ppermute | solution.py:145
  72.1 17.3 %collective-permute-start.10 = (bf16[384,768]{1,0:T(8,128)(2,1)S(1)}, bf16[384,768]{1,0:T(8,128)(2,1)S(1)}, u32[]{:S(2)}, u32[]{:S(2)}) collective-permute-start(bf16[384,768]{1,0:T(8,128)(2,1)S(1)} %get-tuple-element.19.refs_0_.refs_8_), channel_id=1, source_target_pairs={{0,24},{4,28},{8,16},{12,20},{16,8},{20,12},{24,0},{28,4},{1,25},{... | collective-permute-start | bytes 1769480 | tf_op jit(solution)/shard_map/ppermute | solution.py:355
  73.9 25.4 %collective-permute-start.9 = (bf16[384,768]{1,0:T(8,128)(2,1)S(1)}, bf16[384,768]{1,0:T(8,128)(2,1)S(1)}, u32[]{:S(2)}, u32[]{:S(2)}) collective-permute-start(bf16[384,768]{1,0:T(8,128)(2,1)S(1)} %get-tuple-element.19.refs_0_.refs_8_), channel_id=1, source_target_pairs={{0,16},{4,20},{8,24},{12,28},{16,0},{20,4},{24,8},{28,12},{1,17},{... | collective-permute-start | bytes 1769480 | tf_op jit(solution)/shard_map/ppermute | solution.py:355
  76.2 23.2 %collective-permute-start.8 = (bf16[384,768]{1,0:T(8,128)(2,1)S(1)}, bf16[384,768]{1,0:T(8,128)(2,1)S(1)}, u32[]{:S(2)}, u32[]{:S(2)}) collective-permute-start(bf16[384,768]{1,0:T(8,128)(2,1)S(1)} %get-tuple-element.19.refs_0_.refs_8_), channel_id=1, source_target_pairs={{0,8},{4,12},{8,0},{12,4},{16,24},{20,28},{24,16},{28,20},{1,9},{5... | collective-permute-start | bytes 1769480 | tf_op jit(solution)/shard_map/ppermute | solution.py:355
  76.2 23.6 %collective-permute-start.11 = (bf16[384,768]{1,0:T(8,128)(2,1)S(1)}, bf16[384,768]{1,0:T(8,128)(2,1)S(1)}, u32[]{:S(2)}, u32[]{:S(2)}) collective-permute-start(bf16[384,768]{1,0:T(8,128)(2,1)S(1)} %get-tuple-element.19.refs_0_.refs_8_), channel_id=1, source_target_pairs={{0,4},{4,0},{8,12},{12,8},{16,20},{20,16},{24,28},{28,24},{1,5},{5... | collective-permute-start | bytes 1769480 | tf_op jit(solution)/shard_map/ppermute | solution.py:355
  89.3 10.5 %collective-permute-start.14 = (bf16[384,768]{1,0:T(8,128)(2,1)S(1)}, bf16[384,768]{1,0:T(8,128)(2,1)S(1)}, u32[]{:S(2)}, u32[]{:S(2)}) collective-permute-start(bf16[384,768]{1,0:T(8,128)(2,1)S(1)} %collective-permute-done.10.refs_3_.refs_11_), channel_id=1, source_target_pairs={{0,4},{4,0},{8,12},{12,8},{16,20},{20,16},{24,28},{28,24},{1,5},{5... | collective-permute-start | bytes 1769480 | tf_op jit(solution)/shard_map/ppermute | solution.py:355
  99.3 2.0 %collective-permute-start.13 = (bf16[384,768]{1,0:T(8,128)(2,1)S(1)}, bf16[384,768]{1,0:T(8,128)(2,1)S(1)}, u32[]{:S(2)}, u32[]{:S(2)}) collective-permute-start(bf16[384,768]{1,0:T(8,128)(2,1)S(1)} %collective-permute-done.9.refs_2_.refs_10_), channel_id=1, source_target_pairs={{0,4},{4,0},{8,12},{12,8},{16,20},{20,16},{24,28},{28,24},{1,5},{5... | collective-permute-start | bytes 1769480 | tf_op jit(solution)/shard_map/ppermute | solution.py:355
  99.3 2.8 %collective-permute-start.12 = (bf16[384,768]{1,0:T(8,128)(2,1)S(1)}, bf16[384,768]{1,0:T(8,128)(2,1)S(1)}, u32[]{:S(2)}, u32[]{:S(2)}) collective-permute-start(bf16[384,768]{1,0:T(8,128)(2,1)S(1)} %collective-permute-done.8.refs_1_.refs_9_), channel_id=1, source_target_pairs={{0,4},{4,0},{8,12},{12,8},{16,20},{20,16},{24,28},{28,24},{1,5},{5... | collective-permute-start | bytes 1769480 | tf_op jit(solution)/shard_map/ppermute | solution.py:355
  119.6 14.6 %collective-permute-start.15 = (bf16[384,384]{1,0:T(8,128)(2,1)S(1)}, bf16[384,384]{1,0:T(8,128)(2,1)S(1)}, u32[]{:S(2)}, u32[]{:S(2)}) collective-permute-start(bf16[384,384]{1,0:T(8,128)(2,1)S(1)} %get-tuple-element.22), channel_id=1, source_target_pairs={{0,1},{1,2},{2,3},{3,0},{4,5},{5,6},{6,7},{7,4},{8,9},{9,10},{10,1... | collective-permute-start | bytes 884744 | tf_op jit(solution)/shard_map/ppermute | solution.py:371
  126.8 13.7 %collective-permute-start.16 = (bf16[384,384]{1,0:T(8,128)(2,1)S(1)}, bf16[384,384]{1,0:T(8,128)(2,1)S(1)}, u32[]{:S(2)}, u32[]{:S(2)}) collective-permute-start(bf16[384,384]{1,0:T(8,128)(2,1)S(1)} %get-tuple-element.23), channel_id=1, source_target_pairs={{0,3},{1,0},{2,1},{3,2},{4,7},{5,4},{6,5},{7,6},{8,11},{9,8},{10,9... | collective-permute-start | bytes 884744 | tf_op jit(solution)/shard_map/ppermute | solution.py:371
  126.8 22.6 %collective-permute-start.17 = (bf16[384,384]{1,0:T(8,128)(2,1)S(1)}, bf16[384,384]{1,0:T(8,128)(2,1)S(1)}, u32[]{:S(2)}, u32[]{:S(2)}) collective-permute-start(bf16[384,384]{1,0:T(8,128)(2,1)S(1)} %get-tuple-element.24), channel_id=1, source_target_pairs={{0,2},{1,3},{2,0},{3,1},{4,6},{5,7},{6,4},{7,5},{8,10},{9,11},{10,... | collective-permute-start | bytes 884744 | tf_op jit(solution)/shard_map/ppermute | solution.py:371
  (1 other events, 1.3 us)

commit v2 on v0

--- a/solution.py
+++ b/solution.py
@@ -1,14 +1,21 @@
+import functools
 import math
 
 import jax
 import jax.numpy as jnp
 from jax import lax
+from jax.experimental import pallas as pl
+from jax.experimental.pallas import tpu as pltpu
 from jax.sharding import PartitionSpec as P
 
 C = 1536
 HEAD_DIM = 64
 KW = 5
 DILATION_STEP = 4
+EPS = 1e-06
+EDGE = 16
+LOG2E = math.log2(math.e)
+MIB = 1 << 20
 
 
 def padded_2(block, sides, width):
@@ -26,7 +33,7 @@
 
 def row_scale(hidden):
     squares = lax.psum(jnp.sum(hidden * hidden, axis=1), "head")
-    return hidden * lax.rsqrt(squares / C + 1e-06)[:, None]
+    return hidden * lax.rsqrt(squares / C + EPS)[:, None]
 
 
 def reduce_operands(left, right):
@@ -35,7 +42,7 @@
     )
 
 
-def on_device(dna, conv_in, dilated_kernel_weight, w_query, w_key, w_value, w_out):
+def general_form(dna, conv_in, dilated_kernel_weight, w_query, w_key, w_value, w_out):
     local_row_count = dna.shape[0] // 2
     half = (KW - 1) // 2
     padded = padded_2(dna, (("seq", 0),), half)
@@ -62,15 +69,8 @@
     normed = row_scale(second_hidden).astype(jnp.bfloat16)
     local_width = w_query.shape[0]
     heads_here = local_width // HEAD_DIM
-    empty = jnp.zeros((local_row_count, local_width), jnp.float32)
-    totals = (empty, empty, empty)
     piece = lax.all_gather(normed, "head", axis=1, tiled=True)
-    count = piece.shape[1]
-    outs = []
-    for total, weight in zip(totals, (w_query, w_key, w_value)):
-        block = lax.slice_in_dim(weight, 0, count, axis=1)
-        outs.append(total + reduce_operands(piece, block))
-    q_acc, k_acc, v_acc = tuple(outs)
+    q_acc, k_acc, v_acc = (reduce_operands(piece, w) for w in (w_query, w_key, w_value))
     query = q_acc.astype(jnp.bfloat16).reshape(local_row_count, heads_here, HEAD_DIM)
     keys = k_acc.astype(jnp.bfloat16)
     values = v_acc.astype(jnp.bfloat16)
@@ -121,6 +121,440 @@
     return (second_hidden + mixed).astype(jnp.bfloat16)
 
 
+def nbytes(*arrays):
+    return sum(math.prod(a.shape) * jnp.dtype(a.dtype).itemsize for a in arrays)
+
+
+def cost(flops, arrays, transcendentals=0):
+    return pl.CostEstimate(
+        flops=int(flops), bytes_accessed=int(nbytes(*arrays)), transcendentals=int(transcendentals)
+    )
+
+
+def rotate(offset):
+    count = lax.axis_size("head")
+    return [(i, (i + offset) % count) for i in range(count)]
+
+
+def shared(block):
+    count = lax.axis_size("head")
+    return [block] + [lax.ppermute(block, "head", rotate(k)) for k in (1, count - 1, 2)]
+
+
+def owner(k):
+    count = lax.axis_size("head")
+    return lax.rem(lax.axis_index("head") + count - k, count)
+
+
+SHIFTS = (0, 1, 3, 2)
+
+
+def store_wide(wide, start, block):
+    for j in range(wide.shape[0]):
+        rows = pl.ds(start, block.shape[0])
+        wide[j, rows, :] = block[:, 128 * j : 128 * (j + 1)].astype(jnp.float32)
+
+
+def taps_sum(wide, weight_ref, groups):
+    total = None
+    for tap in range(KW):
+        picked = []
+        for start, count in groups:
+            lanes = [
+                wide[j, pl.ds(start + tap, count, stride=2), :] for j in range(wide.shape[0])
+            ]
+            picked.append(jnp.concatenate(lanes, axis=1).astype(jnp.bfloat16))
+        taken = picked[0] if len(picked) == 1 else jnp.concatenate(picked, axis=0)
+        term = reduce_operands(taken, weight_ref[tap])
+        total = term if total is None else total + term
+    return total
+
+
+FIRST = EDGE - KW // 2
+
+
+def conv_middle_kernel(dna_ref, weight_ref, h1_ref, sent_ref, wide):
+    store_wide(wide, 0, dna_ref[pl.ds(0, wide.shape[1]), :])
+    total = taps_sum(wide, weight_ref, [(FIRST, sent_ref.shape[0])])
+    h1_ref[...] = total
+    sent_ref[...] = total.astype(jnp.bfloat16)
+
+
+def conv_edge_kernel(dna_ref, low_ref, high_ref, weight_ref, h1_ref, sent_ref, wide):
+    rows = dna_ref.shape[0]
+    upper = sent_ref.shape[0] - EDGE
+    first = rows - 2 * upper
+    zeros = jnp.zeros((EDGE, dna_ref.shape[1]), jnp.bfloat16)
+    store_wide(wide, 0, zeros)
+    store_wide(wide, EDGE, low_ref[...])
+    store_wide(wide, 2 * EDGE, dna_ref[pl.ds(0, 2 * EDGE), :])
+    store_wide(wide, 4 * EDGE, dna_ref[pl.ds(first, rows - first), :])
+    store_wide(wide, 4 * EDGE + rows - first, high_ref[...])
+    store_wide(wide, 5 * EDGE + rows - first, zeros)
+    total = taps_sum(wide, weight_ref, [(FIRST, EDGE), (4 * EDGE + FIRST, upper)])
+    h1_ref[...] = total
+    sent_ref[...] = total.astype(jnp.bfloat16)
+
+
+def first_conv(kernel, operands, weight, count, deep, name):
+    width, out = weight.shape[2], weight.shape[1]
+    kept = jax.ShapeDtypeStruct((count, out), jnp.float32)
+    sent = jax.ShapeDtypeStruct((count, out), jnp.bfloat16)
+    return pl.pallas_call(
+        kernel,
+        out_shape=(kept, sent),
+        scratch_shapes=[pltpu.VMEM((width // 128, deep, 128), jnp.float32)],
+        compiler_params=pltpu.CompilerParams(vmem_limit_bytes=24 * MIB),
+        cost_estimate=cost(2 * count * out * width * KW, (*operands, weight, kept, sent)),
+        name=name,
+    )(*operands, weight)
+
+
+def inverse_norm(blocks):
+    squares = None
+    for block in blocks:
+        term = jnp.sum(block * block, axis=1, keepdims=True)
+        squares = term if squares is None else squares + term
+    return lax.rsqrt(squares / C + EPS)
+
+
+def wide_blocks(parts, start, count):
+    return [part[pl.ds(start, count), :].astype(jnp.float32) for part in parts]
+
+
+def gelu(value):
+    return jax.nn.gelu(value, approximate=True)
+
+
+def columns_of(shift, width):
+    return pl.ds(pl.multiple_of(owner(shift) * width, 128), width)
+
+
+def dilated_middle_kernel(a0, a1, a2, a3, h1_ref, weight_ref, h2_ref, sent_ref, act):
+    parts = (a0, a1, a2, a3)
+    count, width = a0.shape
+    rows = h2_ref.shape[0]
+    blocks = wide_blocks(parts, 0, count)
+    inverse = inverse_norm(blocks)
+    total = h1_ref[pl.ds(8, rows), :]
+    for slot, (block, shift) in enumerate(zip(blocks, SHIFTS)):
+        act[slot] = gelu(block * inverse)
+        for tap in range(3):
+            taken = act[slot, pl.ds((tap + 1) * DILATION_STEP, rows), :].astype(jnp.bfloat16)
+            total = total + reduce_operands(taken, weight_ref[tap, :, columns_of(shift, width)])
+    h2_ref[...] = total
+    sent_ref[...] = total.astype(jnp.bfloat16)
+
+
+def dilated_edge_kernel(
+    m0, m1, m2, m3, e0, e1, e2, e3, hm_ref, he_ref, h2m_ref, weight_ref, h2_ref, sent_ref, act
+):
+    middle, edge = (m0, m1, m2, m3), (e0, e1, e2, e3)
+    inner, width = m0.shape
+    outer = e0.shape[0]
+    rows = h2_ref.shape[0]
+    upper = outer - EDGE
+    position = lax.axis_index("seq") * rows + lax.broadcasted_iota(jnp.int32, (outer, 1), 0)
+    place = lax.broadcasted_iota(jnp.int32, (outer, 1), 0)
+    position = position + jnp.where(place < EDGE, -8, inner - 8)
+    inside = (position >= 0) & (position < rows * lax.axis_size("seq"))
+    outer_blocks = wide_blocks(edge, 0, outer)
+    outer_inverse = jnp.where(inside, inverse_norm(outer_blocks), 0.0)
+    low_blocks = wide_blocks(middle, 0, EDGE)
+    low_inverse = inverse_norm(low_blocks)
+    high_blocks = wide_blocks(middle, inner - EDGE, EDGE)
+    high_inverse = inverse_norm(high_blocks)
+    last = rows - (outer - EDGE)
+    total = jnp.concatenate(
+        [
+            he_ref[pl.ds(8, 8), :],
+            hm_ref[pl.ds(0, 8), :],
+            hm_ref[pl.ds(inner - 8, 8), :],
+            he_ref[pl.ds(EDGE, upper - 8), :],
+        ],
+        axis=0,
+    )
+    tail = 2 * EDGE
+    for slot, shift in enumerate(SHIFTS):
+        full = gelu(outer_blocks[slot] * outer_inverse)
+        act[slot, pl.ds(0, EDGE), :] = full[:EDGE]
+        act[slot, pl.ds(EDGE, EDGE), :] = gelu(low_blocks[slot] * low_inverse)
+        act[slot, pl.ds(tail, EDGE), :] = gelu(high_blocks[slot] * high_inverse)
+        act[slot, pl.ds(tail + EDGE, upper), :] = full[EDGE:]
+        for tap in range(3):
+            shifted = (tap + 1) * DILATION_STEP
+            taken = jnp.concatenate(
+                [
+                    act[slot, pl.ds(shifted, EDGE), :],
+                    act[slot, pl.ds(tail + shifted, upper), :],
+                ],
+                axis=0,
+            ).astype(jnp.bfloat16)
+            total = total + reduce_operands(taken, weight_ref[tap, :, columns_of(shift, width)])
+    h2_ref[pl.ds(0, EDGE), :] = total[:EDGE]
+    h2_ref[pl.ds(EDGE, last - EDGE), :] = h2m_ref[...]
+    h2_ref[pl.ds(last, rows - last), :] = total[EDGE:]
+    sent_ref[...] = total.astype(jnp.bfloat16)
+
+
+def second_conv(kernel, operands, weight, kept_rows, sent_rows, deep, name):
+    out, width = weight.shape[1], operands[0].shape[1]
+    kept = jax.ShapeDtypeStruct((kept_rows, out), jnp.float32)
+    sent = jax.ShapeDtypeStruct((sent_rows, out), jnp.bfloat16)
+    return pl.pallas_call(
+        kernel,
+        out_shape=(kept, sent),
+        scratch_shapes=[pltpu.VMEM((4, deep, width), jnp.float32)],
+        compiler_params=pltpu.CompilerParams(vmem_limit_bytes=24 * MIB),
+        cost_estimate=cost(
+            2 * sent_rows * out * weight.shape[2] * 3,
+            (*operands, weight, kept, sent),
+            deep * weight.shape[2],
+        ),
+        name=name,
+    )(*operands, weight)
+
+
+def projections(parts, wq, wk, wv, kv_ref):
+    width = parts[0].shape[1]
+    inverse = inverse_norm([part[...].astype(jnp.float32) for part in parts])
+
+    def product(weight_ref):
+        total = None
+        for part, shift in zip(parts, SHIFTS):
+            term = reduce_operands(part[...], weight_ref[:, columns_of(shift, width)])
+            total = term if total is None else total + term
+        return total
+
+    out = wq.shape[0]
+    kv_ref[:, :out] = (product(wk) * inverse).astype(jnp.bfloat16)
+    kv_ref[:, out:] = (product(wv) * inverse).astype(jnp.bfloat16)
+    scale = LOG2E / math.sqrt(HEAD_DIM)
+    return (product(wq) * (inverse * scale)).astype(jnp.bfloat16)
+
+
+def project_middle_kernel(a0, a1, a2, a3, wq, wk, wv, q_ref, kv_ref):
+    q_ref[...] = projections((a0, a1, a2, a3), wq, wk, wv, kv_ref)
+
+
+def project_edge_kernel(a0, a1, a2, a3, qm_ref, wq, wk, wv, q_ref, kv_ref):
+    query = projections((a0, a1, a2, a3), wq, wk, wv, kv_ref)
+    inner, rows = qm_ref.shape[0], q_ref.shape[0]
+    q_ref[pl.ds(0, EDGE), :] = query[:EDGE]
+    q_ref[pl.ds(EDGE, inner), :] = qm_ref[...]
+    q_ref[pl.ds(EDGE + inner, rows - EDGE - inner), :] = query[EDGE:]
+
+
+def project(kernel, operands, weights, q_rows, name):
+    rows, out = operands[0].shape[0], weights[0].shape[0]
+    q = jax.ShapeDtypeStruct((q_rows, out), jnp.bfloat16)
+    kv = jax.ShapeDtypeStruct((rows, 2 * out), jnp.bfloat16)
+    return pl.pallas_call(
+        kernel,
+        out_shape=(q, kv),
+        compiler_params=pltpu.CompilerParams(vmem_limit_bytes=20 * MIB),
+        cost_estimate=cost(6 * rows * out * C, (*operands, *weights, q, kv)),
+        name=name,
+    )(*operands, *weights)
+
+
+TILE = 64
+
+
+def partial_attention(q_ref, blocks, scores, weights, head, lane):
+    rows = q_ref.shape[0]
+    width = q_ref.shape[1]
+    seen = blocks[0].shape[0]
+    pair = head // 2
+    lanes = pl.ds(pair * 2 * HEAD_DIM, 2 * HEAD_DIM)
+    mine = (lane // HEAD_DIM) == head % 2
+    query = q_ref[:, lanes]
+    query = jnp.where(mine, query, jnp.zeros_like(query))
+    for i, block in enumerate(blocks):
+        scores[:, pl.ds(i * seen, seen)] = reduce_operands(query, block[:, lanes])
+    tops, sums = [], []
+    extent = seen * len(blocks)
+    for start in range(0, rows, TILE):
+        tile = scores[pl.ds(start, TILE), pl.ds(0, extent)]
+        top = jnp.max(tile, axis=1, keepdims=True)
+        weight = jnp.exp2(tile - top)
+        sums.append(jnp.sum(weight, axis=1, keepdims=True))
+        tops.append(top)
+        weights[pl.ds(start, TILE), pl.ds(0, extent)] = weight.astype(jnp.bfloat16)
+    out = None
+    for i, block in enumerate(blocks):
+        value = block[:, pl.ds(width + pair * 2 * HEAD_DIM, 2 * HEAD_DIM)]
+        term = jnp.dot(
+            weights[:, pl.ds(i * seen, seen)], value, preferred_element_type=jnp.float32
+        )
+        out = term if out is None else out + term
+    return out, jnp.concatenate(tops, axis=0), jnp.concatenate(sums, axis=0)
+
+
+def attend_part_kernel(count, q_ref, *refs):
+    blocks = refs[:count]
+    out_ref, top_ref, sum_ref, scores, weights = refs[count:]
+    rows, width = q_ref.shape
+    lane = lax.broadcasted_iota(jnp.int32, (rows, 2 * HEAD_DIM), 1)
+    tops, sums = jnp.zeros_like(top_ref), jnp.zeros_like(sum_ref)
+    for pair in range(width // (2 * HEAD_DIM)):
+        halves = []
+        for half in range(2):
+            head = 2 * pair + half
+            out, top, total = partial_attention(
+                q_ref, blocks, scores.at[half], weights.at[half], head, lane
+            )
+            halves.append(out)
+            tops = jnp.where(lane == head, top, tops)
+            sums = jnp.where(lane == head, total, sums)
+        lanes = pl.ds(pair * 2 * HEAD_DIM, 2 * HEAD_DIM)
+        out_ref[:, lanes] = jnp.where(lane < HEAD_DIM, halves[0], halves[1])
+    top_ref[...] = tops
+    sum_ref[...] = sums
+
+
+def attend_last_kernel(count, earlier, q_ref, *refs):
+    blocks = refs[:count]
+    states = [refs[count + 3 * i : count + 3 * i + 3] for i in range(earlier)]
+    w_ref, h2_ref, own_ref, p1, p2, p3, scores, weights, attended = refs[count + 3 * earlier :]
+    rows, width = q_ref.shape
+    lane = lax.broadcasted_iota(jnp.int32, (rows, 2 * HEAD_DIM), 1)
+    for pair in range(width // (2 * HEAD_DIM)):
+        lanes = pl.ds(pair * 2 * HEAD_DIM, 2 * HEAD_DIM)
+        halves = []
+        for half in range(2):
+            head = 2 * pair + half
+            out, top, total = partial_attention(
+                q_ref, blocks, scores.at[half], weights.at[half], head, lane
+            )
+            tops = [top] + [state[1][:, head : head + 1] for state in states]
+            sums = [total] + [state[2][:, head : head + 1] for state in states]
+            outs = [out] + [state[0][:, lanes] for state in states]
+            highest = functools.reduce(jnp.maximum, tops)
+            factors = [jnp.exp2(one - highest) for one in tops]
+            norm = sum(f * one for f, one in zip(factors, sums))
+            mixed = sum(f * one for f, one in zip(factors, outs))
+            halves.append(mixed / norm)
+        merged = jnp.where(lane < HEAD_DIM, halves[0], halves[1])
+        attended[:, lanes] = merged.astype(jnp.bfloat16)
+
+    def product(shift):
+        return jnp.dot(
+            attended[...], w_ref[:, columns_of(shift, width)], preferred_element_type=jnp.float32
+        )
+
+    for ref, shift in ((p3, 2), (p1, 3), (p2, 1)):
+        ref[...] = product(shift).astype(jnp.bfloat16)
+    own_ref[...] = product(0) + h2_ref[...]
+
+
+def attention_scratch(rows, extent):
+    return [
+        pltpu.VMEM((2, rows, extent), jnp.float32),
+        pltpu.VMEM((2, rows, extent), jnp.bfloat16),
+    ]
+
+
+def attend_part(q, blocks, name):
+    rows, width = q.shape
+    extent = sum(block.shape[0] for block in blocks)
+    state = (
+        jax.ShapeDtypeStruct((rows, width), jnp.float32),
+        jax.ShapeDtypeStruct((rows, 2 * HEAD_DIM), jnp.float32),
+        jax.ShapeDtypeStruct((rows, 2 * HEAD_DIM), jnp.float32),
+    )
+    return pl.pallas_call(
+        functools.partial(attend_part_kernel, len(blocks)),
+        out_shape=state,
+        scratch_shapes=attention_scratch(rows, extent),
+        compiler_params=pltpu.CompilerParams(vmem_limit_bytes=24 * MIB),
+        cost_estimate=cost(
+            4 * rows * width * extent, (q, *blocks, *state), rows * extent * width // HEAD_DIM
+        ),
+        name=name,
+    )(q, *blocks)
+
+
+def attend_last(q, blocks, states, w_out, h2, name):
+    rows, width = q.shape
+    extent = sum(block.shape[0] for block in blocks)
+    own = jax.ShapeDtypeStruct((rows, width), jnp.float32)
+    part = jax.ShapeDtypeStruct((rows, width), jnp.bfloat16)
+    flat = [array for state in states for array in state]
+    return pl.pallas_call(
+        functools.partial(attend_last_kernel, len(blocks), len(states)),
+        out_shape=(own, part, part, part),
+        scratch_shapes=attention_scratch(rows, extent) + [pltpu.VMEM((rows, width), jnp.bfloat16)],
+        compiler_params=pltpu.CompilerParams(vmem_limit_bytes=24 * MIB),
+        cost_estimate=cost(
+            4 * rows * width * extent + 2 * rows * width * w_out.shape[1],
+            (q, *blocks, *flat, w_out, h2, own, part, part, part),
+            rows * extent * width // HEAD_DIM,
+        ),
+        name=name,
+    )(q, *blocks, *flat, w_out, h2)
+
+
+def exchanged(block, mask):
+    count = lax.axis_size("seq")
+    return lax.ppermute(block, "seq", [(i, i ^ mask) for i in range(count)])
+
+
+def on_device(dna, conv_in, dilated_kernel_weight, w_query, w_key, w_value, w_out):
+    count = lax.axis_size("seq")
+    rows = dna.shape[0] // 2
+    inner = rows // 2
+    low = lax.ppermute(dna[-EDGE:], "seq", [(i, i + 1) for i in range(count - 1)])
+    high = lax.ppermute(dna[:EDGE], "seq", [(i + 1, i) for i in range(count - 1)])
+    h1_m, sent = first_conv(
+        conv_middle_kernel, (dna,), conv_in, inner + EDGE, rows + 4 * EDGE, "conv_middle"
+    )
+    wide_m = shared(sent)
+    h1_e, sent = first_conv(
+        conv_edge_kernel, (dna, low, high), conv_in, inner, rows + 4 * EDGE, "conv_edge"
+    )
+    wide_e = shared(sent)
+    h2_m, sent = second_conv(
+        dilated_middle_kernel,
+        (*wide_m, h1_m),
+        dilated_kernel_weight,
+        inner,
+        inner,
+        inner + EDGE,
+        "dilated_middle",
+    )
+    normed_m = shared(sent)
+    h2, sent = second_conv(
+        dilated_edge_kernel,
+        (*wide_m, *wide_e, h1_m, h1_e, h2_m),
+        dilated_kernel_weight,
+        rows,
+        inner,
+        inner + 2 * EDGE,
+        "dilated_edge",
+    )
+    normed_e = shared(sent)
+    weights = (w_query, w_key, w_value)
+    q_m, kv_m = project(project_middle_kernel, normed_m, weights, inner, "project_middle")
+    q, kv_e = project(project_edge_kernel, (*normed_e, q_m), weights, rows, "project_edge")
+
+    def with_near(block):
+        return [block, exchanged(block, 1)]
+
+    x_m, y_m = exchanged(kv_m, 2), exchanged(kv_m, 4)
+    d_m = exchanged(x_m, 4)
+    x_e, y_e = exchanged(kv_e, 2), exchanged(kv_e, 4)
+    d_e = exchanged(y_e, 2)
+    first = [kv for block in (kv_m, x_m, y_m, d_m) for kv in with_near(block)]
+    second = [kv for block in (kv_e, x_e, y_e) for kv in with_near(block)]
+    states = [attend_part(q, first, "attend_m"), attend_part(q, second, "attend_e")]
+    own, p1, p2, p3 = attend_last(q, with_near(d_e), states, w_out, h2, "attend_last")
+    total = own
+    for part, shift in ((p1, 1), (p2, 3), (p3, 2)):
+        total = total + lax.ppermute(part, "head", rotate(shift)).astype(jnp.float32)
+    return total.astype(jnp.bfloat16)
+
+
 def solution(mesh):
     in_specs = (
         P("seq", None),
@@ -132,6 +566,7 @@
         P("head", None),
     )
     out_specs = P("seq", "head")
-    return jax.shard_map(
-        on_device, mesh=mesh, in_specs=in_specs, out_specs=out_specs, check_vma=False
-    )
+    seq, head = mesh.shape["seq"], mesh.shape["head"]
+    aligned = (C // head) % 128 == 0
+    body = on_device if head == 4 and seq == 8 and aligned else general_form
+    return jax.shard_map(body, mesh=mesh, in_specs=in_specs, out_specs=out_specs, check_vma=False)

time: 287 us -> 143 us (0.50)
  the two profiles are of different devices: /device:TPU:0 before, /device:TPU:21 now
where the time goes in v2:
time: 143 us
  waiting for transfers between devices  65.8 us (46%)
  Pallas kernels  37.6 us (26%)
  starting transfers between devices  35 us (24%)
  local copies, waits for them, and re-layouts  3.13 us (2%)
    ppermute x3, waiting for transfers between devices, on_device(): lax.ppermute(part, 'head', rotate(shift)).astype(jnp.float32)  25 us
    ppermute x12, waiting for transfers between devices, shared(): lax.ppermute(block, 'head', rotate(k))  24.1 us
    pallas_call x2, Pallas kernels, attend_part(): pl.pallas_call(functools.partial(attend_part_kernel, len(blocks)), out_sh...  18.8 us
    ppermute x14, waiting for transfers between devices, exchanged(): return lax.ppermute(block, 'seq', [(i, i ^ mask) for i in range(count)])  13.2 us
    ppermute x12, starting transfers between devices, shared(): lax.ppermute(block, 'head', rotate(k))  13.2 us
    ppermute x14, starting transfers between devices, exchanged(): return lax.ppermute(block, 'seq', [(i, i ^ mask) for i in range(count)])  10.5 us
    pallas_call x1, Pallas kernels, attend_last(): pl.pallas_call(functools.partial(attend_last_kernel, len(blocks), len(sta...  10.1 us
    ppermute x3, starting transfers between devices, on_device(): lax.ppermute(part, 'head', rotate(shift)).astype(jnp.float32)  4.69 us
  transfers between devices with their start and end apart: 31, of which 14 were waited for; matrix products, arithmetic and copies ran while one was open for 0% of the time, Pallas kernels for 18%

profile of v2, /device:TPU:21, one launch (start us, length us, event | category | flops | bytes accessed | tf_op | source)
XLA Modules:
  0.0 142.6 jit_solution(5743299245023181542)
XLA Ops:
  0.0 1.8 %copy-done.1 = bf16[5,384,768]{2,1,0:T(8,128)(2,1)S(1)} copy-done((bf16[5,384,768]{2,1,0:T(8,128)(2,1)S(1)}, bf16[5,384,768]{2,1,0:T(8,128)(2,1)}, u32[]{:S(2)}) %copy-start.1) | copy-done | bytes 2949144
  5.8 2.0 %collective-permute-start.2 = (bf16[208,384]{1,0:T(8,128)(2,1)S(1)}, bf16[208,384]{1,0:T(8,128)(2,1)S(1)}, u32[]{:S(2)}, u32[]{:S(2)}) collective-permute-start(bf16[208,384]{1,0:T(8,128)(2,1)S(1)} %get-tuple-element.27.a0.m0), channel_id=1, source_target_pairs={{0,2},{1,3},{2,0},{3,1},{4,6},{5,7},{6,4},{7,5},{8,10},{9,11},{10,... | collective-permute-start | bytes 479240 | tf_op jit(solution)/shard_map/ppermute | solution.py:141
  7.8 4.4 %collective-permute-start.3 = (bf16[16,768]{1,0:T(8,128)(2,1)S(1)}, bf16[16,768]{1,0:T(8,128)(2,1)S(1)}, u32[]{:S(2)}, u32[]{:S(2)}) collective-permute-start(bf16[16,768]{1,0:T(8,128)(2,1)S(1)} %get-tuple-element.50), channel_id=1, source_target_pairs={{0,4},{4,8},{8,12},{12,16},{16,20},{20,24},{24,28},{1,5},{5,9},{9,... | collective-permute-start | bytes 73736 | tf_op jit(solution)/shard_map/ppermute | solution.py:507
  12.2 2.2 %collective-permute-start.4 = (bf16[16,768]{1,0:T(8,128)(2,1)S(1)}, bf16[16,768]{1,0:T(8,128)(2,1)S(1)}, u32[]{:S(2)}, u32[]{:S(2)}) collective-permute-start(bf16[16,768]{1,0:T(8,128)(2,1)S(1)} %get-tuple-element.49), channel_id=1, source_target_pairs={{4,0},{8,4},{12,8},{16,12},{20,16},{24,20},{28,24},{5,1},{9,5},{13... | collective-permute-start | bytes 73736 | tf_op jit(solution)/shard_map/ppermute | solution.py:508
  14.4 3.5 %collective-permute-done.4.high_ref = bf16[16,768]{1,0:T(8,128)(2,1)S(1)} collective-permute-done((bf16[16,768]{1,0:T(8,128)(2,1)S(1)}, bf16[16,768]{1,0:T(8,128)(2,1)S(1)}, u32[]{:S(2)}, u32[]{:S(2)}) %collective-permute-start.4) | collective-permute-done | bytes 24608 | tf_op jit(solution)/shard_map/ppermute | solution.py:508
  20.5 2.3 %collective-permute-start.7 = (bf16[192,384]{1,0:T(8,128)(2,1)S(1)}, bf16[192,384]{1,0:T(8,128)(2,1)S(1)}, u32[]{:S(2)}, u32[]{:S(2)}) collective-permute-start(bf16[192,384]{1,0:T(8,128)(2,1)S(1)} %get-tuple-element.28.e0), channel_id=1, source_target_pairs={{0,2},{1,3},{2,0},{3,1},{4,6},{5,7},{6,4},{7,5},{8,10},{9,11},{10,... | collective-permute-start | bytes 442376 | tf_op jit(solution)/shard_map/ppermute | solution.py:141
  26.0 1.9 %collective-permute-start.13 = (bf16[192,384]{1,0:T(8,128)(2,1)S(1)}, bf16[192,384]{1,0:T(8,128)(2,1)S(1)}, u32[]{:S(2)}, u32[]{:S(2)}) collective-permute-start(bf16[192,384]{1,0:T(8,128)(2,1)S(1)} %get-tuple-element.33.a0), channel_id=1, source_target_pairs={{0,2},{1,3},{2,0},{3,1},{4,6},{5,7},{6,4},{7,5},{8,10},{9,11},{10,... | collective-permute-start | bytes 442376 | tf_op jit(solution)/shard_map/ppermute | solution.py:141
  28.3 8.4 %collective-permute-done.7.e3 = bf16[192,384]{1,0:T(8,128)(2,1)S(1)} collective-permute-done((bf16[192,384]{1,0:T(8,128)(2,1)S(1)}, bf16[192,384]{1,0:T(8,128)(2,1)S(1)}, u32[]{:S(2)}, u32[]{:S(2)}) %collective-permute-start.7) | collective-permute-done | bytes 147488 | tf_op jit(solution)/shard_map/ppermute | solution.py:141
  40.0 3.9 %collective-permute-done.11.a1 = bf16[192,384]{1,0:T(8,128)(2,1)S(1)} collective-permute-done((bf16[192,384]{1,0:T(8,128)(2,1)S(1)}, bf16[192,384]{1,0:T(8,128)(2,1)S(1)}, u32[]{:S(2)}, u32[]{:S(2)}) %collective-permute-start.11) | collective-permute-done | bytes 147488 | tf_op jit(solution)/shard_map/ppermute | solution.py:141
  44.9 4.8 %collective-permute-done.13.a3 = bf16[192,384]{1,0:T(8,128)(2,1)S(1)} collective-permute-done((bf16[192,384]{1,0:T(8,128)(2,1)S(1)}, bf16[192,384]{1,0:T(8,128)(2,1)S(1)}, u32[]{:S(2)}, u32[]{:S(2)}) %collective-permute-start.13) | collective-permute-done | bytes 147488 | tf_op jit(solution)/shard_map/ppermute | solution.py:141
  52.3 4.2 %collective-permute-done.8.a1 = bf16[192,384]{1,0:T(8,128)(2,1)S(1)} collective-permute-done((bf16[192,384]{1,0:T(8,128)(2,1)S(1)}, bf16[192,384]{1,0:T(8,128)(2,1)S(1)}, u32[]{:S(2)}, u32[]{:S(2)}) %collective-permute-start.8) | collective-permute-done | bytes 147488 | tf_op jit(solution)/shard_map/ppermute | solution.py:141
  56.6 2.3 %collective-permute-done.10.a3 = bf16[192,384]{1,0:T(8,128)(2,1)S(1)} collective-permute-done((bf16[192,384]{1,0:T(8,128)(2,1)S(1)}, bf16[192,384]{1,0:T(8,128)(2,1)S(1)}, u32[]{:S(2)}, u32[]{:S(2)}) %collective-permute-start.10) | collective-permute-done | bytes 147488 | tf_op jit(solution)/shard_map/ppermute | solution.py:141
  63.6 5.0 %collective-permute-done.14.refs_4_ = bf16[192,768]{1,0:T(8,128)(2,1)S(1)} collective-permute-done((bf16[192,768]{1,0:T(8,128)(2,1)S(1)}, bf16[192,768]{1,0:T(8,128)(2,1)S(1)}, u32[]{:S(2)}, u32[]{:S(2)}) %collective-permute-start.14) | collective-permute-done | bytes 294944 | tf_op jit(solution)/shard_map/ppermute | solution.py:500
  68.7 2.2 %collective-permute-start.26 = (bf16[192,768]{1,0:T(8,128)(2,1)S(1)}, bf16[192,768]{1,0:T(8,128)(2,1)S(1)}, u32[]{:S(2)}, u32[]{:S(2)}) collective-permute-start(bf16[192,768]{1,0:T(8,128)(2,1)S(1)} %collective-permute-done.25.refs_2_), channel_id=1, source_target_pairs={{0,4},{4,0},{8,12},{12,8},{16,20},{20,16},{24,28},{28,24},{1,5},{5... | collective-permute-start | bytes 884744 | tf_op jit(solution)/shard_map/ppermute | solution.py:500
  70.9 4.0 %collective-permute-done.20.refs_4_ = bf16[192,768]{1,0:T(8,128)(2,1)S(1)} collective-permute-done((bf16[192,768]{1,0:T(8,128)(2,1)S(1)}, bf16[192,768]{1,0:T(8,128)(2,1)S(1)}, u32[]{:S(2)}, u32[]{:S(2)}) %collective-permute-start.20) | collective-permute-done | bytes 294944 | tf_op jit(solution)/shard_map/ppermute | solution.py:500
  74.9 2.2 %collective-permute-start.27 = (bf16[192,768]{1,0:T(8,128)(2,1)S(1)}, bf16[192,768]{1,0:T(8,128)(2,1)S(1)}, u32[]{:S(2)}, u32[]{:S(2)}) collective-permute-start(bf16[192,768]{1,0:T(8,128)(2,1)S(1)} %collective-permute-done.14.refs_4_), channel_id=1, source_target_pairs={{0,4},{4,0},{8,12},{12,8},{16,20},{20,16},{24,28},{28,24},{1,5},{5... | collective-permute-start | bytes 884744 | tf_op jit(solution)/shard_map/ppermute | solution.py:500
  77.1 4.2 %collective-permute-done.22.refs_6_ = bf16[192,768]{1,0:T(8,128)(2,1)S(1)} collective-permute-done((bf16[192,768]{1,0:T(8,128)(2,1)S(1)}, bf16[192,768]{1,0:T(8,128)(2,1)S(1)}, u32[]{:S(2)}, u32[]{:S(2)}) %collective-permute-start.22) | collective-permute-done | bytes 294944 | tf_op jit(solution)/shard_map/ppermute | solution.py:500
  83.1 8.8 %attend_e.1 = (f32[384,384]{1,0:T(8,128)S(1)}, f32[384,128]{1,0:T(8,128)S(1)}, f32[384,128]{1,0:T(8,128)S(1)}) custom-call(bf16[384,384]{1,0:T(8,128)(2,1)S(1)} %get-tuple-element.35.q_ref, bf16[192,768]{1,0:T(8,128)(2,1)S(1)} %get-tuple-element.36.refs_0_, bf16[192,768]{1,0:T(8,128)(2,1)S(1)} %collective-permute-done.24.refs_1_, ...), custom_call_target="tpu_custom_call" | custom-call | flops 679477248 | bytes 3047424 | tf_op jit(solution)/shard_map/attend_e/pallas_call | solution.py:466
  92.0 10.0 %attend_m.1 = (f32[384,384]{1,0:T(8,128)S(1)}, f32[384,128]{1,0:T(8,128)S(1)}, f32[384,128]{1,0:T(8,128)S(1)}) custom-call(bf16[384,384]{1,0:T(8,128)(2,1)S(1)} %get-tuple-element.35.q_ref, bf16[192,768]{1,0:T(8,128)(2,1)S(1)} %get-tuple-element.37.refs_0_, bf16[192,768]{1,0:T(8,128)(2,1)S(1)} %collective-permute-done.17.refs_1_, ...), custom_call_target="tpu_custom_call" | custom-call | flops 905969664 | bytes 3637248 | tf_op jit(solution)/shard_map/attend_m/pallas_call | solution.py:466
  102.0 10.1 %attend_last.1 = (f32[384,384]{1,0:T(8,128)S(1)}, bf16[384,384]{1,0:T(8,128)(2,1)S(1)}, bf16[384,384]{1,0:T(8,128)(2,1)S(1)}, bf16[384,384]{1,0:T(8,128)(2,1)S(1)}) custom-call(bf16[384,384]{1,0:T(8,128)(2,1)S(1)} %get-tuple-element.35.q_ref, bf16[192,768]{1,0:T(8,128)(2,1)S(1)} %collective-permute-done.15.refs_0_, ...), custom_call_target="tpu_custom_call" | custom-call | flops 679477248 | bytes 6094848 | tf_op jit(solution)/shard_map/attend_last/pallas_call | solution.py:484
  112.1 3.2 %collective-permute-start.30 = (bf16[384,384]{1,0:T(8,128)(2,1)S(1)}, bf16[384,384]{1,0:T(8,128)(2,1)S(1)}, u32[]{:S(2)}, u32[]{:S(2)}) collective-permute-start(bf16[384,384]{1,0:T(8,128)(2,1)S(1)} %get-tuple-element.48), channel_id=1, source_target_pairs={{0,2},{1,3},{2,0},{3,1},{4,6},{5,7},{6,4},{7,5},{8,10},{9,11},{10,... | collective-permute-start | bytes 884744 | tf_op jit(solution)/shard_map/ppermute | solution.py:554
  116.8 10.2 %collective-permute-done.30 = bf16[384,384]{1,0:T(8,128)(2,1)S(1)} collective-permute-done((bf16[384,384]{1,0:T(8,128)(2,1)S(1)}, bf16[384,384]{1,0:T(8,128)(2,1)S(1)}, u32[]{:S(2)}, u32[]{:S(2)}) %collective-permute-start.30) | collective-permute-done | bytes 294944 | tf_op jit(solution)/shard_map/ppermute | solution.py:554
  127.0 12.7 %collective-permute-done.29 = bf16[384,384]{1,0:T(8,128)(2,1)S(1)} collective-permute-done((bf16[384,384]{1,0:T(8,128)(2,1)S(1)}, bf16[384,384]{1,0:T(8,128)(2,1)S(1)}, u32[]{:S(2)}, u32[]{:S(2)}) %collective-permute-start.29) | collective-permute-done | bytes 294944 | tf_op jit(solution)/shard_map/ppermute | solution.py:554
  139.7 2.1 %collective-permute-done.28 = bf16[384,384]{1,0:T(8,128)(2,1)S(1)} collective-permute-done((bf16[384,384]{1,0:T(8,128)(2,1)S(1)}, bf16[384,384]{1,0:T(8,128)(2,1)S(1)}, u32[]{:S(2)}, u32[]{:S(2)}) %collective-permute-start.28) | collective-permute-done | bytes 294944 | tf_op jit(solution)/shard_map/ppermute | solution.py:554
  (63 shorter events, 26.1 us)
Async XLA Ops:
  4.3 16.3 %collective-permute-start = (bf16[208,384]{1,0:T(8,128)(2,1)S(1)}, bf16[208,384]{1,0:T(8,128)(2,1)S(1)}, u32[]{:S(2)}, u32[]{:S(2)}) collective-permute-start(bf16[208,384]{1,0:T(8,128)(2,1)S(1)} %get-tuple-element.27.a0.m0), channel_id=1, source_target_pairs={{0,1},{1,2},{2,3},{3,0},{4,5},{5,6},{6,7},{7,4},{8,9},{9,10},{10,1... | collective-permute-start | bytes 479240 | tf_op jit(solution)/shard_map/ppermute | solution.py:141
  5.6 17.2 %collective-permute-start.1 = (bf16[208,384]{1,0:T(8,128)(2,1)S(1)}, bf16[208,384]{1,0:T(8,128)(2,1)S(1)}, u32[]{:S(2)}, u32[]{:S(2)}) collective-permute-start(bf16[208,384]{1,0:T(8,128)(2,1)S(1)} %get-tuple-element.27.a0.m0), channel_id=1, source_target_pairs={{0,3},{1,0},{2,1},{3,2},{4,7},{5,4},{6,5},{7,6},{8,11},{9,8},{10,9... | collective-permute-start | bytes 479240 | tf_op jit(solution)/shard_map/ppermute | solution.py:141
  5.8 17.1 %collective-permute-start.2 = (bf16[208,384]{1,0:T(8,128)(2,1)S(1)}, bf16[208,384]{1,0:T(8,128)(2,1)S(1)}, u32[]{:S(2)}, u32[]{:S(2)}) collective-permute-start(bf16[208,384]{1,0:T(8,128)(2,1)S(1)} %get-tuple-element.27.a0.m0), channel_id=1, source_target_pairs={{0,2},{1,3},{2,0},{3,1},{4,6},{5,7},{6,4},{7,5},{8,10},{9,11},{10,... | collective-permute-start | bytes 479240 | tf_op jit(solution)/shard_map/ppermute | solution.py:141
  20.5 16.2 %collective-permute-start.7 = (bf16[192,384]{1,0:T(8,128)(2,1)S(1)}, bf16[192,384]{1,0:T(8,128)(2,1)S(1)}, u32[]{:S(2)}, u32[]{:S(2)}) collective-permute-start(bf16[192,384]{1,0:T(8,128)(2,1)S(1)} %get-tuple-element.28.e0), channel_id=1, source_target_pairs={{0,2},{1,3},{2,0},{3,1},{4,6},{5,7},{6,4},{7,5},{8,10},{9,11},{10,... | collective-permute-start | bytes 442376 | tf_op jit(solution)/shard_map/ppermute | solution.py:141
  24.5 19.4 %collective-permute-start.11 = (bf16[192,384]{1,0:T(8,128)(2,1)S(1)}, bf16[192,384]{1,0:T(8,128)(2,1)S(1)}, u32[]{:S(2)}, u32[]{:S(2)}) collective-permute-start(bf16[192,384]{1,0:T(8,128)(2,1)S(1)} %get-tuple-element.33.a0), channel_id=1, source_target_pairs={{0,1},{1,2},{2,3},{3,0},{4,5},{5,6},{6,7},{7,4},{8,9},{9,10},{10,1... | collective-permute-start | bytes 442376 | tf_op jit(solution)/shard_map/ppermute | solution.py:141
  24.6 20.3 %collective-permute-start.12 = (bf16[192,384]{1,0:T(8,128)(2,1)S(1)}, bf16[192,384]{1,0:T(8,128)(2,1)S(1)}, u32[]{:S(2)}, u32[]{:S(2)}) collective-permute-start(bf16[192,384]{1,0:T(8,128)(2,1)S(1)} %get-tuple-element.33.a0), channel_id=1, source_target_pairs={{0,3},{1,0},{2,1},{3,2},{4,7},{5,4},{6,5},{7,6},{8,11},{9,8},{10,9... | collective-permute-start | bytes 442376 | tf_op jit(solution)/shard_map/ppermute | solution.py:141
  26.0 23.7 %collective-permute-start.13 = (bf16[192,384]{1,0:T(8,128)(2,1)S(1)}, bf16[192,384]{1,0:T(8,128)(2,1)S(1)}, u32[]{:S(2)}, u32[]{:S(2)}) collective-permute-start(bf16[192,384]{1,0:T(8,128)(2,1)S(1)} %get-tuple-element.33.a0), channel_id=1, source_target_pairs={{0,2},{1,3},{2,0},{3,1},{4,6},{5,7},{6,4},{7,5},{8,10},{9,11},{10,... | collective-permute-start | bytes 442376 | tf_op jit(solution)/shard_map/ppermute | solution.py:141
  38.5 18.1 %collective-permute-start.8 = (bf16[192,384]{1,0:T(8,128)(2,1)S(1)}, bf16[192,384]{1,0:T(8,128)(2,1)S(1)}, u32[]{:S(2)}, u32[]{:S(2)}) collective-permute-start(bf16[192,384]{1,0:T(8,128)(2,1)S(1)} %get-tuple-element.32.a0), channel_id=1, source_target_pairs={{0,1},{1,2},{2,3},{3,0},{4,5},{5,6},{6,7},{7,4},{8,9},{9,10},{10,1... | collective-permute-start | bytes 442376 | tf_op jit(solution)/shard_map/ppermute | solution.py:141
  38.6 18.0 %collective-permute-start.9 = (bf16[192,384]{1,0:T(8,128)(2,1)S(1)}, bf16[192,384]{1,0:T(8,128)(2,1)S(1)}, u32[]{:S(2)}, u32[]{:S(2)}) collective-permute-start(bf16[192,384]{1,0:T(8,128)(2,1)S(1)} %get-tuple-element.32.a0), channel_id=1, source_target_pairs={{0,3},{1,0},{2,1},{3,2},{4,7},{5,4},{6,5},{7,6},{8,11},{9,8},{10,9... | collective-permute-start | bytes 442376 | tf_op jit(solution)/shard_map/ppermute | solution.py:141
  43.9 15.0 %collective-permute-start.10 = (bf16[192,384]{1,0:T(8,128)(2,1)S(1)}, bf16[192,384]{1,0:T(8,128)(2,1)S(1)}, u32[]{:S(2)}, u32[]{:S(2)}) collective-permute-start(bf16[192,384]{1,0:T(8,128)(2,1)S(1)} %get-tuple-element.32.a0), channel_id=1, source_target_pairs={{0,2},{1,3},{2,0},{3,1},{4,6},{5,7},{6,4},{7,5},{8,10},{9,11},{10,... | collective-permute-start | bytes 442376 | tf_op jit(solution)/shard_map/ppermute | solution.py:141
  51.2 11.8 %collective-permute-start.18 = (bf16[192,768]{1,0:T(8,128)(2,1)S(1)}, bf16[192,768]{1,0:T(8,128)(2,1)S(1)}, u32[]{:S(2)}, u32[]{:S(2)}) collective-permute-start(bf16[192,768]{1,0:T(8,128)(2,1)S(1)} %get-tuple-element.37.refs_0_), channel_id=1, source_target_pairs={{0,8},{4,12},{8,0},{12,4},{16,24},{20,28},{24,16},{28,20},{1,9},{5... | collective-permute-start | bytes 884744 | tf_op jit(solution)/shard_map/ppermute | solution.py:500
  61.1 13.8 %collective-permute-start.20 = (bf16[192,768]{1,0:T(8,128)(2,1)S(1)}, bf16[192,768]{1,0:T(8,128)(2,1)S(1)}, u32[]{:S(2)}, u32[]{:S(2)}) collective-permute-start(bf16[192,768]{1,0:T(8,128)(2,1)S(1)} %get-tuple-element.37.refs_0_), channel_id=1, source_target_pairs={{0,16},{4,20},{8,24},{12,28},{16,0},{20,4},{24,8},{28,12},{1,17},{... | collective-permute-start | bytes 884744 | tf_op jit(solution)/shard_map/ppermute | solution.py:500
  61.9 15.2 %collective-permute-start.24 = (bf16[192,768]{1,0:T(8,128)(2,1)S(1)}, bf16[192,768]{1,0:T(8,128)(2,1)S(1)}, u32[]{:S(2)}, u32[]{:S(2)}) collective-permute-start(bf16[192,768]{1,0:T(8,128)(2,1)S(1)} %get-tuple-element.36.refs_0_), channel_id=1, source_target_pairs={{0,4},{4,0},{8,12},{12,8},{16,20},{20,16},{24,28},{28,24},{1,5},{5... | collective-permute-start | bytes 884744 | tf_op jit(solution)/shard_map/ppermute | solution.py:500
  63.0 18.2 %collective-permute-start.22 = (bf16[192,768]{1,0:T(8,128)(2,1)S(1)}, bf16[192,768]{1,0:T(8,128)(2,1)S(1)}, u32[]{:S(2)}, u32[]{:S(2)}) collective-permute-start(bf16[192,768]{1,0:T(8,128)(2,1)S(1)} %collective-permute-done.18.refs_2_), channel_id=1, source_target_pairs={{0,16},{4,20},{8,24},{12,28},{16,0},{20,4},{24,8},{28,12},{1,17},{... | collective-permute-start | bytes 884744 | tf_op jit(solution)/shard_map/ppermute | solution.py:500
  68.6 13.9 %collective-permute-start.15 = (bf16[192,768]{1,0:T(8,128)(2,1)S(1)}, bf16[192,768]{1,0:T(8,128)(2,1)S(1)}, u32[]{:S(2)}, u32[]{:S(2)}) collective-permute-start(bf16[192,768]{1,0:T(8,128)(2,1)S(1)} %collective-permute-done.14.refs_4_), channel_id=1, source_target_pairs={{0,8},{4,12},{8,0},{12,4},{16,24},{20,28},{24,16},{28,20},{1,9},{5... | collective-permute-start | bytes 884744 | tf_op jit(solution)/shard_map/ppermute | solution.py:500
  68.7 13.8 %collective-permute-start.26 = (bf16[192,768]{1,0:T(8,128)(2,1)S(1)}, bf16[192,768]{1,0:T(8,128)(2,1)S(1)}, u32[]{:S(2)}, u32[]{:S(2)}) collective-permute-start(bf16[192,768]{1,0:T(8,128)(2,1)S(1)} %collective-permute-done.25.refs_2_), channel_id=1, source_target_pairs={{0,4},{4,0},{8,12},{12,8},{16,20},{20,16},{24,28},{28,24},{1,5},{5... | collective-permute-start | bytes 884744 | tf_op jit(solution)/shard_map/ppermute | solution.py:500
  77.1 14.9 %collective-permute-start.17 = (bf16[192,768]{1,0:T(8,128)(2,1)S(1)}, bf16[192,768]{1,0:T(8,128)(2,1)S(1)}, u32[]{:S(2)}, u32[]{:S(2)}) collective-permute-start(bf16[192,768]{1,0:T(8,128)(2,1)S(1)} %get-tuple-element.37.refs_0_), channel_id=1, source_target_pairs={{0,4},{4,0},{8,12},{12,8},{16,20},{20,16},{24,28},{28,24},{1,5},{5... | collective-permute-start | bytes 884744 | tf_op jit(solution)/shard_map/ppermute | solution.py:500
  81.2 10.7 %collective-permute-start.19 = (bf16[192,768]{1,0:T(8,128)(2,1)S(1)}, bf16[192,768]{1,0:T(8,128)(2,1)S(1)}, u32[]{:S(2)}, u32[]{:S(2)}) collective-permute-start(bf16[192,768]{1,0:T(8,128)(2,1)S(1)} %collective-permute-done.18.refs_2_), channel_id=1, source_target_pairs={{0,4},{4,0},{8,12},{12,8},{16,20},{20,16},{24,28},{28,24},{1,5},{5... | collective-permute-start | bytes 884744 | tf_op jit(solution)/shard_map/ppermute | solution.py:500
  82.5 9.5 %collective-permute-start.21 = (bf16[192,768]{1,0:T(8,128)(2,1)S(1)}, bf16[192,768]{1,0:T(8,128)(2,1)S(1)}, u32[]{:S(2)}, u32[]{:S(2)}) collective-permute-start(bf16[192,768]{1,0:T(8,128)(2,1)S(1)} %collective-permute-done.20.refs_4_), channel_id=1, source_target_pairs={{0,4},{4,0},{8,12},{12,8},{16,20},{20,16},{24,28},{28,24},{1,5},{5... | collective-permute-start | bytes 884744 | tf_op jit(solution)/shard_map/ppermute | solution.py:500
  82.5 9.5 %collective-permute-start.23 = (bf16[192,768]{1,0:T(8,128)(2,1)S(1)}, bf16[192,768]{1,0:T(8,128)(2,1)S(1)}, u32[]{:S(2)}, u32[]{:S(2)}) collective-permute-start(bf16[192,768]{1,0:T(8,128)(2,1)S(1)} %collective-permute-done.22.refs_6_), channel_id=1, source_target_pairs={{0,4},{4,0},{8,12},{12,8},{16,20},{20,16},{24,28},{28,24},{1,5},{5... | collective-permute-start | bytes 884744 | tf_op jit(solution)/shard_map/ppermute | solution.py:500
  83.0 18.9 %collective-permute-start.16 = (bf16[192,768]{1,0:T(8,128)(2,1)S(1)}, bf16[192,768]{1,0:T(8,128)(2,1)S(1)}, u32[]{:S(2)}, u32[]{:S(2)}) collective-permute-start(bf16[192,768]{1,0:T(8,128)(2,1)S(1)} %collective-permute-done.15.refs_0_), channel_id=1, source_target_pairs={{0,4},{4,0},{8,12},{12,8},{16,20},{20,16},{24,28},{28,24},{1,5},{5... | collective-permute-start | bytes 884744 | tf_op jit(solution)/shard_map/ppermute | solution.py:500
  112.1 14.9 %collective-permute-start.30 = (bf16[384,384]{1,0:T(8,128)(2,1)S(1)}, bf16[384,384]{1,0:T(8,128)(2,1)S(1)}, u32[]{:S(2)}, u32[]{:S(2)}) collective-permute-start(bf16[384,384]{1,0:T(8,128)(2,1)S(1)} %get-tuple-element.48), channel_id=1, source_target_pairs={{0,2},{1,3},{2,0},{3,1},{4,6},{5,7},{6,4},{7,5},{8,10},{9,11},{10,... | collective-permute-start | bytes 884744 | tf_op jit(solution)/shard_map/ppermute | solution.py:554
  115.3 24.3 %collective-permute-start.29 = (bf16[384,384]{1,0:T(8,128)(2,1)S(1)}, bf16[384,384]{1,0:T(8,128)(2,1)S(1)}, u32[]{:S(2)}, u32[]{:S(2)}) collective-permute-start(bf16[384,384]{1,0:T(8,128)(2,1)S(1)} %get-tuple-element.47), channel_id=1, source_target_pairs={{0,3},{1,0},{2,1},{3,2},{4,7},{5,4},{6,5},{7,6},{8,11},{9,8},{10,9... | collective-permute-start | bytes 884744 | tf_op jit(solution)/shard_map/ppermute | solution.py:554
  115.4 26.4 %collective-permute-start.28 = (bf16[384,384]{1,0:T(8,128)(2,1)S(1)}, bf16[384,384]{1,0:T(8,128)(2,1)S(1)}, u32[]{:S(2)}, u32[]{:S(2)}) collective-permute-start(bf16[384,384]{1,0:T(8,128)(2,1)S(1)} %get-tuple-element.46), channel_id=1, source_target_pairs={{0,1},{1,2},{2,3},{3,0},{4,5},{5,6},{6,7},{7,4},{8,9},{9,10},{10,1... | collective-permute-start | bytes 884744 | tf_op jit(solution)/shard_map/ppermute | solution.py:554
  (14 other events, 116.0 us)

commit v3 on v2

--- a/solution.py
+++ b/solution.py
@@ -16,6 +16,7 @@
 EDGE = 16
 LOG2E = math.log2(math.e)
 MIB = 1 << 20
+LANES = 128
 
 
 def padded_2(block, sides, width):
@@ -136,9 +137,17 @@
     return [(i, (i + offset) % count) for i in range(count)]
 
 
-def shared(block):
+def after(value, *others):
+    return lax.optimization_barrier((value, *others))[0]
+
+
+def shared(block, earlier=(None, None, None)):
     count = lax.axis_size("head")
-    return [block] + [lax.ppermute(block, "head", rotate(k)) for k in (1, count - 1, 2)]
+    moved = []
+    for k, previous in zip((1, count - 1, 2), earlier):
+        held = block if previous is None else after(block, previous)
+        moved.append(lax.ppermute(held, "head", rotate(k)))
+    return [block, *moved]
 
 
 def owner(k):
@@ -317,20 +326,29 @@
 
 def projections(parts, wq, wk, wv, kv_ref):
     width = parts[0].shape[1]
-    inverse = inverse_norm([part[...].astype(jnp.float32) for part in parts])
-
-    def product(weight_ref):
+    rows, out = parts[0].shape[0], wq.shape[0]
+    blocks = [part[...].astype(jnp.float32) for part in parts]
+    inverse = inverse_norm(blocks)
+    normed = [(block * inverse).astype(jnp.bfloat16) for block in blocks]
+
+    def product(weight_ref, weight_first):
         total = None
-        for part, shift in zip(parts, SHIFTS):
-            term = reduce_operands(part[...], weight_ref[:, columns_of(shift, width)])
+        for part, shift in zip(normed, SHIFTS):
+            weight = weight_ref[:, columns_of(shift, width)]
+            pair = (weight, part) if weight_first else (part, weight)
+            term = reduce_operands(*pair)
             total = term if total is None else total + term
         return total
 
-    out = wq.shape[0]
-    kv_ref[:, :out] = (product(wk) * inverse).astype(jnp.bfloat16)
-    kv_ref[:, out:] = (product(wv) * inverse).astype(jnp.bfloat16)
+    kv_ref[:, :out] = product(wk, False).astype(jnp.bfloat16)
+    value = product(wv, True).astype(jnp.bfloat16)
+    for row in range(0, rows, LANES):
+        for lane in range(0, out, LANES):
+            kv_ref[pl.ds(row, LANES), pl.ds(out + lane, LANES)] = value[
+                lane : lane + LANES, row : row + LANES
+            ]
     scale = LOG2E / math.sqrt(HEAD_DIM)
-    return (product(wq) * (inverse * scale)).astype(jnp.bfloat16)
+    return (product(wq, False) * scale).astype(jnp.bfloat16)
 
 
 def project_middle_kernel(a0, a1, a2, a3, wq, wk, wv, q_ref, kv_ref):
@@ -361,82 +379,110 @@
 TILE = 64
 
 
-def partial_attention(q_ref, blocks, scores, weights, head, lane):
-    rows = q_ref.shape[0]
-    width = q_ref.shape[1]
-    seen = blocks[0].shape[0]
-    pair = head // 2
-    lanes = pl.ds(pair * 2 * HEAD_DIM, 2 * HEAD_DIM)
-    mine = (lane // HEAD_DIM) == head % 2
-    query = q_ref[:, lanes]
-    query = jnp.where(mine, query, jnp.zeros_like(query))
-    for i, block in enumerate(blocks):
-        scores[:, pl.ds(i * seen, seen)] = reduce_operands(query, block[:, lanes])
-    tops, sums = [], []
-    extent = seen * len(blocks)
-    for start in range(0, rows, TILE):
-        tile = scores[pl.ds(start, TILE), pl.ds(0, extent)]
-        top = jnp.max(tile, axis=1, keepdims=True)
-        weight = jnp.exp2(tile - top)
-        sums.append(jnp.sum(weight, axis=1, keepdims=True))
-        tops.append(top)
-        weights[pl.ds(start, TILE), pl.ds(0, extent)] = weight.astype(jnp.bfloat16)
-    out = None
-    for i, block in enumerate(blocks):
-        value = block[:, pl.ds(width + pair * 2 * HEAD_DIM, 2 * HEAD_DIM)]
-        term = jnp.dot(
-            weights[:, pl.ds(i * seen, seen)], value, preferred_element_type=jnp.float32
-        )
-        out = term if out is None else out + term
-    return out, jnp.concatenate(tops, axis=0), jnp.concatenate(sums, axis=0)
-
-
-def attend_part_kernel(count, q_ref, *refs):
-    blocks = refs[:count]
-    out_ref, top_ref, sum_ref, scores, weights = refs[count:]
-    rows, width = q_ref.shape
-    lane = lax.broadcasted_iota(jnp.int32, (rows, 2 * HEAD_DIM), 1)
-    tops, sums = jnp.zeros_like(top_ref), jnp.zeros_like(sum_ref)
-    for pair in range(width // (2 * HEAD_DIM)):
+def partial_attention(query, blocks, scores, weights, head, lane):
+    width = query.shape[1]
+    pair, half = divmod(head, 2)
+    lanes = slice(pair * LANES, (pair + 1) * LANES)
+    mine = query[:, lanes]
+    mine = jnp.where((lane // HEAD_DIM) == half, mine, jnp.zeros_like(mine))
+    keys = jnp.concatenate([block[:, lanes] for block in blocks], axis=0)
+    scores[...] = reduce_operands(keys, mine)
+    columns = scores.shape[1]
+    top = None
+    for start in range(0, scores.shape[0], TILE):
+        tile = jnp.max(scores[pl.ds(start, TILE), :].reshape(-1, 8, columns), axis=0)
+        top = tile if top is None else jnp.maximum(top, tile)
+    top = jnp.max(top, axis=0, keepdims=True)
+    total = None
+    for start in range(0, scores.shape[0], TILE):
+        weight = jnp.exp2(scores[pl.ds(start, TILE), :] - top)
+        tile = jnp.sum(weight.reshape(-1, 8, columns), axis=0)
+        total = tile if total is None else total + tile
+        weights[pl.ds(start, TILE), :] = weight.astype(jnp.bfloat16)
+    values = [
+        block[pl.ds(row + half * HEAD_DIM, HEAD_DIM), pl.ds(width + pair * LANES, LANES)]
+        for block in blocks
+        for row in range(0, block.shape[0], LANES)
+    ]
+    values = jnp.concatenate(values, axis=1)
+    out = jnp.dot(values, weights[...], preferred_element_type=jnp.float32)
+    return out, top, jnp.sum(total, axis=0, keepdims=True)
+
+
+def state_parts(state, head, width, columns):
+    return (
+        state[pl.ds(head * HEAD_DIM, HEAD_DIM), columns],
+        state[pl.ds(width + head, 1), columns],
+        state[pl.ds(width + 8 + head, 1), columns],
+    )
+
+
+def merged_parts(one, other):
+    top = jnp.maximum(one[1], other[1])
+    first, second = jnp.exp2(one[1] - top), jnp.exp2(other[1] - top)
+    return first * one[0] + second * other[0], top, first * one[2] + second * other[2]
+
+
+def attend_kernel(first_column, q_refs, blocks, state, out_ref, scores, weights):
+    width = q_refs[0].shape[1]
+    query = jnp.concatenate([ref[...] for ref in q_refs], axis=0)
+    columns = query.shape[0]
+    lane = lax.broadcasted_iota(jnp.int32, (columns, LANES), 1)
+    out_ref[pl.ds(width, 16), :] = jnp.zeros((16, columns), jnp.float32)
+    for head in range(width // HEAD_DIM):
+        part = partial_attention(
+            query, blocks, scores.at[head % 2], weights.at[head % 2], head, lane
+        )
+        if state is not None:
+            part = merged_parts(
+                part, state_parts(state, head, width, pl.ds(first_column, columns))
+            )
+        out_ref[pl.ds(head * HEAD_DIM, HEAD_DIM), :] = part[0]
+        out_ref[pl.ds(width + head, 1), :] = part[1]
+        out_ref[pl.ds(width + 8 + head, 1), :] = part[2]
+
+
+def attend(queries, blocks, state, first_column, name):
+    rows, width = queries[0].shape
+    columns = rows * len(queries)
+    extent = sum(block.shape[0] for block in blocks)
+    out = jax.ShapeDtypeStruct((width + 16, columns), jnp.float32)
+    operands = (*queries, *blocks) + (() if state is None else (state,))
+
+    def kernel(*refs):
+        q_refs, block_refs = refs[: len(queries)], refs[len(queries) :][: len(blocks)]
+        state_ref = None if state is None else refs[len(operands) - 1]
+        attend_kernel(
+            first_column, q_refs, block_refs, state_ref, *refs[len(operands) :]
+        )
+
+    return pl.pallas_call(
+        kernel,
+        out_shape=out,
+        scratch_shapes=[
+            pltpu.VMEM((2, extent, columns), jnp.float32),
+            pltpu.VMEM((2, extent, columns), jnp.bfloat16),
+        ],
+        compiler_params=pltpu.CompilerParams(vmem_limit_bytes=24 * MIB),
+        cost_estimate=cost(
+            4 * columns * width * extent, (*operands, out), columns * extent * width // HEAD_DIM
+        ),
+        name=name,
+    )(*operands)
+
+
+def mix_kernel(own_state, other_state, w_ref, h2_ref, own_ref, p1, p2, p3, attended):
+    rows, width = h2_ref.shape
+    for pair in range(width // LANES):
         halves = []
-        for half in range(2):
-            head = 2 * pair + half
-            out, top, total = partial_attention(
-                q_ref, blocks, scores.at[half], weights.at[half], head, lane
+        for head in (2 * pair, 2 * pair + 1):
+            out, _, total = merged_parts(
+                state_parts(own_state, head, width, pl.ds(0, rows)),
+                state_parts(other_state, head, width, pl.ds(0, rows)),
             )
-            halves.append(out)
-            tops = jnp.where(lane == head, top, tops)
-            sums = jnp.where(lane == head, total, sums)
-        lanes = pl.ds(pair * 2 * HEAD_DIM, 2 * HEAD_DIM)
-        out_ref[:, lanes] = jnp.where(lane < HEAD_DIM, halves[0], halves[1])
-    top_ref[...] = tops
-    sum_ref[...] = sums
-
-
-def attend_last_kernel(count, earlier, q_ref, *refs):
-    blocks = refs[:count]
-    states = [refs[count + 3 * i : count + 3 * i + 3] for i in range(earlier)]
-    w_ref, h2_ref, own_ref, p1, p2, p3, scores, weights, attended = refs[count + 3 * earlier :]
-    rows, width = q_ref.shape
-    lane = lax.broadcasted_iota(jnp.int32, (rows, 2 * HEAD_DIM), 1)
-    for pair in range(width // (2 * HEAD_DIM)):
-        lanes = pl.ds(pair * 2 * HEAD_DIM, 2 * HEAD_DIM)
-        halves = []
-        for half in range(2):
-            head = 2 * pair + half
-            out, top, total = partial_attention(
-                q_ref, blocks, scores.at[half], weights.at[half], head, lane
-            )
-            tops = [top] + [state[1][:, head : head + 1] for state in states]
-            sums = [total] + [state[2][:, head : head + 1] for state in states]
-            outs = [out] + [state[0][:, lanes] for state in states]
-            highest = functools.reduce(jnp.maximum, tops)
-            factors = [jnp.exp2(one - highest) for one in tops]
-            norm = sum(f * one for f, one in zip(factors, sums))
-            mixed = sum(f * one for f, one in zip(factors, outs))
-            halves.append(mixed / norm)
-        merged = jnp.where(lane < HEAD_DIM, halves[0], halves[1])
-        attended[:, lanes] = merged.astype(jnp.bfloat16)
+            halves.append(out / total)
+        merged = jnp.transpose(jnp.concatenate(halves, axis=0))
+        attended[:, pl.ds(pair * LANES, LANES)] = merged.astype(jnp.bfloat16)
 
     def product(shift):
         return jnp.dot(
@@ -448,51 +494,21 @@
     own_ref[...] = product(0) + h2_ref[...]
 
 
-def attention_scratch(rows, extent):
-    return [
-        pltpu.VMEM((2, rows, extent), jnp.float32),
-        pltpu.VMEM((2, rows, extent), jnp.bfloat16),
-    ]
-
-
-def attend_part(q, blocks, name):
-    rows, width = q.shape
-    extent = sum(block.shape[0] for block in blocks)
-    state = (
-        jax.ShapeDtypeStruct((rows, width), jnp.float32),
-        jax.ShapeDtypeStruct((rows, 2 * HEAD_DIM), jnp.float32),
-        jax.ShapeDtypeStruct((rows, 2 * HEAD_DIM), jnp.float32),
-    )
-    return pl.pallas_call(
-        functools.partial(attend_part_kernel, len(blocks)),
-        out_shape=state,
-        scratch_shapes=attention_scratch(rows, extent),
-        compiler_params=pltpu.CompilerParams(vmem_limit_bytes=24 * MIB),
-        cost_estimate=cost(
-            4 * rows * width * extent, (q, *blocks, *state), rows * extent * width // HEAD_DIM
-        ),
-        name=name,
-    )(q, *blocks)
-
-
-def attend_last(q, blocks, states, w_out, h2, name):
-    rows, width = q.shape
-    extent = sum(block.shape[0] for block in blocks)
+def mix(own_state, other_state, w_out, h2):
+    rows, width = h2.shape
     own = jax.ShapeDtypeStruct((rows, width), jnp.float32)
     part = jax.ShapeDtypeStruct((rows, width), jnp.bfloat16)
-    flat = [array for state in states for array in state]
+    operands = (own_state, other_state, w_out, h2)
     return pl.pallas_call(
-        functools.partial(attend_last_kernel, len(blocks), len(states)),
+        mix_kernel,
         out_shape=(own, part, part, part),
-        scratch_shapes=attention_scratch(rows, extent) + [pltpu.VMEM((rows, width), jnp.bfloat16)],
-        compiler_params=pltpu.CompilerParams(vmem_limit_bytes=24 * MIB),
+        scratch_shapes=[pltpu.VMEM((rows, width), jnp.bfloat16)],
+        compiler_params=pltpu.CompilerParams(vmem_limit_bytes=16 * MIB),
         cost_estimate=cost(
-            4 * rows * width * extent + 2 * rows * width * w_out.shape[1],
-            (q, *blocks, *flat, w_out, h2, own, part, part, part),
-            rows * extent * width // HEAD_DIM,
+            2 * rows * width * w_out.shape[1], (*operands, own, part, part, part)
         ),
-        name=name,
-    )(q, *blocks, *flat, w_out, h2)
+        name="mix",
+    )(*operands)
 
 
 def exchanged(block, mask):
@@ -503,52 +519,53 @@
 def on_device(dna, conv_in, dilated_kernel_weight, w_query, w_key, w_value, w_out):
     count = lax.axis_size("seq")
     rows = dna.shape[0] // 2
-    inner = rows // 2
+    inner = 2 * LANES
+    outer = rows - inner
     low = lax.ppermute(dna[-EDGE:], "seq", [(i, i + 1) for i in range(count - 1)])
     high = lax.ppermute(dna[:EDGE], "seq", [(i + 1, i) for i in range(count - 1)])
     h1_m, sent = first_conv(
-        conv_middle_kernel, (dna,), conv_in, inner + EDGE, rows + 4 * EDGE, "conv_middle"
+        conv_middle_kernel, (dna,), conv_in, inner + EDGE, 2 * (inner + 2 * EDGE), "conv_middle"
     )
     wide_m = shared(sent)
     h1_e, sent = first_conv(
-        conv_edge_kernel, (dna, low, high), conv_in, inner, rows + 4 * EDGE, "conv_edge"
-    )
-    wide_e = shared(sent)
+        conv_edge_kernel, (dna, low, high), conv_in, outer, 2 * (outer + 2 * EDGE), "conv_edge"
+    )
+    wide_e = shared(sent, (None, None, wide_m[1]))
     h2_m, sent = second_conv(
         dilated_middle_kernel,
-        (*wide_m, h1_m),
+        (*wide_m, after(h1_m, sent)),
         dilated_kernel_weight,
         inner,
         inner,
         inner + EDGE,
         "dilated_middle",
     )
-    normed_m = shared(sent)
+    normed_m = shared(sent, wide_e[1:])
     h2, sent = second_conv(
         dilated_edge_kernel,
         (*wide_m, *wide_e, h1_m, h1_e, h2_m),
         dilated_kernel_weight,
         rows,
-        inner,
-        inner + 2 * EDGE,
+        outer,
+        outer + 2 * EDGE,
         "dilated_edge",
     )
-    normed_e = shared(sent)
+    normed_e = shared(sent, normed_m[1:])
+    normed_m[0] = after(normed_m[0], sent)
     weights = (w_query, w_key, w_value)
     q_m, kv_m = project(project_middle_kernel, normed_m, weights, inner, "project_middle")
+    x_m, y_m = exchanged(kv_m, 2), exchanged(kv_m, 4)
+    normed_e[0] = after(normed_e[0], x_m)
+    d_m = exchanged(x_m, 4)
     q, kv_e = project(project_edge_kernel, (*normed_e, q_m), weights, rows, "project_edge")
-
-    def with_near(block):
-        return [block, exchanged(block, 1)]
-
-    x_m, y_m = exchanged(kv_m, 2), exchanged(kv_m, 4)
-    d_m = exchanged(x_m, 4)
-    x_e, y_e = exchanged(kv_e, 2), exchanged(kv_e, 4)
+    x_e, y_e, q_other = exchanged(kv_e, 2), exchanged(kv_e, 4), exchanged(q, 1)
     d_e = exchanged(y_e, 2)
-    first = [kv for block in (kv_m, x_m, y_m, d_m) for kv in with_near(block)]
-    second = [kv for block in (kv_e, x_e, y_e) for kv in with_near(block)]
-    states = [attend_part(q, first, "attend_m"), attend_part(q, second, "attend_e")]
-    own, p1, p2, p3 = attend_last(q, with_near(d_e), states, w_out, h2, "attend_last")
+    state = attend((q, q_other), (kv_m, x_m, y_m, d_m), None, 0, "attend_m")
+    late = (kv_e, x_e, y_e, d_e)
+    state_other = attend((q_other,), late, state, rows, "attend_other")
+    given = exchanged(state_other, 1)
+    state_own = attend((q,), late, state, 0, "attend_own")
+    own, p1, p2, p3 = mix(state_own, given, w_out, h2)
     total = own
     for part, shift in ((p1, 1), (p2, 3), (p3, 2)):
         total = total + lax.ppermute(part, "head", rotate(shift)).astype(jnp.float32)

time: 143 us -> 128 us (0.90)
  the two profiles are of different devices: /device:TPU:21 before, /device:TPU:0 now
where the time goes in v3:
time: 128 us
  waiting for transfers between devices  64.3 us (50%)
  starting transfers between devices  37.2 us (29%)
  Pallas kernels  21.9 us (17%)
  local copies, waits for them, and re-layouts  3.13 us (2%)
    ppermute x3, waiting for transfers between devices, on_device(): lax.ppermute(part, 'head', rotate(shift)).astype(jnp.float32)  25.1 us
    ppermute x12, starting transfers between devices, shared(): moved.append(lax.ppermute(held, 'head', rotate(k)))  21.9 us
    ppermute x12, waiting for transfers between devices, shared(): moved.append(lax.ppermute(held, 'head', rotate(k)))  20.5 us
    ppermute x8, waiting for transfers between devices, exchanged(): return lax.ppermute(block, 'seq', [(i, i ^ mask) for i in range(count)])  15.2 us
    pallas_call x3, Pallas kernels, attend(): pl.pallas_call(kernel, out_shape=out, scratch_shapes=[pltpu.VMEM((2, exte...  12.1 us
    ppermute x8, starting transfers between devices, exchanged(): return lax.ppermute(block, 'seq', [(i, i ^ mask) for i in range(count)])  7.41 us
    ppermute x3, starting transfers between devices, on_device(): lax.ppermute(part, 'head', rotate(shift)).astype(jnp.float32)  5.07 us
    ppermute x1, waiting for transfers between devices, on_device(): lax.ppermute(dna[:EDGE], 'seq', [(i + 1, i) for i in range(count - 1)])  3.5 us
  transfers between devices with their start and end apart: 25, of which 11 were waited for; matrix products, arithmetic and copies ran while one was open for 0% of the time, Pallas kernels for 12%

profile of v3, /device:TPU:0, one launch (start us, length us, event | category | flops | bytes accessed | tf_op | source)
XLA Modules:
  0.0 127.6 jit_solution(10060089049651457296)
XLA Ops:
  0.0 1.8 %copy-done.1 = bf16[5,384,768]{2,1,0:T(8,128)(2,1)S(1)} copy-done((bf16[5,384,768]{2,1,0:T(8,128)(2,1)S(1)}, bf16[5,384,768]{2,1,0:T(8,128)(2,1)}, u32[]{:S(2)}) %copy-start.1) | copy-done | bytes 2949144
  4.4 3.1 %collective-permute-start = (bf16[272,384]{1,0:T(8,128)(2,1)S(1)}, bf16[272,384]{1,0:T(8,128)(2,1)S(1)}, u32[]{:S(2)}, u32[]{:S(2)}) collective-permute-start(bf16[272,384]{1,0:T(8,128)(2,1)S(1)} %get-tuple-element.31.a0.m0), channel_id=1, source_target_pairs={{0,1},{1,2},{2,3},{3,0},{4,5},{5,6},{6,7},{7,4},{8,9},{9,10},{10,1... | collective-permute-start | bytes 626696 | tf_op jit(solution)/shard_map/ppermute | solution.py:149
  7.5 2.1 %collective-permute-start.1 = (bf16[272,384]{1,0:T(8,128)(2,1)S(1)}, bf16[272,384]{1,0:T(8,128)(2,1)S(1)}, u32[]{:S(2)}, u32[]{:S(2)}) collective-permute-start(bf16[272,384]{1,0:T(8,128)(2,1)S(1)} %get-tuple-element.31.a0.m0), channel_id=1, source_target_pairs={{0,3},{1,0},{2,1},{3,2},{4,7},{5,4},{6,5},{7,6},{8,11},{9,8},{10,9... | collective-permute-start | bytes 626696 | tf_op jit(solution)/shard_map/ppermute | solution.py:149
  11.8 1.6 %collective-permute-start.4 = (bf16[16,768]{1,0:T(8,128)(2,1)S(1)}, bf16[16,768]{1,0:T(8,128)(2,1)S(1)}, u32[]{:S(2)}, u32[]{:S(2)}) collective-permute-start(bf16[16,768]{1,0:T(8,128)(2,1)S(1)} %get-tuple-element.57), channel_id=1, source_target_pairs={{4,0},{8,4},{12,8},{16,12},{20,16},{24,20},{28,24},{5,1},{9,5},{13... | collective-permute-start | bytes 73736 | tf_op jit(solution)/shard_map/ppermute | solution.py:525
  13.4 3.5 %collective-permute-done.4.high_ref = bf16[16,768]{1,0:T(8,128)(2,1)S(1)} collective-permute-done((bf16[16,768]{1,0:T(8,128)(2,1)S(1)}, bf16[16,768]{1,0:T(8,128)(2,1)S(1)}, u32[]{:S(2)}, u32[]{:S(2)}) %collective-permute-start.4) | collective-permute-done | bytes 24608 | tf_op jit(solution)/shard_map/ppermute | solution.py:525
  19.9 7.7 %collective-permute-start.7 = (bf16[128,384]{1,0:T(8,128)(2,1)S(1)}, bf16[128,384]{1,0:T(8,128)(2,1)S(1)}, u32[]{:S(2)}, u32[]{:S(2)}) collective-permute-start(bf16[128,384]{1,0:T(8,128)(2,1)S(1)} %get-tuple-element.33.e0), channel_id=1, source_target_pairs={{0,2},{1,3},{2,0},{3,1},{4,6},{5,7},{6,4},{7,5},{8,10},{9,11},{10,... | collective-permute-start | bytes 294920 | tf_op jit(solution)/shard_map/ppermute | solution.py:149
  27.6 4.8 %collective-permute-done.2.a3.m3 = bf16[272,384]{1,0:T(8,128)(2,1)S(1)} collective-permute-done((bf16[272,384]{1,0:T(8,128)(2,1)S(1)}, bf16[272,384]{1,0:T(8,128)(2,1)S(1)}, u32[]{:S(2)}, u32[]{:S(2)}) %collective-permute-start.2) | collective-permute-done | bytes 208928 | tf_op jit(solution)/shard_map/ppermute | solution.py:149
  32.4 2.0 %dilated_middle.1 = (f32[256,384]{1,0:T(8,128)S(1)}, bf16[256,384]{1,0:T(8,128)(2,1)S(1)}) custom-call(bf16[272,384]{1,0:T(8,128)(2,1)S(1)} %get-tuple-element.31.a0.m0, bf16[272,384]{1,0:T(8,128)(2,1)S(1)} %collective-permute-done.a1.m1, bf16[272,384]{1,0:T(8,128)(2,1)S(1)} %collective-permute-done.1.a2.m2, ...), custom_call_target="tpu_custom_call" | custom-call | flops 905969664 | bytes 5382144 | tf_op jit(solution)/shard_map/dilated_middle/pallas_call | solution.py:313
  34.4 2.8 %collective-permute-start.9 = (bf16[256,384]{1,0:T(8,128)(2,1)S(1)}, bf16[256,384]{1,0:T(8,128)(2,1)S(1)}, u32[]{:S(2)}, u32[]{:S(2)}) collective-permute-start(bf16[256,384]{1,0:T(8,128)(2,1)S(1)} %get-tuple-element.43.a0), channel_id=1, source_target_pairs={{0,3},{1,0},{2,1},{3,2},{4,7},{5,4},{6,5},{7,6},{8,11},{9,8},{10,9... | collective-permute-start | bytes 589832 | tf_op jit(solution)/shard_map/ppermute | solution.py:149
  39.4 5.0 %collective-permute-done.9.a2 = bf16[256,384]{1,0:T(8,128)(2,1)S(1)} collective-permute-done((bf16[256,384]{1,0:T(8,128)(2,1)S(1)}, bf16[256,384]{1,0:T(8,128)(2,1)S(1)}, u32[]{:S(2)}, u32[]{:S(2)}) %collective-permute-start.9) | collective-permute-done | bytes 196640 | tf_op jit(solution)/shard_map/ppermute | solution.py:149
  44.4 2.8 %collective-permute-done.8.a1 = bf16[256,384]{1,0:T(8,128)(2,1)S(1)} collective-permute-done((bf16[256,384]{1,0:T(8,128)(2,1)S(1)}, bf16[256,384]{1,0:T(8,128)(2,1)S(1)}, u32[]{:S(2)}, u32[]{:S(2)}) %collective-permute-start.8) | collective-permute-done | bytes 196640 | tf_op jit(solution)/shard_map/ppermute | solution.py:149
  47.2 6.7 %collective-permute-done.10.a3 = bf16[256,384]{1,0:T(8,128)(2,1)S(1)} collective-permute-done((bf16[256,384]{1,0:T(8,128)(2,1)S(1)}, bf16[256,384]{1,0:T(8,128)(2,1)S(1)}, u32[]{:S(2)}, u32[]{:S(2)}) %collective-permute-start.10) | collective-permute-done | bytes 196640 | tf_op jit(solution)/shard_map/ppermute | solution.py:149
  53.9 1.8 %project_middle.1 = (bf16[256,384]{1,0:T(8,128)(2,1)S(1)}, bf16[256,768]{1,0:T(8,128)(2,1)S(1)}) custom-call(bf16[256,384]{1,0:T(8,128)(2,1)S(1)} %get-tuple-element.43.a0, bf16[256,384]{1,0:T(8,128)(2,1)S(1)} %collective-permute-done.8.a1, bf16[256,384]{1,0:T(8,128)(2,1)S(1)} %collective-permute-done.9.a2, bf16[256,384]{1,0:T(8,128)(2,1)S(1)} %collective-permute-done.10.a3, ...), custom_call_target="tpu_custom_call" | custom-call | flops 905969664 | bytes 4915200 | tf_op jit(solution)/shard_map/project_middle/pallas_call | solution.py:370
  55.7 1.6 %collective-permute-start.11 = (bf16[256,768]{1,0:T(8,128)(2,1)S(1)}, bf16[256,768]{1,0:T(8,128)(2,1)S(1)}, u32[]{:S(2)}, u32[]{:S(2)}) collective-permute-start(bf16[256,768]{1,0:T(8,128)(2,1)S(1)} %get-tuple-element.44.refs_2_), channel_id=1, source_target_pairs={{0,8},{4,12},{8,0},{12,4},{16,24},{20,28},{24,16},{28,20},{1,9},{5... | collective-permute-start | bytes 1179656 | tf_op jit(solution)/shard_map/ppermute | solution.py:516
  57.3 2.0 %collective-permute-start.13 = (bf16[128,384]{1,0:T(8,128)(2,1)S(1)}, bf16[128,384]{1,0:T(8,128)(2,1)S(1)}, u32[]{:S(2)}, u32[]{:S(2)}) collective-permute-start(bf16[128,384]{1,0:T(8,128)(2,1)S(1)} %get-tuple-element.48.a0), channel_id=1, source_target_pairs={{0,3},{1,0},{2,1},{3,2},{4,7},{5,4},{6,5},{7,6},{8,11},{9,8},{10,9... | collective-permute-start | bytes 294920 | tf_op jit(solution)/shard_map/ppermute | solution.py:149
  61.3 4.5 %collective-permute-done.11.refs_3_ = bf16[256,768]{1,0:T(8,128)(2,1)S(1)} collective-permute-done((bf16[256,768]{1,0:T(8,128)(2,1)S(1)}, bf16[256,768]{1,0:T(8,128)(2,1)S(1)}, u32[]{:S(2)}, u32[]{:S(2)}) %collective-permute-start.11) | collective-permute-done | bytes 393248 | tf_op jit(solution)/shard_map/ppermute | solution.py:516
  72.1 10.6 %collective-permute-done.16.refs_3_ = bf16[128,768]{1,0:T(8,128)(2,1)S(1)} collective-permute-done((bf16[128,768]{1,0:T(8,128)(2,1)S(1)}, bf16[128,768]{1,0:T(8,128)(2,1)S(1)}, u32[]{:S(2)}, u32[]{:S(2)}) %collective-permute-start.16) | collective-permute-done | bytes 196640 | tf_op jit(solution)/shard_map/ppermute | solution.py:516
  83.3 6.5 %attend_m.1.refs_5_ = f32[400,768]{1,0:T(8,128)S(1)} custom-call(bf16[384,384]{1,0:T(8,128)(2,1)S(1)} %get-tuple-element.50.refs_0_, bf16[384,384]{1,0:T(8,128)(2,1)S(1)} %collective-permute-done.18.refs_1_.refs_0_, bf16[256,768]{1,0:T(8,128)(2,1)S(1)} %get-tuple-element.44.refs_2_, bf16[256,768]{1,0:T(8,128)(2,1)S(1)} %collective-permute-done.11.refs_3_, ...), custom_call_target="tpu_custom_call" | custom-call | flops 1207959552 | bytes 3391488 | tf_op jit(solution)/shard_map/attend_m/pallas_call | solution.py:459
  89.8 2.8 %attend_other.1 = f32[400,384]{1,0:T(8,128)S(1)} custom-call(bf16[384,384]{1,0:T(8,128)(2,1)S(1)} %collective-permute-done.18.refs_1_.refs_0_, bf16[128,768]{1,0:T(8,128)(2,1)S(1)} %get-tuple-element.51.refs_1_, bf16[128,768]{1,0:T(8,128)(2,1)S(1)} %collective-permute-done.15.refs_2_, bf16[128,768]{1,0:T(8,128)(2,1)S(1)} %collective-permute-done.16.refs_3_, ...), custom_call_target="tpu_custom_call" | custom-call | flops 301989888 | bytes 2924544 | tf_op jit(solution)/shard_map/attend_other/pallas_call | solution.py:459
  92.7 2.8 %attend_own.1.own_state = f32[400,384]{1,0:T(8,128)S(1)} custom-call(bf16[384,384]{1,0:T(8,128)(2,1)S(1)} %get-tuple-element.50.refs_0_, bf16[128,768]{1,0:T(8,128)(2,1)S(1)} %get-tuple-element.51.refs_1_, bf16[128,768]{1,0:T(8,128)(2,1)S(1)} %collective-permute-done.15.refs_2_, bf16[128,768]{1,0:T(8,128)(2,1)S(1)} %collective-permute-done.16.refs_3_, ...), custom_call_target="tpu_custom_call" | custom-call | flops 301989888 | bytes 2924544 | tf_op jit(solution)/shard_map/attend_own/pallas_call | solution.py:459
  96.5 3.5 %collective-permute-start.22 = (bf16[384,384]{1,0:T(8,128)(2,1)S(1)}, bf16[384,384]{1,0:T(8,128)(2,1)S(1)}, u32[]{:S(2)}, u32[]{:S(2)}) collective-permute-start(bf16[384,384]{1,0:T(8,128)(2,1)S(1)} %get-tuple-element.54), channel_id=1, source_target_pairs={{0,1},{1,2},{2,3},{3,0},{4,5},{5,6},{6,7},{7,4},{8,9},{9,10},{10,1... | collective-permute-start | bytes 884744 | tf_op jit(solution)/shard_map/ppermute | solution.py:571
  101.6 6.6 %collective-permute-done.22 = bf16[384,384]{1,0:T(8,128)(2,1)S(1)} collective-permute-done((bf16[384,384]{1,0:T(8,128)(2,1)S(1)}, bf16[384,384]{1,0:T(8,128)(2,1)S(1)}, u32[]{:S(2)}, u32[]{:S(2)}) %collective-permute-start.22) | collective-permute-done | bytes 294944 | tf_op jit(solution)/shard_map/ppermute | solution.py:571
  108.2 5.9 %collective-permute-done.23 = bf16[384,384]{1,0:T(8,128)(2,1)S(1)} collective-permute-done((bf16[384,384]{1,0:T(8,128)(2,1)S(1)}, bf16[384,384]{1,0:T(8,128)(2,1)S(1)}, u32[]{:S(2)}, u32[]{:S(2)}) %collective-permute-start.23) | collective-permute-done | bytes 294944 | tf_op jit(solution)/shard_map/ppermute | solution.py:571
  114.1 12.6 %collective-permute-done.24 = bf16[384,384]{1,0:T(8,128)(2,1)S(1)} collective-permute-done((bf16[384,384]{1,0:T(8,128)(2,1)S(1)}, bf16[384,384]{1,0:T(8,128)(2,1)S(1)}, u32[]{:S(2)}, u32[]{:S(2)}) %collective-permute-start.24) | collective-permute-done | bytes 294944 | tf_op jit(solution)/shard_map/ppermute | solution.py:571
  (52 shorter events, 22.3 us)
Async XLA Ops:
  4.4 15.6 %collective-permute-start = (bf16[272,384]{1,0:T(8,128)(2,1)S(1)}, bf16[272,384]{1,0:T(8,128)(2,1)S(1)}, u32[]{:S(2)}, u32[]{:S(2)}) collective-permute-start(bf16[272,384]{1,0:T(8,128)(2,1)S(1)} %get-tuple-element.31.a0.m0), channel_id=1, source_target_pairs={{0,1},{1,2},{2,3},{3,0},{4,5},{5,6},{6,7},{7,4},{8,9},{9,10},{10,1... | collective-permute-start | bytes 626696 | tf_op jit(solution)/shard_map/ppermute | solution.py:149
  7.5 20.2 %collective-permute-start.1 = (bf16[272,384]{1,0:T(8,128)(2,1)S(1)}, bf16[272,384]{1,0:T(8,128)(2,1)S(1)}, u32[]{:S(2)}, u32[]{:S(2)}) collective-permute-start(bf16[272,384]{1,0:T(8,128)(2,1)S(1)} %get-tuple-element.31.a0.m0), channel_id=1, source_target_pairs={{0,3},{1,0},{2,1},{3,2},{4,7},{5,4},{6,5},{7,6},{8,11},{9,8},{10,9... | collective-permute-start | bytes 626696 | tf_op jit(solution)/shard_map/ppermute | solution.py:149
  9.6 22.9 %collective-permute-start.2 = (bf16[272,384]{1,0:T(8,128)(2,1)S(1)}, bf16[272,384]{1,0:T(8,128)(2,1)S(1)}, u32[]{:S(2)}, u32[]{:S(2)}) collective-permute-start(bf16[272,384]{1,0:T(8,128)(2,1)S(1)} %get-tuple-element.31.a0.m0), channel_id=1, source_target_pairs={{0,2},{1,3},{2,0},{3,1},{4,6},{5,7},{6,4},{7,5},{8,10},{9,11},{10,... | collective-permute-start | bytes 626696 | tf_op jit(solution)/shard_map/ppermute | solution.py:149
  11.8 5.1 %collective-permute-start.4 = (bf16[16,768]{1,0:T(8,128)(2,1)S(1)}, bf16[16,768]{1,0:T(8,128)(2,1)S(1)}, u32[]{:S(2)}, u32[]{:S(2)}) collective-permute-start(bf16[16,768]{1,0:T(8,128)(2,1)S(1)} %get-tuple-element.57), channel_id=1, source_target_pairs={{4,0},{8,4},{12,8},{16,12},{20,16},{24,20},{28,24},{5,1},{9,5},{13... | collective-permute-start | bytes 73736 | tf_op jit(solution)/shard_map/ppermute | solution.py:525
  17.9 16.5 %collective-permute-start.6 = (bf16[128,384]{1,0:T(8,128)(2,1)S(1)}, bf16[128,384]{1,0:T(8,128)(2,1)S(1)}, u32[]{:S(2)}, u32[]{:S(2)}) collective-permute-start(bf16[128,384]{1,0:T(8,128)(2,1)S(1)} %get-tuple-element.33.e0), channel_id=1, source_target_pairs={{0,3},{1,0},{2,1},{3,2},{4,7},{5,4},{6,5},{7,6},{8,11},{9,8},{10,9... | collective-permute-start | bytes 294920 | tf_op jit(solution)/shard_map/ppermute | solution.py:149
  19.3 17.9 %collective-permute-start.5 = (bf16[128,384]{1,0:T(8,128)(2,1)S(1)}, bf16[128,384]{1,0:T(8,128)(2,1)S(1)}, u32[]{:S(2)}, u32[]{:S(2)}) collective-permute-start(bf16[128,384]{1,0:T(8,128)(2,1)S(1)} %get-tuple-element.33.e0), channel_id=1, source_target_pairs={{0,1},{1,2},{2,3},{3,0},{4,5},{5,6},{6,7},{7,4},{8,9},{9,10},{10,1... | collective-permute-start | bytes 294920 | tf_op jit(solution)/shard_map/ppermute | solution.py:149
  19.9 17.3 %collective-permute-start.7 = (bf16[128,384]{1,0:T(8,128)(2,1)S(1)}, bf16[128,384]{1,0:T(8,128)(2,1)S(1)}, u32[]{:S(2)}, u32[]{:S(2)}) collective-permute-start(bf16[128,384]{1,0:T(8,128)(2,1)S(1)} %get-tuple-element.33.e0), channel_id=1, source_target_pairs={{0,2},{1,3},{2,0},{3,1},{4,6},{5,7},{6,4},{7,5},{8,10},{9,11},{10,... | collective-permute-start | bytes 294920 | tf_op jit(solution)/shard_map/ppermute | solution.py:149
  34.4 10.0 %collective-permute-start.9 = (bf16[256,384]{1,0:T(8,128)(2,1)S(1)}, bf16[256,384]{1,0:T(8,128)(2,1)S(1)}, u32[]{:S(2)}, u32[]{:S(2)}) collective-permute-start(bf16[256,384]{1,0:T(8,128)(2,1)S(1)} %get-tuple-element.43.a0), channel_id=1, source_target_pairs={{0,3},{1,0},{2,1},{3,2},{4,7},{5,4},{6,5},{7,6},{8,11},{9,8},{10,9... | collective-permute-start | bytes 589832 | tf_op jit(solution)/shard_map/ppermute | solution.py:149
  37.2 10.0 %collective-permute-start.8 = (bf16[256,384]{1,0:T(8,128)(2,1)S(1)}, bf16[256,384]{1,0:T(8,128)(2,1)S(1)}, u32[]{:S(2)}, u32[]{:S(2)}) collective-permute-start(bf16[256,384]{1,0:T(8,128)(2,1)S(1)} %get-tuple-element.43.a0), channel_id=1, source_target_pairs={{0,1},{1,2},{2,3},{3,0},{4,5},{5,6},{6,7},{7,4},{8,9},{9,10},{10,1... | collective-permute-start | bytes 589832 | tf_op jit(solution)/shard_map/ppermute | solution.py:149
  37.2 16.7 %collective-permute-start.10 = (bf16[256,384]{1,0:T(8,128)(2,1)S(1)}, bf16[256,384]{1,0:T(8,128)(2,1)S(1)}, u32[]{:S(2)}, u32[]{:S(2)}) collective-permute-start(bf16[256,384]{1,0:T(8,128)(2,1)S(1)} %get-tuple-element.43.a0), channel_id=1, source_target_pairs={{0,2},{1,3},{2,0},{3,1},{4,6},{5,7},{6,4},{7,5},{8,10},{9,11},{10,... | collective-permute-start | bytes 589832 | tf_op jit(solution)/shard_map/ppermute | solution.py:149
  55.7 10.1 %collective-permute-start.11 = (bf16[256,768]{1,0:T(8,128)(2,1)S(1)}, bf16[256,768]{1,0:T(8,128)(2,1)S(1)}, u32[]{:S(2)}, u32[]{:S(2)}) collective-permute-start(bf16[256,768]{1,0:T(8,128)(2,1)S(1)} %get-tuple-element.44.refs_2_), channel_id=1, source_target_pairs={{0,8},{4,12},{8,0},{12,4},{16,24},{20,28},{24,16},{28,20},{1,9},{5... | collective-permute-start | bytes 1179656 | tf_op jit(solution)/shard_map/ppermute | solution.py:516
  57.3 10.1 %collective-permute-start.13 = (bf16[128,384]{1,0:T(8,128)(2,1)S(1)}, bf16[128,384]{1,0:T(8,128)(2,1)S(1)}, u32[]{:S(2)}, u32[]{:S(2)}) collective-permute-start(bf16[128,384]{1,0:T(8,128)(2,1)S(1)} %get-tuple-element.48.a0), channel_id=1, source_target_pairs={{0,3},{1,0},{2,1},{3,2},{4,7},{5,4},{6,5},{7,6},{8,11},{9,8},{10,9... | collective-permute-start | bytes 294920 | tf_op jit(solution)/shard_map/ppermute | solution.py:149
  59.3 8.1 %collective-permute-start.12 = (bf16[128,384]{1,0:T(8,128)(2,1)S(1)}, bf16[128,384]{1,0:T(8,128)(2,1)S(1)}, u32[]{:S(2)}, u32[]{:S(2)}) collective-permute-start(bf16[128,384]{1,0:T(8,128)(2,1)S(1)} %get-tuple-element.48.a0), channel_id=1, source_target_pairs={{0,1},{1,2},{2,3},{3,0},{4,5},{5,6},{6,7},{7,4},{8,9},{9,10},{10,1... | collective-permute-start | bytes 294920 | tf_op jit(solution)/shard_map/ppermute | solution.py:149
  59.3 9.2 %collective-permute-start.14 = (bf16[128,384]{1,0:T(8,128)(2,1)S(1)}, bf16[128,384]{1,0:T(8,128)(2,1)S(1)}, u32[]{:S(2)}, u32[]{:S(2)}) collective-permute-start(bf16[128,384]{1,0:T(8,128)(2,1)S(1)} %get-tuple-element.48.a0), channel_id=1, source_target_pairs={{0,2},{1,3},{2,0},{3,1},{4,6},{5,7},{6,4},{7,5},{8,10},{9,11},{10,... | collective-permute-start | bytes 294920 | tf_op jit(solution)/shard_map/ppermute | solution.py:149
  59.8 23.4 %collective-permute-start.19 = (bf16[256,768]{1,0:T(8,128)(2,1)S(1)}, bf16[256,768]{1,0:T(8,128)(2,1)S(1)}, u32[]{:S(2)}, u32[]{:S(2)}) collective-permute-start(bf16[256,768]{1,0:T(8,128)(2,1)S(1)} %get-tuple-element.44.refs_2_), channel_id=1, source_target_pairs={{0,16},{4,20},{8,24},{12,28},{16,0},{20,4},{24,8},{28,12},{1,17},{... | collective-permute-start | bytes 1179656 | tf_op jit(solution)/shard_map/ppermute | solution.py:516
  65.9 17.4 %collective-permute-start.20 = (bf16[256,768]{1,0:T(8,128)(2,1)S(1)}, bf16[256,768]{1,0:T(8,128)(2,1)S(1)}, u32[]{:S(2)}, u32[]{:S(2)}) collective-permute-start(bf16[256,768]{1,0:T(8,128)(2,1)S(1)} %collective-permute-done.11.refs_3_), channel_id=1, source_target_pairs={{0,16},{4,20},{8,24},{12,28},{16,0},{20,4},{24,8},{28,12},{1,17},{... | collective-permute-start | bytes 1179656 | tf_op jit(solution)/shard_map/ppermute | solution.py:516
  69.9 13.4 %collective-permute-start.18 = (bf16[384,384]{1,0:T(8,128)(2,1)S(1)}, bf16[384,384]{1,0:T(8,128)(2,1)S(1)}, u32[]{:S(2)}, u32[]{:S(2)}) collective-permute-start(bf16[384,384]{1,0:T(8,128)(2,1)S(1)} %get-tuple-element.50.refs_0_), channel_id=1, source_target_pairs={{0,4},{4,0},{8,12},{12,8},{16,20},{20,16},{24,28},{28,24},{1,5},{5... | collective-permute-start | bytes 884744 | tf_op jit(solution)/shard_map/ppermute | solution.py:516
  69.9 12.7 %collective-permute-start.16 = (bf16[128,768]{1,0:T(8,128)(2,1)S(1)}, bf16[128,768]{1,0:T(8,128)(2,1)S(1)}, u32[]{:S(2)}, u32[]{:S(2)}) collective-permute-start(bf16[128,768]{1,0:T(8,128)(2,1)S(1)} %get-tuple-element.51.refs_1_), channel_id=1, source_target_pairs={{0,16},{4,20},{8,24},{12,28},{16,0},{20,4},{24,8},{28,12},{1,17},{... | collective-permute-start | bytes 589832 | tf_op jit(solution)/shard_map/ppermute | solution.py:516
  71.5 18.3 %collective-permute-start.15 = (bf16[128,768]{1,0:T(8,128)(2,1)S(1)}, bf16[128,768]{1,0:T(8,128)(2,1)S(1)}, u32[]{:S(2)}, u32[]{:S(2)}) collective-permute-start(bf16[128,768]{1,0:T(8,128)(2,1)S(1)} %get-tuple-element.51.refs_1_), channel_id=1, source_target_pairs={{0,8},{4,12},{8,0},{12,4},{16,24},{20,28},{24,16},{28,20},{1,9},{5... | collective-permute-start | bytes 589832 | tf_op jit(solution)/shard_map/ppermute | solution.py:516
  82.7 7.1 %collective-permute-start.17 = (bf16[128,768]{1,0:T(8,128)(2,1)S(1)}, bf16[128,768]{1,0:T(8,128)(2,1)S(1)}, u32[]{:S(2)}, u32[]{:S(2)}) collective-permute-start(bf16[128,768]{1,0:T(8,128)(2,1)S(1)} %collective-permute-done.16.refs_3_), channel_id=1, source_target_pairs={{0,8},{4,12},{8,0},{12,4},{16,24},{20,28},{24,16},{28,20},{1,9},{5... | collective-permute-start | bytes 589832 | tf_op jit(solution)/shard_map/ppermute | solution.py:516
  92.6 2.9 %collective-permute-start.21 = (f32[400,384]{1,0:T(8,128)S(1)}, f32[400,384]{1,0:T(8,128)S(1)}, u32[]{:S(2)}, u32[]{:S(2)}) collective-permute-start(f32[400,384]{1,0:T(8,128)S(1)} %attend_other.1), channel_id=1, source_target_pairs={{0,4},{4,0},{8,12},{12,8},{16,20},{20,16},{24,28},{28,24},{1,5},{5... | collective-permute-start | bytes 1843208 | tf_op jit(solution)/shard_map/ppermute | solution.py:516
  96.5 11.7 %collective-permute-start.22 = (bf16[384,384]{1,0:T(8,128)(2,1)S(1)}, bf16[384,384]{1,0:T(8,128)(2,1)S(1)}, u32[]{:S(2)}, u32[]{:S(2)}) collective-permute-start(bf16[384,384]{1,0:T(8,128)(2,1)S(1)} %get-tuple-element.54), channel_id=1, source_target_pairs={{0,1},{1,2},{2,3},{3,0},{4,5},{5,6},{6,7},{7,4},{8,9},{9,10},{10,1... | collective-permute-start | bytes 884744 | tf_op jit(solution)/shard_map/ppermute | solution.py:571
  100.0 14.1 %collective-permute-start.23 = (bf16[384,384]{1,0:T(8,128)(2,1)S(1)}, bf16[384,384]{1,0:T(8,128)(2,1)S(1)}, u32[]{:S(2)}, u32[]{:S(2)}) collective-permute-start(bf16[384,384]{1,0:T(8,128)(2,1)S(1)} %get-tuple-element.55), channel_id=1, source_target_pairs={{0,3},{1,0},{2,1},{3,2},{4,7},{5,4},{6,5},{7,6},{8,11},{9,8},{10,9... | collective-permute-start | bytes 884744 | tf_op jit(solution)/shard_map/ppermute | solution.py:571
  100.4 26.3 %collective-permute-start.24 = (bf16[384,384]{1,0:T(8,128)(2,1)S(1)}, bf16[384,384]{1,0:T(8,128)(2,1)S(1)}, u32[]{:S(2)}, u32[]{:S(2)}) collective-permute-start(bf16[384,384]{1,0:T(8,128)(2,1)S(1)} %get-tuple-element.56), channel_id=1, source_target_pairs={{0,2},{1,3},{2,0},{3,1},{4,6},{5,7},{6,4},{7,5},{8,10},{9,11},{10,... | collective-permute-start | bytes 884744 | tf_op jit(solution)/shard_map/ppermute | solution.py:571
  (8 other events, 77.7 us)

commit v4 on v3

--- a/solution.py
+++ b/solution.py
@@ -141,13 +141,9 @@
     return lax.optimization_barrier((value, *others))[0]
 
 
-def shared(block, earlier=(None, None, None)):
+def shared(block):
     count = lax.axis_size("head")
-    moved = []
-    for k, previous in zip((1, count - 1, 2), earlier):
-        held = block if previous is None else after(block, previous)
-        moved.append(lax.ppermute(held, "head", rotate(k)))
-    return [block, *moved]
+    return [block] + [lax.ppermute(block, "head", rotate(k)) for k in (1, count - 1, 2)]
 
 
 def owner(k):
@@ -156,6 +152,16 @@
 
 
 SHIFTS = (0, 1, 3, 2)
+
+
+def gathered(block):
+    return lax.all_gather(block, "head", axis=0, tiled=True)
+
+
+def pieces(ref):
+    count = ref.shape[0] // len(SHIFTS)
+    starts = [pl.multiple_of(owner(shift) * count, 16) for shift in SHIFTS]
+    return tuple(ref.at[pl.ds(start, count), :] for start in starts)
 
 
 def store_wide(wide, start, block):
@@ -239,9 +245,9 @@
     return pl.ds(pl.multiple_of(owner(shift) * width, 128), width)
 
 
-def dilated_middle_kernel(a0, a1, a2, a3, h1_ref, weight_ref, h2_ref, sent_ref, act):
-    parts = (a0, a1, a2, a3)
-    count, width = a0.shape
+def dilated_middle_kernel(a_ref, h1_ref, weight_ref, h2_ref, sent_ref, act):
+    parts = pieces(a_ref)
+    count, width = parts[0].shape
     rows = h2_ref.shape[0]
     blocks = wide_blocks(parts, 0, count)
     inverse = inverse_norm(blocks)
@@ -256,10 +262,10 @@
 
 
 def dilated_edge_kernel(
-    m0, m1, m2, m3, e0, e1, e2, e3, hm_ref, he_ref, h2m_ref, weight_ref, h2_ref, sent_ref, act
+    m_ref, e0, e1, e2, e3, hm_ref, he_ref, h2m_ref, weight_ref, h2_ref, sent_ref, act
 ):
-    middle, edge = (m0, m1, m2, m3), (e0, e1, e2, e3)
-    inner, width = m0.shape
+    middle, edge = pieces(m_ref), (e0, e1, e2, e3)
+    inner, width = middle[0].shape
     outer = e0.shape[0]
     rows = h2_ref.shape[0]
     upper = outer - EDGE
@@ -351,8 +357,8 @@
     return (product(wq, False) * scale).astype(jnp.bfloat16)
 
 
-def project_middle_kernel(a0, a1, a2, a3, wq, wk, wv, q_ref, kv_ref):
-    q_ref[...] = projections((a0, a1, a2, a3), wq, wk, wv, kv_ref)
+def project_middle_kernel(a_ref, wq, wk, wv, q_ref, kv_ref):
+    q_ref[...] = projections(pieces(a_ref), wq, wk, wv, kv_ref)
 
 
 def project_edge_kernel(a0, a1, a2, a3, qm_ref, wq, wk, wv, q_ref, kv_ref):
@@ -363,8 +369,8 @@
     q_ref[pl.ds(EDGE + inner, rows - EDGE - inner), :] = query[EDGE:]
 
 
-def project(kernel, operands, weights, q_rows, name):
-    rows, out = operands[0].shape[0], weights[0].shape[0]
+def project(kernel, operands, weights, rows, q_rows, name):
+    out = weights[0].shape[0]
     q = jax.ShapeDtypeStruct((q_rows, out), jnp.bfloat16)
     kv = jax.ShapeDtypeStruct((rows, 2 * out), jnp.bfloat16)
     return pl.pallas_call(
@@ -526,40 +532,41 @@
     h1_m, sent = first_conv(
         conv_middle_kernel, (dna,), conv_in, inner + EDGE, 2 * (inner + 2 * EDGE), "conv_middle"
     )
-    wide_m = shared(sent)
+    wide_m = gathered(sent)
     h1_e, sent = first_conv(
         conv_edge_kernel, (dna, low, high), conv_in, outer, 2 * (outer + 2 * EDGE), "conv_edge"
     )
-    wide_e = shared(sent, (None, None, wide_m[1]))
+    wide_e = shared(sent)
     h2_m, sent = second_conv(
         dilated_middle_kernel,
-        (*wide_m, after(h1_m, sent)),
+        (wide_m, after(h1_m, sent)),
         dilated_kernel_weight,
         inner,
         inner,
         inner + EDGE,
         "dilated_middle",
     )
-    normed_m = shared(sent, wide_e[1:])
+    normed_m = gathered(sent)
     h2, sent = second_conv(
         dilated_edge_kernel,
-        (*wide_m, *wide_e, h1_m, h1_e, h2_m),
+        (wide_m, *wide_e, h1_m, h1_e, h2_m),
         dilated_kernel_weight,
         rows,
         outer,
         outer + 2 * EDGE,
         "dilated_edge",
     )
-    normed_e = shared(sent, normed_m[1:])
-    normed_m[0] = after(normed_m[0], sent)
+    normed_e = shared(sent)
+    normed_m = after(normed_m, sent)
     weights = (w_query, w_key, w_value)
-    q_m, kv_m = project(project_middle_kernel, normed_m, weights, inner, "project_middle")
-    x_m, y_m = exchanged(kv_m, 2), exchanged(kv_m, 4)
-    normed_e[0] = after(normed_e[0], x_m)
-    d_m = exchanged(x_m, 4)
-    q, kv_e = project(project_edge_kernel, (*normed_e, q_m), weights, rows, "project_edge")
-    x_e, y_e, q_other = exchanged(kv_e, 2), exchanged(kv_e, 4), exchanged(q, 1)
-    d_e = exchanged(y_e, 2)
+    q_m, kv_m = project(
+        project_middle_kernel, (normed_m,), weights, inner, inner, "project_middle"
+    )
+    x_m, y_m, d_m = (exchanged(kv_m, mask) for mask in (2, 4, 6))
+    q, kv_e = project(
+        project_edge_kernel, (*normed_e, q_m), weights, outer, rows, "project_edge"
+    )
+    q_other, x_e, y_e, d_e = exchanged(q, 1), *(exchanged(kv_e, mask) for mask in (2, 4, 6))
     state = attend((q, q_other), (kv_m, x_m, y_m, d_m), None, 0, "attend_m")
     late = (kv_e, x_e, y_e, d_e)
     state_other = attend((q_other,), late, state, rows, "attend_other")

time: 128 us -> 132 us (1.031)
  blocking collectives: 0 us -> 41 us
  waiting for transfers between devices: 64.3 us -> 38.2 us
  starting transfers between devices: 37.2 us -> 25.5 us
    all_gather x0 -> x2, blocking collectives: none -> 41 us  [gathered(): return lax.all_gather(block, 'head', axis=0, tiled=True)]
    ppermute x12 -> x6, waiting for transfers between devices: 20.5 us -> 0.02 us  [shared(): lax.ppermute(block, 'head', rotate(k))]
    ppermute x12 -> x6, starting transfers between devices: 21.9 us -> 7.75 us  [shared(): lax.ppermute(block, 'head', rotate(k))]
    ppermute x1, waiting for transfers between devices: 3.5 us -> 0.01 us  [on_device(): lax.ppermute(dna[:EDGE], 'seq', [(i + 1, i) for i in range(count - 1)])]
    ppermute x8, waiting for transfers between devices: 15.2 us -> 12.7 us  [exchanged(): return lax.ppermute(block, 'seq', [(i, i ^ mask) for i in range(count)])]
    ppermute x8, starting transfers between devices: 7.41 us -> 9.34 us  [exchanged(): return lax.ppermute(block, 'seq', [(i, i ^ mask) for i in range(count)])]
  transfers between devices with their start and end apart: 25 -> 19, of which waited for: 11 -> 5; matrix products, arithmetic and copies ran while one was open for 0% -> 0% of each run, Pallas kernels for 12% -> 12%
where the time goes in v4:
time: 132 us
  blocking collectives  41 us (31%)
  waiting for transfers between devices  38.2 us (29%)
  starting transfers between devices  25.5 us (19%)
  Pallas kernels  22.2 us (17%)
  local copies, waits for them, and re-layouts  3.89 us (3%)
    all_gather x2, blocking collectives, gathered(): return lax.all_gather(block, 'head', axis=0, tiled=True)  41 us
    ppermute x3, waiting for transfers between devices, on_device(): lax.ppermute(part, 'head', rotate(shift)).astype(jnp.float32)  25.5 us
    ppermute x8, waiting for transfers between devices, exchanged(): return lax.ppermute(block, 'seq', [(i, i ^ mask) for i in range(count)])  12.7 us
    pallas_call x3, Pallas kernels, attend(): pl.pallas_call(kernel, out_shape=out, scratch_shapes=[pltpu.VMEM((2, exte...  12.3 us
    ppermute x8, starting transfers between devices, exchanged(): return lax.ppermute(block, 'seq', [(i, i ^ mask) for i in range(count)])  9.34 us
    ppermute x6, starting transfers between devices, shared(): lax.ppermute(block, 'head', rotate(k))  7.75 us
    ppermute x3, starting transfers between devices, on_device(): lax.ppermute(part, 'head', rotate(shift)).astype(jnp.float32)  4.73 us
    pallas_call x2, Pallas kernels, second_conv(): pl.pallas_call(kernel, out_shape=(kept, sent), scratch_shapes=[pltpu.VMEM...  3.51 us
  transfers between devices with their start and end apart: 19, of which 5 were waited for; matrix products, arithmetic and copies ran while one was open for 0% of the time, Pallas kernels for 12%

profile of v4, /device:TPU:0, one launch (start us, length us, event | category | flops | bytes accessed | tf_op | source)
XLA Modules:
  0.0 131.8 jit_solution(13686877639481406504)
XLA Ops:
  0.8 2.3 %collective-permute-start = (bf16[16,768]{1,0:T(8,128)(2,1)S(1)}, bf16[16,768]{1,0:T(8,128)(2,1)S(1)}, u32[]{:S(2)}, u32[]{:S(2)}) collective-permute-start(bf16[16,768]{1,0:T(8,128)(2,1)S(1)} %get-tuple-element.42), channel_id=1, source_target_pairs={{0,4},{4,8},{8,12},{12,16},{16,20},{20,24},{24,28},{1,5},{5,9},{9,... | collective-permute-start | bytes 73736 | tf_op jit(solution)/shard_map/ppermute | solution.py:530
  3.1 1.3 collective-permute-start.1
  4.4 1.8 %copy-done.1 = bf16[5,384,768]{2,1,0:T(8,128)(2,1)S(1)} copy-done((bf16[5,384,768]{2,1,0:T(8,128)(2,1)S(1)}, bf16[5,384,768]{2,1,0:T(8,128)(2,1)}, u32[]{:S(2)}) %copy-start.1) | copy-done | bytes 2949144
  8.8 20.0 %all_gather.6.a_ref.m_ref = bf16[1088,384]{1,0:T(8,128)(2,1)S(1)} all-gather(bf16[272,384]{1,0:T(8,128)(2,1)S(1)} %get-tuple-element.23), channel_id=1, replica_groups=mesh['seq'=8,'head'=4] {'head'}, dimensions={0}, use_global_device_ids=true | all-gather | bytes 1044480 | tf_op jit(solution)/shard_map/all_gather | solution.py:158
  30.5 3.2 %collective-permute-start.3 = (bf16[128,384]{1,0:T(8,128)(2,1)S(1)}, bf16[128,384]{1,0:T(8,128)(2,1)S(1)}, u32[]{:S(2)}, u32[]{:S(2)}) collective-permute-start(bf16[128,384]{1,0:T(8,128)(2,1)S(1)} %get-tuple-element.24.e0), channel_id=1, source_target_pairs={{0,3},{1,0},{2,1},{3,2},{4,7},{5,4},{6,5},{7,6},{8,11},{9,8},{10,9... | collective-permute-start | bytes 294920 | tf_op jit(solution)/shard_map/ppermute | solution.py:146
  33.7 2.0 %dilated_middle.1 = (f32[256,384]{1,0:T(8,128)S(1)}, bf16[256,384]{1,0:T(8,128)(2,1)S(1)}) custom-call(bf16[1088,384]{1,0:T(8,128)(2,1)S(1)} %all_gather.6.a_ref.m_ref, f32[272,384]{1,0:T(8,128)S(1)} %get-tuple-element.27.h1_ref.hm_ref, bf16[3,384,1536]{2,1,0:T(8,128)(2,1)S(1)} %copy-done), custom_call_target="tpu_custom_call" | custom-call | flops 905969664 | bytes 5382144 | tf_op jit(solution)/shard_map/dilated_middle/pallas_call | solution.py:319
  35.6 21.0 %all_gather.7.a_ref = bf16[1024,384]{1,0:T(8,128)(2,1)S(1)} all-gather(bf16[256,384]{1,0:T(8,128)(2,1)S(1)} %get-tuple-element.30), channel_id=1, replica_groups=mesh['seq'=8,'head'=4] {'head'}, dimensions={0}, use_global_device_ids=true | all-gather | bytes 983040 | tf_op jit(solution)/shard_map/all_gather | solution.py:158
  56.7 1.6 %dilated_edge.1 = (f32[384,384]{1,0:T(8,128)S(1)}, bf16[128,384]{1,0:T(8,128)(2,1)S(1)}) custom-call(bf16[1088,384]{1,0:T(8,128)(2,1)S(1)} %all_gather.6.a_ref.m_ref, bf16[128,384]{1,0:T(8,128)(2,1)S(1)} %get-tuple-element.24.e0, bf16[128,384]{1,0:T(8,128)(2,1)S(1)} %collective-permute-done.2.e1, bf16[128,384]{1,0:T(8,128)(2,1)S(1)} %collective-permute-done.3.e2, ...), custom_call_target="tpu_custom_call" | custom-call | flops 452984832 | bytes 6463488 | tf_op jit(solution)/shard_map/dilated_edge/pallas_call | solution.py:319
  58.4 3.8 %collective-permute-start.6 = (bf16[128,384]{1,0:T(8,128)(2,1)S(1)}, bf16[128,384]{1,0:T(8,128)(2,1)S(1)}, u32[]{:S(2)}, u32[]{:S(2)}) collective-permute-start(bf16[128,384]{1,0:T(8,128)(2,1)S(1)} %get-tuple-element.29.a0), channel_id=1, source_target_pairs={{0,3},{1,0},{2,1},{3,2},{4,7},{5,4},{6,5},{7,6},{8,11},{9,8},{10,9... | collective-permute-start | bytes 294920 | tf_op jit(solution)/shard_map/ppermute | solution.py:146
  62.2 1.8 %project_middle.1 = (bf16[256,384]{1,0:T(8,128)(2,1)S(1)}, bf16[256,768]{1,0:T(8,128)(2,1)S(1)}) custom-call(bf16[1024,384]{1,0:T(8,128)(2,1)S(1)} %all_gather.7.a_ref, bf16[384,1536]{1,0:T(8,128)(2,1)S(1)} %copy-done.3, bf16[384,1536]{1,0:T(8,128)(2,1)S(1)} %copy-done.4, bf16[384,1536]{1,0:T(8,128)(2,1)S(1)} %copy-done.5), custom_call_target="tpu_custom_call" | custom-call | flops 905969664 | bytes 4915200 | tf_op jit(solution)/shard_map/project_middle/pallas_call | solution.py:376
  64.0 2.8 %collective-permute-start.12 = (bf16[256,768]{1,0:T(8,128)(2,1)S(1)}, bf16[256,768]{1,0:T(8,128)(2,1)S(1)}, u32[]{:S(2)}, u32[]{:S(2)}) collective-permute-start(bf16[256,768]{1,0:T(8,128)(2,1)S(1)} %get-tuple-element.35.refs_2_), channel_id=1, source_target_pairs={{0,8},{4,12},{8,0},{12,4},{16,24},{20,28},{24,16},{28,20},{1,9},{5... | collective-permute-start | bytes 1179656 | tf_op jit(solution)/shard_map/ppermute | solution.py:522
  66.8 1.6 %collective-permute-start.13 = (bf16[256,768]{1,0:T(8,128)(2,1)S(1)}, bf16[256,768]{1,0:T(8,128)(2,1)S(1)}, u32[]{:S(2)}, u32[]{:S(2)}) collective-permute-start(bf16[256,768]{1,0:T(8,128)(2,1)S(1)} %get-tuple-element.35.refs_2_), channel_id=1, source_target_pairs={{0,16},{4,20},{8,24},{12,28},{16,0},{20,4},{24,8},{28,12},{1,17},{... | collective-permute-start | bytes 1179656 | tf_op jit(solution)/shard_map/ppermute | solution.py:522
  69.3 1.3 project_edge.1
  70.6 2.6 %collective-permute-start.10 = (bf16[128,768]{1,0:T(8,128)(2,1)S(1)}, bf16[128,768]{1,0:T(8,128)(2,1)S(1)}, u32[]{:S(2)}, u32[]{:S(2)}) collective-permute-start(bf16[128,768]{1,0:T(8,128)(2,1)S(1)} %get-tuple-element.34.refs_1_), channel_id=1, source_target_pairs={{0,24},{4,28},{8,16},{12,20},{16,8},{20,12},{24,0},{28,4},{1,25},{... | collective-permute-start | bytes 589832 | tf_op jit(solution)/shard_map/ppermute | solution.py:522
  73.2 1.4 %collective-permute-start.8 = (bf16[128,768]{1,0:T(8,128)(2,1)S(1)}, bf16[128,768]{1,0:T(8,128)(2,1)S(1)}, u32[]{:S(2)}, u32[]{:S(2)}) collective-permute-start(bf16[128,768]{1,0:T(8,128)(2,1)S(1)} %get-tuple-element.34.refs_1_), channel_id=1, source_target_pairs={{0,8},{4,12},{8,0},{12,4},{16,24},{20,28},{24,16},{28,20},{1,9},{5... | collective-permute-start | bytes 589832 | tf_op jit(solution)/shard_map/ppermute | solution.py:522
  74.6 2.3 %collective-permute-done.12.refs_3_ = bf16[256,768]{1,0:T(8,128)(2,1)S(1)} collective-permute-done((bf16[256,768]{1,0:T(8,128)(2,1)S(1)}, bf16[256,768]{1,0:T(8,128)(2,1)S(1)}, u32[]{:S(2)}, u32[]{:S(2)}) %collective-permute-start.12) | collective-permute-done | bytes 393248 | tf_op jit(solution)/shard_map/ppermute | solution.py:522
  76.9 10.4 %collective-permute-done.13.refs_4_ = bf16[256,768]{1,0:T(8,128)(2,1)S(1)} collective-permute-done((bf16[256,768]{1,0:T(8,128)(2,1)S(1)}, bf16[256,768]{1,0:T(8,128)(2,1)S(1)}, u32[]{:S(2)}, u32[]{:S(2)}) %collective-permute-start.13) | collective-permute-done | bytes 393248 | tf_op jit(solution)/shard_map/ppermute | solution.py:522
  87.3 6.5 %attend_m.1.refs_5_ = f32[400,768]{1,0:T(8,128)S(1)} custom-call(bf16[384,384]{1,0:T(8,128)(2,1)S(1)} %get-tuple-element.33.refs_0_, bf16[384,384]{1,0:T(8,128)(2,1)S(1)} %collective-permute-done.11.refs_1_.refs_0_, bf16[256,768]{1,0:T(8,128)(2,1)S(1)} %get-tuple-element.35.refs_2_, bf16[256,768]{1,0:T(8,128)(2,1)S(1)} %collective-permute-done.12.refs_3_, ...), custom_call_target="tpu_custom_call" | custom-call | flops 1207959552 | bytes 3391488 | tf_op jit(solution)/shard_map/attend_m/pallas_call | solution.py:465
  93.9 2.8 %attend_other.1 = f32[400,384]{1,0:T(8,128)S(1)} custom-call(bf16[384,384]{1,0:T(8,128)(2,1)S(1)} %collective-permute-done.11.refs_1_.refs_0_, bf16[128,768]{1,0:T(8,128)(2,1)S(1)} %get-tuple-element.34.refs_1_, bf16[128,768]{1,0:T(8,128)(2,1)S(1)} %collective-permute-done.8.refs_2_, bf16[128,768]{1,0:T(8,128)(2,1)S(1)} %collective-permute-done.9.refs_3_, ...), custom_call_target="tpu_custom_call" | custom-call | flops 301989888 | bytes 2924544 | tf_op jit(solution)/shard_map/attend_other/pallas_call | solution.py:465
  96.7 3.0 %attend_own.1.own_state = f32[400,384]{1,0:T(8,128)S(1)} custom-call(bf16[384,384]{1,0:T(8,128)(2,1)S(1)} %get-tuple-element.33.refs_0_, bf16[128,768]{1,0:T(8,128)(2,1)S(1)} %get-tuple-element.34.refs_1_, bf16[128,768]{1,0:T(8,128)(2,1)S(1)} %collective-permute-done.8.refs_2_, bf16[128,768]{1,0:T(8,128)(2,1)S(1)} %collective-permute-done.9.refs_3_, ...), custom_call_target="tpu_custom_call" | custom-call | flops 301989888 | bytes 2924544 | tf_op jit(solution)/shard_map/attend_own/pallas_call | solution.py:465
  101.4 3.3 %collective-permute-start.17 = (bf16[384,384]{1,0:T(8,128)(2,1)S(1)}, bf16[384,384]{1,0:T(8,128)(2,1)S(1)}, u32[]{:S(2)}, u32[]{:S(2)}) collective-permute-start(bf16[384,384]{1,0:T(8,128)(2,1)S(1)} %get-tuple-element.39), channel_id=1, source_target_pairs={{0,3},{1,0},{2,1},{3,2},{4,7},{5,4},{6,5},{7,6},{8,11},{9,8},{10,9... | collective-permute-start | bytes 884744 | tf_op jit(solution)/shard_map/ppermute | solution.py:578
  105.5 7.0 %collective-permute-done.16 = bf16[384,384]{1,0:T(8,128)(2,1)S(1)} collective-permute-done((bf16[384,384]{1,0:T(8,128)(2,1)S(1)}, bf16[384,384]{1,0:T(8,128)(2,1)S(1)}, u32[]{:S(2)}, u32[]{:S(2)}) %collective-permute-start.16) | collective-permute-done | bytes 294944 | tf_op jit(solution)/shard_map/ppermute | solution.py:578
  112.5 5.3 %collective-permute-done.17 = bf16[384,384]{1,0:T(8,128)(2,1)S(1)} collective-permute-done((bf16[384,384]{1,0:T(8,128)(2,1)S(1)}, bf16[384,384]{1,0:T(8,128)(2,1)S(1)}, u32[]{:S(2)}, u32[]{:S(2)}) %collective-permute-start.17) | collective-permute-done | bytes 294944 | tf_op jit(solution)/shard_map/ppermute | solution.py:578
  117.7 13.2 %collective-permute-done.18 = bf16[384,384]{1,0:T(8,128)(2,1)S(1)} collective-permute-done((bf16[384,384]{1,0:T(8,128)(2,1)S(1)}, bf16[384,384]{1,0:T(8,128)(2,1)S(1)}, u32[]{:S(2)}, u32[]{:S(2)}) %collective-permute-start.18) | collective-permute-done | bytes 294944 | tf_op jit(solution)/shard_map/ppermute | solution.py:578
  (42 shorter events, 9.3 us)
Async XLA Ops:
  0.8 28.0 %collective-permute-start = (bf16[16,768]{1,0:T(8,128)(2,1)S(1)}, bf16[16,768]{1,0:T(8,128)(2,1)S(1)}, u32[]{:S(2)}, u32[]{:S(2)}) collective-permute-start(bf16[16,768]{1,0:T(8,128)(2,1)S(1)} %get-tuple-element.42), channel_id=1, source_target_pairs={{0,4},{4,8},{8,12},{12,16},{16,20},{20,24},{24,28},{1,5},{5,9},{9,... | collective-permute-start | bytes 73736 | tf_op jit(solution)/shard_map/ppermute | solution.py:530
  3.1 25.7 %collective-permute-start.1 = (bf16[16,768]{1,0:T(8,128)(2,1)S(1)}, bf16[16,768]{1,0:T(8,128)(2,1)S(1)}, u32[]{:S(2)}, u32[]{:S(2)}) collective-permute-start(bf16[16,768]{1,0:T(8,128)(2,1)S(1)} %get-tuple-element.41), channel_id=1, source_target_pairs={{4,0},{8,4},{12,8},{16,12},{20,16},{24,20},{28,24},{5,1},{9,5},{13... | collective-permute-start | bytes 73736 | tf_op jit(solution)/shard_map/ppermute | solution.py:531
  28.8 4.9 %copy-start = (bf16[3,384,1536]{2,1,0:T(8,128)(2,1)S(1)}, bf16[3,384,1536]{2,1,0:T(8,128)(2,1)}, u32[]{:S(2)}) copy-start(bf16[3,384,1536]{2,1,0:T(8,128)(2,1)} %weight_ref.7) | copy-start | bytes 10616836
  29.8 26.9 %collective-permute-start.2 = (bf16[128,384]{1,0:T(8,128)(2,1)S(1)}, bf16[128,384]{1,0:T(8,128)(2,1)S(1)}, u32[]{:S(2)}, u32[]{:S(2)}) collective-permute-start(bf16[128,384]{1,0:T(8,128)(2,1)S(1)} %get-tuple-element.24.e0), channel_id=1, source_target_pairs={{0,1},{1,2},{2,3},{3,0},{4,5},{5,6},{6,7},{7,4},{8,9},{9,10},{10,1... | collective-permute-start | bytes 294920 | tf_op jit(solution)/shard_map/ppermute | solution.py:146
  30.5 26.2 %collective-permute-start.3 = (bf16[128,384]{1,0:T(8,128)(2,1)S(1)}, bf16[128,384]{1,0:T(8,128)(2,1)S(1)}, u32[]{:S(2)}, u32[]{:S(2)}) collective-permute-start(bf16[128,384]{1,0:T(8,128)(2,1)S(1)} %get-tuple-element.24.e0), channel_id=1, source_target_pairs={{0,3},{1,0},{2,1},{3,2},{4,7},{5,4},{6,5},{7,6},{8,11},{9,8},{10,9... | collective-permute-start | bytes 294920 | tf_op jit(solution)/shard_map/ppermute | solution.py:146
  33.7 23.0 %collective-permute-start.4 = (bf16[128,384]{1,0:T(8,128)(2,1)S(1)}, bf16[128,384]{1,0:T(8,128)(2,1)S(1)}, u32[]{:S(2)}, u32[]{:S(2)}) collective-permute-start(bf16[128,384]{1,0:T(8,128)(2,1)S(1)} %get-tuple-element.24.e0), channel_id=1, source_target_pairs={{0,2},{1,3},{2,0},{3,1},{4,6},{5,7},{6,4},{7,5},{8,10},{9,11},{10,... | collective-permute-start | bytes 294920 | tf_op jit(solution)/shard_map/ppermute | solution.py:146
  56.7 5.5 %copy-start.3 = (bf16[384,1536]{1,0:T(8,128)(2,1)S(1)}, bf16[384,1536]{1,0:T(8,128)(2,1)}, u32[]{:S(2)}) copy-start(bf16[384,1536]{1,0:T(8,128)(2,1)} %wq.3) | copy-start | bytes 3538948
  56.7 5.5 %copy-start.4 = (bf16[384,1536]{1,0:T(8,128)(2,1)S(1)}, bf16[384,1536]{1,0:T(8,128)(2,1)}, u32[]{:S(2)}) copy-start(bf16[384,1536]{1,0:T(8,128)(2,1)} %wk.3) | copy-start | bytes 3538948
  56.7 5.5 %copy-start.5 = (bf16[384,1536]{1,0:T(8,128)(2,1)S(1)}, bf16[384,1536]{1,0:T(8,128)(2,1)}, u32[]{:S(2)}) copy-start(bf16[384,1536]{1,0:T(8,128)(2,1)} %wv.3) | copy-start | bytes 3538948
  58.3 10.2 %collective-permute-start.5 = (bf16[128,384]{1,0:T(8,128)(2,1)S(1)}, bf16[128,384]{1,0:T(8,128)(2,1)S(1)}, u32[]{:S(2)}, u32[]{:S(2)}) collective-permute-start(bf16[128,384]{1,0:T(8,128)(2,1)S(1)} %get-tuple-element.29.a0), channel_id=1, source_target_pairs={{0,1},{1,2},{2,3},{3,0},{4,5},{5,6},{6,7},{7,4},{8,9},{9,10},{10,1... | collective-permute-start | bytes 294920 | tf_op jit(solution)/shard_map/ppermute | solution.py:146
  58.4 10.9 %collective-permute-start.6 = (bf16[128,384]{1,0:T(8,128)(2,1)S(1)}, bf16[128,384]{1,0:T(8,128)(2,1)S(1)}, u32[]{:S(2)}, u32[]{:S(2)}) collective-permute-start(bf16[128,384]{1,0:T(8,128)(2,1)S(1)} %get-tuple-element.29.a0), channel_id=1, source_target_pairs={{0,3},{1,0},{2,1},{3,2},{4,7},{5,4},{6,5},{7,6},{8,11},{9,8},{10,9... | collective-permute-start | bytes 294920 | tf_op jit(solution)/shard_map/ppermute | solution.py:146
  62.2 7.1 %collective-permute-start.7 = (bf16[128,384]{1,0:T(8,128)(2,1)S(1)}, bf16[128,384]{1,0:T(8,128)(2,1)S(1)}, u32[]{:S(2)}, u32[]{:S(2)}) collective-permute-start(bf16[128,384]{1,0:T(8,128)(2,1)S(1)} %get-tuple-element.29.a0), channel_id=1, source_target_pairs={{0,2},{1,3},{2,0},{3,1},{4,6},{5,7},{6,4},{7,5},{8,10},{9,11},{10,... | collective-permute-start | bytes 294920 | tf_op jit(solution)/shard_map/ppermute | solution.py:146
  64.0 12.9 %collective-permute-start.12 = (bf16[256,768]{1,0:T(8,128)(2,1)S(1)}, bf16[256,768]{1,0:T(8,128)(2,1)S(1)}, u32[]{:S(2)}, u32[]{:S(2)}) collective-permute-start(bf16[256,768]{1,0:T(8,128)(2,1)S(1)} %get-tuple-element.35.refs_2_), channel_id=1, source_target_pairs={{0,8},{4,12},{8,0},{12,4},{16,24},{20,28},{24,16},{28,20},{1,9},{5... | collective-permute-start | bytes 1179656 | tf_op jit(solution)/shard_map/ppermute | solution.py:522
  66.8 20.5 %collective-permute-start.13 = (bf16[256,768]{1,0:T(8,128)(2,1)S(1)}, bf16[256,768]{1,0:T(8,128)(2,1)S(1)}, u32[]{:S(2)}, u32[]{:S(2)}) collective-permute-start(bf16[256,768]{1,0:T(8,128)(2,1)S(1)} %get-tuple-element.35.refs_2_), channel_id=1, source_target_pairs={{0,16},{4,20},{8,24},{12,28},{16,0},{20,4},{24,8},{28,12},{1,17},{... | collective-permute-start | bytes 1179656 | tf_op jit(solution)/shard_map/ppermute | solution.py:522
  68.4 18.9 %collective-permute-start.14 = (bf16[256,768]{1,0:T(8,128)(2,1)S(1)}, bf16[256,768]{1,0:T(8,128)(2,1)S(1)}, u32[]{:S(2)}, u32[]{:S(2)}) collective-permute-start(bf16[256,768]{1,0:T(8,128)(2,1)S(1)} %get-tuple-element.35.refs_2_), channel_id=1, source_target_pairs={{0,24},{4,28},{8,16},{12,20},{16,8},{20,12},{24,0},{28,4},{1,25},{... | collective-permute-start | bytes 1179656 | tf_op jit(solution)/shard_map/ppermute | solution.py:522
  70.6 2.7 %collective-permute-start.11 = (bf16[384,384]{1,0:T(8,128)(2,1)S(1)}, bf16[384,384]{1,0:T(8,128)(2,1)S(1)}, u32[]{:S(2)}, u32[]{:S(2)}) collective-permute-start(bf16[384,384]{1,0:T(8,128)(2,1)S(1)} %get-tuple-element.33.refs_0_), channel_id=1, source_target_pairs={{0,4},{4,0},{8,12},{12,8},{16,20},{20,16},{24,28},{28,24},{1,5},{5... | collective-permute-start | bytes 884744 | tf_op jit(solution)/shard_map/ppermute | solution.py:522
  70.6 23.2 %collective-permute-start.10 = (bf16[128,768]{1,0:T(8,128)(2,1)S(1)}, bf16[128,768]{1,0:T(8,128)(2,1)S(1)}, u32[]{:S(2)}, u32[]{:S(2)}) collective-permute-start(bf16[128,768]{1,0:T(8,128)(2,1)S(1)} %get-tuple-element.34.refs_1_), channel_id=1, source_target_pairs={{0,24},{4,28},{8,16},{12,20},{16,8},{20,12},{24,0},{28,4},{1,25},{... | collective-permute-start | bytes 589832 | tf_op jit(solution)/shard_map/ppermute | solution.py:522
  73.2 20.6 %collective-permute-start.8 = (bf16[128,768]{1,0:T(8,128)(2,1)S(1)}, bf16[128,768]{1,0:T(8,128)(2,1)S(1)}, u32[]{:S(2)}, u32[]{:S(2)}) collective-permute-start(bf16[128,768]{1,0:T(8,128)(2,1)S(1)} %get-tuple-element.34.refs_1_), channel_id=1, source_target_pairs={{0,8},{4,12},{8,0},{12,4},{16,24},{20,28},{24,16},{28,20},{1,9},{5... | collective-permute-start | bytes 589832 | tf_op jit(solution)/shard_map/ppermute | solution.py:522
  76.9 17.0 %collective-permute-start.9 = (bf16[128,768]{1,0:T(8,128)(2,1)S(1)}, bf16[128,768]{1,0:T(8,128)(2,1)S(1)}, u32[]{:S(2)}, u32[]{:S(2)}) collective-permute-start(bf16[128,768]{1,0:T(8,128)(2,1)S(1)} %get-tuple-element.34.refs_1_), channel_id=1, source_target_pairs={{0,16},{4,20},{8,24},{12,28},{16,0},{20,4},{24,8},{28,12},{1,17},{... | collective-permute-start | bytes 589832 | tf_op jit(solution)/shard_map/ppermute | solution.py:522
  96.7 3.1 %copy-start.6 = (bf16[384,1536]{1,0:T(8,128)(2,1)S(1)}, bf16[384,1536]{1,0:T(8,128)(2,1)}, u32[]{:S(2)}) copy-start(bf16[384,1536]{1,0:T(8,128)(2,1)} %w_ref.1) | copy-start | bytes 3538948
  96.7 3.1 %collective-permute-start.15 = (f32[400,384]{1,0:T(8,128)S(1)}, f32[400,384]{1,0:T(8,128)S(1)}, u32[]{:S(2)}, u32[]{:S(2)}) collective-permute-start(f32[400,384]{1,0:T(8,128)S(1)} %attend_other.1), channel_id=1, source_target_pairs={{0,4},{4,0},{8,12},{12,8},{16,20},{20,16},{24,28},{28,24},{1,5},{5... | collective-permute-start | bytes 1843208 | tf_op jit(solution)/shard_map/ppermute | solution.py:522
  100.8 11.7 %collective-permute-start.16 = (bf16[384,384]{1,0:T(8,128)(2,1)S(1)}, bf16[384,384]{1,0:T(8,128)(2,1)S(1)}, u32[]{:S(2)}, u32[]{:S(2)}) collective-permute-start(bf16[384,384]{1,0:T(8,128)(2,1)S(1)} %get-tuple-element.38), channel_id=1, source_target_pairs={{0,1},{1,2},{2,3},{3,0},{4,5},{5,6},{6,7},{7,4},{8,9},{9,10},{10,1... | collective-permute-start | bytes 884744 | tf_op jit(solution)/shard_map/ppermute | solution.py:578
  101.4 16.3 %collective-permute-start.17 = (bf16[384,384]{1,0:T(8,128)(2,1)S(1)}, bf16[384,384]{1,0:T(8,128)(2,1)S(1)}, u32[]{:S(2)}, u32[]{:S(2)}) collective-permute-start(bf16[384,384]{1,0:T(8,128)(2,1)S(1)} %get-tuple-element.39), channel_id=1, source_target_pairs={{0,3},{1,0},{2,1},{3,2},{4,7},{5,4},{6,5},{7,6},{8,11},{9,8},{10,9... | collective-permute-start | bytes 884744 | tf_op jit(solution)/shard_map/ppermute | solution.py:578
  104.6 26.3 %collective-permute-start.18 = (bf16[384,384]{1,0:T(8,128)(2,1)S(1)}, bf16[384,384]{1,0:T(8,128)(2,1)S(1)}, u32[]{:S(2)}, u32[]{:S(2)}) collective-permute-start(bf16[384,384]{1,0:T(8,128)(2,1)S(1)} %get-tuple-element.40), channel_id=1, source_target_pairs={{0,2},{1,3},{2,0},{3,1},{4,6},{5,7},{6,4},{7,5},{8,10},{9,11},{10,... | collective-permute-start | bytes 884744 | tf_op jit(solution)/shard_map/ppermute | solution.py:578
  (2 other events, 3.1 us)

commit v5 on v3

--- a/solution.py
+++ b/solution.py
@@ -554,14 +554,11 @@
     normed_m[0] = after(normed_m[0], sent)
     weights = (w_query, w_key, w_value)
     q_m, kv_m = project(project_middle_kernel, normed_m, weights, inner, "project_middle")
-    x_m, y_m = exchanged(kv_m, 2), exchanged(kv_m, 4)
-    normed_e[0] = after(normed_e[0], x_m)
-    d_m = exchanged(x_m, 4)
+    x_m, y_m, d_m = (exchanged(kv_m, mask) for mask in (2, 4, 6))
     q, kv_e = project(project_edge_kernel, (*normed_e, q_m), weights, rows, "project_edge")
-    x_e, y_e, q_other = exchanged(kv_e, 2), exchanged(kv_e, 4), exchanged(q, 1)
-    d_e = exchanged(y_e, 2)
-    state = attend((q, q_other), (kv_m, x_m, y_m, d_m), None, 0, "attend_m")
-    late = (kv_e, x_e, y_e, d_e)
+    q_other, x_e, y_e, d_e = exchanged(q, 1), *(exchanged(kv_e, mask) for mask in (2, 4, 6))
+    state = attend((q, q_other), (kv_m, kv_e, x_m, y_m, d_m), None, 0, "attend_m")
+    late = (x_e, y_e, d_e)
     state_other = attend((q_other,), late, state, rows, "attend_other")
     given = exchanged(state_other, 1)
     state_own = attend((q,), late, state, 0, "attend_own")

time: 128 us -> 125 us (0.977)
  waiting for transfers between devices: 64.3 us -> 55.2 us
  starting transfers between devices: 37.2 us -> 43.7 us
    ppermute x12, waiting for transfers between devices: 20.5 us -> 15 us  [shared(): moved.append(lax.ppermute(held, 'head', rotate(k)))]
    ppermute x12, starting transfers between devices: 21.9 us -> 27 us  [shared(): moved.append(lax.ppermute(held, 'head', rotate(k)))]
    ppermute x8, waiting for transfers between devices: 15.2 us -> 11.3 us  [exchanged(): return lax.ppermute(block, 'seq', [(i, i ^ mask) for i in range(count)])]
    ppermute x8, starting transfers between devices: 7.41 us -> 9.18 us  [exchanged(): return lax.ppermute(block, 'seq', [(i, i ^ mask) for i in range(count)])]
  transfers between devices with their start and end apart: 25 -> 25, of which waited for: 11 -> 11; matrix products, arithmetic and copies ran while one was open for 0% -> 0% of each run, Pallas kernels for 12% -> 14%
where the time goes in v5:
time: 125 us
  waiting for transfers between devices  55.2 us (44%)
  starting transfers between devices  43.7 us (35%)
  Pallas kernels  21.9 us (18%)
  local copies, waits for them, and re-layouts  3.13 us (3%)
    ppermute x12, starting transfers between devices, shared(): moved.append(lax.ppermute(held, 'head', rotate(k)))  27 us
    ppermute x3, waiting for transfers between devices, on_device(): lax.ppermute(part, 'head', rotate(shift)).astype(jnp.float32)  25.5 us
    ppermute x12, waiting for transfers between devices, shared(): moved.append(lax.ppermute(held, 'head', rotate(k)))  15 us
    pallas_call x3, Pallas kernels, attend(): pl.pallas_call(kernel, out_shape=out, scratch_shapes=[pltpu.VMEM((2, exte...  12.1 us
    ppermute x8, waiting for transfers between devices, exchanged(): return lax.ppermute(block, 'seq', [(i, i ^ mask) for i in range(count)])  11.3 us
    ppermute x8, starting transfers between devices, exchanged(): return lax.ppermute(block, 'seq', [(i, i ^ mask) for i in range(count)])  9.18 us
    ppermute x3, starting transfers between devices, on_device(): lax.ppermute(part, 'head', rotate(shift)).astype(jnp.float32)  4.75 us
    ppermute x1, waiting for transfers between devices, on_device(): lax.ppermute(dna[:EDGE], 'seq', [(i + 1, i) for i in range(count - 1)])  3.5 us
  transfers between devices with their start and end apart: 25, of which 11 were waited for; matrix products, arithmetic and copies ran while one was open for 0% of the time, Pallas kernels for 14%

profile of v5, /device:TPU:0, one launch (start us, length us, event | category | flops | bytes accessed | tf_op | source)
XLA Modules:
  0.0 125.0 jit_solution(2516903955581075540)
XLA Ops:
  0.0 1.8 %copy-done.1 = bf16[5,384,768]{2,1,0:T(8,128)(2,1)S(1)} copy-done((bf16[5,384,768]{2,1,0:T(8,128)(2,1)S(1)}, bf16[5,384,768]{2,1,0:T(8,128)(2,1)}, u32[]{:S(2)}) %copy-start.1) | copy-done | bytes 2949144
  4.4 3.1 %collective-permute-start = (bf16[272,384]{1,0:T(8,128)(2,1)S(1)}, bf16[272,384]{1,0:T(8,128)(2,1)S(1)}, u32[]{:S(2)}, u32[]{:S(2)}) collective-permute-start(bf16[272,384]{1,0:T(8,128)(2,1)S(1)} %get-tuple-element.30.a0.m0), channel_id=1, source_target_pairs={{0,1},{1,2},{2,3},{3,0},{4,5},{5,6},{6,7},{7,4},{8,9},{9,10},{10,1... | collective-permute-start | bytes 626696 | tf_op jit(solution)/shard_map/ppermute | solution.py:149
  7.5 2.1 %collective-permute-start.1 = (bf16[272,384]{1,0:T(8,128)(2,1)S(1)}, bf16[272,384]{1,0:T(8,128)(2,1)S(1)}, u32[]{:S(2)}, u32[]{:S(2)}) collective-permute-start(bf16[272,384]{1,0:T(8,128)(2,1)S(1)} %get-tuple-element.30.a0.m0), channel_id=1, source_target_pairs={{0,3},{1,0},{2,1},{3,2},{4,7},{5,4},{6,5},{7,6},{8,11},{9,8},{10,9... | collective-permute-start | bytes 626696 | tf_op jit(solution)/shard_map/ppermute | solution.py:149
  13.4 3.5 %collective-permute-done.4.high_ref = bf16[16,768]{1,0:T(8,128)(2,1)S(1)} collective-permute-done((bf16[16,768]{1,0:T(8,128)(2,1)S(1)}, bf16[16,768]{1,0:T(8,128)(2,1)S(1)}, u32[]{:S(2)}, u32[]{:S(2)}) %collective-permute-start.4) | collective-permute-done | bytes 24608 | tf_op jit(solution)/shard_map/ppermute | solution.py:525
  19.9 7.7 %collective-permute-start.7 = (bf16[128,384]{1,0:T(8,128)(2,1)S(1)}, bf16[128,384]{1,0:T(8,128)(2,1)S(1)}, u32[]{:S(2)}, u32[]{:S(2)}) collective-permute-start(bf16[128,384]{1,0:T(8,128)(2,1)S(1)} %get-tuple-element.32.e0), channel_id=1, source_target_pairs={{0,2},{1,3},{2,0},{3,1},{4,6},{5,7},{6,4},{7,5},{8,10},{9,11},{10,... | collective-permute-start | bytes 294920 | tf_op jit(solution)/shard_map/ppermute | solution.py:149
  27.6 4.8 %collective-permute-done.2.a3.m3 = bf16[272,384]{1,0:T(8,128)(2,1)S(1)} collective-permute-done((bf16[272,384]{1,0:T(8,128)(2,1)S(1)}, bf16[272,384]{1,0:T(8,128)(2,1)S(1)}, u32[]{:S(2)}, u32[]{:S(2)}) %collective-permute-start.2) | collective-permute-done | bytes 208928 | tf_op jit(solution)/shard_map/ppermute | solution.py:149
  32.4 2.0 %dilated_middle.1 = (f32[256,384]{1,0:T(8,128)S(1)}, bf16[256,384]{1,0:T(8,128)(2,1)S(1)}) custom-call(bf16[272,384]{1,0:T(8,128)(2,1)S(1)} %get-tuple-element.30.a0.m0, bf16[272,384]{1,0:T(8,128)(2,1)S(1)} %collective-permute-done.a1.m1, bf16[272,384]{1,0:T(8,128)(2,1)S(1)} %collective-permute-done.1.a2.m2, ...), custom_call_target="tpu_custom_call" | custom-call | flops 905969664 | bytes 5382144 | tf_op jit(solution)/shard_map/dilated_middle/pallas_call | solution.py:313
  34.4 2.8 %collective-permute-start.10 = (bf16[256,384]{1,0:T(8,128)(2,1)S(1)}, bf16[256,384]{1,0:T(8,128)(2,1)S(1)}, u32[]{:S(2)}, u32[]{:S(2)}) collective-permute-start(bf16[256,384]{1,0:T(8,128)(2,1)S(1)} %get-tuple-element.45.a0), channel_id=1, source_target_pairs={{0,3},{1,0},{2,1},{3,2},{4,7},{5,4},{6,5},{7,6},{8,11},{9,8},{10,9... | collective-permute-start | bytes 589832 | tf_op jit(solution)/shard_map/ppermute | solution.py:149
  39.4 5.1 %collective-permute-done.10.a2 = bf16[256,384]{1,0:T(8,128)(2,1)S(1)} collective-permute-done((bf16[256,384]{1,0:T(8,128)(2,1)S(1)}, bf16[256,384]{1,0:T(8,128)(2,1)S(1)}, u32[]{:S(2)}, u32[]{:S(2)}) %collective-permute-start.10) | collective-permute-done | bytes 196640 | tf_op jit(solution)/shard_map/ppermute | solution.py:149
  44.5 2.4 %collective-permute-start.11 = (bf16[128,384]{1,0:T(8,128)(2,1)S(1)}, bf16[128,384]{1,0:T(8,128)(2,1)S(1)}, u32[]{:S(2)}, u32[]{:S(2)}) collective-permute-start(bf16[128,384]{1,0:T(8,128)(2,1)S(1)} %get-tuple-element.44.a0), channel_id=1, source_target_pairs={{0,3},{1,0},{2,1},{3,2},{4,7},{5,4},{6,5},{7,6},{8,11},{9,8},{10,9... | collective-permute-start | bytes 294920 | tf_op jit(solution)/shard_map/ppermute | solution.py:149
  47.2 5.2 %collective-permute-start.9 = (bf16[128,384]{1,0:T(8,128)(2,1)S(1)}, bf16[128,384]{1,0:T(8,128)(2,1)S(1)}, u32[]{:S(2)}, u32[]{:S(2)}) collective-permute-start(bf16[128,384]{1,0:T(8,128)(2,1)S(1)} %get-tuple-element.44.a0), channel_id=1, source_target_pairs={{0,1},{1,2},{2,3},{3,0},{4,5},{5,6},{6,7},{7,4},{8,9},{9,10},{10,1... | collective-permute-start | bytes 294920 | tf_op jit(solution)/shard_map/ppermute | solution.py:149
  52.4 4.7 %collective-permute-done.12.a3 = bf16[256,384]{1,0:T(8,128)(2,1)S(1)} collective-permute-done((bf16[256,384]{1,0:T(8,128)(2,1)S(1)}, bf16[256,384]{1,0:T(8,128)(2,1)S(1)}, u32[]{:S(2)}, u32[]{:S(2)}) %collective-permute-start.12) | collective-permute-done | bytes 196640 | tf_op jit(solution)/shard_map/ppermute | solution.py:149
  57.1 1.8 %project_middle.1 = (bf16[256,384]{1,0:T(8,128)(2,1)S(1)}, bf16[256,768]{1,0:T(8,128)(2,1)S(1)}) custom-call(bf16[256,384]{1,0:T(8,128)(2,1)S(1)} %get-tuple-element.45.a0, bf16[256,384]{1,0:T(8,128)(2,1)S(1)} %collective-permute-done.8.a1, bf16[256,384]{1,0:T(8,128)(2,1)S(1)} %collective-permute-done.10.a2, ...), custom_call_target="tpu_custom_call" | custom-call | flops 905969664 | bytes 4915200 | tf_op jit(solution)/shard_map/project_middle/pallas_call | solution.py:370
  67.0 3.9 %collective-permute-done.18.refs_4_ = bf16[256,768]{1,0:T(8,128)(2,1)S(1)} collective-permute-done((bf16[256,768]{1,0:T(8,128)(2,1)S(1)}, bf16[256,768]{1,0:T(8,128)(2,1)S(1)}, u32[]{:S(2)}, u32[]{:S(2)}) %collective-permute-start.18) | collective-permute-done | bytes 393248 | tf_op jit(solution)/shard_map/ppermute | solution.py:516
  71.0 2.4 %collective-permute-start.16 = (bf16[128,768]{1,0:T(8,128)(2,1)S(1)}, bf16[128,768]{1,0:T(8,128)(2,1)S(1)}, u32[]{:S(2)}, u32[]{:S(2)}) collective-permute-start(bf16[128,768]{1,0:T(8,128)(2,1)S(1)} %get-tuple-element.48.refs_3_), channel_id=1, source_target_pairs={{0,24},{4,28},{8,16},{12,20},{16,8},{20,12},{24,0},{28,4},{1,25},{... | collective-permute-start | bytes 589832 | tf_op jit(solution)/shard_map/ppermute | solution.py:516
  73.4 7.3 %collective-permute-done.19.refs_5_ = bf16[256,768]{1,0:T(8,128)(2,1)S(1)} collective-permute-done((bf16[256,768]{1,0:T(8,128)(2,1)S(1)}, bf16[256,768]{1,0:T(8,128)(2,1)S(1)}, u32[]{:S(2)}, u32[]{:S(2)}) %collective-permute-start.19) | collective-permute-done | bytes 393248 | tf_op jit(solution)/shard_map/ppermute | solution.py:516
  80.7 7.1 %attend_m.1.refs_4_ = f32[400,768]{1,0:T(8,128)S(1)} custom-call(bf16[384,384]{1,0:T(8,128)(2,1)S(1)} %get-tuple-element.47.refs_0_, bf16[384,384]{1,0:T(8,128)(2,1)S(1)} %collective-permute-done.17.refs_1_.refs_0_, bf16[256,768]{1,0:T(8,128)(2,1)S(1)} %get-tuple-element.49.refs_2_, bf16[128,768]{1,0:T(8,128)(2,1)S(1)} %get-tuple-element.48.refs_3_, ...), custom_call_target="tpu_custom_call" | custom-call | flops 1358954496 | bytes 3588096 | tf_op jit(solution)/shard_map/attend_m/pallas_call | solution.py:459
  87.8 2.4 %attend_other.1 = f32[400,384]{1,0:T(8,128)S(1)} custom-call(bf16[384,384]{1,0:T(8,128)(2,1)S(1)} %collective-permute-done.17.refs_1_.refs_0_, bf16[128,768]{1,0:T(8,128)(2,1)S(1)} %collective-permute-done.14.refs_1_, bf16[128,768]{1,0:T(8,128)(2,1)S(1)} %collective-permute-done.15.refs_2_, bf16[128,768]{1,0:T(8,128)(2,1)S(1)} %collective-permute-done.16.refs_3_, ...), custom_call_target="tpu_custom_call" | custom-call | flops 226492416 | bytes 2727936 | tf_op jit(solution)/shard_map/attend_other/pallas_call | solution.py:459
  90.3 2.6 %attend_own.1.own_state = f32[400,384]{1,0:T(8,128)S(1)} custom-call(bf16[384,384]{1,0:T(8,128)(2,1)S(1)} %get-tuple-element.47.refs_0_, bf16[128,768]{1,0:T(8,128)(2,1)S(1)} %collective-permute-done.14.refs_1_, bf16[128,768]{1,0:T(8,128)(2,1)S(1)} %collective-permute-done.15.refs_2_, bf16[128,768]{1,0:T(8,128)(2,1)S(1)} %collective-permute-done.16.refs_3_, ...), custom_call_target="tpu_custom_call" | custom-call | flops 226492416 | bytes 2727936 | tf_op jit(solution)/shard_map/attend_own/pallas_call | solution.py:459
  93.9 1.9 %collective-permute-start.22 = (bf16[384,384]{1,0:T(8,128)(2,1)S(1)}, bf16[384,384]{1,0:T(8,128)(2,1)S(1)}, u32[]{:S(2)}, u32[]{:S(2)}) collective-permute-start(bf16[384,384]{1,0:T(8,128)(2,1)S(1)} %get-tuple-element.52), channel_id=1, source_target_pairs={{0,1},{1,2},{2,3},{3,0},{4,5},{5,6},{6,7},{7,4},{8,9},{9,10},{10,1... | collective-permute-start | bytes 884744 | tf_op jit(solution)/shard_map/ppermute | solution.py:568
  95.8 2.0 %collective-permute-start.23 = (bf16[384,384]{1,0:T(8,128)(2,1)S(1)}, bf16[384,384]{1,0:T(8,128)(2,1)S(1)}, u32[]{:S(2)}, u32[]{:S(2)}) collective-permute-start(bf16[384,384]{1,0:T(8,128)(2,1)S(1)} %get-tuple-element.53), channel_id=1, source_target_pairs={{0,3},{1,0},{2,1},{3,2},{4,7},{5,4},{6,5},{7,6},{8,11},{9,8},{10,9... | collective-permute-start | bytes 884744 | tf_op jit(solution)/shard_map/ppermute | solution.py:568
  98.7 6.9 %collective-permute-done.22 = bf16[384,384]{1,0:T(8,128)(2,1)S(1)} collective-permute-done((bf16[384,384]{1,0:T(8,128)(2,1)S(1)}, bf16[384,384]{1,0:T(8,128)(2,1)S(1)}, u32[]{:S(2)}, u32[]{:S(2)}) %collective-permute-start.22) | collective-permute-done | bytes 294944 | tf_op jit(solution)/shard_map/ppermute | solution.py:568
  105.6 5.7 %collective-permute-done.23 = bf16[384,384]{1,0:T(8,128)(2,1)S(1)} collective-permute-done((bf16[384,384]{1,0:T(8,128)(2,1)S(1)}, bf16[384,384]{1,0:T(8,128)(2,1)S(1)}, u32[]{:S(2)}, u32[]{:S(2)}) %collective-permute-start.23) | collective-permute-done | bytes 294944 | tf_op jit(solution)/shard_map/ppermute | solution.py:568
  111.3 12.9 %collective-permute-done.24 = bf16[384,384]{1,0:T(8,128)(2,1)S(1)} collective-permute-done((bf16[384,384]{1,0:T(8,128)(2,1)S(1)}, bf16[384,384]{1,0:T(8,128)(2,1)S(1)}, u32[]{:S(2)}, u32[]{:S(2)}) %collective-permute-start.24) | collective-permute-done | bytes 294944 | tf_op jit(solution)/shard_map/ppermute | solution.py:568
  (52 shorter events, 22.7 us)
Async XLA Ops:
  4.4 15.6 %collective-permute-start = (bf16[272,384]{1,0:T(8,128)(2,1)S(1)}, bf16[272,384]{1,0:T(8,128)(2,1)S(1)}, u32[]{:S(2)}, u32[]{:S(2)}) collective-permute-start(bf16[272,384]{1,0:T(8,128)(2,1)S(1)} %get-tuple-element.30.a0.m0), channel_id=1, source_target_pairs={{0,1},{1,2},{2,3},{3,0},{4,5},{5,6},{6,7},{7,4},{8,9},{9,10},{10,1... | collective-permute-start | bytes 626696 | tf_op jit(solution)/shard_map/ppermute | solution.py:149
  7.5 20.2 %collective-permute-start.1 = (bf16[272,384]{1,0:T(8,128)(2,1)S(1)}, bf16[272,384]{1,0:T(8,128)(2,1)S(1)}, u32[]{:S(2)}, u32[]{:S(2)}) collective-permute-start(bf16[272,384]{1,0:T(8,128)(2,1)S(1)} %get-tuple-element.30.a0.m0), channel_id=1, source_target_pairs={{0,3},{1,0},{2,1},{3,2},{4,7},{5,4},{6,5},{7,6},{8,11},{9,8},{10,9... | collective-permute-start | bytes 626696 | tf_op jit(solution)/shard_map/ppermute | solution.py:149
  9.6 22.9 %collective-permute-start.2 = (bf16[272,384]{1,0:T(8,128)(2,1)S(1)}, bf16[272,384]{1,0:T(8,128)(2,1)S(1)}, u32[]{:S(2)}, u32[]{:S(2)}) collective-permute-start(bf16[272,384]{1,0:T(8,128)(2,1)S(1)} %get-tuple-element.30.a0.m0), channel_id=1, source_target_pairs={{0,2},{1,3},{2,0},{3,1},{4,6},{5,7},{6,4},{7,5},{8,10},{9,11},{10,... | collective-permute-start | bytes 626696 | tf_op jit(solution)/shard_map/ppermute | solution.py:149
  10.5 2.9 %collective-permute-start.3 = (bf16[16,768]{1,0:T(8,128)(2,1)S(1)}, bf16[16,768]{1,0:T(8,128)(2,1)S(1)}, u32[]{:S(2)}, u32[]{:S(2)}) collective-permute-start(bf16[16,768]{1,0:T(8,128)(2,1)S(1)} %get-tuple-element.56), channel_id=1, source_target_pairs={{0,4},{4,8},{8,12},{12,16},{16,20},{20,24},{24,28},{1,5},{5,9},{9,... | collective-permute-start | bytes 73736 | tf_op jit(solution)/shard_map/ppermute | solution.py:524
  11.8 5.1 %collective-permute-start.4 = (bf16[16,768]{1,0:T(8,128)(2,1)S(1)}, bf16[16,768]{1,0:T(8,128)(2,1)S(1)}, u32[]{:S(2)}, u32[]{:S(2)}) collective-permute-start(bf16[16,768]{1,0:T(8,128)(2,1)S(1)} %get-tuple-element.55), channel_id=1, source_target_pairs={{4,0},{8,4},{12,8},{16,12},{20,16},{24,20},{28,24},{5,1},{9,5},{13... | collective-permute-start | bytes 73736 | tf_op jit(solution)/shard_map/ppermute | solution.py:525
  17.9 16.5 %collective-permute-start.6 = (bf16[128,384]{1,0:T(8,128)(2,1)S(1)}, bf16[128,384]{1,0:T(8,128)(2,1)S(1)}, u32[]{:S(2)}, u32[]{:S(2)}) collective-permute-start(bf16[128,384]{1,0:T(8,128)(2,1)S(1)} %get-tuple-element.32.e0), channel_id=1, source_target_pairs={{0,3},{1,0},{2,1},{3,2},{4,7},{5,4},{6,5},{7,6},{8,11},{9,8},{10,9... | collective-permute-start | bytes 294920 | tf_op jit(solution)/shard_map/ppermute | solution.py:149
  19.3 17.9 %collective-permute-start.5 = (bf16[128,384]{1,0:T(8,128)(2,1)S(1)}, bf16[128,384]{1,0:T(8,128)(2,1)S(1)}, u32[]{:S(2)}, u32[]{:S(2)}) collective-permute-start(bf16[128,384]{1,0:T(8,128)(2,1)S(1)} %get-tuple-element.32.e0), channel_id=1, source_target_pairs={{0,1},{1,2},{2,3},{3,0},{4,5},{5,6},{6,7},{7,4},{8,9},{9,10},{10,1... | collective-permute-start | bytes 294920 | tf_op jit(solution)/shard_map/ppermute | solution.py:149
  19.9 17.3 %collective-permute-start.7 = (bf16[128,384]{1,0:T(8,128)(2,1)S(1)}, bf16[128,384]{1,0:T(8,128)(2,1)S(1)}, u32[]{:S(2)}, u32[]{:S(2)}) collective-permute-start(bf16[128,384]{1,0:T(8,128)(2,1)S(1)} %get-tuple-element.32.e0), channel_id=1, source_target_pairs={{0,2},{1,3},{2,0},{3,1},{4,6},{5,7},{6,4},{7,5},{8,10},{9,11},{10,... | collective-permute-start | bytes 294920 | tf_op jit(solution)/shard_map/ppermute | solution.py:149
  34.4 10.1 %collective-permute-start.10 = (bf16[256,384]{1,0:T(8,128)(2,1)S(1)}, bf16[256,384]{1,0:T(8,128)(2,1)S(1)}, u32[]{:S(2)}, u32[]{:S(2)}) collective-permute-start(bf16[256,384]{1,0:T(8,128)(2,1)S(1)} %get-tuple-element.45.a0), channel_id=1, source_target_pairs={{0,3},{1,0},{2,1},{3,2},{4,7},{5,4},{6,5},{7,6},{8,11},{9,8},{10,9... | collective-permute-start | bytes 589832 | tf_op jit(solution)/shard_map/ppermute | solution.py:149
  37.2 10.0 %collective-permute-start.8 = (bf16[256,384]{1,0:T(8,128)(2,1)S(1)}, bf16[256,384]{1,0:T(8,128)(2,1)S(1)}, u32[]{:S(2)}, u32[]{:S(2)}) collective-permute-start(bf16[256,384]{1,0:T(8,128)(2,1)S(1)} %get-tuple-element.45.a0), channel_id=1, source_target_pairs={{0,1},{1,2},{2,3},{3,0},{4,5},{5,6},{6,7},{7,4},{8,9},{9,10},{10,1... | collective-permute-start | bytes 589832 | tf_op jit(solution)/shard_map/ppermute | solution.py:149
  37.2 19.8 %collective-permute-start.12 = (bf16[256,384]{1,0:T(8,128)(2,1)S(1)}, bf16[256,384]{1,0:T(8,128)(2,1)S(1)}, u32[]{:S(2)}, u32[]{:S(2)}) collective-permute-start(bf16[256,384]{1,0:T(8,128)(2,1)S(1)} %get-tuple-element.45.a0), channel_id=1, source_target_pairs={{0,2},{1,3},{2,0},{3,1},{4,6},{5,7},{6,4},{7,5},{8,10},{9,11},{10,... | collective-permute-start | bytes 589832 | tf_op jit(solution)/shard_map/ppermute | solution.py:149
  44.5 17.4 %collective-permute-start.11 = (bf16[128,384]{1,0:T(8,128)(2,1)S(1)}, bf16[128,384]{1,0:T(8,128)(2,1)S(1)}, u32[]{:S(2)}, u32[]{:S(2)}) collective-permute-start(bf16[128,384]{1,0:T(8,128)(2,1)S(1)} %get-tuple-element.44.a0), channel_id=1, source_target_pairs={{0,3},{1,0},{2,1},{3,2},{4,7},{5,4},{6,5},{7,6},{8,11},{9,8},{10,9... | collective-permute-start | bytes 294920 | tf_op jit(solution)/shard_map/ppermute | solution.py:149
  47.2 15.3 %collective-permute-start.9 = (bf16[128,384]{1,0:T(8,128)(2,1)S(1)}, bf16[128,384]{1,0:T(8,128)(2,1)S(1)}, u32[]{:S(2)}, u32[]{:S(2)}) collective-permute-start(bf16[128,384]{1,0:T(8,128)(2,1)S(1)} %get-tuple-element.44.a0), channel_id=1, source_target_pairs={{0,1},{1,2},{2,3},{3,0},{4,5},{5,6},{6,7},{7,4},{8,9},{9,10},{10,1... | collective-permute-start | bytes 294920 | tf_op jit(solution)/shard_map/ppermute | solution.py:149
  57.1 5.5 %collective-permute-start.13 = (bf16[128,384]{1,0:T(8,128)(2,1)S(1)}, bf16[128,384]{1,0:T(8,128)(2,1)S(1)}, u32[]{:S(2)}, u32[]{:S(2)}) collective-permute-start(bf16[128,384]{1,0:T(8,128)(2,1)S(1)} %get-tuple-element.44.a0), channel_id=1, source_target_pairs={{0,2},{1,3},{2,0},{3,1},{4,6},{5,7},{6,4},{7,5},{8,10},{9,11},{10,... | collective-permute-start | bytes 294920 | tf_op jit(solution)/shard_map/ppermute | solution.py:149
  58.9 12.1 %collective-permute-start.18 = (bf16[256,768]{1,0:T(8,128)(2,1)S(1)}, bf16[256,768]{1,0:T(8,128)(2,1)S(1)}, u32[]{:S(2)}, u32[]{:S(2)}) collective-permute-start(bf16[256,768]{1,0:T(8,128)(2,1)S(1)} %get-tuple-element.49.refs_2_), channel_id=1, source_target_pairs={{0,8},{4,12},{8,0},{12,4},{16,24},{20,28},{24,16},{28,20},{1,9},{5... | collective-permute-start | bytes 1179656 | tf_op jit(solution)/shard_map/ppermute | solution.py:516
  60.4 20.3 %collective-permute-start.19 = (bf16[256,768]{1,0:T(8,128)(2,1)S(1)}, bf16[256,768]{1,0:T(8,128)(2,1)S(1)}, u32[]{:S(2)}, u32[]{:S(2)}) collective-permute-start(bf16[256,768]{1,0:T(8,128)(2,1)S(1)} %get-tuple-element.49.refs_2_), channel_id=1, source_target_pairs={{0,16},{4,20},{8,24},{12,28},{16,0},{20,4},{24,8},{28,12},{1,17},{... | collective-permute-start | bytes 1179656 | tf_op jit(solution)/shard_map/ppermute | solution.py:516
  61.9 18.8 %collective-permute-start.20 = (bf16[256,768]{1,0:T(8,128)(2,1)S(1)}, bf16[256,768]{1,0:T(8,128)(2,1)S(1)}, u32[]{:S(2)}, u32[]{:S(2)}) collective-permute-start(bf16[256,768]{1,0:T(8,128)(2,1)S(1)} %get-tuple-element.49.refs_2_), channel_id=1, source_target_pairs={{0,24},{4,28},{8,16},{12,20},{16,8},{20,12},{24,0},{28,4},{1,25},{... | collective-permute-start | bytes 1179656 | tf_op jit(solution)/shard_map/ppermute | solution.py:516
  64.0 23.8 %collective-permute-start.14 = (bf16[128,768]{1,0:T(8,128)(2,1)S(1)}, bf16[128,768]{1,0:T(8,128)(2,1)S(1)}, u32[]{:S(2)}, u32[]{:S(2)}) collective-permute-start(bf16[128,768]{1,0:T(8,128)(2,1)S(1)} %get-tuple-element.48.refs_3_), channel_id=1, source_target_pairs={{0,8},{4,12},{8,0},{12,4},{16,24},{20,28},{24,16},{28,20},{1,9},{5... | collective-permute-start | bytes 589832 | tf_op jit(solution)/shard_map/ppermute | solution.py:516
  65.5 22.3 %collective-permute-start.15 = (bf16[128,768]{1,0:T(8,128)(2,1)S(1)}, bf16[128,768]{1,0:T(8,128)(2,1)S(1)}, u32[]{:S(2)}, u32[]{:S(2)}) collective-permute-start(bf16[128,768]{1,0:T(8,128)(2,1)S(1)} %get-tuple-element.48.refs_3_), channel_id=1, source_target_pairs={{0,16},{4,20},{8,24},{12,28},{16,0},{20,4},{24,8},{28,12},{1,17},{... | collective-permute-start | bytes 589832 | tf_op jit(solution)/shard_map/ppermute | solution.py:516
  71.0 16.8 %collective-permute-start.16 = (bf16[128,768]{1,0:T(8,128)(2,1)S(1)}, bf16[128,768]{1,0:T(8,128)(2,1)S(1)}, u32[]{:S(2)}, u32[]{:S(2)}) collective-permute-start(bf16[128,768]{1,0:T(8,128)(2,1)S(1)} %get-tuple-element.48.refs_3_), channel_id=1, source_target_pairs={{0,24},{4,28},{8,16},{12,20},{16,8},{20,12},{24,0},{28,4},{1,25},{... | collective-permute-start | bytes 589832 | tf_op jit(solution)/shard_map/ppermute | solution.py:516
  90.2 2.7 %collective-permute-start.21 = (f32[400,384]{1,0:T(8,128)S(1)}, f32[400,384]{1,0:T(8,128)S(1)}, u32[]{:S(2)}, u32[]{:S(2)}) collective-permute-start(f32[400,384]{1,0:T(8,128)S(1)} %attend_other.1), channel_id=1, source_target_pairs={{0,4},{4,0},{8,12},{12,8},{16,20},{20,16},{24,28},{28,24},{1,5},{5... | collective-permute-start | bytes 1843208 | tf_op jit(solution)/shard_map/ppermute | solution.py:516
  93.9 11.7 %collective-permute-start.22 = (bf16[384,384]{1,0:T(8,128)(2,1)S(1)}, bf16[384,384]{1,0:T(8,128)(2,1)S(1)}, u32[]{:S(2)}, u32[]{:S(2)}) collective-permute-start(bf16[384,384]{1,0:T(8,128)(2,1)S(1)} %get-tuple-element.52), channel_id=1, source_target_pairs={{0,1},{1,2},{2,3},{3,0},{4,5},{5,6},{6,7},{7,4},{8,9},{9,10},{10,1... | collective-permute-start | bytes 884744 | tf_op jit(solution)/shard_map/ppermute | solution.py:568
  95.8 15.5 %collective-permute-start.23 = (bf16[384,384]{1,0:T(8,128)(2,1)S(1)}, bf16[384,384]{1,0:T(8,128)(2,1)S(1)}, u32[]{:S(2)}, u32[]{:S(2)}) collective-permute-start(bf16[384,384]{1,0:T(8,128)(2,1)S(1)} %get-tuple-element.53), channel_id=1, source_target_pairs={{0,3},{1,0},{2,1},{3,2},{4,7},{5,4},{6,5},{7,6},{8,11},{9,8},{10,9... | collective-permute-start | bytes 884744 | tf_op jit(solution)/shard_map/ppermute | solution.py:568
  97.8 26.4 %collective-permute-start.24 = (bf16[384,384]{1,0:T(8,128)(2,1)S(1)}, bf16[384,384]{1,0:T(8,128)(2,1)S(1)}, u32[]{:S(2)}, u32[]{:S(2)}) collective-permute-start(bf16[384,384]{1,0:T(8,128)(2,1)S(1)} %get-tuple-element.54), channel_id=1, source_target_pairs={{0,2},{1,3},{2,0},{3,1},{4,6},{5,7},{6,4},{7,5},{8,10},{9,11},{10,... | collective-permute-start | bytes 884744 | tf_op jit(solution)/shard_map/ppermute | solution.py:568
  (8 other events, 85.8 us)

commit v6 on v5

--- a/solution.py
+++ b/solution.py
@@ -331,24 +331,29 @@
     inverse = inverse_norm(blocks)
     normed = [(block * inverse).astype(jnp.bfloat16) for block in blocks]
 
-    def product(weight_ref, weight_first):
+    def product(weight_ref, start=0, stop=rows, weight_first=False):
         total = None
         for part, shift in zip(normed, SHIFTS):
             weight = weight_ref[:, columns_of(shift, width)]
-            pair = (weight, part) if weight_first else (part, weight)
+            taken = part[start:stop]
+            pair = (weight, taken) if weight_first else (taken, weight)
             term = reduce_operands(*pair)
             total = term if total is None else total + term
         return total
 
-    kv_ref[:, :out] = product(wk, False).astype(jnp.bfloat16)
-    value = product(wv, True).astype(jnp.bfloat16)
-    for row in range(0, rows, LANES):
+    kv_ref[:, :out] = product(wk).astype(jnp.bfloat16)
+    turned = rows - rows % LANES
+    value = product(wv, 0, turned, True).astype(jnp.bfloat16)
+    for row in range(0, turned, LANES):
         for lane in range(0, out, LANES):
             kv_ref[pl.ds(row, LANES), pl.ds(out + lane, LANES)] = value[
                 lane : lane + LANES, row : row + LANES
             ]
+    if turned < rows:
+        value = product(wv, turned, rows)
+        kv_ref[pl.ds(turned, rows - turned), out:] = value.astype(jnp.bfloat16)
     scale = LOG2E / math.sqrt(HEAD_DIM)
-    return (product(wq, False) * scale).astype(jnp.bfloat16)
+    return (product(wq) * scale).astype(jnp.bfloat16)
 
 
 def project_middle_kernel(a0, a1, a2, a3, wq, wk, wv, q_ref, kv_ref):
@@ -379,13 +384,41 @@
 TILE = 64
 
 
-def partial_attention(query, blocks, scores, weights, head, lane):
-    width = query.shape[1]
+def split_rows(block):
+    turned = block.shape[0] - block.shape[0] % LANES
+    return turned, block.shape[0] - turned
+
+
+def turned_values(blocks, width, pair):
+    lanes = pl.ds(width + pair * LANES, LANES)
+    values = []
+    for block in blocks:
+        for row in range(0, split_rows(block)[0], LANES):
+            values.append(block[pl.ds(row, LANES), lanes])
+    rest = []
+    for block in blocks:
+        start, count = split_rows(block)
+        if count:
+            rest.append(block[pl.ds(start, count), lanes].astype(jnp.float32))
+    if rest:
+        values.append(jnp.transpose(jnp.concatenate(rest, axis=0)).astype(jnp.bfloat16))
+    return jnp.concatenate(values, axis=1)
+
+
+def ordered_keys(blocks, pair):
+    lanes = pl.ds(pair * LANES, LANES)
+    keys = [block[pl.ds(0, split_rows(block)[0]), lanes] for block in blocks]
+    for block in blocks:
+        start, count = split_rows(block)
+        if count:
+            keys.append(block[pl.ds(start, count), lanes])
+    return jnp.concatenate(keys, axis=0)
+
+
+def partial_attention(query, keys, values, scores, weights, head, lane):
     pair, half = divmod(head, 2)
-    lanes = slice(pair * LANES, (pair + 1) * LANES)
-    mine = query[:, lanes]
+    mine = query[:, pair * LANES : (pair + 1) * LANES]
     mine = jnp.where((lane // HEAD_DIM) == half, mine, jnp.zeros_like(mine))
-    keys = jnp.concatenate([block[:, lanes] for block in blocks], axis=0)
     scores[...] = reduce_operands(keys, mine)
     columns = scores.shape[1]
     top = None
@@ -399,12 +432,7 @@
         tile = jnp.sum(weight.reshape(-1, 8, columns), axis=0)
         total = tile if total is None else total + tile
         weights[pl.ds(start, TILE), :] = weight.astype(jnp.bfloat16)
-    values = [
-        block[pl.ds(row + half * HEAD_DIM, HEAD_DIM), pl.ds(width + pair * LANES, LANES)]
-        for block in blocks
-        for row in range(0, block.shape[0], LANES)
-    ]
-    values = jnp.concatenate(values, axis=1)
+    values = values[half * HEAD_DIM : (half + 1) * HEAD_DIM]
     out = jnp.dot(values, weights[...], preferred_element_type=jnp.float32)
     return out, top, jnp.sum(total, axis=0, keepdims=True)
 
@@ -430,8 +458,11 @@
     lane = lax.broadcasted_iota(jnp.int32, (columns, LANES), 1)
     out_ref[pl.ds(width, 16), :] = jnp.zeros((16, columns), jnp.float32)
     for head in range(width // HEAD_DIM):
+        if head % 2 == 0:
+            keys = ordered_keys(blocks, head // 2)
+            values = turned_values(blocks, width, head // 2)
         part = partial_attention(
-            query, blocks, scores.at[head % 2], weights.at[head % 2], head, lane
+            query, keys, values, scores.at[head % 2], weights.at[head % 2], head, lane
         )
         if state is not None:
             part = merged_parts(
@@ -519,7 +550,7 @@
 def on_device(dna, conv_in, dilated_kernel_weight, w_query, w_key, w_value, w_out):
     count = lax.axis_size("seq")
     rows = dna.shape[0] // 2
-    inner = 2 * LANES
+    inner = rows // 2
     outer = rows - inner
     low = lax.ppermute(dna[-EDGE:], "seq", [(i, i + 1) for i in range(count - 1)])
     high = lax.ppermute(dna[:EDGE], "seq", [(i + 1, i) for i in range(count - 1)])

time: 125 us -> 126 us (level)
  starting transfers between devices: 43.7 us -> 50.8 us
  waiting for transfers between devices: 55.2 us -> 48.3 us
    ppermute x3, starting transfers between devices: 4.75 us -> 8.5 us  [on_device(): lax.ppermute(part, 'head', rotate(shift)).astype(jnp.float32)]
    ppermute x8, waiting for transfers between devices: 11.3 us -> 7.81 us  [exchanged(): return lax.ppermute(block, 'seq', [(i, i ^ mask) for i in range(count)])]
    ppermute x1, waiting for transfers between devices: 3.5 us -> 0.25 us  [on_device(): lax.ppermute(dna[:EDGE], 'seq', [(i + 1, i) for i in range(count - 1)])]
    ppermute x8, starting transfers between devices: 9.18 us -> 11.2 us  [exchanged(): return lax.ppermute(block, 'seq', [(i, i ^ mask) for i in range(count)])]
where the time goes in v6:
time: 126 us
  starting transfers between devices  50.8 us (40%)
  waiting for transfers between devices  48.3 us (38%)
  Pallas kernels  22.5 us (18%)
  local copies, waits for them, and re-layouts  3.13 us (2%)
    ppermute x12, starting transfers between devices, shared(): moved.append(lax.ppermute(held, 'head', rotate(k)))  28.2 us
    ppermute x3, waiting for transfers between devices, on_device(): lax.ppermute(part, 'head', rotate(shift)).astype(jnp.float32)  24.9 us
    ppermute x12, waiting for transfers between devices, shared(): moved.append(lax.ppermute(held, 'head', rotate(k)))  15.4 us
    pallas_call x3, Pallas kernels, attend(): pl.pallas_call(kernel, out_shape=out, scratch_shapes=[pltpu.VMEM((2, exte...  12.1 us
    ppermute x8, starting transfers between devices, exchanged(): return lax.ppermute(block, 'seq', [(i, i ^ mask) for i in range(count)])  11.2 us
    ppermute x3, starting transfers between devices, on_device(): lax.ppermute(part, 'head', rotate(shift)).astype(jnp.float32)  8.5 us
    ppermute x8, waiting for transfers between devices, exchanged(): return lax.ppermute(block, 'seq', [(i, i ^ mask) for i in range(count)])  7.81 us
    pallas_call x2, Pallas kernels, project(): pl.pallas_call(kernel, out_shape=(q, kv), compiler_params=pltpu.CompilerP...  3.72 us
  transfers between devices with their start and end apart: 25, of which 11 were waited for; matrix products, arithmetic and copies ran while one was open for 0% of the time, Pallas kernels for 14%

profile of v6, /device:TPU:0, one launch (start us, length us, event | category | flops | bytes accessed | tf_op | source)
XLA Modules:
  0.0 125.8 jit_solution(8081795872740966552)
XLA Ops:
  0.0 1.8 %copy-done.1 = bf16[5,384,768]{2,1,0:T(8,128)(2,1)S(1)} copy-done((bf16[5,384,768]{2,1,0:T(8,128)(2,1)S(1)}, bf16[5,384,768]{2,1,0:T(8,128)(2,1)}, u32[]{:S(2)}) %copy-start.1) | copy-done | bytes 2949144
  4.3 3.1 %collective-permute-start = (bf16[208,384]{1,0:T(8,128)(2,1)S(1)}, bf16[208,384]{1,0:T(8,128)(2,1)S(1)}, u32[]{:S(2)}, u32[]{:S(2)}) collective-permute-start(bf16[208,384]{1,0:T(8,128)(2,1)S(1)} %get-tuple-element.30.a0.m0), channel_id=1, source_target_pairs={{0,1},{1,2},{2,3},{3,0},{4,5},{5,6},{6,7},{7,4},{8,9},{9,10},{10,1... | collective-permute-start | bytes 479240 | tf_op jit(solution)/shard_map/ppermute | solution.py:149
  10.4 2.4 %collective-permute-start.1 = (bf16[208,384]{1,0:T(8,128)(2,1)S(1)}, bf16[208,384]{1,0:T(8,128)(2,1)S(1)}, u32[]{:S(2)}, u32[]{:S(2)}) collective-permute-start(bf16[208,384]{1,0:T(8,128)(2,1)S(1)} %get-tuple-element.30.a0.m0), channel_id=1, source_target_pairs={{0,3},{1,0},{2,1},{3,2},{4,7},{5,4},{6,5},{7,6},{8,11},{9,8},{10,9... | collective-permute-start | bytes 479240 | tf_op jit(solution)/shard_map/ppermute | solution.py:149
  14.8 2.3 %collective-permute-start.6 = (bf16[192,384]{1,0:T(8,128)(2,1)S(1)}, bf16[192,384]{1,0:T(8,128)(2,1)S(1)}, u32[]{:S(2)}, u32[]{:S(2)}) collective-permute-start(bf16[192,384]{1,0:T(8,128)(2,1)S(1)} %get-tuple-element.32.e0), channel_id=1, source_target_pairs={{0,3},{1,0},{2,1},{3,2},{4,7},{5,4},{6,5},{7,6},{8,11},{9,8},{10,9... | collective-permute-start | bytes 442376 | tf_op jit(solution)/shard_map/ppermute | solution.py:149
  17.2 2.4 %collective-permute-start.7 = (bf16[192,384]{1,0:T(8,128)(2,1)S(1)}, bf16[192,384]{1,0:T(8,128)(2,1)S(1)}, u32[]{:S(2)}, u32[]{:S(2)}) collective-permute-start(bf16[192,384]{1,0:T(8,128)(2,1)S(1)} %get-tuple-element.32.e0), channel_id=1, source_target_pairs={{0,2},{1,3},{2,0},{3,1},{4,6},{5,7},{6,4},{7,5},{8,10},{9,11},{10,... | collective-permute-start | bytes 442376 | tf_op jit(solution)/shard_map/ppermute | solution.py:149
  19.5 3.8 %collective-permute-done.2.a3.m3 = bf16[208,384]{1,0:T(8,128)(2,1)S(1)} collective-permute-done((bf16[208,384]{1,0:T(8,128)(2,1)S(1)}, bf16[208,384]{1,0:T(8,128)(2,1)S(1)}, u32[]{:S(2)}, u32[]{:S(2)}) %collective-permute-start.2) | collective-permute-done | bytes 159776 | tf_op jit(solution)/shard_map/ppermute | solution.py:149
  25.0 11.4 %collective-permute-start.10 = (bf16[192,384]{1,0:T(8,128)(2,1)S(1)}, bf16[192,384]{1,0:T(8,128)(2,1)S(1)}, u32[]{:S(2)}, u32[]{:S(2)}) collective-permute-start(bf16[192,384]{1,0:T(8,128)(2,1)S(1)} %get-tuple-element.45.a0), channel_id=1, source_target_pairs={{0,3},{1,0},{2,1},{3,2},{4,7},{5,4},{6,5},{7,6},{8,11},{9,8},{10,9... | collective-permute-start | bytes 442376 | tf_op jit(solution)/shard_map/ppermute | solution.py:149
  38.8 1.9 %collective-permute-done.10.a2 = bf16[192,384]{1,0:T(8,128)(2,1)S(1)} collective-permute-done((bf16[192,384]{1,0:T(8,128)(2,1)S(1)}, bf16[192,384]{1,0:T(8,128)(2,1)S(1)}, u32[]{:S(2)}, u32[]{:S(2)}) %collective-permute-start.10) | collective-permute-done | bytes 147488 | tf_op jit(solution)/shard_map/ppermute | solution.py:149
  40.7 4.3 %collective-permute-start.11 = (bf16[192,384]{1,0:T(8,128)(2,1)S(1)}, bf16[192,384]{1,0:T(8,128)(2,1)S(1)}, u32[]{:S(2)}, u32[]{:S(2)}) collective-permute-start(bf16[192,384]{1,0:T(8,128)(2,1)S(1)} %get-tuple-element.44.a0), channel_id=1, source_target_pairs={{0,3},{1,0},{2,1},{3,2},{4,7},{5,4},{6,5},{7,6},{8,11},{9,8},{10,9... | collective-permute-start | bytes 442376 | tf_op jit(solution)/shard_map/ppermute | solution.py:149
  46.4 7.4 %collective-permute-done.12.a3 = bf16[192,384]{1,0:T(8,128)(2,1)S(1)} collective-permute-done((bf16[192,384]{1,0:T(8,128)(2,1)S(1)}, bf16[192,384]{1,0:T(8,128)(2,1)S(1)}, u32[]{:S(2)}, u32[]{:S(2)}) %collective-permute-start.12) | collective-permute-done | bytes 147488 | tf_op jit(solution)/shard_map/ppermute | solution.py:149
  53.8 1.9 %project_middle.1 = (bf16[192,384]{1,0:T(8,128)(2,1)S(1)}, bf16[192,768]{1,0:T(8,128)(2,1)S(1)}) custom-call(bf16[192,384]{1,0:T(8,128)(2,1)S(1)} %get-tuple-element.45.a0, bf16[192,384]{1,0:T(8,128)(2,1)S(1)} %collective-permute-done.8.a1, bf16[192,384]{1,0:T(8,128)(2,1)S(1)} %collective-permute-done.10.a2, ...), custom_call_target="tpu_custom_call" | custom-call | flops 679477248 | bytes 4571136 | tf_op jit(solution)/shard_map/project_middle/pallas_call | solution.py:375
  55.7 3.9 %collective-permute-start.18 = (bf16[192,768]{1,0:T(8,128)(2,1)S(1)}, bf16[192,768]{1,0:T(8,128)(2,1)S(1)}, u32[]{:S(2)}, u32[]{:S(2)}) collective-permute-start(bf16[192,768]{1,0:T(8,128)(2,1)S(1)} %get-tuple-element.49.refs_2_), channel_id=1, source_target_pairs={{0,8},{4,12},{8,0},{12,4},{16,24},{20,28},{24,16},{28,20},{1,9},{5... | collective-permute-start | bytes 884744 | tf_op jit(solution)/shard_map/ppermute | solution.py:547
  61.7 1.9 %collective-permute-done.13.a3 = bf16[192,384]{1,0:T(8,128)(2,1)S(1)} collective-permute-done((bf16[192,384]{1,0:T(8,128)(2,1)S(1)}, bf16[192,384]{1,0:T(8,128)(2,1)S(1)}, u32[]{:S(2)}, u32[]{:S(2)}) %collective-permute-start.13) | collective-permute-done | bytes 147488 | tf_op jit(solution)/shard_map/ppermute | solution.py:149
  63.6 1.9 %project_edge.1 = (bf16[384,384]{1,0:T(8,128)(2,1)S(1)}, bf16[192,768]{1,0:T(8,128)(2,1)S(1)}) custom-call(bf16[192,384]{1,0:T(8,128)(2,1)S(1)} %get-tuple-element.44.a0, bf16[192,384]{1,0:T(8,128)(2,1)S(1)} %collective-permute-done.9.a1, bf16[192,384]{1,0:T(8,128)(2,1)S(1)} %collective-permute-done.11.a2, bf16[192,384]{1,0:T(8,128)(2,1)S(1)} %collective-permute-done.13.a3, ...), custom_call_target="tpu_custom_call" | custom-call | flops 679477248 | bytes 4866048 | tf_op jit(solution)/shard_map/project_edge/pallas_call | solution.py:375
  65.6 2.8 %collective-permute-start.14 = (bf16[192,768]{1,0:T(8,128)(2,1)S(1)}, bf16[192,768]{1,0:T(8,128)(2,1)S(1)}, u32[]{:S(2)}, u32[]{:S(2)}) collective-permute-start(bf16[192,768]{1,0:T(8,128)(2,1)S(1)} %get-tuple-element.48.refs_3_), channel_id=1, source_target_pairs={{0,8},{4,12},{8,0},{12,4},{16,24},{20,28},{24,16},{28,20},{1,9},{5... | collective-permute-start | bytes 884744 | tf_op jit(solution)/shard_map/ppermute | solution.py:547
  69.6 2.5 %collective-permute-done.19.refs_5_ = bf16[192,768]{1,0:T(8,128)(2,1)S(1)} collective-permute-done((bf16[192,768]{1,0:T(8,128)(2,1)S(1)}, bf16[192,768]{1,0:T(8,128)(2,1)S(1)}, u32[]{:S(2)}, u32[]{:S(2)}) %collective-permute-start.19) | collective-permute-done | bytes 294944 | tf_op jit(solution)/shard_map/ppermute | solution.py:547
  73.0 6.0 %attend_m.1.refs_4_ = f32[400,768]{1,0:T(8,128)S(1)} custom-call(bf16[384,384]{1,0:T(8,128)(2,1)S(1)} %get-tuple-element.47.refs_0_, bf16[384,384]{1,0:T(8,128)(2,1)S(1)} %collective-permute-done.17.refs_1_.refs_0_, bf16[192,768]{1,0:T(8,128)(2,1)S(1)} %get-tuple-element.49.refs_2_, bf16[192,768]{1,0:T(8,128)(2,1)S(1)} %get-tuple-element.48.refs_3_, ...), custom_call_target="tpu_custom_call" | custom-call | flops 1132462080 | bytes 3293184 | tf_op jit(solution)/shard_map/attend_m/pallas_call | solution.py:490
  79.0 5.3 %collective-permute-done.15.refs_2_ = bf16[192,768]{1,0:T(8,128)(2,1)S(1)} collective-permute-done((bf16[192,768]{1,0:T(8,128)(2,1)S(1)}, bf16[192,768]{1,0:T(8,128)(2,1)S(1)}, u32[]{:S(2)}, u32[]{:S(2)}) %collective-permute-start.15) | collective-permute-done | bytes 294944 | tf_op jit(solution)/shard_map/ppermute | solution.py:547
  84.3 3.0 %attend_other.1 = f32[400,384]{1,0:T(8,128)S(1)} custom-call(bf16[384,384]{1,0:T(8,128)(2,1)S(1)} %collective-permute-done.17.refs_1_.refs_0_, bf16[192,768]{1,0:T(8,128)(2,1)S(1)} %collective-permute-done.14.refs_1_, bf16[192,768]{1,0:T(8,128)(2,1)S(1)} %collective-permute-done.15.refs_2_, bf16[192,768]{1,0:T(8,128)(2,1)S(1)} %collective-permute-done.16.refs_3_, ...), custom_call_target="tpu_custom_call" | custom-call | flops 339738624 | bytes 3022848 | tf_op jit(solution)/shard_map/attend_other/pallas_call | solution.py:490
  87.4 3.2 %attend_own.1.own_state = f32[400,384]{1,0:T(8,128)S(1)} custom-call(bf16[384,384]{1,0:T(8,128)(2,1)S(1)} %get-tuple-element.47.refs_0_, bf16[192,768]{1,0:T(8,128)(2,1)S(1)} %collective-permute-done.14.refs_1_, bf16[192,768]{1,0:T(8,128)(2,1)S(1)} %collective-permute-done.15.refs_2_, bf16[192,768]{1,0:T(8,128)(2,1)S(1)} %collective-permute-done.16.refs_3_, ...), custom_call_target="tpu_custom_call" | custom-call | flops 339738624 | bytes 3022848 | tf_op jit(solution)/shard_map/attend_own/pallas_call | solution.py:490
  91.6 7.0 %collective-permute-start.22 = (bf16[384,384]{1,0:T(8,128)(2,1)S(1)}, bf16[384,384]{1,0:T(8,128)(2,1)S(1)}, u32[]{:S(2)}, u32[]{:S(2)}) collective-permute-start(bf16[384,384]{1,0:T(8,128)(2,1)S(1)} %get-tuple-element.52), channel_id=1, source_target_pairs={{0,1},{1,2},{2,3},{3,0},{4,5},{5,6},{6,7},{7,4},{8,9},{9,10},{10,1... | collective-permute-start | bytes 884744 | tf_op jit(solution)/shard_map/ppermute | solution.py:599
  100.1 6.1 %collective-permute-done.22 = bf16[384,384]{1,0:T(8,128)(2,1)S(1)} collective-permute-done((bf16[384,384]{1,0:T(8,128)(2,1)S(1)}, bf16[384,384]{1,0:T(8,128)(2,1)S(1)}, u32[]{:S(2)}, u32[]{:S(2)}) %collective-permute-start.22) | collective-permute-done | bytes 294944 | tf_op jit(solution)/shard_map/ppermute | solution.py:599
  106.2 6.1 %collective-permute-done.23 = bf16[384,384]{1,0:T(8,128)(2,1)S(1)} collective-permute-done((bf16[384,384]{1,0:T(8,128)(2,1)S(1)}, bf16[384,384]{1,0:T(8,128)(2,1)S(1)}, u32[]{:S(2)}, u32[]{:S(2)}) %collective-permute-start.23) | collective-permute-done | bytes 294944 | tf_op jit(solution)/shard_map/ppermute | solution.py:599
  112.3 12.6 %collective-permute-done.24 = bf16[384,384]{1,0:T(8,128)(2,1)S(1)} collective-permute-done((bf16[384,384]{1,0:T(8,128)(2,1)S(1)}, bf16[384,384]{1,0:T(8,128)(2,1)S(1)}, u32[]{:S(2)}, u32[]{:S(2)}) %collective-permute-start.24) | collective-permute-done | bytes 294944 | tf_op jit(solution)/shard_map/ppermute | solution.py:599
  (52 shorter events, 20.7 us)
Async XLA Ops:
  4.3 12.9 %collective-permute-start = (bf16[208,384]{1,0:T(8,128)(2,1)S(1)}, bf16[208,384]{1,0:T(8,128)(2,1)S(1)}, u32[]{:S(2)}, u32[]{:S(2)}) collective-permute-start(bf16[208,384]{1,0:T(8,128)(2,1)S(1)} %get-tuple-element.30.a0.m0), channel_id=1, source_target_pairs={{0,1},{1,2},{2,3},{3,0},{4,5},{5,6},{6,7},{7,4},{8,9},{9,10},{10,1... | collective-permute-start | bytes 479240 | tf_op jit(solution)/shard_map/ppermute | solution.py:149
  7.3 6.1 %collective-permute-start.3 = (bf16[16,768]{1,0:T(8,128)(2,1)S(1)}, bf16[16,768]{1,0:T(8,128)(2,1)S(1)}, u32[]{:S(2)}, u32[]{:S(2)}) collective-permute-start(bf16[16,768]{1,0:T(8,128)(2,1)S(1)} %get-tuple-element.56), channel_id=1, source_target_pairs={{0,4},{4,8},{8,12},{12,16},{16,20},{20,24},{24,28},{1,5},{5,9},{9,... | collective-permute-start | bytes 73736 | tf_op jit(solution)/shard_map/ppermute | solution.py:555
  8.8 4.9 %collective-permute-start.4 = (bf16[16,768]{1,0:T(8,128)(2,1)S(1)}, bf16[16,768]{1,0:T(8,128)(2,1)S(1)}, u32[]{:S(2)}, u32[]{:S(2)}) collective-permute-start(bf16[16,768]{1,0:T(8,128)(2,1)S(1)} %get-tuple-element.55), channel_id=1, source_target_pairs={{4,0},{8,4},{12,8},{16,12},{20,16},{24,20},{28,24},{5,1},{9,5},{13... | collective-permute-start | bytes 73736 | tf_op jit(solution)/shard_map/ppermute | solution.py:556
  10.4 9.1 %collective-permute-start.1 = (bf16[208,384]{1,0:T(8,128)(2,1)S(1)}, bf16[208,384]{1,0:T(8,128)(2,1)S(1)}, u32[]{:S(2)}, u32[]{:S(2)}) collective-permute-start(bf16[208,384]{1,0:T(8,128)(2,1)S(1)} %get-tuple-element.30.a0.m0), channel_id=1, source_target_pairs={{0,3},{1,0},{2,1},{3,2},{4,7},{5,4},{6,5},{7,6},{8,11},{9,8},{10,9... | collective-permute-start | bytes 479240 | tf_op jit(solution)/shard_map/ppermute | solution.py:149
  12.8 10.6 %collective-permute-start.2 = (bf16[208,384]{1,0:T(8,128)(2,1)S(1)}, bf16[208,384]{1,0:T(8,128)(2,1)S(1)}, u32[]{:S(2)}, u32[]{:S(2)}) collective-permute-start(bf16[208,384]{1,0:T(8,128)(2,1)S(1)} %get-tuple-element.30.a0.m0), channel_id=1, source_target_pairs={{0,2},{1,3},{2,0},{3,1},{4,6},{5,7},{6,4},{7,5},{8,10},{9,11},{10,... | collective-permute-start | bytes 479240 | tf_op jit(solution)/shard_map/ppermute | solution.py:149
  14.8 10.2 %collective-permute-start.6 = (bf16[192,384]{1,0:T(8,128)(2,1)S(1)}, bf16[192,384]{1,0:T(8,128)(2,1)S(1)}, u32[]{:S(2)}, u32[]{:S(2)}) collective-permute-start(bf16[192,384]{1,0:T(8,128)(2,1)S(1)} %get-tuple-element.32.e0), channel_id=1, source_target_pairs={{0,3},{1,0},{2,1},{3,2},{4,7},{5,4},{6,5},{7,6},{8,11},{9,8},{10,9... | collective-permute-start | bytes 442376 | tf_op jit(solution)/shard_map/ppermute | solution.py:149
  17.1 19.3 %collective-permute-start.5 = (bf16[192,384]{1,0:T(8,128)(2,1)S(1)}, bf16[192,384]{1,0:T(8,128)(2,1)S(1)}, u32[]{:S(2)}, u32[]{:S(2)}) collective-permute-start(bf16[192,384]{1,0:T(8,128)(2,1)S(1)} %get-tuple-element.32.e0), channel_id=1, source_target_pairs={{0,1},{1,2},{2,3},{3,0},{4,5},{5,6},{6,7},{7,4},{8,9},{9,10},{10,1... | collective-permute-start | bytes 442376 | tf_op jit(solution)/shard_map/ppermute | solution.py:149
  17.2 19.6 %collective-permute-start.7 = (bf16[192,384]{1,0:T(8,128)(2,1)S(1)}, bf16[192,384]{1,0:T(8,128)(2,1)S(1)}, u32[]{:S(2)}, u32[]{:S(2)}) collective-permute-start(bf16[192,384]{1,0:T(8,128)(2,1)S(1)} %get-tuple-element.32.e0), channel_id=1, source_target_pairs={{0,2},{1,3},{2,0},{3,1},{4,6},{5,7},{6,4},{7,5},{8,10},{9,11},{10,... | collective-permute-start | bytes 442376 | tf_op jit(solution)/shard_map/ppermute | solution.py:149
  25.0 15.7 %collective-permute-start.10 = (bf16[192,384]{1,0:T(8,128)(2,1)S(1)}, bf16[192,384]{1,0:T(8,128)(2,1)S(1)}, u32[]{:S(2)}, u32[]{:S(2)}) collective-permute-start(bf16[192,384]{1,0:T(8,128)(2,1)S(1)} %get-tuple-element.45.a0), channel_id=1, source_target_pairs={{0,3},{1,0},{2,1},{3,2},{4,7},{5,4},{6,5},{7,6},{8,11},{9,8},{10,9... | collective-permute-start | bytes 442376 | tf_op jit(solution)/shard_map/ppermute | solution.py:149
  36.4 8.6 %collective-permute-start.8 = (bf16[192,384]{1,0:T(8,128)(2,1)S(1)}, bf16[192,384]{1,0:T(8,128)(2,1)S(1)}, u32[]{:S(2)}, u32[]{:S(2)}) collective-permute-start(bf16[192,384]{1,0:T(8,128)(2,1)S(1)} %get-tuple-element.45.a0), channel_id=1, source_target_pairs={{0,1},{1,2},{2,3},{3,0},{4,5},{5,6},{6,7},{7,4},{8,9},{9,10},{10,1... | collective-permute-start | bytes 442376 | tf_op jit(solution)/shard_map/ppermute | solution.py:149
  36.7 17.0 %collective-permute-start.12 = (bf16[192,384]{1,0:T(8,128)(2,1)S(1)}, bf16[192,384]{1,0:T(8,128)(2,1)S(1)}, u32[]{:S(2)}, u32[]{:S(2)}) collective-permute-start(bf16[192,384]{1,0:T(8,128)(2,1)S(1)} %get-tuple-element.45.a0), channel_id=1, source_target_pairs={{0,2},{1,3},{2,0},{3,1},{4,6},{5,7},{6,4},{7,5},{8,10},{9,11},{10,... | collective-permute-start | bytes 442376 | tf_op jit(solution)/shard_map/ppermute | solution.py:149
  40.7 19.7 %collective-permute-start.11 = (bf16[192,384]{1,0:T(8,128)(2,1)S(1)}, bf16[192,384]{1,0:T(8,128)(2,1)S(1)}, u32[]{:S(2)}, u32[]{:S(2)}) collective-permute-start(bf16[192,384]{1,0:T(8,128)(2,1)S(1)} %get-tuple-element.44.a0), channel_id=1, source_target_pairs={{0,3},{1,0},{2,1},{3,2},{4,7},{5,4},{6,5},{7,6},{8,11},{9,8},{10,9... | collective-permute-start | bytes 442376 | tf_op jit(solution)/shard_map/ppermute | solution.py:149
  45.0 16.7 %collective-permute-start.9 = (bf16[192,384]{1,0:T(8,128)(2,1)S(1)}, bf16[192,384]{1,0:T(8,128)(2,1)S(1)}, u32[]{:S(2)}, u32[]{:S(2)}) collective-permute-start(bf16[192,384]{1,0:T(8,128)(2,1)S(1)} %get-tuple-element.44.a0), channel_id=1, source_target_pairs={{0,1},{1,2},{2,3},{3,0},{4,5},{5,6},{6,7},{7,4},{8,9},{9,10},{10,1... | collective-permute-start | bytes 442376 | tf_op jit(solution)/shard_map/ppermute | solution.py:149
  53.8 9.9 %collective-permute-start.13 = (bf16[192,384]{1,0:T(8,128)(2,1)S(1)}, bf16[192,384]{1,0:T(8,128)(2,1)S(1)}, u32[]{:S(2)}, u32[]{:S(2)}) collective-permute-start(bf16[192,384]{1,0:T(8,128)(2,1)S(1)} %get-tuple-element.44.a0), channel_id=1, source_target_pairs={{0,2},{1,3},{2,0},{3,1},{4,6},{5,7},{6,4},{7,5},{8,10},{9,11},{10,... | collective-permute-start | bytes 442376 | tf_op jit(solution)/shard_map/ppermute | solution.py:149
  55.7 12.8 %collective-permute-start.18 = (bf16[192,768]{1,0:T(8,128)(2,1)S(1)}, bf16[192,768]{1,0:T(8,128)(2,1)S(1)}, u32[]{:S(2)}, u32[]{:S(2)}) collective-permute-start(bf16[192,768]{1,0:T(8,128)(2,1)S(1)} %get-tuple-element.49.refs_2_), channel_id=1, source_target_pairs={{0,8},{4,12},{8,0},{12,4},{16,24},{20,28},{24,16},{28,20},{1,9},{5... | collective-permute-start | bytes 884744 | tf_op jit(solution)/shard_map/ppermute | solution.py:547
  59.6 12.5 %collective-permute-start.19 = (bf16[192,768]{1,0:T(8,128)(2,1)S(1)}, bf16[192,768]{1,0:T(8,128)(2,1)S(1)}, u32[]{:S(2)}, u32[]{:S(2)}) collective-permute-start(bf16[192,768]{1,0:T(8,128)(2,1)S(1)} %get-tuple-element.49.refs_2_), channel_id=1, source_target_pairs={{0,16},{4,20},{8,24},{12,28},{16,0},{20,4},{24,8},{28,12},{1,17},{... | collective-permute-start | bytes 884744 | tf_op jit(solution)/shard_map/ppermute | solution.py:547
  60.4 12.6 %collective-permute-start.20 = (bf16[192,768]{1,0:T(8,128)(2,1)S(1)}, bf16[192,768]{1,0:T(8,128)(2,1)S(1)}, u32[]{:S(2)}, u32[]{:S(2)}) collective-permute-start(bf16[192,768]{1,0:T(8,128)(2,1)S(1)} %get-tuple-element.49.refs_2_), channel_id=1, source_target_pairs={{0,24},{4,28},{8,16},{12,20},{16,8},{20,12},{24,0},{28,4},{1,25},{... | collective-permute-start | bytes 884744 | tf_op jit(solution)/shard_map/ppermute | solution.py:547
  65.5 7.5 %collective-permute-start.17 = (bf16[384,384]{1,0:T(8,128)(2,1)S(1)}, bf16[384,384]{1,0:T(8,128)(2,1)S(1)}, u32[]{:S(2)}, u32[]{:S(2)}) collective-permute-start(bf16[384,384]{1,0:T(8,128)(2,1)S(1)} %get-tuple-element.47.refs_0_), channel_id=1, source_target_pairs={{0,4},{4,0},{8,12},{12,8},{16,20},{20,16},{24,28},{28,24},{1,5},{5... | collective-permute-start | bytes 884744 | tf_op jit(solution)/shard_map/ppermute | solution.py:547
  65.6 13.4 %collective-permute-start.14 = (bf16[192,768]{1,0:T(8,128)(2,1)S(1)}, bf16[192,768]{1,0:T(8,128)(2,1)S(1)}, u32[]{:S(2)}, u32[]{:S(2)}) collective-permute-start(bf16[192,768]{1,0:T(8,128)(2,1)S(1)} %get-tuple-element.48.refs_3_), channel_id=1, source_target_pairs={{0,8},{4,12},{8,0},{12,4},{16,24},{20,28},{24,16},{28,20},{1,9},{5... | collective-permute-start | bytes 884744 | tf_op jit(solution)/shard_map/ppermute | solution.py:547
  68.4 15.9 %collective-permute-start.15 = (bf16[192,768]{1,0:T(8,128)(2,1)S(1)}, bf16[192,768]{1,0:T(8,128)(2,1)S(1)}, u32[]{:S(2)}, u32[]{:S(2)}) collective-permute-start(bf16[192,768]{1,0:T(8,128)(2,1)S(1)} %get-tuple-element.48.refs_3_), channel_id=1, source_target_pairs={{0,16},{4,20},{8,24},{12,28},{16,0},{20,4},{24,8},{28,12},{1,17},{... | collective-permute-start | bytes 884744 | tf_op jit(solution)/shard_map/ppermute | solution.py:547
  72.1 12.2 %collective-permute-start.16 = (bf16[192,768]{1,0:T(8,128)(2,1)S(1)}, bf16[192,768]{1,0:T(8,128)(2,1)S(1)}, u32[]{:S(2)}, u32[]{:S(2)}) collective-permute-start(bf16[192,768]{1,0:T(8,128)(2,1)S(1)} %get-tuple-element.48.refs_3_), channel_id=1, source_target_pairs={{0,24},{4,28},{8,16},{12,20},{16,8},{20,12},{24,0},{28,4},{1,25},{... | collective-permute-start | bytes 884744 | tf_op jit(solution)/shard_map/ppermute | solution.py:547
  91.6 14.6 %collective-permute-start.22 = (bf16[384,384]{1,0:T(8,128)(2,1)S(1)}, bf16[384,384]{1,0:T(8,128)(2,1)S(1)}, u32[]{:S(2)}, u32[]{:S(2)}) collective-permute-start(bf16[384,384]{1,0:T(8,128)(2,1)S(1)} %get-tuple-element.52), channel_id=1, source_target_pairs={{0,1},{1,2},{2,3},{3,0},{4,5},{5,6},{6,7},{7,4},{8,9},{9,10},{10,1... | collective-permute-start | bytes 884744 | tf_op jit(solution)/shard_map/ppermute | solution.py:599
  98.5 13.8 %collective-permute-start.23 = (bf16[384,384]{1,0:T(8,128)(2,1)S(1)}, bf16[384,384]{1,0:T(8,128)(2,1)S(1)}, u32[]{:S(2)}, u32[]{:S(2)}) collective-permute-start(bf16[384,384]{1,0:T(8,128)(2,1)S(1)} %get-tuple-element.53), channel_id=1, source_target_pairs={{0,3},{1,0},{2,1},{3,2},{4,7},{5,4},{6,5},{7,6},{8,11},{9,8},{10,9... | collective-permute-start | bytes 884744 | tf_op jit(solution)/shard_map/ppermute | solution.py:599
  98.5 26.4 %collective-permute-start.24 = (bf16[384,384]{1,0:T(8,128)(2,1)S(1)}, bf16[384,384]{1,0:T(8,128)(2,1)S(1)}, u32[]{:S(2)}, u32[]{:S(2)}) collective-permute-start(bf16[384,384]{1,0:T(8,128)(2,1)S(1)} %get-tuple-element.54), channel_id=1, source_target_pairs={{0,2},{1,3},{2,0},{3,1},{4,6},{5,7},{6,4},{7,5},{8,10},{9,11},{10,... | collective-permute-start | bytes 884744 | tf_op jit(solution)/shard_map/ppermute | solution.py:599
  (8 other events, 74.3 us)

commit v7 on v6

--- a/solution.py
+++ b/solution.py
@@ -145,7 +145,7 @@
     count = lax.axis_size("head")
     moved = []
     for k, previous in zip((1, count - 1, 2), earlier):
-        held = block if previous is None else after(block, previous)
+        held = block if previous is None else after(block, *previous)
         moved.append(lax.ppermute(held, "head", rotate(k)))
     return [block, *moved]
 
@@ -515,13 +515,13 @@
         merged = jnp.transpose(jnp.concatenate(halves, axis=0))
         attended[:, pl.ds(pair * LANES, LANES)] = merged.astype(jnp.bfloat16)
 
-    def product(shift):
-        return jnp.dot(
-            attended[...], w_ref[:, columns_of(shift, width)], preferred_element_type=jnp.float32
-        )
-
-    for ref, shift in ((p3, 2), (p1, 3), (p2, 1)):
-        ref[...] = product(shift).astype(jnp.bfloat16)
+    def product(mask):
+        target = jnp.bitwise_xor(lax.axis_index("head"), mask)
+        columns = pl.ds(pl.multiple_of(target * width, LANES), width)
+        return jnp.dot(attended[...], w_ref[:, columns], preferred_element_type=jnp.float32)
+
+    for ref, mask in ((p3, 3), (p2, 2), (p1, 1)):
+        ref[...] = product(mask).astype(jnp.bfloat16)
     own_ref[...] = product(0) + h2_ref[...]
 
 
@@ -561,7 +561,7 @@
     h1_e, sent = first_conv(
         conv_edge_kernel, (dna, low, high), conv_in, outer, 2 * (outer + 2 * EDGE), "conv_edge"
     )
-    wide_e = shared(sent, (None, None, wide_m[1]))
+    wide_e = shared(sent, (None, None, wide_m[1:2]))
     h2_m, sent = second_conv(
         dilated_middle_kernel,
         (*wide_m, after(h1_m, sent)),
@@ -571,7 +571,7 @@
         inner + EDGE,
         "dilated_middle",
     )
-    normed_m = shared(sent, wide_e[1:])
+    normed_m = shared(sent, [[part] for part in wide_e[1:]])
     h2, sent = second_conv(
         dilated_edge_kernel,
         (*wide_m, *wide_e, h1_m, h1_e, h2_m),
@@ -581,7 +581,7 @@
         outer + 2 * EDGE,
         "dilated_edge",
     )
-    normed_e = shared(sent, normed_m[1:])
+    normed_e = shared(sent, [normed_m[1:]] * 3)
     normed_m[0] = after(normed_m[0], sent)
     weights = (w_query, w_key, w_value)
     q_m, kv_m = project(project_middle_kernel, normed_m, weights, inner, "project_middle")
@@ -594,9 +594,14 @@
     given = exchanged(state_other, 1)
     state_own = attend((q,), late, state, 0, "attend_own")
     own, p1, p2, p3 = mix(state_own, given, w_out, h2)
+    inward = lax.ppermute(p3, "head", [(0, 1), (3, 2)])
+    across = lax.ppermute(p3, "head", [(1, 2), (2, 1)])
+    joined = (p2.astype(jnp.float32) + inward.astype(jnp.float32)).astype(jnp.bfloat16)
+    skipped = lax.ppermute(joined, "head", [(i, i ^ 2) for i in range(4)])
+    beside = lax.ppermute(after(p1, inward), "head", [(i, i ^ 1) for i in range(4)])
     total = own
-    for part, shift in ((p1, 1), (p2, 3), (p3, 2)):
-        total = total + lax.ppermute(part, "head", rotate(shift)).astype(jnp.float32)
+    for part in (across, beside, skipped):
+        total = total + part.astype(jnp.float32)
     return total.astype(jnp.bfloat16)
 
 

time: 126 us -> 124 us (0.984)
  starting transfers between devices: 50.8 us -> 46.5 us
  waiting for transfers between devices: 48.3 us -> 50.1 us
    ppermute x12, waiting for transfers between devices: 15.4 us -> 21.1 us  [shared(): moved.append(lax.ppermute(held, 'head', rotate(k)))]
    ppermute x3 -> x4, waiting for transfers between devices: 24.9 us -> 21.2 us  [the longest x1 11.8 us: on_device(): lax.ppermute(after(p1, inward), 'head', [(i, i ^ 1) for i in range(4)])]
    ppermute x3 -> x4, starting transfers between devices: 8.5 us -> 6.16 us  [the longest x1 2.48 us: on_device(): lax.ppermute(after(p1, inward), 'head', [(i, i ^ 1) for i in range(4)])]
    ppermute x12, starting transfers between devices: 28.2 us -> 26.4 us  [shared(): moved.append(lax.ppermute(held, 'head', rotate(k)))]
  transfers between devices with their start and end apart: 25 -> 26, of which waited for: 11 -> 12; matrix products, arithmetic and copies ran while one was open for 0% -> 0% of each run, Pallas kernels for 14% -> 14%
where the time goes in v7:
time: 124 us; the launch traced here: 123 us
  waiting for transfers between devices  50.1 us (40%)
  starting transfers between devices  46.5 us (38%)
  Pallas kernels  22.4 us (18%)
  local copies, waits for them, and re-layouts  3.13 us (3%)
    ppermute x12, starting transfers between devices, shared(): moved.append(lax.ppermute(held, 'head', rotate(k)))  26.4 us
    ppermute x12, waiting for transfers between devices, shared(): moved.append(lax.ppermute(held, 'head', rotate(k)))  21.1 us
    pallas_call x3, Pallas kernels, attend(): pl.pallas_call(kernel, out_shape=out, scratch_shapes=[pltpu.VMEM((2, exte...  12.1 us
    ppermute x1, waiting for transfers between devices, on_device(): lax.ppermute(after(p1, inward), 'head', [(i, i ^ 1) for i in range(4)])  11.8 us
    ppermute x8, starting transfers between devices, exchanged(): return lax.ppermute(block, 'seq', [(i, i ^ mask) for i in range(count)])  11 us
    ppermute x8, waiting for transfers between devices, exchanged(): return lax.ppermute(block, 'seq', [(i, i ^ mask) for i in range(count)])  7.59 us
    ppermute x1, waiting for transfers between devices, on_device(): inward = lax.ppermute(p3, 'head', [(0, 1), (3, 2)])  6.21 us
    pallas_call x2, Pallas kernels, project(): pl.pallas_call(kernel, out_shape=(q, kv), compiler_params=pltpu.CompilerP...  3.72 us
  transfers between devices with their start and end apart: 26, of which 12 were waited for; matrix products, arithmetic and copies ran while one was open for 0% of the time, Pallas kernels for 14%

profile of v7, /device:TPU:0, one launch (start us, length us, event | category | flops | bytes accessed | tf_op | source)
XLA Modules:
  0.0 123.3 jit_solution(10054110404822072204)
XLA Ops:
  4.3 3.1 %collective-permute-start = (bf16[208,384]{1,0:T(8,128)(2,1)S(1)}, bf16[208,384]{1,0:T(8,128)(2,1)S(1)}, u32[]{:S(2)}, u32[]{:S(2)}) collective-permute-start(bf16[208,384]{1,0:T(8,128)(2,1)S(1)} %get-tuple-element.29.a0.m0), channel_id=1, source_target_pairs={{0,1},{1,2},{2,3},{3,0},{4,5},{5,6},{6,7},{7,4},{8,9},{9,10},{10,1... | collective-permute-start | bytes 479240 | tf_op jit(solution)/shard_map/ppermute | solution.py:149
  10.4 2.4 %collective-permute-start.1 = (bf16[208,384]{1,0:T(8,128)(2,1)S(1)}, bf16[208,384]{1,0:T(8,128)(2,1)S(1)}, u32[]{:S(2)}, u32[]{:S(2)}) collective-permute-start(bf16[208,384]{1,0:T(8,128)(2,1)S(1)} %get-tuple-element.29.a0.m0), channel_id=1, source_target_pairs={{0,3},{1,0},{2,1},{3,2},{4,7},{5,4},{6,5},{7,6},{8,11},{9,8},{10,9... | collective-permute-start | bytes 479240 | tf_op jit(solution)/shard_map/ppermute | solution.py:149
  14.8 2.3 %collective-permute-start.6 = (bf16[192,384]{1,0:T(8,128)(2,1)S(1)}, bf16[192,384]{1,0:T(8,128)(2,1)S(1)}, u32[]{:S(2)}, u32[]{:S(2)}) collective-permute-start(bf16[192,384]{1,0:T(8,128)(2,1)S(1)} %get-tuple-element.31.e0), channel_id=1, source_target_pairs={{0,3},{1,0},{2,1},{3,2},{4,7},{5,4},{6,5},{7,6},{8,11},{9,8},{10,9... | collective-permute-start | bytes 442376 | tf_op jit(solution)/shard_map/ppermute | solution.py:149
  17.2 2.4 %collective-permute-start.7 = (bf16[192,384]{1,0:T(8,128)(2,1)S(1)}, bf16[192,384]{1,0:T(8,128)(2,1)S(1)}, u32[]{:S(2)}, u32[]{:S(2)}) collective-permute-start(bf16[192,384]{1,0:T(8,128)(2,1)S(1)} %get-tuple-element.31.e0), channel_id=1, source_target_pairs={{0,2},{1,3},{2,0},{3,1},{4,6},{5,7},{6,4},{7,5},{8,10},{9,11},{10,... | collective-permute-start | bytes 442376 | tf_op jit(solution)/shard_map/ppermute | solution.py:149
  19.5 3.8 %collective-permute-done.2.a3.m3 = bf16[208,384]{1,0:T(8,128)(2,1)S(1)} collective-permute-done((bf16[208,384]{1,0:T(8,128)(2,1)S(1)}, bf16[208,384]{1,0:T(8,128)(2,1)S(1)}, u32[]{:S(2)}, u32[]{:S(2)}) %collective-permute-start.2) | collective-permute-done | bytes 159776 | tf_op jit(solution)/shard_map/ppermute | solution.py:149
  25.0 11.4 %collective-permute-start.9 = (bf16[192,384]{1,0:T(8,128)(2,1)S(1)}, bf16[192,384]{1,0:T(8,128)(2,1)S(1)}, u32[]{:S(2)}, u32[]{:S(2)}) collective-permute-start(bf16[192,384]{1,0:T(8,128)(2,1)S(1)} %get-tuple-element.42.a0), channel_id=1, source_target_pairs={{0,3},{1,0},{2,1},{3,2},{4,7},{5,4},{6,5},{7,6},{8,11},{9,8},{10,9... | collective-permute-start | bytes 442376 | tf_op jit(solution)/shard_map/ppermute | solution.py:149
  38.8 1.9 %collective-permute-done.9.a2 = bf16[192,384]{1,0:T(8,128)(2,1)S(1)} collective-permute-done((bf16[192,384]{1,0:T(8,128)(2,1)S(1)}, bf16[192,384]{1,0:T(8,128)(2,1)S(1)}, u32[]{:S(2)}, u32[]{:S(2)}) %collective-permute-start.9) | collective-permute-done | bytes 147488 | tf_op jit(solution)/shard_map/ppermute | solution.py:149
  40.7 3.4 %collective-permute-done.8.a1 = bf16[192,384]{1,0:T(8,128)(2,1)S(1)} collective-permute-done((bf16[192,384]{1,0:T(8,128)(2,1)S(1)}, bf16[192,384]{1,0:T(8,128)(2,1)S(1)}, u32[]{:S(2)}, u32[]{:S(2)}) %collective-permute-start.8) | collective-permute-done | bytes 147488 | tf_op jit(solution)/shard_map/ppermute | solution.py:149
  44.1 6.4 %collective-permute-done.10.a3 = bf16[192,384]{1,0:T(8,128)(2,1)S(1)} collective-permute-done((bf16[192,384]{1,0:T(8,128)(2,1)S(1)}, bf16[192,384]{1,0:T(8,128)(2,1)S(1)}, u32[]{:S(2)}, u32[]{:S(2)}) %collective-permute-start.10) | collective-permute-done | bytes 147488 | tf_op jit(solution)/shard_map/ppermute | solution.py:149
  50.9 3.4 %collective-permute-start.12 = (bf16[192,384]{1,0:T(8,128)(2,1)S(1)}, bf16[192,384]{1,0:T(8,128)(2,1)S(1)}, u32[]{:S(2)}, u32[]{:S(2)}) collective-permute-start(bf16[192,384]{1,0:T(8,128)(2,1)S(1)} %get-tuple-element.41.a0), channel_id=1, source_target_pairs={{0,3},{1,0},{2,1},{3,2},{4,7},{5,4},{6,5},{7,6},{8,11},{9,8},{10,9... | collective-permute-start | bytes 442376 | tf_op jit(solution)/shard_map/ppermute | solution.py:149
  54.4 1.9 %project_middle.1 = (bf16[192,384]{1,0:T(8,128)(2,1)S(1)}, bf16[192,768]{1,0:T(8,128)(2,1)S(1)}) custom-call(bf16[192,384]{1,0:T(8,128)(2,1)S(1)} %get-tuple-element.42.a0, bf16[192,384]{1,0:T(8,128)(2,1)S(1)} %collective-permute-done.8.a1, bf16[192,384]{1,0:T(8,128)(2,1)S(1)} %collective-permute-done.9.a2, bf16[192,384]{1,0:T(8,128)(2,1)S(1)} %collective-permute-done.10.a3, ...), custom_call_target="tpu_custom_call" | custom-call | flops 679477248 | bytes 4571136 | tf_op jit(solution)/shard_map/project_middle/pallas_call | solution.py:375
  56.2 3.3 %collective-permute-start.18 = (bf16[192,768]{1,0:T(8,128)(2,1)S(1)}, bf16[192,768]{1,0:T(8,128)(2,1)S(1)}, u32[]{:S(2)}, u32[]{:S(2)}) collective-permute-start(bf16[192,768]{1,0:T(8,128)(2,1)S(1)} %get-tuple-element.46.refs_2_), channel_id=1, source_target_pairs={{0,8},{4,12},{8,0},{12,4},{16,24},{20,28},{24,16},{28,20},{1,9},{5... | collective-permute-start | bytes 884744 | tf_op jit(solution)/shard_map/ppermute | solution.py:547
  60.2 2.3 %collective-permute-start.20 = (bf16[192,768]{1,0:T(8,128)(2,1)S(1)}, bf16[192,768]{1,0:T(8,128)(2,1)S(1)}, u32[]{:S(2)}, u32[]{:S(2)}) collective-permute-start(bf16[192,768]{1,0:T(8,128)(2,1)S(1)} %get-tuple-element.46.refs_2_), channel_id=1, source_target_pairs={{0,24},{4,28},{8,16},{12,20},{16,8},{20,12},{24,0},{28,4},{1,25},{... | collective-permute-start | bytes 884744 | tf_op jit(solution)/shard_map/ppermute | solution.py:547
  62.4 5.2 %collective-permute-done.13.a3 = bf16[192,384]{1,0:T(8,128)(2,1)S(1)} collective-permute-done((bf16[192,384]{1,0:T(8,128)(2,1)S(1)}, bf16[192,384]{1,0:T(8,128)(2,1)S(1)}, u32[]{:S(2)}, u32[]{:S(2)}) %collective-permute-start.13) | collective-permute-done | bytes 147488 | tf_op jit(solution)/shard_map/ppermute | solution.py:149
  69.6 2.8 %collective-permute-start.14 = (bf16[192,768]{1,0:T(8,128)(2,1)S(1)}, bf16[192,768]{1,0:T(8,128)(2,1)S(1)}, u32[]{:S(2)}, u32[]{:S(2)}) collective-permute-start(bf16[192,768]{1,0:T(8,128)(2,1)S(1)} %get-tuple-element.45.refs_3_), channel_id=1, source_target_pairs={{0,8},{4,12},{8,0},{12,4},{16,24},{20,28},{24,16},{28,20},{1,9},{5... | collective-permute-start | bytes 884744 | tf_op jit(solution)/shard_map/ppermute | solution.py:547
  75.2 5.9 %attend_m.1.refs_4_ = f32[400,768]{1,0:T(8,128)S(1)} custom-call(bf16[384,384]{1,0:T(8,128)(2,1)S(1)} %get-tuple-element.44.refs_0_, bf16[384,384]{1,0:T(8,128)(2,1)S(1)} %collective-permute-done.17.refs_1_.refs_0_, bf16[192,768]{1,0:T(8,128)(2,1)S(1)} %get-tuple-element.46.refs_2_, bf16[192,768]{1,0:T(8,128)(2,1)S(1)} %get-tuple-element.45.refs_3_, ...), custom_call_target="tpu_custom_call" | custom-call | flops 1132462080 | bytes 3293184 | tf_op jit(solution)/shard_map/attend_m/pallas_call | solution.py:490
  81.2 6.6 %collective-permute-done.15.refs_2_ = bf16[192,768]{1,0:T(8,128)(2,1)S(1)} collective-permute-done((bf16[192,768]{1,0:T(8,128)(2,1)S(1)}, bf16[192,768]{1,0:T(8,128)(2,1)S(1)}, u32[]{:S(2)}, u32[]{:S(2)}) %collective-permute-start.15) | collective-permute-done | bytes 294944 | tf_op jit(solution)/shard_map/ppermute | solution.py:547
  87.8 3.0 %attend_other.1 = f32[400,384]{1,0:T(8,128)S(1)} custom-call(bf16[384,384]{1,0:T(8,128)(2,1)S(1)} %collective-permute-done.17.refs_1_.refs_0_, bf16[192,768]{1,0:T(8,128)(2,1)S(1)} %collective-permute-done.14.refs_1_, bf16[192,768]{1,0:T(8,128)(2,1)S(1)} %collective-permute-done.15.refs_2_, bf16[192,768]{1,0:T(8,128)(2,1)S(1)} %collective-permute-done.16.refs_3_, ...), custom_call_target="tpu_custom_call" | custom-call | flops 339738624 | bytes 3022848 | tf_op jit(solution)/shard_map/attend_other/pallas_call | solution.py:490
  90.9 3.2 %attend_own.1.own_state = f32[400,384]{1,0:T(8,128)S(1)} custom-call(bf16[384,384]{1,0:T(8,128)(2,1)S(1)} %get-tuple-element.44.refs_0_, bf16[192,768]{1,0:T(8,128)(2,1)S(1)} %collective-permute-done.14.refs_1_, bf16[192,768]{1,0:T(8,128)(2,1)S(1)} %collective-permute-done.15.refs_2_, bf16[192,768]{1,0:T(8,128)(2,1)S(1)} %collective-permute-done.16.refs_3_, ...), custom_call_target="tpu_custom_call" | custom-call | flops 339738624 | bytes 3022848 | tf_op jit(solution)/shard_map/attend_own/pallas_call | solution.py:490
  95.0 2.3 %collective-permute-start.23 = (bf16[384,384]{1,0:T(8,128)(2,1)S(1)}, bf16[384,384]{1,0:T(8,128)(2,1)S(1)}, u32[]{:S(2)}, u32[]{:S(2)}) collective-permute-start(bf16[384,384]{1,0:T(8,128)(2,1)S(1)} %get-tuple-element.49), channel_id=1, source_target_pairs={{0,1},{3,2},{4,5},{7,6},{8,9},{11,10},{12,13},{15,14},{16,17},{19,... | collective-permute-start | bytes 884744 | tf_op jit(solution)/shard_map/ppermute | solution.py:597
  98.0 6.2 %collective-permute-done.23 = bf16[384,384]{1,0:T(8,128)(2,1)S(1)} collective-permute-done((bf16[384,384]{1,0:T(8,128)(2,1)S(1)}, bf16[384,384]{1,0:T(8,128)(2,1)S(1)}, u32[]{:S(2)}, u32[]{:S(2)}) %collective-permute-start.23) | collective-permute-done | bytes 294944 | tf_op jit(solution)/shard_map/ppermute | solution.py:597
  104.2 2.5 %collective-permute-start.24 = (bf16[384,384]{1,0:T(8,128)(2,1)S(1)}, bf16[384,384]{1,0:T(8,128)(2,1)S(1)}, u32[]{:S(2)}, u32[]{:S(2)}) collective-permute-start(bf16[384,384]{1,0:T(8,128)(2,1)S(1)} %get-tuple-element.51), channel_id=1, source_target_pairs={{0,1},{1,0},{2,3},{3,2},{4,5},{5,4},{6,7},{7,6},{8,9},{9,8},{10,11... | collective-permute-start | bytes 884744 | tf_op jit(solution)/shard_map/ppermute | solution.py:601
  107.5 11.8 %collective-permute-done.24 = bf16[384,384]{1,0:T(8,128)(2,1)S(1)} collective-permute-done((bf16[384,384]{1,0:T(8,128)(2,1)S(1)}, bf16[384,384]{1,0:T(8,128)(2,1)S(1)}, u32[]{:S(2)}, u32[]{:S(2)}) %collective-permute-start.24) | collective-permute-done | bytes 294944 | tf_op jit(solution)/shard_map/ppermute | solution.py:601
  119.3 3.2 %collective-permute-done.25 = bf16[384,384]{1,0:T(8,128)(2,1)S(1)} collective-permute-done((bf16[384,384]{1,0:T(8,128)(2,1)S(1)}, bf16[384,384]{1,0:T(8,128)(2,1)S(1)}, u32[]{:S(2)}, u32[]{:S(2)}) %collective-permute-start.25) | collective-permute-done | bytes 294944 | tf_op jit(solution)/shard_map/ppermute | solution.py:600
  (55 shorter events, 22.6 us)
Async XLA Ops:
  4.3 12.9 %collective-permute-start = (bf16[208,384]{1,0:T(8,128)(2,1)S(1)}, bf16[208,384]{1,0:T(8,128)(2,1)S(1)}, u32[]{:S(2)}, u32[]{:S(2)}) collective-permute-start(bf16[208,384]{1,0:T(8,128)(2,1)S(1)} %get-tuple-element.29.a0.m0), channel_id=1, source_target_pairs={{0,1},{1,2},{2,3},{3,0},{4,5},{5,6},{6,7},{7,4},{8,9},{9,10},{10,1... | collective-permute-start | bytes 479240 | tf_op jit(solution)/shard_map/ppermute | solution.py:149
  7.3 6.1 %collective-permute-start.3 = (bf16[16,768]{1,0:T(8,128)(2,1)S(1)}, bf16[16,768]{1,0:T(8,128)(2,1)S(1)}, u32[]{:S(2)}, u32[]{:S(2)}) collective-permute-start(bf16[16,768]{1,0:T(8,128)(2,1)S(1)} %get-tuple-element.54), channel_id=1, source_target_pairs={{0,4},{4,8},{8,12},{12,16},{16,20},{20,24},{24,28},{1,5},{5,9},{9,... | collective-permute-start | bytes 73736 | tf_op jit(solution)/shard_map/ppermute | solution.py:555
  10.4 9.1 %collective-permute-start.1 = (bf16[208,384]{1,0:T(8,128)(2,1)S(1)}, bf16[208,384]{1,0:T(8,128)(2,1)S(1)}, u32[]{:S(2)}, u32[]{:S(2)}) collective-permute-start(bf16[208,384]{1,0:T(8,128)(2,1)S(1)} %get-tuple-element.29.a0.m0), channel_id=1, source_target_pairs={{0,3},{1,0},{2,1},{3,2},{4,7},{5,4},{6,5},{7,6},{8,11},{9,8},{10,9... | collective-permute-start | bytes 479240 | tf_op jit(solution)/shard_map/ppermute | solution.py:149
  12.8 10.6 %collective-permute-start.2 = (bf16[208,384]{1,0:T(8,128)(2,1)S(1)}, bf16[208,384]{1,0:T(8,128)(2,1)S(1)}, u32[]{:S(2)}, u32[]{:S(2)}) collective-permute-start(bf16[208,384]{1,0:T(8,128)(2,1)S(1)} %get-tuple-element.29.a0.m0), channel_id=1, source_target_pairs={{0,2},{1,3},{2,0},{3,1},{4,6},{5,7},{6,4},{7,5},{8,10},{9,11},{10,... | collective-permute-start | bytes 479240 | tf_op jit(solution)/shard_map/ppermute | solution.py:149
  14.8 10.2 %collective-permute-start.6 = (bf16[192,384]{1,0:T(8,128)(2,1)S(1)}, bf16[192,384]{1,0:T(8,128)(2,1)S(1)}, u32[]{:S(2)}, u32[]{:S(2)}) collective-permute-start(bf16[192,384]{1,0:T(8,128)(2,1)S(1)} %get-tuple-element.31.e0), channel_id=1, source_target_pairs={{0,3},{1,0},{2,1},{3,2},{4,7},{5,4},{6,5},{7,6},{8,11},{9,8},{10,9... | collective-permute-start | bytes 442376 | tf_op jit(solution)/shard_map/ppermute | solution.py:149
  17.1 19.3 %collective-permute-start.5 = (bf16[192,384]{1,0:T(8,128)(2,1)S(1)}, bf16[192,384]{1,0:T(8,128)(2,1)S(1)}, u32[]{:S(2)}, u32[]{:S(2)}) collective-permute-start(bf16[192,384]{1,0:T(8,128)(2,1)S(1)} %get-tuple-element.31.e0), channel_id=1, source_target_pairs={{0,1},{1,2},{2,3},{3,0},{4,5},{5,6},{6,7},{7,4},{8,9},{9,10},{10,1... | collective-permute-start | bytes 442376 | tf_op jit(solution)/shard_map/ppermute | solution.py:149
  17.2 19.6 %collective-permute-start.7 = (bf16[192,384]{1,0:T(8,128)(2,1)S(1)}, bf16[192,384]{1,0:T(8,128)(2,1)S(1)}, u32[]{:S(2)}, u32[]{:S(2)}) collective-permute-start(bf16[192,384]{1,0:T(8,128)(2,1)S(1)} %get-tuple-element.31.e0), channel_id=1, source_target_pairs={{0,2},{1,3},{2,0},{3,1},{4,6},{5,7},{6,4},{7,5},{8,10},{9,11},{10,... | collective-permute-start | bytes 442376 | tf_op jit(solution)/shard_map/ppermute | solution.py:149
  25.0 15.7 %collective-permute-start.9 = (bf16[192,384]{1,0:T(8,128)(2,1)S(1)}, bf16[192,384]{1,0:T(8,128)(2,1)S(1)}, u32[]{:S(2)}, u32[]{:S(2)}) collective-permute-start(bf16[192,384]{1,0:T(8,128)(2,1)S(1)} %get-tuple-element.42.a0), channel_id=1, source_target_pairs={{0,3},{1,0},{2,1},{3,2},{4,7},{5,4},{6,5},{7,6},{8,11},{9,8},{10,9... | collective-permute-start | bytes 442376 | tf_op jit(solution)/shard_map/ppermute | solution.py:149
  36.4 7.7 %collective-permute-start.8 = (bf16[192,384]{1,0:T(8,128)(2,1)S(1)}, bf16[192,384]{1,0:T(8,128)(2,1)S(1)}, u32[]{:S(2)}, u32[]{:S(2)}) collective-permute-start(bf16[192,384]{1,0:T(8,128)(2,1)S(1)} %get-tuple-element.42.a0), channel_id=1, source_target_pairs={{0,1},{1,2},{2,3},{3,0},{4,5},{5,6},{6,7},{7,4},{8,9},{9,10},{10,1... | collective-permute-start | bytes 442376 | tf_op jit(solution)/shard_map/ppermute | solution.py:149
  36.7 13.8 %collective-permute-start.10 = (bf16[192,384]{1,0:T(8,128)(2,1)S(1)}, bf16[192,384]{1,0:T(8,128)(2,1)S(1)}, u32[]{:S(2)}, u32[]{:S(2)}) collective-permute-start(bf16[192,384]{1,0:T(8,128)(2,1)S(1)} %get-tuple-element.42.a0), channel_id=1, source_target_pairs={{0,2},{1,3},{2,0},{3,1},{4,6},{5,7},{6,4},{7,5},{8,10},{9,11},{10,... | collective-permute-start | bytes 442376 | tf_op jit(solution)/shard_map/ppermute | solution.py:149
  50.5 9.7 %collective-permute-start.11 = (bf16[192,384]{1,0:T(8,128)(2,1)S(1)}, bf16[192,384]{1,0:T(8,128)(2,1)S(1)}, u32[]{:S(2)}, u32[]{:S(2)}) collective-permute-start(bf16[192,384]{1,0:T(8,128)(2,1)S(1)} %get-tuple-element.41.a0), channel_id=1, source_target_pairs={{0,1},{1,2},{2,3},{3,0},{4,5},{5,6},{6,7},{7,4},{8,9},{9,10},{10,1... | collective-permute-start | bytes 442376 | tf_op jit(solution)/shard_map/ppermute | solution.py:149
  50.9 11.5 %collective-permute-start.12 = (bf16[192,384]{1,0:T(8,128)(2,1)S(1)}, bf16[192,384]{1,0:T(8,128)(2,1)S(1)}, u32[]{:S(2)}, u32[]{:S(2)}) collective-permute-start(bf16[192,384]{1,0:T(8,128)(2,1)S(1)} %get-tuple-element.41.a0), channel_id=1, source_target_pairs={{0,3},{1,0},{2,1},{3,2},{4,7},{5,4},{6,5},{7,6},{8,11},{9,8},{10,9... | collective-permute-start | bytes 442376 | tf_op jit(solution)/shard_map/ppermute | solution.py:149
  54.3 13.3 %collective-permute-start.13 = (bf16[192,384]{1,0:T(8,128)(2,1)S(1)}, bf16[192,384]{1,0:T(8,128)(2,1)S(1)}, u32[]{:S(2)}, u32[]{:S(2)}) collective-permute-start(bf16[192,384]{1,0:T(8,128)(2,1)S(1)} %get-tuple-element.41.a0), channel_id=1, source_target_pairs={{0,2},{1,3},{2,0},{3,1},{4,6},{5,7},{6,4},{7,5},{8,10},{9,11},{10,... | collective-permute-start | bytes 442376 | tf_op jit(solution)/shard_map/ppermute | solution.py:149
  56.2 16.2 %collective-permute-start.18 = (bf16[192,768]{1,0:T(8,128)(2,1)S(1)}, bf16[192,768]{1,0:T(8,128)(2,1)S(1)}, u32[]{:S(2)}, u32[]{:S(2)}) collective-permute-start(bf16[192,768]{1,0:T(8,128)(2,1)S(1)} %get-tuple-element.46.refs_2_), channel_id=1, source_target_pairs={{0,8},{4,12},{8,0},{12,4},{16,24},{20,28},{24,16},{28,20},{1,9},{5... | collective-permute-start | bytes 884744 | tf_op jit(solution)/shard_map/ppermute | solution.py:547
  59.6 14.2 %collective-permute-start.19 = (bf16[192,768]{1,0:T(8,128)(2,1)S(1)}, bf16[192,768]{1,0:T(8,128)(2,1)S(1)}, u32[]{:S(2)}, u32[]{:S(2)}) collective-permute-start(bf16[192,768]{1,0:T(8,128)(2,1)S(1)} %get-tuple-element.46.refs_2_), channel_id=1, source_target_pairs={{0,16},{4,20},{8,24},{12,28},{16,0},{20,4},{24,8},{28,12},{1,17},{... | collective-permute-start | bytes 884744 | tf_op jit(solution)/shard_map/ppermute | solution.py:547
  60.2 15.1 %collective-permute-start.20 = (bf16[192,768]{1,0:T(8,128)(2,1)S(1)}, bf16[192,768]{1,0:T(8,128)(2,1)S(1)}, u32[]{:S(2)}, u32[]{:S(2)}) collective-permute-start(bf16[192,768]{1,0:T(8,128)(2,1)S(1)} %get-tuple-element.46.refs_2_), channel_id=1, source_target_pairs={{0,24},{4,28},{8,16},{12,20},{16,8},{20,12},{24,0},{28,4},{1,25},{... | collective-permute-start | bytes 884744 | tf_op jit(solution)/shard_map/ppermute | solution.py:547
  69.5 5.7 %collective-permute-start.17 = (bf16[384,384]{1,0:T(8,128)(2,1)S(1)}, bf16[384,384]{1,0:T(8,128)(2,1)S(1)}, u32[]{:S(2)}, u32[]{:S(2)}) collective-permute-start(bf16[384,384]{1,0:T(8,128)(2,1)S(1)} %get-tuple-element.44.refs_0_), channel_id=1, source_target_pairs={{0,4},{4,0},{8,12},{12,8},{16,20},{20,16},{24,28},{28,24},{1,5},{5... | collective-permute-start | bytes 884744 | tf_op jit(solution)/shard_map/ppermute | solution.py:547
  69.6 11.6 %collective-permute-start.14 = (bf16[192,768]{1,0:T(8,128)(2,1)S(1)}, bf16[192,768]{1,0:T(8,128)(2,1)S(1)}, u32[]{:S(2)}, u32[]{:S(2)}) collective-permute-start(bf16[192,768]{1,0:T(8,128)(2,1)S(1)} %get-tuple-element.45.refs_3_), channel_id=1, source_target_pairs={{0,8},{4,12},{8,0},{12,4},{16,24},{20,28},{24,16},{28,20},{1,9},{5... | collective-permute-start | bytes 884744 | tf_op jit(solution)/shard_map/ppermute | solution.py:547
  72.4 15.4 %collective-permute-start.15 = (bf16[192,768]{1,0:T(8,128)(2,1)S(1)}, bf16[192,768]{1,0:T(8,128)(2,1)S(1)}, u32[]{:S(2)}, u32[]{:S(2)}) collective-permute-start(bf16[192,768]{1,0:T(8,128)(2,1)S(1)} %get-tuple-element.45.refs_3_), channel_id=1, source_target_pairs={{0,16},{4,20},{8,24},{12,28},{16,0},{20,4},{24,8},{28,12},{1,17},{... | collective-permute-start | bytes 884744 | tf_op jit(solution)/shard_map/ppermute | solution.py:547
  73.8 14.0 %collective-permute-start.16 = (bf16[192,768]{1,0:T(8,128)(2,1)S(1)}, bf16[192,768]{1,0:T(8,128)(2,1)S(1)}, u32[]{:S(2)}, u32[]{:S(2)}) collective-permute-start(bf16[192,768]{1,0:T(8,128)(2,1)S(1)} %get-tuple-element.45.refs_3_), channel_id=1, source_target_pairs={{0,24},{4,28},{8,16},{12,20},{16,8},{20,12},{24,0},{28,4},{1,25},{... | collective-permute-start | bytes 884744 | tf_op jit(solution)/shard_map/ppermute | solution.py:547
  95.0 9.2 %collective-permute-start.23 = (bf16[384,384]{1,0:T(8,128)(2,1)S(1)}, bf16[384,384]{1,0:T(8,128)(2,1)S(1)}, u32[]{:S(2)}, u32[]{:S(2)}) collective-permute-start(bf16[384,384]{1,0:T(8,128)(2,1)S(1)} %get-tuple-element.49), channel_id=1, source_target_pairs={{0,1},{3,2},{4,5},{7,6},{8,9},{11,10},{12,13},{15,14},{16,17},{19,... | collective-permute-start | bytes 884744 | tf_op jit(solution)/shard_map/ppermute | solution.py:597
  97.3 10.2 %collective-permute-start.22 = (bf16[384,384]{1,0:T(8,128)(2,1)S(1)}, bf16[384,384]{1,0:T(8,128)(2,1)S(1)}, u32[]{:S(2)}, u32[]{:S(2)}) collective-permute-start(bf16[384,384]{1,0:T(8,128)(2,1)S(1)} %get-tuple-element.49), channel_id=1, source_target_pairs={{1,2},{2,1},{5,6},{6,5},{9,10},{10,9},{13,14},{14,13},{17,18},{18,... | collective-permute-start | bytes 884744 | tf_op jit(solution)/shard_map/ppermute | solution.py:598
  104.2 15.1 %collective-permute-start.24 = (bf16[384,384]{1,0:T(8,128)(2,1)S(1)}, bf16[384,384]{1,0:T(8,128)(2,1)S(1)}, u32[]{:S(2)}, u32[]{:S(2)}) collective-permute-start(bf16[384,384]{1,0:T(8,128)(2,1)S(1)} %get-tuple-element.51), channel_id=1, source_target_pairs={{0,1},{1,0},{2,3},{3,2},{4,5},{5,4},{6,7},{7,6},{8,9},{9,8},{10,11... | collective-permute-start | bytes 884744 | tf_op jit(solution)/shard_map/ppermute | solution.py:601
  106.8 15.7 %collective-permute-start.25 = (bf16[384,384]{1,0:T(8,128)(2,1)S(1)}, bf16[384,384]{1,0:T(8,128)(2,1)S(1)}, u32[]{:S(2)}, u32[]{:S(2)}) collective-permute-start(bf16[384,384]{1,0:T(8,128)(2,1)S(1)} %add_convert_fusion.1), channel_id=1, source_target_pairs={{0,2},{1,3},{2,0},{3,1},{4,6},{5,7},{6,4},{7,5},{8,10},{9,11},{10,... | collective-permute-start | bytes 884744 | tf_op jit(solution)/shard_map/ppermute | solution.py:600
  (9 other events, 80.9 us)

commit v8 on v7

--- a/solution.py
+++ b/solution.py
@@ -132,30 +132,34 @@
     )
 
 
-def rotate(offset):
-    count = lax.axis_size("head")
-    return [(i, (i + offset) % count) for i in range(count)]
-
-
 def after(value, *others):
     return lax.optimization_barrier((value, *others))[0]
 
 
-def shared(block, earlier=(None, None, None)):
+def swapped(block, mask):
     count = lax.axis_size("head")
-    moved = []
-    for k, previous in zip((1, count - 1, 2), earlier):
-        held = block if previous is None else after(block, *previous)
-        moved.append(lax.ppermute(held, "head", rotate(k)))
-    return [block, *moved]
-
-
-def owner(k):
-    count = lax.axis_size("head")
-    return lax.rem(lax.axis_index("head") + count - k, count)
-
-
-SHIFTS = (0, 1, 3, 2)
+    return lax.ppermute(block, "head", [(i, i ^ mask) for i in range(count)])
+
+
+def shared(block, earlier=None):
+    near = far = block
+    if earlier is not None:
+        near, far = after(block, earlier[1]), after(block, earlier[2])
+    far = swapped(far, 2)
+    near = swapped(near, 1)
+    return [block, near, far]
+
+
+def forwarded(parts, gate=None):
+    far = parts[2] if gate is None else after(parts[2], gate)
+    return [*parts, swapped(far, 1)]
+
+
+def owner(mask):
+    return jnp.bitwise_xor(lax.axis_index("head"), mask)
+
+
+MASKS = (0, 1, 2, 3)
 
 
 def store_wide(wide, start, block):
@@ -235,8 +239,8 @@
     return jax.nn.gelu(value, approximate=True)
 
 
-def columns_of(shift, width):
-    return pl.ds(pl.multiple_of(owner(shift) * width, 128), width)
+def columns_of(mask, width):
+    return pl.ds(pl.multiple_of(owner(mask) * width, LANES), width)
 
 
 def dilated_middle_kernel(a0, a1, a2, a3, h1_ref, weight_ref, h2_ref, sent_ref, act):
@@ -246,11 +250,11 @@
     blocks = wide_blocks(parts, 0, count)
     inverse = inverse_norm(blocks)
     total = h1_ref[pl.ds(8, rows), :]
-    for slot, (block, shift) in enumerate(zip(blocks, SHIFTS)):
+    for slot, (block, mask) in enumerate(zip(blocks, MASKS)):
         act[slot] = gelu(block * inverse)
         for tap in range(3):
             taken = act[slot, pl.ds((tap + 1) * DILATION_STEP, rows), :].astype(jnp.bfloat16)
-            total = total + reduce_operands(taken, weight_ref[tap, :, columns_of(shift, width)])
+            total = total + reduce_operands(taken, weight_ref[tap, :, columns_of(mask, width)])
     h2_ref[...] = total
     sent_ref[...] = total.astype(jnp.bfloat16)
 
@@ -284,7 +288,7 @@
         axis=0,
     )
     tail = 2 * EDGE
-    for slot, shift in enumerate(SHIFTS):
+    for slot, mask in enumerate(MASKS):
         full = gelu(outer_blocks[slot] * outer_inverse)
         act[slot, pl.ds(0, EDGE), :] = full[:EDGE]
         act[slot, pl.ds(EDGE, EDGE), :] = gelu(low_blocks[slot] * low_inverse)
@@ -299,7 +303,7 @@
                 ],
                 axis=0,
             ).astype(jnp.bfloat16)
-            total = total + reduce_operands(taken, weight_ref[tap, :, columns_of(shift, width)])
+            total = total + reduce_operands(taken, weight_ref[tap, :, columns_of(mask, width)])
     h2_ref[pl.ds(0, EDGE), :] = total[:EDGE]
     h2_ref[pl.ds(EDGE, last - EDGE), :] = h2m_ref[...]
     h2_ref[pl.ds(last, rows - last), :] = total[EDGE:]
@@ -333,8 +337,8 @@
 
     def product(weight_ref, start=0, stop=rows, weight_first=False):
         total = None
-        for part, shift in zip(normed, SHIFTS):
-            weight = weight_ref[:, columns_of(shift, width)]
+        for part, mask in zip(normed, MASKS):
+            weight = weight_ref[:, columns_of(mask, width)]
             taken = part[start:stop]
             pair = (weight, taken) if weight_first else (taken, weight)
             term = reduce_operands(*pair)
@@ -516,9 +520,9 @@
         attended[:, pl.ds(pair * LANES, LANES)] = merged.astype(jnp.bfloat16)
 
     def product(mask):
-        target = jnp.bitwise_xor(lax.axis_index("head"), mask)
-        columns = pl.ds(pl.multiple_of(target * width, LANES), width)
-        return jnp.dot(attended[...], w_ref[:, columns], preferred_element_type=jnp.float32)
+        return jnp.dot(
+            attended[...], w_ref[:, columns_of(mask, width)], preferred_element_type=jnp.float32
+        )
 
     for ref, mask in ((p3, 3), (p2, 2), (p1, 1)):
         ref[...] = product(mask).astype(jnp.bfloat16)
@@ -557,11 +561,11 @@
     h1_m, sent = first_conv(
         conv_middle_kernel, (dna,), conv_in, inner + EDGE, 2 * (inner + 2 * EDGE), "conv_middle"
     )
-    wide_m = shared(sent)
+    wide_m = forwarded(shared(sent))
     h1_e, sent = first_conv(
-        conv_edge_kernel, (dna, low, high), conv_in, outer, 2 * (outer + 2 * EDGE), "conv_edge"
-    )
-    wide_e = shared(sent, (None, None, wide_m[1:2]))
+        conv_edge_kernel, (dna, after(low, wide_m[2]), high), conv_in, outer, 2 * (outer + 2 * EDGE), "conv_edge"
+    )
+    wide_e = shared(sent)
     h2_m, sent = second_conv(
         dilated_middle_kernel,
         (*wide_m, after(h1_m, sent)),
@@ -571,7 +575,8 @@
         inner + EDGE,
         "dilated_middle",
     )
-    normed_m = shared(sent, [[part] for part in wide_e[1:]])
+    normed_m = forwarded(shared(sent, wide_e))
+    wide_e = forwarded(wide_e, sent)
     h2, sent = second_conv(
         dilated_edge_kernel,
         (*wide_m, *wide_e, h1_m, h1_e, h2_m),
@@ -581,11 +586,12 @@
         outer + 2 * EDGE,
         "dilated_edge",
     )
-    normed_e = shared(sent, [normed_m[1:]] * 3)
+    normed_e = shared(sent, normed_m)
     normed_m[0] = after(normed_m[0], sent)
     weights = (w_query, w_key, w_value)
     q_m, kv_m = project(project_middle_kernel, normed_m, weights, inner, "project_middle")
     x_m, y_m, d_m = (exchanged(kv_m, mask) for mask in (2, 4, 6))
+    normed_e = forwarded(normed_e, kv_m)
     q, kv_e = project(project_edge_kernel, (*normed_e, q_m), weights, rows, "project_edge")
     q_other, x_e, y_e, d_e = exchanged(q, 1), *(exchanged(kv_e, mask) for mask in (2, 4, 6))
     state = attend((q, q_other), (kv_m, kv_e, x_m, y_m, d_m), None, 0, "attend_m")
@@ -594,13 +600,10 @@
     given = exchanged(state_other, 1)
     state_own = attend((q,), late, state, 0, "attend_own")
     own, p1, p2, p3 = mix(state_own, given, w_out, h2)
-    inward = lax.ppermute(p3, "head", [(0, 1), (3, 2)])
-    across = lax.ppermute(p3, "head", [(1, 2), (2, 1)])
+    inward = swapped(p3, 1)
     joined = (p2.astype(jnp.float32) + inward.astype(jnp.float32)).astype(jnp.bfloat16)
-    skipped = lax.ppermute(joined, "head", [(i, i ^ 2) for i in range(4)])
-    beside = lax.ppermute(after(p1, inward), "head", [(i, i ^ 1) for i in range(4)])
     total = own
-    for part in (across, beside, skipped):
+    for part in (swapped(after(p1, joined), 1), swapped(joined, 2)):
         total = total + part.astype(jnp.float32)
     return total.astype(jnp.bfloat16)
 

time: 124 us -> 112 us (0.903)
  starting transfers between devices: 46.5 us -> 30.8 us
  waiting for transfers between devices: 50.1 us -> 54.3 us
    ppermute x16 -> x15, starting transfers between devices: 32.5 us -> 20 us  [swapped(): return lax.ppermute(block, 'head', [(i, i ^ mask) for i in range(count)])]
    ppermute x8, waiting for transfers between devices: 7.59 us -> 12.1 us  [exchanged(): return lax.ppermute(block, 'seq', [(i, i ^ mask) for i in range(count)])]
    ppermute x8, starting transfers between devices: 11 us -> 7.83 us  [exchanged(): return lax.ppermute(block, 'seq', [(i, i ^ mask) for i in range(count)])]
    ppermute x16 -> x15, waiting for transfers between devices: 42.3 us -> 42.2 us  [swapped(): return lax.ppermute(block, 'head', [(i, i ^ mask) for i in range(count)])]
  transfers between devices with their start and end apart: 26 -> 25, of which waited for: 12 -> 15; matrix products, arithmetic and copies ran while one was open for 0% -> 0% of each run, Pallas kernels for 14% -> 16%
where the time goes in v8:
time: 112 us
  waiting for transfers between devices  54.3 us (48%)
  starting transfers between devices  30.8 us (28%)
  Pallas kernels  22.4 us (20%)
  local copies, waits for them, and re-layouts  3.13 us (3%)
    ppermute x15, waiting for transfers between devices, swapped(): return lax.ppermute(block, 'head', [(i, i ^ mask) for i in range(count)])  42.2 us
    ppermute x15, starting transfers between devices, swapped(): return lax.ppermute(block, 'head', [(i, i ^ mask) for i in range(count)])  20 us
    pallas_call x3, Pallas kernels, attend(): pl.pallas_call(kernel, out_shape=out, scratch_shapes=[pltpu.VMEM((2, exte...  12.1 us
    ppermute x8, waiting for transfers between devices, exchanged(): return lax.ppermute(block, 'seq', [(i, i ^ mask) for i in range(count)])  12.1 us
    ppermute x8, starting transfers between devices, exchanged(): return lax.ppermute(block, 'seq', [(i, i ^ mask) for i in range(count)])  7.83 us
    pallas_call x2, Pallas kernels, project(): pl.pallas_call(kernel, out_shape=(q, kv), compiler_params=pltpu.CompilerP...  3.69 us
    pallas_call x2, Pallas kernels, second_conv(): pl.pallas_call(kernel, out_shape=(kept, sent), scratch_shapes=[pltpu.VMEM...  3.42 us
    unnamed x14, local copies, waits for them, and re-layouts  3.13 us
  transfers between devices with their start and end apart: 25, of which 15 were waited for; matrix products, arithmetic and copies ran while one was open for 0% of the time, Pallas kernels for 16%

profile of v8, /device:TPU:0, one launch (start us, length us, event | category | flops | bytes accessed | tf_op | source)
XLA Modules:
  0.0 111.7 jit_solution(5910090037973514426)
XLA Ops:
  0.0 1.8 %copy-done.1 = bf16[5,384,768]{2,1,0:T(8,128)(2,1)S(1)} copy-done((bf16[5,384,768]{2,1,0:T(8,128)(2,1)S(1)}, bf16[5,384,768]{2,1,0:T(8,128)(2,1)}, u32[]{:S(2)}) %copy-start.1) | copy-done | bytes 2949144
  4.3 4.1 %collective-permute-start.1 = (bf16[208,384]{1,0:T(8,128)(2,1)S(1)}, bf16[208,384]{1,0:T(8,128)(2,1)S(1)}, u32[]{:S(2)}, u32[]{:S(2)}) collective-permute-start(bf16[208,384]{1,0:T(8,128)(2,1)S(1)} %get-tuple-element.31.a0.m0), channel_id=1, source_target_pairs={{0,2},{1,3},{2,0},{3,1},{4,6},{5,7},{6,4},{7,5},{8,10},{9,11},{10,... | collective-permute-start | bytes 479240 | tf_op jit(solution)/shard_map/ppermute | solution.py:141
  13.0 2.9 %collective-permute-done.1.a2.m2 = bf16[208,384]{1,0:T(8,128)(2,1)S(1)} collective-permute-done((bf16[208,384]{1,0:T(8,128)(2,1)S(1)}, bf16[208,384]{1,0:T(8,128)(2,1)S(1)}, u32[]{:S(2)}, u32[]{:S(2)}) %collective-permute-start.1) | collective-permute-done | bytes 159776 | tf_op jit(solution)/shard_map/ppermute | solution.py:141
  17.8 3.5 %collective-permute-start.6 = (bf16[192,384]{1,0:T(8,128)(2,1)S(1)}, bf16[192,384]{1,0:T(8,128)(2,1)S(1)}, u32[]{:S(2)}, u32[]{:S(2)}) collective-permute-start(bf16[192,384]{1,0:T(8,128)(2,1)S(1)} %get-tuple-element.33.e0), channel_id=1, source_target_pairs={{0,2},{1,3},{2,0},{3,1},{4,6},{5,7},{6,4},{7,5},{8,10},{9,11},{10,... | collective-permute-start | bytes 442376 | tf_op jit(solution)/shard_map/ppermute | solution.py:141
  21.3 3.3 %collective-permute-done.2.a3.m3 = bf16[208,384]{1,0:T(8,128)(2,1)S(1)} collective-permute-done((bf16[208,384]{1,0:T(8,128)(2,1)S(1)}, bf16[208,384]{1,0:T(8,128)(2,1)S(1)}, u32[]{:S(2)}, u32[]{:S(2)}) %collective-permute-start.2) | collective-permute-done | bytes 159776 | tf_op jit(solution)/shard_map/ppermute | solution.py:141
  26.3 2.4 %collective-permute-done.6.e2 = bf16[192,384]{1,0:T(8,128)(2,1)S(1)} collective-permute-done((bf16[192,384]{1,0:T(8,128)(2,1)S(1)}, bf16[192,384]{1,0:T(8,128)(2,1)S(1)}, u32[]{:S(2)}, u32[]{:S(2)}) %collective-permute-start.6) | collective-permute-done | bytes 147488 | tf_op jit(solution)/shard_map/ppermute | solution.py:141
  29.0 2.3 %collective-permute-start.7 = (bf16[192,384]{1,0:T(8,128)(2,1)S(1)}, bf16[192,384]{1,0:T(8,128)(2,1)S(1)}, u32[]{:S(2)}, u32[]{:S(2)}) collective-permute-start(bf16[192,384]{1,0:T(8,128)(2,1)S(1)} %collective-permute-done.6.e2), channel_id=1, source_target_pairs={{0,1},{1,0},{2,3},{3,2},{4,5},{5,4},{6,7},{7,6},{8,9},{9,8},{10,11... | collective-permute-start | bytes 442376 | tf_op jit(solution)/shard_map/ppermute | solution.py:141
  31.3 5.4 %collective-permute-done.10.a2 = bf16[192,384]{1,0:T(8,128)(2,1)S(1)} collective-permute-done((bf16[192,384]{1,0:T(8,128)(2,1)S(1)}, bf16[192,384]{1,0:T(8,128)(2,1)S(1)}, u32[]{:S(2)}, u32[]{:S(2)}) %collective-permute-start.10) | collective-permute-done | bytes 147488 | tf_op jit(solution)/shard_map/ppermute | solution.py:141
  36.7 2.1 %collective-permute-done.7.e3 = bf16[192,384]{1,0:T(8,128)(2,1)S(1)} collective-permute-done((bf16[192,384]{1,0:T(8,128)(2,1)S(1)}, bf16[192,384]{1,0:T(8,128)(2,1)S(1)}, u32[]{:S(2)}, u32[]{:S(2)}) %collective-permute-start.7) | collective-permute-done | bytes 147488 | tf_op jit(solution)/shard_map/ppermute | solution.py:141
  43.3 2.9 %collective-permute-done.12.a3 = bf16[192,384]{1,0:T(8,128)(2,1)S(1)} collective-permute-done((bf16[192,384]{1,0:T(8,128)(2,1)S(1)}, bf16[192,384]{1,0:T(8,128)(2,1)S(1)}, u32[]{:S(2)}, u32[]{:S(2)}) %collective-permute-start.12) | collective-permute-done | bytes 147488 | tf_op jit(solution)/shard_map/ppermute | solution.py:141
  46.2 1.8 %project_middle.1 = (bf16[192,384]{1,0:T(8,128)(2,1)S(1)}, bf16[192,768]{1,0:T(8,128)(2,1)S(1)}) custom-call(bf16[192,384]{1,0:T(8,128)(2,1)S(1)} %get-tuple-element.45.a0, bf16[192,384]{1,0:T(8,128)(2,1)S(1)} %collective-permute-done.8.a1, bf16[192,384]{1,0:T(8,128)(2,1)S(1)} %collective-permute-done.10.a2, ...), custom_call_target="tpu_custom_call" | custom-call | flops 679477248 | bytes 4571136 | tf_op jit(solution)/shard_map/project_middle/pallas_call | solution.py:379
  48.5 2.7 %collective-permute-start.18 = (bf16[192,768]{1,0:T(8,128)(2,1)S(1)}, bf16[192,768]{1,0:T(8,128)(2,1)S(1)}, u32[]{:S(2)}, u32[]{:S(2)}) collective-permute-start(bf16[192,768]{1,0:T(8,128)(2,1)S(1)} %get-tuple-element.46.refs_2_), channel_id=1, source_target_pairs={{0,8},{4,12},{8,0},{12,4},{16,24},{20,28},{24,16},{28,20},{1,9},{5... | collective-permute-start | bytes 884744 | tf_op jit(solution)/shard_map/ppermute | solution.py:551
  53.6 1.8 %project_edge.1 = (bf16[384,384]{1,0:T(8,128)(2,1)S(1)}, bf16[192,768]{1,0:T(8,128)(2,1)S(1)}) custom-call(bf16[192,384]{1,0:T(8,128)(2,1)S(1)} %get-tuple-element.44.a0, bf16[192,384]{1,0:T(8,128)(2,1)S(1)} %collective-permute-done.9.a1, bf16[192,384]{1,0:T(8,128)(2,1)S(1)} %collective-permute-done.11.a2, bf16[192,384]{1,0:T(8,128)(2,1)S(1)} %collective-permute-done.13.a3, ...), custom_call_target="tpu_custom_call" | custom-call | flops 679477248 | bytes 4866048 | tf_op jit(solution)/shard_map/project_edge/pallas_call | solution.py:379
  55.6 2.8 %collective-permute-start.14 = (bf16[192,768]{1,0:T(8,128)(2,1)S(1)}, bf16[192,768]{1,0:T(8,128)(2,1)S(1)}, u32[]{:S(2)}, u32[]{:S(2)}) collective-permute-start(bf16[192,768]{1,0:T(8,128)(2,1)S(1)} %get-tuple-element.50.refs_3_), channel_id=1, source_target_pairs={{0,8},{4,12},{8,0},{12,4},{16,24},{20,28},{24,16},{28,20},{1,9},{5... | collective-permute-start | bytes 884744 | tf_op jit(solution)/shard_map/ppermute | solution.py:551
  59.4 5.9 %collective-permute-done.19.refs_5_ = bf16[192,768]{1,0:T(8,128)(2,1)S(1)} collective-permute-done((bf16[192,768]{1,0:T(8,128)(2,1)S(1)}, bf16[192,768]{1,0:T(8,128)(2,1)S(1)}, u32[]{:S(2)}, u32[]{:S(2)}) %collective-permute-start.19) | collective-permute-done | bytes 294944 | tf_op jit(solution)/shard_map/ppermute | solution.py:551
  65.3 6.2 %attend_m.1.refs_4_ = f32[400,768]{1,0:T(8,128)S(1)} custom-call(bf16[384,384]{1,0:T(8,128)(2,1)S(1)} %get-tuple-element.49.refs_0_, bf16[384,384]{1,0:T(8,128)(2,1)S(1)} %collective-permute-done.17.refs_1_.refs_0_, bf16[192,768]{1,0:T(8,128)(2,1)S(1)} %get-tuple-element.46.refs_2_, bf16[192,768]{1,0:T(8,128)(2,1)S(1)} %get-tuple-element.50.refs_3_, ...), custom_call_target="tpu_custom_call" | custom-call | flops 1132462080 | bytes 3293184 | tf_op jit(solution)/shard_map/attend_m/pallas_call | solution.py:494
  71.8 5.1 %collective-permute-done.15.refs_2_ = bf16[192,768]{1,0:T(8,128)(2,1)S(1)} collective-permute-done((bf16[192,768]{1,0:T(8,128)(2,1)S(1)}, bf16[192,768]{1,0:T(8,128)(2,1)S(1)}, u32[]{:S(2)}, u32[]{:S(2)}) %collective-permute-start.15) | collective-permute-done | bytes 294944 | tf_op jit(solution)/shard_map/ppermute | solution.py:551
  76.9 3.0 %attend_other.1 = f32[400,384]{1,0:T(8,128)S(1)} custom-call(bf16[384,384]{1,0:T(8,128)(2,1)S(1)} %collective-permute-done.17.refs_1_.refs_0_, bf16[192,768]{1,0:T(8,128)(2,1)S(1)} %collective-permute-done.14.refs_1_, bf16[192,768]{1,0:T(8,128)(2,1)S(1)} %collective-permute-done.15.refs_2_, bf16[192,768]{1,0:T(8,128)(2,1)S(1)} %collective-permute-done.16.refs_3_, ...), custom_call_target="tpu_custom_call" | custom-call | flops 339738624 | bytes 3022848 | tf_op jit(solution)/shard_map/attend_other/pallas_call | solution.py:494
  79.9 3.0 %attend_own.1.own_state = f32[400,384]{1,0:T(8,128)S(1)} custom-call(bf16[384,384]{1,0:T(8,128)(2,1)S(1)} %get-tuple-element.49.refs_0_, bf16[192,768]{1,0:T(8,128)(2,1)S(1)} %collective-permute-done.14.refs_1_, bf16[192,768]{1,0:T(8,128)(2,1)S(1)} %collective-permute-done.15.refs_2_, bf16[192,768]{1,0:T(8,128)(2,1)S(1)} %collective-permute-done.16.refs_3_, ...), custom_call_target="tpu_custom_call" | custom-call | flops 339738624 | bytes 3022848 | tf_op jit(solution)/shard_map/attend_own/pallas_call | solution.py:494
  83.9 1.8 %collective-permute-start.22 = (bf16[384,384]{1,0:T(8,128)(2,1)S(1)}, bf16[384,384]{1,0:T(8,128)(2,1)S(1)}, u32[]{:S(2)}, u32[]{:S(2)}) collective-permute-start(bf16[384,384]{1,0:T(8,128)(2,1)S(1)} %get-tuple-element.55), channel_id=1, source_target_pairs={{0,1},{1,0},{2,3},{3,2},{4,5},{5,4},{6,7},{7,6},{8,9},{9,8},{10,11... | collective-permute-start | bytes 884744 | tf_op jit(solution)/shard_map/ppermute | solution.py:141
  85.7 7.7 %collective-permute-done.22 = bf16[384,384]{1,0:T(8,128)(2,1)S(1)} collective-permute-done((bf16[384,384]{1,0:T(8,128)(2,1)S(1)}, bf16[384,384]{1,0:T(8,128)(2,1)S(1)}, u32[]{:S(2)}, u32[]{:S(2)}) %collective-permute-start.22) | collective-permute-done | bytes 294944 | tf_op jit(solution)/shard_map/ppermute | solution.py:141
  93.5 1.8 %collective-permute-start.23 = (bf16[384,384]{1,0:T(8,128)(2,1)S(1)}, bf16[384,384]{1,0:T(8,128)(2,1)S(1)}, u32[]{:S(2)}, u32[]{:S(2)}) collective-permute-start(bf16[384,384]{1,0:T(8,128)(2,1)S(1)} %get-tuple-element.56), channel_id=1, source_target_pairs={{0,1},{1,0},{2,3},{3,2},{4,5},{5,4},{6,7},{7,6},{8,9},{9,8},{10,11... | collective-permute-start | bytes 884744 | tf_op jit(solution)/shard_map/ppermute | solution.py:141
  96.4 11.8 %collective-permute-done.23 = bf16[384,384]{1,0:T(8,128)(2,1)S(1)} collective-permute-done((bf16[384,384]{1,0:T(8,128)(2,1)S(1)}, bf16[384,384]{1,0:T(8,128)(2,1)S(1)}, u32[]{:S(2)}, u32[]{:S(2)}) %collective-permute-start.23) | collective-permute-done | bytes 294944 | tf_op jit(solution)/shard_map/ppermute | solution.py:141
  108.2 2.7 %collective-permute-done.24 = bf16[384,384]{1,0:T(8,128)(2,1)S(1)} collective-permute-done((bf16[384,384]{1,0:T(8,128)(2,1)S(1)}, bf16[384,384]{1,0:T(8,128)(2,1)S(1)}, u32[]{:S(2)}, u32[]{:S(2)}) %collective-permute-start.24) | collective-permute-done | bytes 294944 | tf_op jit(solution)/shard_map/ppermute | solution.py:141
  (53 shorter events, 22.8 us)
Async XLA Ops:
  4.3 11.7 %collective-permute-start.1 = (bf16[208,384]{1,0:T(8,128)(2,1)S(1)}, bf16[208,384]{1,0:T(8,128)(2,1)S(1)}, u32[]{:S(2)}, u32[]{:S(2)}) collective-permute-start(bf16[208,384]{1,0:T(8,128)(2,1)S(1)} %get-tuple-element.31.a0.m0), channel_id=1, source_target_pairs={{0,2},{1,3},{2,0},{3,1},{4,6},{5,7},{6,4},{7,5},{8,10},{9,11},{10,... | collective-permute-start | bytes 479240 | tf_op jit(solution)/shard_map/ppermute | solution.py:141
  8.4 8.3 %collective-permute-start.3 = (bf16[16,768]{1,0:T(8,128)(2,1)S(1)}, bf16[16,768]{1,0:T(8,128)(2,1)S(1)}, u32[]{:S(2)}, u32[]{:S(2)}) collective-permute-start(bf16[16,768]{1,0:T(8,128)(2,1)S(1)} %get-tuple-element.58), channel_id=1, source_target_pairs={{0,4},{4,8},{8,12},{12,16},{16,20},{20,24},{24,28},{1,5},{5,9},{9,... | collective-permute-start | bytes 73736 | tf_op jit(solution)/shard_map/ppermute | solution.py:559
  9.8 6.8 %collective-permute-start.4 = (bf16[16,768]{1,0:T(8,128)(2,1)S(1)}, bf16[16,768]{1,0:T(8,128)(2,1)S(1)}, u32[]{:S(2)}, u32[]{:S(2)}) collective-permute-start(bf16[16,768]{1,0:T(8,128)(2,1)S(1)} %get-tuple-element.57), channel_id=1, source_target_pairs={{4,0},{8,4},{12,8},{16,12},{20,16},{24,20},{28,24},{5,1},{9,5},{13... | collective-permute-start | bytes 73736 | tf_op jit(solution)/shard_map/ppermute | solution.py:560
  11.4 9.9 %collective-permute-start = (bf16[208,384]{1,0:T(8,128)(2,1)S(1)}, bf16[208,384]{1,0:T(8,128)(2,1)S(1)}, u32[]{:S(2)}, u32[]{:S(2)}) collective-permute-start(bf16[208,384]{1,0:T(8,128)(2,1)S(1)} %get-tuple-element.31.a0.m0), channel_id=1, source_target_pairs={{0,1},{1,0},{2,3},{3,2},{4,5},{5,4},{6,7},{7,6},{8,9},{9,8},{10,11... | collective-permute-start | bytes 479240 | tf_op jit(solution)/shard_map/ppermute | solution.py:141
  16.0 8.6 %collective-permute-start.2 = (bf16[208,384]{1,0:T(8,128)(2,1)S(1)}, bf16[208,384]{1,0:T(8,128)(2,1)S(1)}, u32[]{:S(2)}, u32[]{:S(2)}) collective-permute-start(bf16[208,384]{1,0:T(8,128)(2,1)S(1)} %collective-permute-done.1.a2.m2), channel_id=1, source_target_pairs={{0,1},{1,0},{2,3},{3,2},{4,5},{5,4},{6,7},{7,6},{8,9},{9,8},{10,11... | collective-permute-start | bytes 479240 | tf_op jit(solution)/shard_map/ppermute | solution.py:141
  17.8 10.9 %collective-permute-start.6 = (bf16[192,384]{1,0:T(8,128)(2,1)S(1)}, bf16[192,384]{1,0:T(8,128)(2,1)S(1)}, u32[]{:S(2)}, u32[]{:S(2)}) collective-permute-start(bf16[192,384]{1,0:T(8,128)(2,1)S(1)} %get-tuple-element.33.e0), channel_id=1, source_target_pairs={{0,2},{1,3},{2,0},{3,1},{4,6},{5,7},{6,4},{7,5},{8,10},{9,11},{10,... | collective-permute-start | bytes 442376 | tf_op jit(solution)/shard_map/ppermute | solution.py:141
  21.3 9.9 %collective-permute-start.5 = (bf16[192,384]{1,0:T(8,128)(2,1)S(1)}, bf16[192,384]{1,0:T(8,128)(2,1)S(1)}, u32[]{:S(2)}, u32[]{:S(2)}) collective-permute-start(bf16[192,384]{1,0:T(8,128)(2,1)S(1)} %get-tuple-element.33.e0), channel_id=1, source_target_pairs={{0,1},{1,0},{2,3},{3,2},{4,5},{5,4},{6,7},{7,6},{8,9},{9,8},{10,11... | collective-permute-start | bytes 442376 | tf_op jit(solution)/shard_map/ppermute | solution.py:141
  28.7 8.0 %collective-permute-start.10 = (bf16[192,384]{1,0:T(8,128)(2,1)S(1)}, bf16[192,384]{1,0:T(8,128)(2,1)S(1)}, u32[]{:S(2)}, u32[]{:S(2)}) collective-permute-start(bf16[192,384]{1,0:T(8,128)(2,1)S(1)} %get-tuple-element.45.a0), channel_id=1, source_target_pairs={{0,2},{1,3},{2,0},{3,1},{4,6},{5,7},{6,4},{7,5},{8,10},{9,11},{10,... | collective-permute-start | bytes 442376 | tf_op jit(solution)/shard_map/ppermute | solution.py:141
  29.0 9.8 %collective-permute-start.7 = (bf16[192,384]{1,0:T(8,128)(2,1)S(1)}, bf16[192,384]{1,0:T(8,128)(2,1)S(1)}, u32[]{:S(2)}, u32[]{:S(2)}) collective-permute-start(bf16[192,384]{1,0:T(8,128)(2,1)S(1)} %collective-permute-done.6.e2), channel_id=1, source_target_pairs={{0,1},{1,0},{2,3},{3,2},{4,5},{5,4},{6,7},{7,6},{8,9},{9,8},{10,11... | collective-permute-start | bytes 442376 | tf_op jit(solution)/shard_map/ppermute | solution.py:141
  31.2 10.5 %collective-permute-start.8 = (bf16[192,384]{1,0:T(8,128)(2,1)S(1)}, bf16[192,384]{1,0:T(8,128)(2,1)S(1)}, u32[]{:S(2)}, u32[]{:S(2)}) collective-permute-start(bf16[192,384]{1,0:T(8,128)(2,1)S(1)} %get-tuple-element.45.a0), channel_id=1, source_target_pairs={{0,1},{1,0},{2,3},{3,2},{4,5},{5,4},{6,7},{7,6},{8,9},{9,8},{10,11... | collective-permute-start | bytes 442376 | tf_op jit(solution)/shard_map/ppermute | solution.py:141
  36.7 9.5 %collective-permute-start.12 = (bf16[192,384]{1,0:T(8,128)(2,1)S(1)}, bf16[192,384]{1,0:T(8,128)(2,1)S(1)}, u32[]{:S(2)}, u32[]{:S(2)}) collective-permute-start(bf16[192,384]{1,0:T(8,128)(2,1)S(1)} %collective-permute-done.10.a2), channel_id=1, source_target_pairs={{0,1},{1,0},{2,3},{3,2},{4,5},{5,4},{6,7},{7,6},{8,9},{9,8},{10,11... | collective-permute-start | bytes 442376 | tf_op jit(solution)/shard_map/ppermute | solution.py:141
  40.5 8.0 %collective-permute-start.11 = (bf16[192,384]{1,0:T(8,128)(2,1)S(1)}, bf16[192,384]{1,0:T(8,128)(2,1)S(1)}, u32[]{:S(2)}, u32[]{:S(2)}) collective-permute-start(bf16[192,384]{1,0:T(8,128)(2,1)S(1)} %get-tuple-element.44.a0), channel_id=1, source_target_pairs={{0,2},{1,3},{2,0},{3,1},{4,6},{5,7},{6,4},{7,5},{8,10},{9,11},{10,... | collective-permute-start | bytes 442376 | tf_op jit(solution)/shard_map/ppermute | solution.py:141
  41.8 11.3 %collective-permute-start.9 = (bf16[192,384]{1,0:T(8,128)(2,1)S(1)}, bf16[192,384]{1,0:T(8,128)(2,1)S(1)}, u32[]{:S(2)}, u32[]{:S(2)}) collective-permute-start(bf16[192,384]{1,0:T(8,128)(2,1)S(1)} %get-tuple-element.44.a0), channel_id=1, source_target_pairs={{0,1},{1,0},{2,3},{3,2},{4,5},{5,4},{6,7},{7,6},{8,9},{9,8},{10,11... | collective-permute-start | bytes 442376 | tf_op jit(solution)/shard_map/ppermute | solution.py:141
  48.5 5.1 %collective-permute-start.13 = (bf16[192,384]{1,0:T(8,128)(2,1)S(1)}, bf16[192,384]{1,0:T(8,128)(2,1)S(1)}, u32[]{:S(2)}, u32[]{:S(2)}) collective-permute-start(bf16[192,384]{1,0:T(8,128)(2,1)S(1)} %collective-permute-done.11.a2), channel_id=1, source_target_pairs={{0,1},{1,0},{2,3},{3,2},{4,5},{5,4},{6,7},{7,6},{8,9},{9,8},{10,11... | collective-permute-start | bytes 442376 | tf_op jit(solution)/shard_map/ppermute | solution.py:141
  48.5 10.6 %collective-permute-start.18 = (bf16[192,768]{1,0:T(8,128)(2,1)S(1)}, bf16[192,768]{1,0:T(8,128)(2,1)S(1)}, u32[]{:S(2)}, u32[]{:S(2)}) collective-permute-start(bf16[192,768]{1,0:T(8,128)(2,1)S(1)} %get-tuple-element.46.refs_2_), channel_id=1, source_target_pairs={{0,8},{4,12},{8,0},{12,4},{16,24},{20,28},{24,16},{28,20},{1,9},{5... | collective-permute-start | bytes 884744 | tf_op jit(solution)/shard_map/ppermute | solution.py:551
  51.2 14.1 %collective-permute-start.19 = (bf16[192,768]{1,0:T(8,128)(2,1)S(1)}, bf16[192,768]{1,0:T(8,128)(2,1)S(1)}, u32[]{:S(2)}, u32[]{:S(2)}) collective-permute-start(bf16[192,768]{1,0:T(8,128)(2,1)S(1)} %get-tuple-element.46.refs_2_), channel_id=1, source_target_pairs={{0,16},{4,20},{8,24},{12,28},{16,0},{20,4},{24,8},{28,12},{1,17},{... | collective-permute-start | bytes 884744 | tf_op jit(solution)/shard_map/ppermute | solution.py:551
  51.8 13.5 %collective-permute-start.20 = (bf16[192,768]{1,0:T(8,128)(2,1)S(1)}, bf16[192,768]{1,0:T(8,128)(2,1)S(1)}, u32[]{:S(2)}, u32[]{:S(2)}) collective-permute-start(bf16[192,768]{1,0:T(8,128)(2,1)S(1)} %get-tuple-element.46.refs_2_), channel_id=1, source_target_pairs={{0,24},{4,28},{8,16},{12,20},{16,8},{20,12},{24,0},{28,4},{1,25},{... | collective-permute-start | bytes 884744 | tf_op jit(solution)/shard_map/ppermute | solution.py:551
  55.5 9.8 %collective-permute-start.17 = (bf16[384,384]{1,0:T(8,128)(2,1)S(1)}, bf16[384,384]{1,0:T(8,128)(2,1)S(1)}, u32[]{:S(2)}, u32[]{:S(2)}) collective-permute-start(bf16[384,384]{1,0:T(8,128)(2,1)S(1)} %get-tuple-element.49.refs_0_), channel_id=1, source_target_pairs={{0,4},{4,0},{8,12},{12,8},{16,20},{20,16},{24,28},{28,24},{1,5},{5... | collective-permute-start | bytes 884744 | tf_op jit(solution)/shard_map/ppermute | solution.py:551
  55.6 16.2 %collective-permute-start.14 = (bf16[192,768]{1,0:T(8,128)(2,1)S(1)}, bf16[192,768]{1,0:T(8,128)(2,1)S(1)}, u32[]{:S(2)}, u32[]{:S(2)}) collective-permute-start(bf16[192,768]{1,0:T(8,128)(2,1)S(1)} %get-tuple-element.50.refs_3_), channel_id=1, source_target_pairs={{0,8},{4,12},{8,0},{12,4},{16,24},{20,28},{24,16},{28,20},{1,9},{5... | collective-permute-start | bytes 884744 | tf_op jit(solution)/shard_map/ppermute | solution.py:551
  59.1 17.7 %collective-permute-start.15 = (bf16[192,768]{1,0:T(8,128)(2,1)S(1)}, bf16[192,768]{1,0:T(8,128)(2,1)S(1)}, u32[]{:S(2)}, u32[]{:S(2)}) collective-permute-start(bf16[192,768]{1,0:T(8,128)(2,1)S(1)} %get-tuple-element.50.refs_3_), channel_id=1, source_target_pairs={{0,16},{4,20},{8,24},{12,28},{16,0},{20,4},{24,8},{28,12},{1,17},{... | collective-permute-start | bytes 884744 | tf_op jit(solution)/shard_map/ppermute | solution.py:551
  65.3 11.6 %collective-permute-start.16 = (bf16[192,768]{1,0:T(8,128)(2,1)S(1)}, bf16[192,768]{1,0:T(8,128)(2,1)S(1)}, u32[]{:S(2)}, u32[]{:S(2)}) collective-permute-start(bf16[192,768]{1,0:T(8,128)(2,1)S(1)} %get-tuple-element.50.refs_3_), channel_id=1, source_target_pairs={{0,24},{4,28},{8,16},{12,20},{16,8},{20,12},{24,0},{28,4},{1,25},{... | collective-permute-start | bytes 884744 | tf_op jit(solution)/shard_map/ppermute | solution.py:551
  83.9 9.5 %collective-permute-start.22 = (bf16[384,384]{1,0:T(8,128)(2,1)S(1)}, bf16[384,384]{1,0:T(8,128)(2,1)S(1)}, u32[]{:S(2)}, u32[]{:S(2)}) collective-permute-start(bf16[384,384]{1,0:T(8,128)(2,1)S(1)} %get-tuple-element.55), channel_id=1, source_target_pairs={{0,1},{1,0},{2,3},{3,2},{4,5},{5,4},{6,7},{7,6},{8,9},{9,8},{10,11... | collective-permute-start | bytes 884744 | tf_op jit(solution)/shard_map/ppermute | solution.py:141
  93.5 14.7 %collective-permute-start.23 = (bf16[384,384]{1,0:T(8,128)(2,1)S(1)}, bf16[384,384]{1,0:T(8,128)(2,1)S(1)}, u32[]{:S(2)}, u32[]{:S(2)}) collective-permute-start(bf16[384,384]{1,0:T(8,128)(2,1)S(1)} %get-tuple-element.56), channel_id=1, source_target_pairs={{0,1},{1,0},{2,3},{3,2},{4,5},{5,4},{6,7},{7,6},{8,9},{9,8},{10,11... | collective-permute-start | bytes 884744 | tf_op jit(solution)/shard_map/ppermute | solution.py:141
  95.3 15.6 %collective-permute-start.24 = (bf16[384,384]{1,0:T(8,128)(2,1)S(1)}, bf16[384,384]{1,0:T(8,128)(2,1)S(1)}, u32[]{:S(2)}, u32[]{:S(2)}) collective-permute-start(bf16[384,384]{1,0:T(8,128)(2,1)S(1)} %add_convert_fusion.1), channel_id=1, source_target_pairs={{0,2},{1,3},{2,0},{3,1},{4,6},{5,7},{6,4},{7,5},{8,10},{9,11},{10,... | collective-permute-start | bytes 884744 | tf_op jit(solution)/shard_map/ppermute | solution.py:141
  (8 other events, 46.5 us)

commit v9 on v8

--- a/solution.py
+++ b/solution.py
@@ -563,7 +563,7 @@
     )
     wide_m = forwarded(shared(sent))
     h1_e, sent = first_conv(
-        conv_edge_kernel, (dna, after(low, wide_m[2]), high), conv_in, outer, 2 * (outer + 2 * EDGE), "conv_edge"
+        conv_edge_kernel, (dna, after(low, *wide_m[1:3]), high), conv_in, outer, 2 * (outer + 2 * EDGE), "conv_edge"
     )
     wide_e = shared(sent)
     h2_m, sent = second_conv(
@@ -575,7 +575,7 @@
         inner + EDGE,
         "dilated_middle",
     )
-    normed_m = forwarded(shared(sent, wide_e))
+    normed_m = shared(sent, wide_e)
     wide_e = forwarded(wide_e, sent)
     h2, sent = second_conv(
         dilated_edge_kernel,
@@ -587,7 +587,7 @@
         "dilated_edge",
     )
     normed_e = shared(sent, normed_m)
-    normed_m[0] = after(normed_m[0], sent)
+    normed_m = forwarded(normed_m, sent)
     weights = (w_query, w_key, w_value)
     q_m, kv_m = project(project_middle_kernel, normed_m, weights, inner, "project_middle")
     x_m, y_m, d_m = (exchanged(kv_m, mask) for mask in (2, 4, 6))

time: 112 us -> 112 us (level)
  waiting for transfers between devices: 54.3 us -> 50.5 us
  starting transfers between devices: 30.8 us -> 34.5 us
    ppermute x8, waiting for transfers between devices: 12.1 us -> 5.06 us  [exchanged(): return lax.ppermute(block, 'seq', [(i, i ^ mask) for i in range(count)])]
    ppermute x8, starting transfers between devices: 7.83 us -> 12 us  [exchanged(): return lax.ppermute(block, 'seq', [(i, i ^ mask) for i in range(count)])]
    ppermute x15, waiting for transfers between devices: 42.2 us -> 45.5 us  [swapped(): return lax.ppermute(block, 'head', [(i, i ^ mask) for i in range(count)])]
  transfers between devices with their start and end apart: 25 -> 25, of which waited for: 15 -> 13; matrix products, arithmetic and copies ran while one was open for 0% -> 0% of each run, Pallas kernels for 16% -> 16%
where the time goes in v9:
time: 112 us
  waiting for transfers between devices  50.5 us (45%)
  starting transfers between devices  34.5 us (31%)
  Pallas kernels  22.4 us (20%)
  local copies, waits for them, and re-layouts  3.13 us (3%)
    ppermute x15, waiting for transfers between devices, swapped(): return lax.ppermute(block, 'head', [(i, i ^ mask) for i in range(count)])  45.5 us
    ppermute x15, starting transfers between devices, swapped(): return lax.ppermute(block, 'head', [(i, i ^ mask) for i in range(count)])  19.7 us
    pallas_call x3, Pallas kernels, attend(): pl.pallas_call(kernel, out_shape=out, scratch_shapes=[pltpu.VMEM((2, exte...  12.1 us
    ppermute x8, starting transfers between devices, exchanged(): return lax.ppermute(block, 'seq', [(i, i ^ mask) for i in range(count)])  12 us
    ppermute x8, waiting for transfers between devices, exchanged(): return lax.ppermute(block, 'seq', [(i, i ^ mask) for i in range(count)])  5.06 us
    pallas_call x2, Pallas kernels, project(): pl.pallas_call(kernel, out_shape=(q, kv), compiler_params=pltpu.CompilerP...  3.69 us
    pallas_call x2, Pallas kernels, second_conv(): pl.pallas_call(kernel, out_shape=(kept, sent), scratch_shapes=[pltpu.VMEM...  3.42 us
    unnamed x14, local copies, waits for them, and re-layouts  3.13 us
  transfers between devices with their start and end apart: 25, of which 13 were waited for; matrix products, arithmetic and copies ran while one was open for 0% of the time, Pallas kernels for 16%

profile of v9, /device:TPU:0, one launch (start us, length us, event | category | flops | bytes accessed | tf_op | source)
XLA Modules:
  0.0 111.7 jit_solution(13654209906728678019)
XLA Ops:
  0.0 1.8 %copy-done.1 = bf16[5,384,768]{2,1,0:T(8,128)(2,1)S(1)} copy-done((bf16[5,384,768]{2,1,0:T(8,128)(2,1)S(1)}, bf16[5,384,768]{2,1,0:T(8,128)(2,1)}, u32[]{:S(2)}) %copy-start.1) | copy-done | bytes 2949144
  4.3 4.1 %collective-permute-start.1 = (bf16[208,384]{1,0:T(8,128)(2,1)S(1)}, bf16[208,384]{1,0:T(8,128)(2,1)S(1)}, u32[]{:S(2)}, u32[]{:S(2)}) collective-permute-start(bf16[208,384]{1,0:T(8,128)(2,1)S(1)} %get-tuple-element.31.a0.m0), channel_id=1, source_target_pairs={{0,2},{1,3},{2,0},{3,1},{4,6},{5,7},{6,4},{7,5},{8,10},{9,11},{10,... | collective-permute-start | bytes 479240 | tf_op jit(solution)/shard_map/ppermute | solution.py:141
  12.8 3.2 %collective-permute-done.1.a2.m2 = bf16[208,384]{1,0:T(8,128)(2,1)S(1)} collective-permute-done((bf16[208,384]{1,0:T(8,128)(2,1)S(1)}, bf16[208,384]{1,0:T(8,128)(2,1)S(1)}, u32[]{:S(2)}, u32[]{:S(2)}) %collective-permute-start.1) | collective-permute-done | bytes 159776 | tf_op jit(solution)/shard_map/ppermute | solution.py:141
  17.8 3.4 %collective-permute-start.6 = (bf16[192,384]{1,0:T(8,128)(2,1)S(1)}, bf16[192,384]{1,0:T(8,128)(2,1)S(1)}, u32[]{:S(2)}, u32[]{:S(2)}) collective-permute-start(bf16[192,384]{1,0:T(8,128)(2,1)S(1)} %get-tuple-element.33.e0), channel_id=1, source_target_pairs={{0,2},{1,3},{2,0},{3,1},{4,6},{5,7},{6,4},{7,5},{8,10},{9,11},{10,... | collective-permute-start | bytes 442376 | tf_op jit(solution)/shard_map/ppermute | solution.py:141
  23.4 4.9 %collective-permute-done.6.e2 = bf16[192,384]{1,0:T(8,128)(2,1)S(1)} collective-permute-done((bf16[192,384]{1,0:T(8,128)(2,1)S(1)}, bf16[192,384]{1,0:T(8,128)(2,1)S(1)}, u32[]{:S(2)}, u32[]{:S(2)}) %collective-permute-start.6) | collective-permute-done | bytes 147488 | tf_op jit(solution)/shard_map/ppermute | solution.py:141
  28.3 2.9 %collective-permute-start.10 = (bf16[192,384]{1,0:T(8,128)(2,1)S(1)}, bf16[192,384]{1,0:T(8,128)(2,1)S(1)}, u32[]{:S(2)}, u32[]{:S(2)}) collective-permute-start(bf16[192,384]{1,0:T(8,128)(2,1)S(1)} %get-tuple-element.43.a0), channel_id=1, source_target_pairs={{0,2},{1,3},{2,0},{3,1},{4,6},{5,7},{6,4},{7,5},{8,10},{9,11},{10,... | collective-permute-start | bytes 442376 | tf_op jit(solution)/shard_map/ppermute | solution.py:141
  31.2 5.3 %collective-permute-done.7.e3 = bf16[192,384]{1,0:T(8,128)(2,1)S(1)} collective-permute-done((bf16[192,384]{1,0:T(8,128)(2,1)S(1)}, bf16[192,384]{1,0:T(8,128)(2,1)S(1)}, u32[]{:S(2)}, u32[]{:S(2)}) %collective-permute-start.7) | collective-permute-done | bytes 147488 | tf_op jit(solution)/shard_map/ppermute | solution.py:141
  36.5 1.8 %dilated_edge.1 = (f32[384,384]{1,0:T(8,128)S(1)}, bf16[192,384]{1,0:T(8,128)(2,1)S(1)}) custom-call(bf16[208,384]{1,0:T(8,128)(2,1)S(1)} %get-tuple-element.31.a0.m0, bf16[208,384]{1,0:T(8,128)(2,1)S(1)} %collective-permute-done.a1.m1, bf16[208,384]{1,0:T(8,128)(2,1)S(1)} %collective-permute-done.1.a2.m2, ...), custom_call_target="tpu_custom_call" | custom-call | flops 679477248 | bytes 6414336 | tf_op jit(solution)/shard_map/dilated_edge/pallas_call | solution.py:317
  38.9 3.4 %collective-permute-start.11 = (bf16[192,384]{1,0:T(8,128)(2,1)S(1)}, bf16[192,384]{1,0:T(8,128)(2,1)S(1)}, u32[]{:S(2)}, u32[]{:S(2)}) collective-permute-start(bf16[192,384]{1,0:T(8,128)(2,1)S(1)} %get-tuple-element.44.a0), channel_id=1, source_target_pairs={{0,2},{1,3},{2,0},{3,1},{4,6},{5,7},{6,4},{7,5},{8,10},{9,11},{10,... | collective-permute-start | bytes 442376 | tf_op jit(solution)/shard_map/ppermute | solution.py:141
  42.3 6.2 %collective-permute-done.12.a3 = bf16[192,384]{1,0:T(8,128)(2,1)S(1)} collective-permute-done((bf16[192,384]{1,0:T(8,128)(2,1)S(1)}, bf16[192,384]{1,0:T(8,128)(2,1)S(1)}, u32[]{:S(2)}, u32[]{:S(2)}) %collective-permute-start.12) | collective-permute-done | bytes 147488 | tf_op jit(solution)/shard_map/ppermute | solution.py:141
  48.6 1.8 %project_middle.1 = (bf16[192,384]{1,0:T(8,128)(2,1)S(1)}, bf16[192,768]{1,0:T(8,128)(2,1)S(1)}) custom-call(bf16[192,384]{1,0:T(8,128)(2,1)S(1)} %get-tuple-element.43.a0, bf16[192,384]{1,0:T(8,128)(2,1)S(1)} %collective-permute-done.8.a1, bf16[192,384]{1,0:T(8,128)(2,1)S(1)} %collective-permute-done.10.a2, ...), custom_call_target="tpu_custom_call" | custom-call | flops 679477248 | bytes 4571136 | tf_op jit(solution)/shard_map/project_middle/pallas_call | solution.py:379
  50.5 2.0 %collective-permute-start.18 = (bf16[192,768]{1,0:T(8,128)(2,1)S(1)}, bf16[192,768]{1,0:T(8,128)(2,1)S(1)}, u32[]{:S(2)}, u32[]{:S(2)}) collective-permute-start(bf16[192,768]{1,0:T(8,128)(2,1)S(1)} %get-tuple-element.46.refs_2_), channel_id=1, source_target_pairs={{0,8},{4,12},{8,0},{12,4},{16,24},{20,28},{24,16},{28,20},{1,9},{5... | collective-permute-start | bytes 884744 | tf_op jit(solution)/shard_map/ppermute | solution.py:551
  55.6 1.8 %project_edge.1 = (bf16[384,384]{1,0:T(8,128)(2,1)S(1)}, bf16[192,768]{1,0:T(8,128)(2,1)S(1)}) custom-call(bf16[192,384]{1,0:T(8,128)(2,1)S(1)} %get-tuple-element.44.a0, bf16[192,384]{1,0:T(8,128)(2,1)S(1)} %collective-permute-done.9.a1, bf16[192,384]{1,0:T(8,128)(2,1)S(1)} %collective-permute-done.11.a2, bf16[192,384]{1,0:T(8,128)(2,1)S(1)} %collective-permute-done.13.a3, ...), custom_call_target="tpu_custom_call" | custom-call | flops 679477248 | bytes 4866048 | tf_op jit(solution)/shard_map/project_edge/pallas_call | solution.py:379
  57.6 2.0 %collective-permute-start.14 = (bf16[192,768]{1,0:T(8,128)(2,1)S(1)}, bf16[192,768]{1,0:T(8,128)(2,1)S(1)}, u32[]{:S(2)}, u32[]{:S(2)}) collective-permute-start(bf16[192,768]{1,0:T(8,128)(2,1)S(1)} %get-tuple-element.50.refs_3_), channel_id=1, source_target_pairs={{0,8},{4,12},{8,0},{12,4},{16,24},{20,28},{24,16},{28,20},{1,9},{5... | collective-permute-start | bytes 884744 | tf_op jit(solution)/shard_map/ppermute | solution.py:551
  61.6 4.4 %collective-permute-start.16 = (bf16[192,768]{1,0:T(8,128)(2,1)S(1)}, bf16[192,768]{1,0:T(8,128)(2,1)S(1)}, u32[]{:S(2)}, u32[]{:S(2)}) collective-permute-start(bf16[192,768]{1,0:T(8,128)(2,1)S(1)} %get-tuple-element.50.refs_3_), channel_id=1, source_target_pairs={{0,24},{4,28},{8,16},{12,20},{16,8},{20,12},{24,0},{28,4},{1,25},{... | collective-permute-start | bytes 884744 | tf_op jit(solution)/shard_map/ppermute | solution.py:551
  66.1 6.1 %attend_m.1.refs_4_ = f32[400,768]{1,0:T(8,128)S(1)} custom-call(bf16[384,384]{1,0:T(8,128)(2,1)S(1)} %get-tuple-element.49.refs_0_, bf16[384,384]{1,0:T(8,128)(2,1)S(1)} %collective-permute-done.17.refs_1_.refs_0_, bf16[192,768]{1,0:T(8,128)(2,1)S(1)} %get-tuple-element.46.refs_2_, bf16[192,768]{1,0:T(8,128)(2,1)S(1)} %get-tuple-element.50.refs_3_, ...), custom_call_target="tpu_custom_call" | custom-call | flops 1132462080 | bytes 3293184 | tf_op jit(solution)/shard_map/attend_m/pallas_call | solution.py:494
  72.2 2.8 %collective-permute-done.15.refs_2_ = bf16[192,768]{1,0:T(8,128)(2,1)S(1)} collective-permute-done((bf16[192,768]{1,0:T(8,128)(2,1)S(1)}, bf16[192,768]{1,0:T(8,128)(2,1)S(1)}, u32[]{:S(2)}, u32[]{:S(2)}) %collective-permute-start.15) | collective-permute-done | bytes 294944 | tf_op jit(solution)/shard_map/ppermute | solution.py:551
  75.1 1.9 %collective-permute-done.16.refs_3_ = bf16[192,768]{1,0:T(8,128)(2,1)S(1)} collective-permute-done((bf16[192,768]{1,0:T(8,128)(2,1)S(1)}, bf16[192,768]{1,0:T(8,128)(2,1)S(1)}, u32[]{:S(2)}, u32[]{:S(2)}) %collective-permute-start.16) | collective-permute-done | bytes 294944 | tf_op jit(solution)/shard_map/ppermute | solution.py:551
  76.9 3.0 %attend_other.1 = f32[400,384]{1,0:T(8,128)S(1)} custom-call(bf16[384,384]{1,0:T(8,128)(2,1)S(1)} %collective-permute-done.17.refs_1_.refs_0_, bf16[192,768]{1,0:T(8,128)(2,1)S(1)} %collective-permute-done.14.refs_1_, bf16[192,768]{1,0:T(8,128)(2,1)S(1)} %collective-permute-done.15.refs_2_, bf16[192,768]{1,0:T(8,128)(2,1)S(1)} %collective-permute-done.16.refs_3_, ...), custom_call_target="tpu_custom_call" | custom-call | flops 339738624 | bytes 3022848 | tf_op jit(solution)/shard_map/attend_other/pallas_call | solution.py:494
  80.0 3.0 %attend_own.1.own_state = f32[400,384]{1,0:T(8,128)S(1)} custom-call(bf16[384,384]{1,0:T(8,128)(2,1)S(1)} %get-tuple-element.49.refs_0_, bf16[192,768]{1,0:T(8,128)(2,1)S(1)} %collective-permute-done.14.refs_1_, bf16[192,768]{1,0:T(8,128)(2,1)S(1)} %collective-permute-done.15.refs_2_, bf16[192,768]{1,0:T(8,128)(2,1)S(1)} %collective-permute-done.16.refs_3_, ...), custom_call_target="tpu_custom_call" | custom-call | flops 339738624 | bytes 3022848 | tf_op jit(solution)/shard_map/attend_own/pallas_call | solution.py:494
  84.0 1.7 %collective-permute-start.22 = (bf16[384,384]{1,0:T(8,128)(2,1)S(1)}, bf16[384,384]{1,0:T(8,128)(2,1)S(1)}, u32[]{:S(2)}, u32[]{:S(2)}) collective-permute-start(bf16[384,384]{1,0:T(8,128)(2,1)S(1)} %get-tuple-element.55), channel_id=1, source_target_pairs={{0,1},{1,0},{2,3},{3,2},{4,5},{5,4},{6,7},{7,6},{8,9},{9,8},{10,11... | collective-permute-start | bytes 884744 | tf_op jit(solution)/shard_map/ppermute | solution.py:141
  85.7 7.7 %collective-permute-done.22 = bf16[384,384]{1,0:T(8,128)(2,1)S(1)} collective-permute-done((bf16[384,384]{1,0:T(8,128)(2,1)S(1)}, bf16[384,384]{1,0:T(8,128)(2,1)S(1)}, u32[]{:S(2)}, u32[]{:S(2)}) %collective-permute-start.22) | collective-permute-done | bytes 294944 | tf_op jit(solution)/shard_map/ppermute | solution.py:141
  95.3 11.2 %collective-permute-done.23 = bf16[384,384]{1,0:T(8,128)(2,1)S(1)} collective-permute-done((bf16[384,384]{1,0:T(8,128)(2,1)S(1)}, bf16[384,384]{1,0:T(8,128)(2,1)S(1)}, u32[]{:S(2)}, u32[]{:S(2)}) %collective-permute-start.23) | collective-permute-done | bytes 294944 | tf_op jit(solution)/shard_map/ppermute | solution.py:141
  106.4 4.5 %collective-permute-done.24 = bf16[384,384]{1,0:T(8,128)(2,1)S(1)} collective-permute-done((bf16[384,384]{1,0:T(8,128)(2,1)S(1)}, bf16[384,384]{1,0:T(8,128)(2,1)S(1)}, u32[]{:S(2)}, u32[]{:S(2)}) %collective-permute-start.24) | collective-permute-done | bytes 294944 | tf_op jit(solution)/shard_map/ppermute | solution.py:141
  (53 shorter events, 20.6 us)
Async XLA Ops:
  4.3 11.7 %collective-permute-start.1 = (bf16[208,384]{1,0:T(8,128)(2,1)S(1)}, bf16[208,384]{1,0:T(8,128)(2,1)S(1)}, u32[]{:S(2)}, u32[]{:S(2)}) collective-permute-start(bf16[208,384]{1,0:T(8,128)(2,1)S(1)} %get-tuple-element.31.a0.m0), channel_id=1, source_target_pairs={{0,2},{1,3},{2,0},{3,1},{4,6},{5,7},{6,4},{7,5},{8,10},{9,11},{10,... | collective-permute-start | bytes 479240 | tf_op jit(solution)/shard_map/ppermute | solution.py:141
  8.4 8.3 %collective-permute-start = (bf16[208,384]{1,0:T(8,128)(2,1)S(1)}, bf16[208,384]{1,0:T(8,128)(2,1)S(1)}, u32[]{:S(2)}, u32[]{:S(2)}) collective-permute-start(bf16[208,384]{1,0:T(8,128)(2,1)S(1)} %get-tuple-element.31.a0.m0), channel_id=1, source_target_pairs={{0,1},{1,0},{2,3},{3,2},{4,5},{5,4},{6,7},{7,6},{8,9},{9,8},{10,11... | collective-permute-start | bytes 479240 | tf_op jit(solution)/shard_map/ppermute | solution.py:141
  9.9 6.7 %collective-permute-start.3 = (bf16[16,768]{1,0:T(8,128)(2,1)S(1)}, bf16[16,768]{1,0:T(8,128)(2,1)S(1)}, u32[]{:S(2)}, u32[]{:S(2)}) collective-permute-start(bf16[16,768]{1,0:T(8,128)(2,1)S(1)} %get-tuple-element.58), channel_id=1, source_target_pairs={{0,4},{4,8},{8,12},{12,16},{16,20},{20,24},{24,28},{1,5},{5,9},{9,... | collective-permute-start | bytes 73736 | tf_op jit(solution)/shard_map/ppermute | solution.py:559
  11.2 5.4 %collective-permute-start.4 = (bf16[16,768]{1,0:T(8,128)(2,1)S(1)}, bf16[16,768]{1,0:T(8,128)(2,1)S(1)}, u32[]{:S(2)}, u32[]{:S(2)}) collective-permute-start(bf16[16,768]{1,0:T(8,128)(2,1)S(1)} %get-tuple-element.57), channel_id=1, source_target_pairs={{4,0},{8,4},{12,8},{16,12},{20,16},{24,20},{28,24},{5,1},{9,5},{13... | collective-permute-start | bytes 73736 | tf_op jit(solution)/shard_map/ppermute | solution.py:560
  16.0 5.8 %collective-permute-start.2 = (bf16[208,384]{1,0:T(8,128)(2,1)S(1)}, bf16[208,384]{1,0:T(8,128)(2,1)S(1)}, u32[]{:S(2)}, u32[]{:S(2)}) collective-permute-start(bf16[208,384]{1,0:T(8,128)(2,1)S(1)} %collective-permute-done.1.a2.m2), channel_id=1, source_target_pairs={{0,1},{1,0},{2,3},{3,2},{4,5},{5,4},{6,7},{7,6},{8,9},{9,8},{10,11... | collective-permute-start | bytes 479240 | tf_op jit(solution)/shard_map/ppermute | solution.py:141
  17.8 10.5 %collective-permute-start.6 = (bf16[192,384]{1,0:T(8,128)(2,1)S(1)}, bf16[192,384]{1,0:T(8,128)(2,1)S(1)}, u32[]{:S(2)}, u32[]{:S(2)}) collective-permute-start(bf16[192,384]{1,0:T(8,128)(2,1)S(1)} %get-tuple-element.33.e0), channel_id=1, source_target_pairs={{0,2},{1,3},{2,0},{3,1},{4,6},{5,7},{6,4},{7,5},{8,10},{9,11},{10,... | collective-permute-start | bytes 442376 | tf_op jit(solution)/shard_map/ppermute | solution.py:141
  21.2 10.0 %collective-permute-start.5 = (bf16[192,384]{1,0:T(8,128)(2,1)S(1)}, bf16[192,384]{1,0:T(8,128)(2,1)S(1)}, u32[]{:S(2)}, u32[]{:S(2)}) collective-permute-start(bf16[192,384]{1,0:T(8,128)(2,1)S(1)} %get-tuple-element.33.e0), channel_id=1, source_target_pairs={{0,1},{1,0},{2,3},{3,2},{4,5},{5,4},{6,7},{7,6},{8,9},{9,8},{10,11... | collective-permute-start | bytes 442376 | tf_op jit(solution)/shard_map/ppermute | solution.py:141
  28.3 8.2 %collective-permute-start.7 = (bf16[192,384]{1,0:T(8,128)(2,1)S(1)}, bf16[192,384]{1,0:T(8,128)(2,1)S(1)}, u32[]{:S(2)}, u32[]{:S(2)}) collective-permute-start(bf16[192,384]{1,0:T(8,128)(2,1)S(1)} %collective-permute-done.6.e2), channel_id=1, source_target_pairs={{0,1},{1,0},{2,3},{3,2},{4,5},{5,4},{6,7},{7,6},{8,9},{9,8},{10,11... | collective-permute-start | bytes 442376 | tf_op jit(solution)/shard_map/ppermute | solution.py:141
  28.3 10.6 %collective-permute-start.10 = (bf16[192,384]{1,0:T(8,128)(2,1)S(1)}, bf16[192,384]{1,0:T(8,128)(2,1)S(1)}, u32[]{:S(2)}, u32[]{:S(2)}) collective-permute-start(bf16[192,384]{1,0:T(8,128)(2,1)S(1)} %get-tuple-element.43.a0), channel_id=1, source_target_pairs={{0,2},{1,3},{2,0},{3,1},{4,6},{5,7},{6,4},{7,5},{8,10},{9,11},{10,... | collective-permute-start | bytes 442376 | tf_op jit(solution)/shard_map/ppermute | solution.py:141
  31.2 11.1 %collective-permute-start.8 = (bf16[192,384]{1,0:T(8,128)(2,1)S(1)}, bf16[192,384]{1,0:T(8,128)(2,1)S(1)}, u32[]{:S(2)}, u32[]{:S(2)}) collective-permute-start(bf16[192,384]{1,0:T(8,128)(2,1)S(1)} %get-tuple-element.43.a0), channel_id=1, source_target_pairs={{0,1},{1,0},{2,3},{3,2},{4,5},{5,4},{6,7},{7,6},{8,9},{9,8},{10,11... | collective-permute-start | bytes 442376 | tf_op jit(solution)/shard_map/ppermute | solution.py:141
  38.9 9.7 %collective-permute-start.12 = (bf16[192,384]{1,0:T(8,128)(2,1)S(1)}, bf16[192,384]{1,0:T(8,128)(2,1)S(1)}, u32[]{:S(2)}, u32[]{:S(2)}) collective-permute-start(bf16[192,384]{1,0:T(8,128)(2,1)S(1)} %collective-permute-done.10.a2), channel_id=1, source_target_pairs={{0,1},{1,0},{2,3},{3,2},{4,5},{5,4},{6,7},{7,6},{8,9},{9,8},{10,11... | collective-permute-start | bytes 442376 | tf_op jit(solution)/shard_map/ppermute | solution.py:141
  38.9 11.6 %collective-permute-start.11 = (bf16[192,384]{1,0:T(8,128)(2,1)S(1)}, bf16[192,384]{1,0:T(8,128)(2,1)S(1)}, u32[]{:S(2)}, u32[]{:S(2)}) collective-permute-start(bf16[192,384]{1,0:T(8,128)(2,1)S(1)} %get-tuple-element.44.a0), channel_id=1, source_target_pairs={{0,2},{1,3},{2,0},{3,1},{4,6},{5,7},{6,4},{7,5},{8,10},{9,11},{10,... | collective-permute-start | bytes 442376 | tf_op jit(solution)/shard_map/ppermute | solution.py:141
  42.3 12.0 %collective-permute-start.9 = (bf16[192,384]{1,0:T(8,128)(2,1)S(1)}, bf16[192,384]{1,0:T(8,128)(2,1)S(1)}, u32[]{:S(2)}, u32[]{:S(2)}) collective-permute-start(bf16[192,384]{1,0:T(8,128)(2,1)S(1)} %get-tuple-element.44.a0), channel_id=1, source_target_pairs={{0,1},{1,0},{2,3},{3,2},{4,5},{5,4},{6,7},{7,6},{8,9},{9,8},{10,11... | collective-permute-start | bytes 442376 | tf_op jit(solution)/shard_map/ppermute | solution.py:141
  50.4 5.2 %collective-permute-start.13 = (bf16[192,384]{1,0:T(8,128)(2,1)S(1)}, bf16[192,384]{1,0:T(8,128)(2,1)S(1)}, u32[]{:S(2)}, u32[]{:S(2)}) collective-permute-start(bf16[192,384]{1,0:T(8,128)(2,1)S(1)} %collective-permute-done.11.a2), channel_id=1, source_target_pairs={{0,1},{1,0},{2,3},{3,2},{4,5},{5,4},{6,7},{7,6},{8,9},{9,8},{10,11... | collective-permute-start | bytes 442376 | tf_op jit(solution)/shard_map/ppermute | solution.py:141
  50.5 9.4 %collective-permute-start.18 = (bf16[192,768]{1,0:T(8,128)(2,1)S(1)}, bf16[192,768]{1,0:T(8,128)(2,1)S(1)}, u32[]{:S(2)}, u32[]{:S(2)}) collective-permute-start(bf16[192,768]{1,0:T(8,128)(2,1)S(1)} %get-tuple-element.46.refs_2_), channel_id=1, source_target_pairs={{0,8},{4,12},{8,0},{12,4},{16,24},{20,28},{24,16},{28,20},{1,9},{5... | collective-permute-start | bytes 884744 | tf_op jit(solution)/shard_map/ppermute | solution.py:551
  52.5 9.1 %collective-permute-start.19 = (bf16[192,768]{1,0:T(8,128)(2,1)S(1)}, bf16[192,768]{1,0:T(8,128)(2,1)S(1)}, u32[]{:S(2)}, u32[]{:S(2)}) collective-permute-start(bf16[192,768]{1,0:T(8,128)(2,1)S(1)} %get-tuple-element.46.refs_2_), channel_id=1, source_target_pairs={{0,16},{4,20},{8,24},{12,28},{16,0},{20,4},{24,8},{28,12},{1,17},{... | collective-permute-start | bytes 884744 | tf_op jit(solution)/shard_map/ppermute | solution.py:551
  52.9 13.2 %collective-permute-start.20 = (bf16[192,768]{1,0:T(8,128)(2,1)S(1)}, bf16[192,768]{1,0:T(8,128)(2,1)S(1)}, u32[]{:S(2)}, u32[]{:S(2)}) collective-permute-start(bf16[192,768]{1,0:T(8,128)(2,1)S(1)} %get-tuple-element.46.refs_2_), channel_id=1, source_target_pairs={{0,24},{4,28},{8,16},{12,20},{16,8},{20,12},{24,0},{28,4},{1,25},{... | collective-permute-start | bytes 884744 | tf_op jit(solution)/shard_map/ppermute | solution.py:551
  57.5 8.6 %collective-permute-start.17 = (bf16[384,384]{1,0:T(8,128)(2,1)S(1)}, bf16[384,384]{1,0:T(8,128)(2,1)S(1)}, u32[]{:S(2)}, u32[]{:S(2)}) collective-permute-start(bf16[384,384]{1,0:T(8,128)(2,1)S(1)} %get-tuple-element.49.refs_0_), channel_id=1, source_target_pairs={{0,4},{4,0},{8,12},{12,8},{16,20},{20,16},{24,28},{28,24},{1,5},{5... | collective-permute-start | bytes 884744 | tf_op jit(solution)/shard_map/ppermute | solution.py:551
  57.6 14.7 %collective-permute-start.14 = (bf16[192,768]{1,0:T(8,128)(2,1)S(1)}, bf16[192,768]{1,0:T(8,128)(2,1)S(1)}, u32[]{:S(2)}, u32[]{:S(2)}) collective-permute-start(bf16[192,768]{1,0:T(8,128)(2,1)S(1)} %get-tuple-element.50.refs_3_), channel_id=1, source_target_pairs={{0,8},{4,12},{8,0},{12,4},{16,24},{20,28},{24,16},{28,20},{1,9},{5... | collective-permute-start | bytes 884744 | tf_op jit(solution)/shard_map/ppermute | solution.py:551
  59.9 15.2 %collective-permute-start.15 = (bf16[192,768]{1,0:T(8,128)(2,1)S(1)}, bf16[192,768]{1,0:T(8,128)(2,1)S(1)}, u32[]{:S(2)}, u32[]{:S(2)}) collective-permute-start(bf16[192,768]{1,0:T(8,128)(2,1)S(1)} %get-tuple-element.50.refs_3_), channel_id=1, source_target_pairs={{0,16},{4,20},{8,24},{12,28},{16,0},{20,4},{24,8},{28,12},{1,17},{... | collective-permute-start | bytes 884744 | tf_op jit(solution)/shard_map/ppermute | solution.py:551
  61.6 15.3 %collective-permute-start.16 = (bf16[192,768]{1,0:T(8,128)(2,1)S(1)}, bf16[192,768]{1,0:T(8,128)(2,1)S(1)}, u32[]{:S(2)}, u32[]{:S(2)}) collective-permute-start(bf16[192,768]{1,0:T(8,128)(2,1)S(1)} %get-tuple-element.50.refs_3_), channel_id=1, source_target_pairs={{0,24},{4,28},{8,16},{12,20},{16,8},{20,12},{24,0},{28,4},{1,25},{... | collective-permute-start | bytes 884744 | tf_op jit(solution)/shard_map/ppermute | solution.py:551
  84.0 9.5 %collective-permute-start.22 = (bf16[384,384]{1,0:T(8,128)(2,1)S(1)}, bf16[384,384]{1,0:T(8,128)(2,1)S(1)}, u32[]{:S(2)}, u32[]{:S(2)}) collective-permute-start(bf16[384,384]{1,0:T(8,128)(2,1)S(1)} %get-tuple-element.55), channel_id=1, source_target_pairs={{0,1},{1,0},{2,3},{3,2},{4,5},{5,4},{6,7},{7,6},{8,9},{9,8},{10,11... | collective-permute-start | bytes 884744 | tf_op jit(solution)/shard_map/ppermute | solution.py:141
  93.5 12.9 %collective-permute-start.23 = (bf16[384,384]{1,0:T(8,128)(2,1)S(1)}, bf16[384,384]{1,0:T(8,128)(2,1)S(1)}, u32[]{:S(2)}, u32[]{:S(2)}) collective-permute-start(bf16[384,384]{1,0:T(8,128)(2,1)S(1)} %get-tuple-element.56), channel_id=1, source_target_pairs={{0,1},{1,0},{2,3},{3,2},{4,5},{5,4},{6,7},{7,6},{8,9},{9,8},{10,11... | collective-permute-start | bytes 884744 | tf_op jit(solution)/shard_map/ppermute | solution.py:141
  95.3 15.6 %collective-permute-start.24 = (bf16[384,384]{1,0:T(8,128)(2,1)S(1)}, bf16[384,384]{1,0:T(8,128)(2,1)S(1)}, u32[]{:S(2)}, u32[]{:S(2)}) collective-permute-start(bf16[384,384]{1,0:T(8,128)(2,1)S(1)} %add_convert_fusion.1), channel_id=1, source_target_pairs={{0,2},{1,3},{2,0},{3,1},{4,6},{5,7},{6,4},{7,5},{8,10},{9,11},{10,... | collective-permute-start | bytes 884744 | tf_op jit(solution)/shard_map/ppermute | solution.py:141
  (8 other events, 55.9 us)

commit v10 on v8

--- a/solution.py
+++ b/solution.py
@@ -168,9 +168,11 @@
         wide[j, rows, :] = block[:, 128 * j : 128 * (j + 1)].astype(jnp.float32)
 
 
-def taps_sum(wide, weight_ref, groups):
+def taps_sum(wide, weight_ref, groups, copies=None):
     total = None
     for tap in range(KW):
+        if copies is not None:
+            copies[tap].wait()
         picked = []
         for start, count in groups:
             lanes = [
@@ -186,9 +188,17 @@
 FIRST = EDGE - KW // 2
 
 
-def conv_middle_kernel(dna_ref, weight_ref, h1_ref, sent_ref, wide):
-    store_wide(wide, 0, dna_ref[pl.ds(0, wide.shape[1]), :])
-    total = taps_sum(wide, weight_ref, [(FIRST, sent_ref.shape[0])])
+def conv_middle_kernel(dna_ref, weight_ref, h1_ref, sent_ref, wide, rows, weights, sems):
+    first = pltpu.make_async_copy(dna_ref.at[pl.ds(0, rows.shape[0]), :], rows, sems.at[KW])
+    copies = [
+        pltpu.make_async_copy(weight_ref.at[tap], weights.at[tap], sems.at[tap])
+        for tap in range(KW)
+    ]
+    for copy in (first, *copies):
+        copy.start()
+    first.wait()
+    store_wide(wide, 0, rows[...])
+    total = taps_sum(wide, weights, [(FIRST, sent_ref.shape[0])], copies)
     h1_ref[...] = total
     sent_ref[...] = total.astype(jnp.bfloat16)
 
@@ -209,14 +219,26 @@
     sent_ref[...] = total.astype(jnp.bfloat16)
 
 
-def first_conv(kernel, operands, weight, count, deep, name):
+def first_conv(kernel, operands, weight, count, deep, name, streamed=False):
     width, out = weight.shape[2], weight.shape[1]
     kept = jax.ShapeDtypeStruct((count, out), jnp.float32)
     sent = jax.ShapeDtypeStruct((count, out), jnp.bfloat16)
+    scratch = [pltpu.VMEM((width // 128, deep, 128), jnp.float32)]
+    place = pltpu.VMEM
+    if streamed:
+        place = pltpu.HBM
+        operands = [pltpu.with_memory_space_constraint(a, place) for a in operands]
+        weight = pltpu.with_memory_space_constraint(weight, place)
+        scratch += [
+            pltpu.VMEM((deep, width), jnp.bfloat16),
+            pltpu.VMEM(weight.shape, jnp.bfloat16),
+            pltpu.SemaphoreType.DMA((KW + 1,)),
+        ]
     return pl.pallas_call(
         kernel,
         out_shape=(kept, sent),
-        scratch_shapes=[pltpu.VMEM((width // 128, deep, 128), jnp.float32)],
+        in_specs=[pl.BlockSpec(memory_space=place)] * (len(operands) + 1),
+        scratch_shapes=scratch,
         compiler_params=pltpu.CompilerParams(vmem_limit_bytes=24 * MIB),
         cost_estimate=cost(2 * count * out * width * KW, (*operands, weight, kept, sent)),
         name=name,
@@ -559,11 +581,17 @@
     low = lax.ppermute(dna[-EDGE:], "seq", [(i, i + 1) for i in range(count - 1)])
     high = lax.ppermute(dna[:EDGE], "seq", [(i + 1, i) for i in range(count - 1)])
     h1_m, sent = first_conv(
-        conv_middle_kernel, (dna,), conv_in, inner + EDGE, 2 * (inner + 2 * EDGE), "conv_middle"
+        conv_middle_kernel,
+        (dna,),
+        conv_in,
+        inner + EDGE,
+        2 * (inner + 2 * EDGE),
+        "conv_middle",
+        True,
     )
     wide_m = forwarded(shared(sent))
     h1_e, sent = first_conv(
-        conv_edge_kernel, (dna, after(low, wide_m[2]), high), conv_in, outer, 2 * (outer + 2 * EDGE), "conv_edge"
+        conv_edge_kernel, (dna, after(low, *wide_m[1:3]), high), conv_in, outer, 2 * (outer + 2 * EDGE), "conv_edge"
     )
     wide_e = shared(sent)
     h2_m, sent = second_conv(
@@ -603,7 +631,7 @@
     inward = swapped(p3, 1)
     joined = (p2.astype(jnp.float32) + inward.astype(jnp.float32)).astype(jnp.bfloat16)
     total = own
-    for part in (swapped(after(p1, joined), 1), swapped(joined, 2)):
+    for part in (swapped(joined, 2), swapped(after(p1, joined), 1)):
         total = total + part.astype(jnp.float32)
     return total.astype(jnp.bfloat16)
 

time: 112 us -> 111 us (level)
  local copies, waits for them, and re-layouts: 3.13 us -> 0.04 us
  Pallas kernels: 22.4 us -> 24.3 us
    ppermute x15, waiting for transfers between devices: 42.2 us -> 46.2 us  [swapped(): return lax.ppermute(block, 'head', [(i, i ^ mask) for i in range(count)])]
    ppermute x8, waiting for transfers between devices: 12.1 us -> 8.5 us  [exchanged(): return lax.ppermute(block, 'seq', [(i, i ^ mask) for i in range(count)])]
    unnamed x14, local copies, waits for them, and re-layouts: 3.13 us -> 0.03 us
    ppermute x8, starting transfers between devices: 7.83 us -> 9.9 us  [exchanged(): return lax.ppermute(block, 'seq', [(i, i ^ mask) for i in range(count)])]
    ppermute x15, starting transfers between devices: 20 us -> 18 us  [swapped(): return lax.ppermute(block, 'head', [(i, i ^ mask) for i in range(count)])]
    pallas_call x2, Pallas kernels: 2.27 us -> 4.14 us  [first_conv(): pl.pallas_call(kernel, out_shape=(kept, sent), in_specs=[pl.BlockSpec(mem...]
where the time goes in v10:
time: 111 us
  waiting for transfers between devices  54.7 us (49%)
  starting transfers between devices  30.8 us (28%)
  Pallas kernels  24.3 us (22%)
    ppermute x15, waiting for transfers between devices, swapped(): return lax.ppermute(block, 'head', [(i, i ^ mask) for i in range(count)])  46.2 us
    ppermute x15, starting transfers between devices, swapped(): return lax.ppermute(block, 'head', [(i, i ^ mask) for i in range(count)])  18 us
    pallas_call x3, Pallas kernels, attend(): pl.pallas_call(kernel, out_shape=out, scratch_shapes=[pltpu.VMEM((2, exte...  12.1 us
    ppermute x8, starting transfers between devices, exchanged(): return lax.ppermute(block, 'seq', [(i, i ^ mask) for i in range(count)])  9.9 us
    ppermute x8, waiting for transfers between devices, exchanged(): return lax.ppermute(block, 'seq', [(i, i ^ mask) for i in range(count)])  8.5 us
    pallas_call x2, Pallas kernels, first_conv(): pl.pallas_call(kernel, out_shape=(kept, sent), in_specs=[pl.BlockSpec(mem...  4.14 us
    pallas_call x2, Pallas kernels, project(): pl.pallas_call(kernel, out_shape=(q, kv), compiler_params=pltpu.CompilerP...  3.7 us
    pallas_call x2, Pallas kernels, second_conv(): pl.pallas_call(kernel, out_shape=(kept, sent), scratch_shapes=[pltpu.VMEM...  3.42 us
  transfers between devices with their start and end apart: 25, of which 15 were waited for; matrix products, arithmetic and copies ran while one was open for 0% of the time, Pallas kernels for 16%

profile of v10, /device:TPU:0, one launch (start us, length us, event | category | flops | bytes accessed | tf_op | source)
XLA Modules:
  0.0 111.0 jit_solution(10539013207786425128)
XLA Ops:
  0.0 3.0 %conv_middle.1 = (f32[208,384]{1,0:T(8,128)S(1)}, bf16[208,384]{1,0:T(8,128)(2,1)S(1)}) custom-call(bf16[768,768]{1,0:T(8,128)(2,1)} %dna_ref.3, bf16[5,384,768]{2,1,0:T(8,128)(2,1)} %weight_ref.5), custom_call_target="tpu_custom_call" | custom-call | flops 613416960 | bytes 4608000 | tf_op jit(solution)/shard_map/conv_middle/pallas_call | solution.py:237
  3.0 4.1 %collective-permute-start.1 = (bf16[208,384]{1,0:T(8,128)(2,1)S(1)}, bf16[208,384]{1,0:T(8,128)(2,1)S(1)}, u32[]{:S(2)}, u32[]{:S(2)}) collective-permute-start(bf16[208,384]{1,0:T(8,128)(2,1)S(1)} %get-tuple-element.31.a0.m0), channel_id=1, source_target_pairs={{0,2},{1,3},{2,0},{3,1},{4,6},{5,7},{6,4},{7,5},{8,10},{9,11},{10,... | collective-permute-start | bytes 479240 | tf_op jit(solution)/shard_map/ppermute | solution.py:141
  11.6 3.2 %collective-permute-done.1.a2.m2 = bf16[208,384]{1,0:T(8,128)(2,1)S(1)} collective-permute-done((bf16[208,384]{1,0:T(8,128)(2,1)S(1)}, bf16[208,384]{1,0:T(8,128)(2,1)S(1)}, u32[]{:S(2)}, u32[]{:S(2)}) %collective-permute-start.1) | collective-permute-done | bytes 159776 | tf_op jit(solution)/shard_map/ppermute | solution.py:141
  16.5 3.4 %collective-permute-start.6 = (bf16[192,384]{1,0:T(8,128)(2,1)S(1)}, bf16[192,384]{1,0:T(8,128)(2,1)S(1)}, u32[]{:S(2)}, u32[]{:S(2)}) collective-permute-start(bf16[192,384]{1,0:T(8,128)(2,1)S(1)} %get-tuple-element.33.e0), channel_id=1, source_target_pairs={{0,2},{1,3},{2,0},{3,1},{4,6},{5,7},{6,4},{7,5},{8,10},{9,11},{10,... | collective-permute-start | bytes 442376 | tf_op jit(solution)/shard_map/ppermute | solution.py:141
  22.2 4.9 %collective-permute-done.6.e2 = bf16[192,384]{1,0:T(8,128)(2,1)S(1)} collective-permute-done((bf16[192,384]{1,0:T(8,128)(2,1)S(1)}, bf16[192,384]{1,0:T(8,128)(2,1)S(1)}, u32[]{:S(2)}, u32[]{:S(2)}) %collective-permute-start.6) | collective-permute-done | bytes 147488 | tf_op jit(solution)/shard_map/ppermute | solution.py:141
  27.6 2.3 %collective-permute-start.7 = (bf16[192,384]{1,0:T(8,128)(2,1)S(1)}, bf16[192,384]{1,0:T(8,128)(2,1)S(1)}, u32[]{:S(2)}, u32[]{:S(2)}) collective-permute-start(bf16[192,384]{1,0:T(8,128)(2,1)S(1)} %collective-permute-done.6.e2), channel_id=1, source_target_pairs={{0,1},{1,0},{2,3},{3,2},{4,5},{5,4},{6,7},{7,6},{8,9},{9,8},{10,11... | collective-permute-start | bytes 442376 | tf_op jit(solution)/shard_map/ppermute | solution.py:141
  30.0 5.8 %collective-permute-done.10.a2 = bf16[192,384]{1,0:T(8,128)(2,1)S(1)} collective-permute-done((bf16[192,384]{1,0:T(8,128)(2,1)S(1)}, bf16[192,384]{1,0:T(8,128)(2,1)S(1)}, u32[]{:S(2)}, u32[]{:S(2)}) %collective-permute-start.10) | collective-permute-done | bytes 147488 | tf_op jit(solution)/shard_map/ppermute | solution.py:141
  35.8 2.0 %collective-permute-done.7.e3 = bf16[192,384]{1,0:T(8,128)(2,1)S(1)} collective-permute-done((bf16[192,384]{1,0:T(8,128)(2,1)S(1)}, bf16[192,384]{1,0:T(8,128)(2,1)S(1)}, u32[]{:S(2)}, u32[]{:S(2)}) %collective-permute-start.7) | collective-permute-done | bytes 147488 | tf_op jit(solution)/shard_map/ppermute | solution.py:141
  41.0 5.3 %collective-permute-done.12.a3 = bf16[192,384]{1,0:T(8,128)(2,1)S(1)} collective-permute-done((bf16[192,384]{1,0:T(8,128)(2,1)S(1)}, bf16[192,384]{1,0:T(8,128)(2,1)S(1)}, u32[]{:S(2)}, u32[]{:S(2)}) %collective-permute-start.12) | collective-permute-done | bytes 147488 | tf_op jit(solution)/shard_map/ppermute | solution.py:141
  46.3 1.9 %project_middle.1 = (bf16[192,384]{1,0:T(8,128)(2,1)S(1)}, bf16[192,768]{1,0:T(8,128)(2,1)S(1)}) custom-call(bf16[192,384]{1,0:T(8,128)(2,1)S(1)} %get-tuple-element.45.a0, bf16[192,384]{1,0:T(8,128)(2,1)S(1)} %collective-permute-done.8.a1, bf16[192,384]{1,0:T(8,128)(2,1)S(1)} %collective-permute-done.10.a2, ...), custom_call_target="tpu_custom_call" | custom-call | flops 679477248 | bytes 4571136 | tf_op jit(solution)/shard_map/project_middle/pallas_call | solution.py:401
  48.2 2.0 %collective-permute-start.18 = (bf16[192,768]{1,0:T(8,128)(2,1)S(1)}, bf16[192,768]{1,0:T(8,128)(2,1)S(1)}, u32[]{:S(2)}, u32[]{:S(2)}) collective-permute-start(bf16[192,768]{1,0:T(8,128)(2,1)S(1)} %get-tuple-element.46.refs_2_), channel_id=1, source_target_pairs={{0,8},{4,12},{8,0},{12,4},{16,24},{20,28},{24,16},{28,20},{1,9},{5... | collective-permute-start | bytes 884744 | tf_op jit(solution)/shard_map/ppermute | solution.py:573
  53.4 1.8 %project_edge.1 = (bf16[384,384]{1,0:T(8,128)(2,1)S(1)}, bf16[192,768]{1,0:T(8,128)(2,1)S(1)}) custom-call(bf16[192,384]{1,0:T(8,128)(2,1)S(1)} %get-tuple-element.44.a0, bf16[192,384]{1,0:T(8,128)(2,1)S(1)} %collective-permute-done.9.a1, bf16[192,384]{1,0:T(8,128)(2,1)S(1)} %collective-permute-done.11.a2, bf16[192,384]{1,0:T(8,128)(2,1)S(1)} %collective-permute-done.13.a3, ...), custom_call_target="tpu_custom_call" | custom-call | flops 679477248 | bytes 4866048 | tf_op jit(solution)/shard_map/project_edge/pallas_call | solution.py:401
  55.3 2.1 %collective-permute-start.14 = (bf16[192,768]{1,0:T(8,128)(2,1)S(1)}, bf16[192,768]{1,0:T(8,128)(2,1)S(1)}, u32[]{:S(2)}, u32[]{:S(2)}) collective-permute-start(bf16[192,768]{1,0:T(8,128)(2,1)S(1)} %get-tuple-element.50.refs_3_), channel_id=1, source_target_pairs={{0,8},{4,12},{8,0},{12,4},{16,24},{20,28},{24,16},{28,20},{1,9},{5... | collective-permute-start | bytes 884744 | tf_op jit(solution)/shard_map/ppermute | solution.py:573
  58.3 2.1 %collective-permute-start.15 = (bf16[192,768]{1,0:T(8,128)(2,1)S(1)}, bf16[192,768]{1,0:T(8,128)(2,1)S(1)}, u32[]{:S(2)}, u32[]{:S(2)}) collective-permute-start(bf16[192,768]{1,0:T(8,128)(2,1)S(1)} %get-tuple-element.50.refs_3_), channel_id=1, source_target_pairs={{0,16},{4,20},{8,24},{12,28},{16,0},{20,4},{24,8},{28,12},{1,17},{... | collective-permute-start | bytes 884744 | tf_op jit(solution)/shard_map/ppermute | solution.py:573
  61.0 2.0 %collective-permute-start.16 = (bf16[192,768]{1,0:T(8,128)(2,1)S(1)}, bf16[192,768]{1,0:T(8,128)(2,1)S(1)}, u32[]{:S(2)}, u32[]{:S(2)}) collective-permute-start(bf16[192,768]{1,0:T(8,128)(2,1)S(1)} %get-tuple-element.50.refs_3_), channel_id=1, source_target_pairs={{0,24},{4,28},{8,16},{12,20},{16,8},{20,12},{24,0},{28,4},{1,25},{... | collective-permute-start | bytes 884744 | tf_op jit(solution)/shard_map/ppermute | solution.py:573
  63.0 3.1 %collective-permute-done.20.refs_6_ = bf16[192,768]{1,0:T(8,128)(2,1)S(1)} collective-permute-done((bf16[192,768]{1,0:T(8,128)(2,1)S(1)}, bf16[192,768]{1,0:T(8,128)(2,1)S(1)}, u32[]{:S(2)}, u32[]{:S(2)}) %collective-permute-start.20) | collective-permute-done | bytes 294944 | tf_op jit(solution)/shard_map/ppermute | solution.py:573
  66.1 6.2 %attend_m.1.refs_4_ = f32[400,768]{1,0:T(8,128)S(1)} custom-call(bf16[384,384]{1,0:T(8,128)(2,1)S(1)} %get-tuple-element.49.refs_0_, bf16[384,384]{1,0:T(8,128)(2,1)S(1)} %collective-permute-done.17.refs_1_.refs_0_, bf16[192,768]{1,0:T(8,128)(2,1)S(1)} %get-tuple-element.46.refs_2_, bf16[192,768]{1,0:T(8,128)(2,1)S(1)} %get-tuple-element.50.refs_3_, ...), custom_call_target="tpu_custom_call" | custom-call | flops 1132462080 | bytes 3293184 | tf_op jit(solution)/shard_map/attend_m/pallas_call | solution.py:516
  72.3 3.8 %collective-permute-done.15.refs_2_ = bf16[192,768]{1,0:T(8,128)(2,1)S(1)} collective-permute-done((bf16[192,768]{1,0:T(8,128)(2,1)S(1)}, bf16[192,768]{1,0:T(8,128)(2,1)S(1)}, u32[]{:S(2)}, u32[]{:S(2)}) %collective-permute-start.15) | collective-permute-done | bytes 294944 | tf_op jit(solution)/shard_map/ppermute | solution.py:573
  76.1 3.0 %attend_other.1 = f32[400,384]{1,0:T(8,128)S(1)} custom-call(bf16[384,384]{1,0:T(8,128)(2,1)S(1)} %collective-permute-done.17.refs_1_.refs_0_, bf16[192,768]{1,0:T(8,128)(2,1)S(1)} %collective-permute-done.14.refs_1_, bf16[192,768]{1,0:T(8,128)(2,1)S(1)} %collective-permute-done.15.refs_2_, bf16[192,768]{1,0:T(8,128)(2,1)S(1)} %collective-permute-done.16.refs_3_, ...), custom_call_target="tpu_custom_call" | custom-call | flops 339738624 | bytes 3022848 | tf_op jit(solution)/shard_map/attend_other/pallas_call | solution.py:516
  79.2 3.0 %attend_own.1.own_state = f32[400,384]{1,0:T(8,128)S(1)} custom-call(bf16[384,384]{1,0:T(8,128)(2,1)S(1)} %get-tuple-element.49.refs_0_, bf16[192,768]{1,0:T(8,128)(2,1)S(1)} %collective-permute-done.14.refs_1_, bf16[192,768]{1,0:T(8,128)(2,1)S(1)} %collective-permute-done.15.refs_2_, bf16[192,768]{1,0:T(8,128)(2,1)S(1)} %collective-permute-done.16.refs_3_, ...), custom_call_target="tpu_custom_call" | custom-call | flops 339738624 | bytes 3022848 | tf_op jit(solution)/shard_map/attend_own/pallas_call | solution.py:516
  83.2 1.8 %collective-permute-start.22 = (bf16[384,384]{1,0:T(8,128)(2,1)S(1)}, bf16[384,384]{1,0:T(8,128)(2,1)S(1)}, u32[]{:S(2)}, u32[]{:S(2)}) collective-permute-start(bf16[384,384]{1,0:T(8,128)(2,1)S(1)} %get-tuple-element.54), channel_id=1, source_target_pairs={{0,1},{1,0},{2,3},{3,2},{4,5},{5,4},{6,7},{7,6},{8,9},{9,8},{10,11... | collective-permute-start | bytes 884744 | tf_op jit(solution)/shard_map/ppermute | solution.py:141
  85.0 7.7 %collective-permute-done.22 = bf16[384,384]{1,0:T(8,128)(2,1)S(1)} collective-permute-done((bf16[384,384]{1,0:T(8,128)(2,1)S(1)}, bf16[384,384]{1,0:T(8,128)(2,1)S(1)}, u32[]{:S(2)}, u32[]{:S(2)}) %collective-permute-start.22) | collective-permute-done | bytes 294944 | tf_op jit(solution)/shard_map/ppermute | solution.py:141
  95.2 11.8 %collective-permute-done.24 = bf16[384,384]{1,0:T(8,128)(2,1)S(1)} collective-permute-done((bf16[384,384]{1,0:T(8,128)(2,1)S(1)}, bf16[384,384]{1,0:T(8,128)(2,1)S(1)}, u32[]{:S(2)}, u32[]{:S(2)}) %collective-permute-start.24) | collective-permute-done | bytes 294944 | tf_op jit(solution)/shard_map/ppermute | solution.py:141
  107.0 3.1 %collective-permute-done.23 = bf16[384,384]{1,0:T(8,128)(2,1)S(1)} collective-permute-done((bf16[384,384]{1,0:T(8,128)(2,1)S(1)}, bf16[384,384]{1,0:T(8,128)(2,1)S(1)}, u32[]{:S(2)}, u32[]{:S(2)}) %collective-permute-start.23) | collective-permute-done | bytes 294944 | tf_op jit(solution)/shard_map/ppermute | solution.py:141
  (53 shorter events, 21.3 us)
Async XLA Ops:
  3.0 11.7 %collective-permute-start.1 = (bf16[208,384]{1,0:T(8,128)(2,1)S(1)}, bf16[208,384]{1,0:T(8,128)(2,1)S(1)}, u32[]{:S(2)}, u32[]{:S(2)}) collective-permute-start(bf16[208,384]{1,0:T(8,128)(2,1)S(1)} %get-tuple-element.31.a0.m0), channel_id=1, source_target_pairs={{0,2},{1,3},{2,0},{3,1},{4,6},{5,7},{6,4},{7,5},{8,10},{9,11},{10,... | collective-permute-start | bytes 479240 | tf_op jit(solution)/shard_map/ppermute | solution.py:141
  7.1 8.3 %collective-permute-start = (bf16[208,384]{1,0:T(8,128)(2,1)S(1)}, bf16[208,384]{1,0:T(8,128)(2,1)S(1)}, u32[]{:S(2)}, u32[]{:S(2)}) collective-permute-start(bf16[208,384]{1,0:T(8,128)(2,1)S(1)} %get-tuple-element.31.a0.m0), channel_id=1, source_target_pairs={{0,1},{1,0},{2,3},{3,2},{4,5},{5,4},{6,7},{7,6},{8,9},{9,8},{10,11... | collective-permute-start | bytes 479240 | tf_op jit(solution)/shard_map/ppermute | solution.py:141
  8.7 6.7 %collective-permute-start.3 = (bf16[16,768]{1,0:T(8,128)(2,1)S(1)}, bf16[16,768]{1,0:T(8,128)(2,1)S(1)}, u32[]{:S(2)}, u32[]{:S(2)}) collective-permute-start(bf16[16,768]{1,0:T(8,128)(2,1)S(1)} %get-tuple-element.58), channel_id=1, source_target_pairs={{0,4},{4,8},{8,12},{12,16},{16,20},{20,24},{24,28},{1,5},{5,9},{9,... | collective-permute-start | bytes 73736 | tf_op jit(solution)/shard_map/ppermute | solution.py:581
  10.0 5.4 %collective-permute-start.4 = (bf16[16,768]{1,0:T(8,128)(2,1)S(1)}, bf16[16,768]{1,0:T(8,128)(2,1)S(1)}, u32[]{:S(2)}, u32[]{:S(2)}) collective-permute-start(bf16[16,768]{1,0:T(8,128)(2,1)S(1)} %get-tuple-element.57), channel_id=1, source_target_pairs={{4,0},{8,4},{12,8},{16,12},{20,16},{24,20},{28,24},{5,1},{9,5},{13... | collective-permute-start | bytes 73736 | tf_op jit(solution)/shard_map/ppermute | solution.py:582
  14.8 5.7 %collective-permute-start.2 = (bf16[208,384]{1,0:T(8,128)(2,1)S(1)}, bf16[208,384]{1,0:T(8,128)(2,1)S(1)}, u32[]{:S(2)}, u32[]{:S(2)}) collective-permute-start(bf16[208,384]{1,0:T(8,128)(2,1)S(1)} %collective-permute-done.1.a2.m2), channel_id=1, source_target_pairs={{0,1},{1,0},{2,3},{3,2},{4,5},{5,4},{6,7},{7,6},{8,9},{9,8},{10,11... | collective-permute-start | bytes 479240 | tf_op jit(solution)/shard_map/ppermute | solution.py:141
  16.5 10.6 %collective-permute-start.6 = (bf16[192,384]{1,0:T(8,128)(2,1)S(1)}, bf16[192,384]{1,0:T(8,128)(2,1)S(1)}, u32[]{:S(2)}, u32[]{:S(2)}) collective-permute-start(bf16[192,384]{1,0:T(8,128)(2,1)S(1)} %get-tuple-element.33.e0), channel_id=1, source_target_pairs={{0,2},{1,3},{2,0},{3,1},{4,6},{5,7},{6,4},{7,5},{8,10},{9,11},{10,... | collective-permute-start | bytes 442376 | tf_op jit(solution)/shard_map/ppermute | solution.py:141
  20.0 10.0 %collective-permute-start.5 = (bf16[192,384]{1,0:T(8,128)(2,1)S(1)}, bf16[192,384]{1,0:T(8,128)(2,1)S(1)}, u32[]{:S(2)}, u32[]{:S(2)}) collective-permute-start(bf16[192,384]{1,0:T(8,128)(2,1)S(1)} %get-tuple-element.33.e0), channel_id=1, source_target_pairs={{0,1},{1,0},{2,3},{3,2},{4,5},{5,4},{6,7},{7,6},{8,9},{9,8},{10,11... | collective-permute-start | bytes 442376 | tf_op jit(solution)/shard_map/ppermute | solution.py:141
  27.1 8.7 %collective-permute-start.10 = (bf16[192,384]{1,0:T(8,128)(2,1)S(1)}, bf16[192,384]{1,0:T(8,128)(2,1)S(1)}, u32[]{:S(2)}, u32[]{:S(2)}) collective-permute-start(bf16[192,384]{1,0:T(8,128)(2,1)S(1)} %get-tuple-element.45.a0), channel_id=1, source_target_pairs={{0,2},{1,3},{2,0},{3,1},{4,6},{5,7},{6,4},{7,5},{8,10},{9,11},{10,... | collective-permute-start | bytes 442376 | tf_op jit(solution)/shard_map/ppermute | solution.py:141
  27.6 10.2 %collective-permute-start.7 = (bf16[192,384]{1,0:T(8,128)(2,1)S(1)}, bf16[192,384]{1,0:T(8,128)(2,1)S(1)}, u32[]{:S(2)}, u32[]{:S(2)}) collective-permute-start(bf16[192,384]{1,0:T(8,128)(2,1)S(1)} %collective-permute-done.6.e2), channel_id=1, source_target_pairs={{0,1},{1,0},{2,3},{3,2},{4,5},{5,4},{6,7},{7,6},{8,9},{9,8},{10,11... | collective-permute-start | bytes 442376 | tf_op jit(solution)/shard_map/ppermute | solution.py:141
  30.0 11.0 %collective-permute-start.8 = (bf16[192,384]{1,0:T(8,128)(2,1)S(1)}, bf16[192,384]{1,0:T(8,128)(2,1)S(1)}, u32[]{:S(2)}, u32[]{:S(2)}) collective-permute-start(bf16[192,384]{1,0:T(8,128)(2,1)S(1)} %get-tuple-element.45.a0), channel_id=1, source_target_pairs={{0,1},{1,0},{2,3},{3,2},{4,5},{5,4},{6,7},{7,6},{8,9},{9,8},{10,11... | collective-permute-start | bytes 442376 | tf_op jit(solution)/shard_map/ppermute | solution.py:141
  35.8 10.5 %collective-permute-start.12 = (bf16[192,384]{1,0:T(8,128)(2,1)S(1)}, bf16[192,384]{1,0:T(8,128)(2,1)S(1)}, u32[]{:S(2)}, u32[]{:S(2)}) collective-permute-start(bf16[192,384]{1,0:T(8,128)(2,1)S(1)} %collective-permute-done.10.a2), channel_id=1, source_target_pairs={{0,1},{1,0},{2,3},{3,2},{4,5},{5,4},{6,7},{7,6},{8,9},{9,8},{10,11... | collective-permute-start | bytes 442376 | tf_op jit(solution)/shard_map/ppermute | solution.py:141
  39.6 8.6 %collective-permute-start.11 = (bf16[192,384]{1,0:T(8,128)(2,1)S(1)}, bf16[192,384]{1,0:T(8,128)(2,1)S(1)}, u32[]{:S(2)}, u32[]{:S(2)}) collective-permute-start(bf16[192,384]{1,0:T(8,128)(2,1)S(1)} %get-tuple-element.44.a0), channel_id=1, source_target_pairs={{0,2},{1,3},{2,0},{3,1},{4,6},{5,7},{6,4},{7,5},{8,10},{9,11},{10,... | collective-permute-start | bytes 442376 | tf_op jit(solution)/shard_map/ppermute | solution.py:141
  41.0 10.9 %collective-permute-start.9 = (bf16[192,384]{1,0:T(8,128)(2,1)S(1)}, bf16[192,384]{1,0:T(8,128)(2,1)S(1)}, u32[]{:S(2)}, u32[]{:S(2)}) collective-permute-start(bf16[192,384]{1,0:T(8,128)(2,1)S(1)} %get-tuple-element.44.a0), channel_id=1, source_target_pairs={{0,1},{1,0},{2,3},{3,2},{4,5},{5,4},{6,7},{7,6},{8,9},{9,8},{10,11... | collective-permute-start | bytes 442376 | tf_op jit(solution)/shard_map/ppermute | solution.py:141
  48.2 5.2 %collective-permute-start.13 = (bf16[192,384]{1,0:T(8,128)(2,1)S(1)}, bf16[192,384]{1,0:T(8,128)(2,1)S(1)}, u32[]{:S(2)}, u32[]{:S(2)}) collective-permute-start(bf16[192,384]{1,0:T(8,128)(2,1)S(1)} %collective-permute-done.11.a2), channel_id=1, source_target_pairs={{0,1},{1,0},{2,3},{3,2},{4,5},{5,4},{6,7},{7,6},{8,9},{9,8},{10,11... | collective-permute-start | bytes 442376 | tf_op jit(solution)/shard_map/ppermute | solution.py:141
  48.2 10.0 %collective-permute-start.18 = (bf16[192,768]{1,0:T(8,128)(2,1)S(1)}, bf16[192,768]{1,0:T(8,128)(2,1)S(1)}, u32[]{:S(2)}, u32[]{:S(2)}) collective-permute-start(bf16[192,768]{1,0:T(8,128)(2,1)S(1)} %get-tuple-element.46.refs_2_), channel_id=1, source_target_pairs={{0,8},{4,12},{8,0},{12,4},{16,24},{20,28},{24,16},{28,20},{1,9},{5... | collective-permute-start | bytes 884744 | tf_op jit(solution)/shard_map/ppermute | solution.py:573
  50.2 10.7 %collective-permute-start.19 = (bf16[192,768]{1,0:T(8,128)(2,1)S(1)}, bf16[192,768]{1,0:T(8,128)(2,1)S(1)}, u32[]{:S(2)}, u32[]{:S(2)}) collective-permute-start(bf16[192,768]{1,0:T(8,128)(2,1)S(1)} %get-tuple-element.46.refs_2_), channel_id=1, source_target_pairs={{0,16},{4,20},{8,24},{12,28},{16,0},{20,4},{24,8},{28,12},{1,17},{... | collective-permute-start | bytes 884744 | tf_op jit(solution)/shard_map/ppermute | solution.py:573
  50.5 15.6 %collective-permute-start.20 = (bf16[192,768]{1,0:T(8,128)(2,1)S(1)}, bf16[192,768]{1,0:T(8,128)(2,1)S(1)}, u32[]{:S(2)}, u32[]{:S(2)}) collective-permute-start(bf16[192,768]{1,0:T(8,128)(2,1)S(1)} %get-tuple-element.46.refs_2_), channel_id=1, source_target_pairs={{0,24},{4,28},{8,16},{12,20},{16,8},{20,12},{24,0},{28,4},{1,25},{... | collective-permute-start | bytes 884744 | tf_op jit(solution)/shard_map/ppermute | solution.py:573
  55.2 10.9 %collective-permute-start.17 = (bf16[384,384]{1,0:T(8,128)(2,1)S(1)}, bf16[384,384]{1,0:T(8,128)(2,1)S(1)}, u32[]{:S(2)}, u32[]{:S(2)}) collective-permute-start(bf16[384,384]{1,0:T(8,128)(2,1)S(1)} %get-tuple-element.49.refs_0_), channel_id=1, source_target_pairs={{0,4},{4,0},{8,12},{12,8},{16,20},{20,16},{24,28},{28,24},{1,5},{5... | collective-permute-start | bytes 884744 | tf_op jit(solution)/shard_map/ppermute | solution.py:573
  55.3 17.0 %collective-permute-start.14 = (bf16[192,768]{1,0:T(8,128)(2,1)S(1)}, bf16[192,768]{1,0:T(8,128)(2,1)S(1)}, u32[]{:S(2)}, u32[]{:S(2)}) collective-permute-start(bf16[192,768]{1,0:T(8,128)(2,1)S(1)} %get-tuple-element.50.refs_3_), channel_id=1, source_target_pairs={{0,8},{4,12},{8,0},{12,4},{16,24},{20,28},{24,16},{28,20},{1,9},{5... | collective-permute-start | bytes 884744 | tf_op jit(solution)/shard_map/ppermute | solution.py:573
  58.3 17.9 %collective-permute-start.15 = (bf16[192,768]{1,0:T(8,128)(2,1)S(1)}, bf16[192,768]{1,0:T(8,128)(2,1)S(1)}, u32[]{:S(2)}, u32[]{:S(2)}) collective-permute-start(bf16[192,768]{1,0:T(8,128)(2,1)S(1)} %get-tuple-element.50.refs_3_), channel_id=1, source_target_pairs={{0,16},{4,20},{8,24},{12,28},{16,0},{20,4},{24,8},{28,12},{1,17},{... | collective-permute-start | bytes 884744 | tf_op jit(solution)/shard_map/ppermute | solution.py:573
  61.0 15.2 %collective-permute-start.16 = (bf16[192,768]{1,0:T(8,128)(2,1)S(1)}, bf16[192,768]{1,0:T(8,128)(2,1)S(1)}, u32[]{:S(2)}, u32[]{:S(2)}) collective-permute-start(bf16[192,768]{1,0:T(8,128)(2,1)S(1)} %get-tuple-element.50.refs_3_), channel_id=1, source_target_pairs={{0,24},{4,28},{8,16},{12,20},{16,8},{20,12},{24,0},{28,4},{1,25},{... | collective-permute-start | bytes 884744 | tf_op jit(solution)/shard_map/ppermute | solution.py:573
  83.2 9.5 %collective-permute-start.22 = (bf16[384,384]{1,0:T(8,128)(2,1)S(1)}, bf16[384,384]{1,0:T(8,128)(2,1)S(1)}, u32[]{:S(2)}, u32[]{:S(2)}) collective-permute-start(bf16[384,384]{1,0:T(8,128)(2,1)S(1)} %get-tuple-element.54), channel_id=1, source_target_pairs={{0,1},{1,0},{2,3},{3,2},{4,5},{5,4},{6,7},{7,6},{8,9},{9,8},{10,11... | collective-permute-start | bytes 884744 | tf_op jit(solution)/shard_map/ppermute | solution.py:141
  92.7 14.3 %collective-permute-start.24 = (bf16[384,384]{1,0:T(8,128)(2,1)S(1)}, bf16[384,384]{1,0:T(8,128)(2,1)S(1)}, u32[]{:S(2)}, u32[]{:S(2)}) collective-permute-start(bf16[384,384]{1,0:T(8,128)(2,1)S(1)} %get-tuple-element.56), channel_id=1, source_target_pairs={{0,1},{1,0},{2,3},{3,2},{4,5},{5,4},{6,7},{7,6},{8,9},{9,8},{10,11... | collective-permute-start | bytes 884744 | tf_op jit(solution)/shard_map/ppermute | solution.py:141
  94.5 15.6 %collective-permute-start.23 = (bf16[384,384]{1,0:T(8,128)(2,1)S(1)}, bf16[384,384]{1,0:T(8,128)(2,1)S(1)}, u32[]{:S(2)}, u32[]{:S(2)}) collective-permute-start(bf16[384,384]{1,0:T(8,128)(2,1)S(1)} %add_convert_fusion.1), channel_id=1, source_target_pairs={{0,2},{1,3},{2,0},{3,1},{4,6},{5,7},{6,4},{7,5},{8,10},{9,11},{10,... | collective-permute-start | bytes 884744 | tf_op jit(solution)/shard_map/ppermute | solution.py:141
  (8 other events, 66.1 us)

commit v11 on v10

--- a/solution.py
+++ b/solution.py
@@ -415,14 +415,14 @@
     return turned, block.shape[0] - turned
 
 
-def turned_values(blocks, width, pair):
-    lanes = pl.ds(width + pair * LANES, LANES)
+def turned_values(blocks, pair):
+    lanes = pl.ds(pair * LANES, LANES)
     values = []
-    for block in blocks:
+    for _, block in blocks:
         for row in range(0, split_rows(block)[0], LANES):
             values.append(block[pl.ds(row, LANES), lanes])
     rest = []
-    for block in blocks:
+    for _, block in blocks:
         start, count = split_rows(block)
         if count:
             rest.append(block[pl.ds(start, count), lanes].astype(jnp.float32))
@@ -433,8 +433,8 @@
 
 def ordered_keys(blocks, pair):
     lanes = pl.ds(pair * LANES, LANES)
-    keys = [block[pl.ds(0, split_rows(block)[0]), lanes] for block in blocks]
-    for block in blocks:
+    keys = [block[pl.ds(0, split_rows(block)[0]), lanes] for block, _ in blocks]
+    for block, _ in blocks:
         start, count = split_rows(block)
         if count:
             keys.append(block[pl.ds(start, count), lanes])
@@ -486,7 +486,7 @@
     for head in range(width // HEAD_DIM):
         if head % 2 == 0:
             keys = ordered_keys(blocks, head // 2)
-            values = turned_values(blocks, width, head // 2)
+            values = turned_values(blocks, head // 2)
         part = partial_attention(
             query, keys, values, scores.at[head % 2], weights.at[head % 2], head, lane
         )
@@ -502,12 +502,20 @@
 def attend(queries, blocks, state, first_column, name):
     rows, width = queries[0].shape
     columns = rows * len(queries)
-    extent = sum(block.shape[0] for block in blocks)
+    extent = sum(block[0].shape[0] for block in blocks)
     out = jax.ShapeDtypeStruct((width + 16, columns), jnp.float32)
-    operands = (*queries, *blocks) + (() if state is None else (state,))
+    flat = [array for block in blocks for array in block]
+    operands = (*queries, *flat) + (() if state is None else (state,))
 
     def kernel(*refs):
-        q_refs, block_refs = refs[: len(queries)], refs[len(queries) :][: len(blocks)]
+        q_refs, rest = refs[: len(queries)], list(refs[len(queries) :])
+        block_refs = []
+        for block in blocks:
+            first = rest.pop(0)
+            if len(block) == 2:
+                block_refs.append((first, rest.pop(0)))
+            else:
+                block_refs.append((first.at[:, pl.ds(0, width)], first.at[:, pl.ds(width, width)]))
         state_ref = None if state is None else refs[len(operands) - 1]
         attend_kernel(
             first_column, q_refs, block_refs, state_ref, *refs[len(operands) :]
@@ -618,12 +626,14 @@
     normed_m[0] = after(normed_m[0], sent)
     weights = (w_query, w_key, w_value)
     q_m, kv_m = project(project_middle_kernel, normed_m, weights, inner, "project_middle")
-    x_m, y_m, d_m = (exchanged(kv_m, mask) for mask in (2, 4, 6))
+    x_m, y_m = exchanged(kv_m, 2), exchanged(kv_m, 4)
+    width = q_m.shape[1]
+    d_m = (exchanged(x_m[:, :width], 4), exchanged(y_m[:, width:], 2))
     normed_e = forwarded(normed_e, kv_m)
     q, kv_e = project(project_edge_kernel, (*normed_e, q_m), weights, rows, "project_edge")
     q_other, x_e, y_e, d_e = exchanged(q, 1), *(exchanged(kv_e, mask) for mask in (2, 4, 6))
-    state = attend((q, q_other), (kv_m, kv_e, x_m, y_m, d_m), None, 0, "attend_m")
-    late = (x_e, y_e, d_e)
+    state = attend((q, q_other), ((kv_m,), (kv_e,), (x_m,), (y_m,), d_m), None, 0, "attend_m")
+    late = ((x_e,), (y_e,), (d_e,))
     state_other = attend((q_other,), late, state, rows, "attend_other")
     given = exchanged(state_other, 1)
     state_own = attend((q,), late, state, 0, "attend_own")

time: 111 us -> 117 us (1.054)
  waiting for transfers between devices: 54.7 us -> 62.2 us
  starting transfers between devices: 30.8 us -> 29.2 us
    ppermute x8 -> x9, waiting for transfers between devices: 8.5 us -> 19.4 us  [exchanged(): return lax.ppermute(block, 'seq', [(i, i ^ mask) for i in range(count)])]
    ppermute x15, waiting for transfers between devices: 46.2 us -> 42.8 us  [swapped(): return lax.ppermute(block, 'head', [(i, i ^ mask) for i in range(count)])]
    ppermute x8 -> x9, starting transfers between devices: 9.9 us -> 8 us  [exchanged(): return lax.ppermute(block, 'seq', [(i, i ^ mask) for i in range(count)])]
  transfers between devices with their start and end apart: 25 -> 26, of which waited for: 15 -> 12; matrix products, arithmetic and copies ran while one was open for 0% -> 0% of each run, Pallas kernels for 16% -> 15%
where the time goes in v11:
time: 117 us
  waiting for transfers between devices  62.2 us (53%)
  starting transfers between devices  29.2 us (25%)
  Pallas kernels  24.4 us (21%)
    ppermute x15, waiting for transfers between devices, swapped(): return lax.ppermute(block, 'head', [(i, i ^ mask) for i in range(count)])  42.8 us
    ppermute x9, waiting for transfers between devices, exchanged(): return lax.ppermute(block, 'seq', [(i, i ^ mask) for i in range(count)])  19.4 us
    ppermute x15, starting transfers between devices, swapped(): return lax.ppermute(block, 'head', [(i, i ^ mask) for i in range(count)])  18.4 us
    pallas_call x3, Pallas kernels, attend(): pl.pallas_call(kernel, out_shape=out, scratch_shapes=[pltpu.VMEM((2, exte...  12.1 us
    ppermute x9, starting transfers between devices, exchanged(): return lax.ppermute(block, 'seq', [(i, i ^ mask) for i in range(count)])  8 us
    pallas_call x2, Pallas kernels, first_conv(): pl.pallas_call(kernel, out_shape=(kept, sent), in_specs=[pl.BlockSpec(mem...  4.14 us
    pallas_call x2, Pallas kernels, project(): pl.pallas_call(kernel, out_shape=(q, kv), compiler_params=pltpu.CompilerP...  3.7 us
    pallas_call x2, Pallas kernels, second_conv(): pl.pallas_call(kernel, out_shape=(kept, sent), scratch_shapes=[pltpu.VMEM...  3.42 us
  transfers between devices with their start and end apart: 26, of which 12 were waited for; matrix products, arithmetic and copies ran while one was open for 0% of the time, Pallas kernels for 15%

profile of v11, /device:TPU:0, one launch (start us, length us, event | category | flops | bytes accessed | tf_op | source)
XLA Modules:
  0.0 117.0 jit_solution(12997784150861976717)
XLA Ops:
  0.0 3.0 %conv_middle.1 = (f32[208,384]{1,0:T(8,128)S(1)}, bf16[208,384]{1,0:T(8,128)(2,1)S(1)}) custom-call(bf16[768,768]{1,0:T(8,128)(2,1)} %dna_ref.3, bf16[5,384,768]{2,1,0:T(8,128)(2,1)} %weight_ref.5), custom_call_target="tpu_custom_call" | custom-call | flops 613416960 | bytes 4608000 | tf_op jit(solution)/shard_map/conv_middle/pallas_call | solution.py:237
  3.0 4.1 %collective-permute-start.1 = (bf16[208,384]{1,0:T(8,128)(2,1)S(1)}, bf16[208,384]{1,0:T(8,128)(2,1)S(1)}, u32[]{:S(2)}, u32[]{:S(2)}) collective-permute-start(bf16[208,384]{1,0:T(8,128)(2,1)S(1)} %get-tuple-element.31.a0.m0), channel_id=1, source_target_pairs={{0,2},{1,3},{2,0},{3,1},{4,6},{5,7},{6,4},{7,5},{8,10},{9,11},{10,... | collective-permute-start | bytes 479240 | tf_op jit(solution)/shard_map/ppermute | solution.py:141
  11.6 3.2 %collective-permute-done.1.a2.m2 = bf16[208,384]{1,0:T(8,128)(2,1)S(1)} collective-permute-done((bf16[208,384]{1,0:T(8,128)(2,1)S(1)}, bf16[208,384]{1,0:T(8,128)(2,1)S(1)}, u32[]{:S(2)}, u32[]{:S(2)}) %collective-permute-start.1) | collective-permute-done | bytes 159776 | tf_op jit(solution)/shard_map/ppermute | solution.py:141
  16.5 3.4 %collective-permute-start.6 = (bf16[192,384]{1,0:T(8,128)(2,1)S(1)}, bf16[192,384]{1,0:T(8,128)(2,1)S(1)}, u32[]{:S(2)}, u32[]{:S(2)}) collective-permute-start(bf16[192,384]{1,0:T(8,128)(2,1)S(1)} %get-tuple-element.33.e0), channel_id=1, source_target_pairs={{0,2},{1,3},{2,0},{3,1},{4,6},{5,7},{6,4},{7,5},{8,10},{9,11},{10,... | collective-permute-start | bytes 442376 | tf_op jit(solution)/shard_map/ppermute | solution.py:141
  22.2 4.9 %collective-permute-done.6.e2 = bf16[192,384]{1,0:T(8,128)(2,1)S(1)} collective-permute-done((bf16[192,384]{1,0:T(8,128)(2,1)S(1)}, bf16[192,384]{1,0:T(8,128)(2,1)S(1)}, u32[]{:S(2)}, u32[]{:S(2)}) %collective-permute-start.6) | collective-permute-done | bytes 147488 | tf_op jit(solution)/shard_map/ppermute | solution.py:141
  27.6 2.3 %collective-permute-start.7 = (bf16[192,384]{1,0:T(8,128)(2,1)S(1)}, bf16[192,384]{1,0:T(8,128)(2,1)S(1)}, u32[]{:S(2)}, u32[]{:S(2)}) collective-permute-start(bf16[192,384]{1,0:T(8,128)(2,1)S(1)} %collective-permute-done.6.e2), channel_id=1, source_target_pairs={{0,1},{1,0},{2,3},{3,2},{4,5},{5,4},{6,7},{7,6},{8,9},{9,8},{10,11... | collective-permute-start | bytes 442376 | tf_op jit(solution)/shard_map/ppermute | solution.py:141
  30.0 5.8 %collective-permute-done.10.a2 = bf16[192,384]{1,0:T(8,128)(2,1)S(1)} collective-permute-done((bf16[192,384]{1,0:T(8,128)(2,1)S(1)}, bf16[192,384]{1,0:T(8,128)(2,1)S(1)}, u32[]{:S(2)}, u32[]{:S(2)}) %collective-permute-start.10) | collective-permute-done | bytes 147488 | tf_op jit(solution)/shard_map/ppermute | solution.py:141
  35.8 2.0 %collective-permute-done.7.e3 = bf16[192,384]{1,0:T(8,128)(2,1)S(1)} collective-permute-done((bf16[192,384]{1,0:T(8,128)(2,1)S(1)}, bf16[192,384]{1,0:T(8,128)(2,1)S(1)}, u32[]{:S(2)}, u32[]{:S(2)}) %collective-permute-start.7) | collective-permute-done | bytes 147488 | tf_op jit(solution)/shard_map/ppermute | solution.py:141
  37.8 1.8 %dilated_edge.1 = (f32[384,384]{1,0:T(8,128)S(1)}, bf16[192,384]{1,0:T(8,128)(2,1)S(1)}) custom-call(bf16[208,384]{1,0:T(8,128)(2,1)S(1)} %get-tuple-element.31.a0.m0, bf16[208,384]{1,0:T(8,128)(2,1)S(1)} %collective-permute-done.a1.m1, bf16[208,384]{1,0:T(8,128)(2,1)S(1)} %collective-permute-done.1.a2.m2, ...), custom_call_target="tpu_custom_call" | custom-call | flops 679477248 | bytes 6414336 | tf_op jit(solution)/shard_map/dilated_edge/pallas_call | solution.py:339
  41.0 3.1 %collective-permute-done.12.a3 = bf16[192,384]{1,0:T(8,128)(2,1)S(1)} collective-permute-done((bf16[192,384]{1,0:T(8,128)(2,1)S(1)}, bf16[192,384]{1,0:T(8,128)(2,1)S(1)}, u32[]{:S(2)}, u32[]{:S(2)}) %collective-permute-start.12) | collective-permute-done | bytes 147488 | tf_op jit(solution)/shard_map/ppermute | solution.py:141
  44.1 1.8 %project_middle.1 = (bf16[192,384]{1,0:T(8,128)(2,1)S(1)}, bf16[192,768]{1,0:T(8,128)(2,1)S(1)}) custom-call(bf16[192,384]{1,0:T(8,128)(2,1)S(1)} %get-tuple-element.45.a0, bf16[192,384]{1,0:T(8,128)(2,1)S(1)} %collective-permute-done.8.a1, bf16[192,384]{1,0:T(8,128)(2,1)S(1)} %collective-permute-done.10.a2, ...), custom_call_target="tpu_custom_call" | custom-call | flops 679477248 | bytes 4571136 | tf_op jit(solution)/shard_map/project_middle/pallas_call | solution.py:401
  46.0 2.0 %collective-permute-start.18 = (bf16[192,768]{1,0:T(8,128)(2,1)S(1)}, bf16[192,768]{1,0:T(8,128)(2,1)S(1)}, u32[]{:S(2)}, u32[]{:S(2)}) collective-permute-start(bf16[192,768]{1,0:T(8,128)(2,1)S(1)} %get-tuple-element.46.refs_2_), channel_id=1, source_target_pairs={{0,8},{4,12},{8,0},{12,4},{16,24},{20,28},{24,16},{28,20},{1,9},{5... | collective-permute-start | bytes 884744 | tf_op jit(solution)/shard_map/ppermute | solution.py:581
  48.0 2.0 %collective-permute-start.13 = (bf16[192,384]{1,0:T(8,128)(2,1)S(1)}, bf16[192,384]{1,0:T(8,128)(2,1)S(1)}, u32[]{:S(2)}, u32[]{:S(2)}) collective-permute-start(bf16[192,384]{1,0:T(8,128)(2,1)S(1)} %collective-permute-done.11.a2), channel_id=1, source_target_pairs={{0,1},{1,0},{2,3},{3,2},{4,5},{5,4},{6,7},{7,6},{8,9},{9,8},{10,11... | collective-permute-start | bytes 442376 | tf_op jit(solution)/shard_map/ppermute | solution.py:141
  50.3 4.3 %collective-permute-done.18.refs_4_ = bf16[192,768]{1,0:T(8,128)(2,1)S(1)} collective-permute-done((bf16[192,768]{1,0:T(8,128)(2,1)S(1)}, bf16[192,768]{1,0:T(8,128)(2,1)S(1)}, u32[]{:S(2)}, u32[]{:S(2)}) %collective-permute-start.18) | collective-permute-done | bytes 294944 | tf_op jit(solution)/shard_map/ppermute | solution.py:581
  56.3 1.9 %project_edge.1 = (bf16[384,384]{1,0:T(8,128)(2,1)S(1)}, bf16[192,768]{1,0:T(8,128)(2,1)S(1)}) custom-call(bf16[192,384]{1,0:T(8,128)(2,1)S(1)} %get-tuple-element.44.a0, bf16[192,384]{1,0:T(8,128)(2,1)S(1)} %collective-permute-done.9.a1, bf16[192,384]{1,0:T(8,128)(2,1)S(1)} %collective-permute-done.11.a2, bf16[192,384]{1,0:T(8,128)(2,1)S(1)} %collective-permute-done.13.a3, ...), custom_call_target="tpu_custom_call" | custom-call | flops 679477248 | bytes 4866048 | tf_op jit(solution)/shard_map/project_edge/pallas_call | solution.py:401
  58.6 1.9 %collective-permute-start.15 = (bf16[192,768]{1,0:T(8,128)(2,1)S(1)}, bf16[192,768]{1,0:T(8,128)(2,1)S(1)}, u32[]{:S(2)}, u32[]{:S(2)}) collective-permute-start(bf16[192,768]{1,0:T(8,128)(2,1)S(1)} %get-tuple-element.50.refs_3_), channel_id=1, source_target_pairs={{0,16},{4,20},{8,24},{12,28},{16,0},{20,4},{24,8},{28,12},{1,17},{... | collective-permute-start | bytes 884744 | tf_op jit(solution)/shard_map/ppermute | solution.py:581
  62.2 15.0 %collective-permute-done.21.refs_7_ = bf16[192,384]{1,0:T(8,128)(2,1)S(1)} collective-permute-done((bf16[192,384]{1,0:T(8,128)(2,1)S(1)}, bf16[192,384]{1,0:T(8,128)(2,1)S(1)}, u32[]{:S(2)}, u32[]{:S(2)}) %collective-permute-start.21) | collective-permute-done | bytes 147488 | tf_op jit(solution)/shard_map/ppermute | solution.py:581
  77.2 6.2 %attend_m.1.refs_4_ = f32[400,768]{1,0:T(8,128)S(1)} custom-call(bf16[384,384]{1,0:T(8,128)(2,1)S(1)} %get-tuple-element.49.refs_0_, bf16[384,384]{1,0:T(8,128)(2,1)S(1)} %collective-permute-done.17.refs_1_.refs_0_, bf16[192,768]{1,0:T(8,128)(2,1)S(1)} %get-tuple-element.46.refs_2_, bf16[192,768]{1,0:T(8,128)(2,1)S(1)} %get-tuple-element.50.refs_3_, ...), custom_call_target="tpu_custom_call" | custom-call | flops 1132462080 | bytes 3293184 | tf_op jit(solution)/shard_map/attend_m/pallas_call | solution.py:524
  83.5 3.0 %attend_other.1 = f32[400,384]{1,0:T(8,128)S(1)} custom-call(bf16[384,384]{1,0:T(8,128)(2,1)S(1)} %collective-permute-done.17.refs_1_.refs_0_, bf16[192,768]{1,0:T(8,128)(2,1)S(1)} %collective-permute-done.14.refs_1_, bf16[192,768]{1,0:T(8,128)(2,1)S(1)} %collective-permute-done.15.refs_2_, bf16[192,768]{1,0:T(8,128)(2,1)S(1)} %collective-permute-done.16.refs_3_, ...), custom_call_target="tpu_custom_call" | custom-call | flops 339738624 | bytes 3022848 | tf_op jit(solution)/shard_map/attend_other/pallas_call | solution.py:524
  86.5 3.0 %attend_own.1.own_state = f32[400,384]{1,0:T(8,128)S(1)} custom-call(bf16[384,384]{1,0:T(8,128)(2,1)S(1)} %get-tuple-element.49.refs_0_, bf16[192,768]{1,0:T(8,128)(2,1)S(1)} %collective-permute-done.14.refs_1_, bf16[192,768]{1,0:T(8,128)(2,1)S(1)} %collective-permute-done.15.refs_2_, bf16[192,768]{1,0:T(8,128)(2,1)S(1)} %collective-permute-done.16.refs_3_, ...), custom_call_target="tpu_custom_call" | custom-call | flops 339738624 | bytes 3022848 | tf_op jit(solution)/shard_map/attend_own/pallas_call | solution.py:524
  90.6 9.3 %collective-permute-done.23 = bf16[384,384]{1,0:T(8,128)(2,1)S(1)} collective-permute-done((bf16[384,384]{1,0:T(8,128)(2,1)S(1)}, bf16[384,384]{1,0:T(8,128)(2,1)S(1)}, u32[]{:S(2)}, u32[]{:S(2)}) %collective-permute-start.23) | collective-permute-done | bytes 294944 | tf_op jit(solution)/shard_map/ppermute | solution.py:141
  100.4 2.2 %collective-permute-start.24 = (bf16[384,384]{1,0:T(8,128)(2,1)S(1)}, bf16[384,384]{1,0:T(8,128)(2,1)S(1)}, u32[]{:S(2)}, u32[]{:S(2)}) collective-permute-start(bf16[384,384]{1,0:T(8,128)(2,1)S(1)} %add_convert_fusion.1), channel_id=1, source_target_pairs={{0,2},{1,3},{2,0},{3,1},{4,6},{5,7},{6,4},{7,5},{8,10},{9,11},{10,... | collective-permute-start | bytes 884744 | tf_op jit(solution)/shard_map/ppermute | solution.py:141
  102.6 11.7 %collective-permute-done.25 = bf16[384,384]{1,0:T(8,128)(2,1)S(1)} collective-permute-done((bf16[384,384]{1,0:T(8,128)(2,1)S(1)}, bf16[384,384]{1,0:T(8,128)(2,1)S(1)}, u32[]{:S(2)}, u32[]{:S(2)}) %collective-permute-start.25) | collective-permute-done | bytes 294944 | tf_op jit(solution)/shard_map/ppermute | solution.py:141
  114.3 1.8 %collective-permute-done.24 = bf16[384,384]{1,0:T(8,128)(2,1)S(1)} collective-permute-done((bf16[384,384]{1,0:T(8,128)(2,1)S(1)}, bf16[384,384]{1,0:T(8,128)(2,1)S(1)}, u32[]{:S(2)}, u32[]{:S(2)}) %collective-permute-start.24) | collective-permute-done | bytes 294944 | tf_op jit(solution)/shard_map/ppermute | solution.py:141
  (57 shorter events, 16.9 us)
Async XLA Ops:
  3.0 11.7 %collective-permute-start.1 = (bf16[208,384]{1,0:T(8,128)(2,1)S(1)}, bf16[208,384]{1,0:T(8,128)(2,1)S(1)}, u32[]{:S(2)}, u32[]{:S(2)}) collective-permute-start(bf16[208,384]{1,0:T(8,128)(2,1)S(1)} %get-tuple-element.31.a0.m0), channel_id=1, source_target_pairs={{0,2},{1,3},{2,0},{3,1},{4,6},{5,7},{6,4},{7,5},{8,10},{9,11},{10,... | collective-permute-start | bytes 479240 | tf_op jit(solution)/shard_map/ppermute | solution.py:141
  7.1 8.3 %collective-permute-start = (bf16[208,384]{1,0:T(8,128)(2,1)S(1)}, bf16[208,384]{1,0:T(8,128)(2,1)S(1)}, u32[]{:S(2)}, u32[]{:S(2)}) collective-permute-start(bf16[208,384]{1,0:T(8,128)(2,1)S(1)} %get-tuple-element.31.a0.m0), channel_id=1, source_target_pairs={{0,1},{1,0},{2,3},{3,2},{4,5},{5,4},{6,7},{7,6},{8,9},{9,8},{10,11... | collective-permute-start | bytes 479240 | tf_op jit(solution)/shard_map/ppermute | solution.py:141
  8.7 6.7 %collective-permute-start.3 = (bf16[16,768]{1,0:T(8,128)(2,1)S(1)}, bf16[16,768]{1,0:T(8,128)(2,1)S(1)}, u32[]{:S(2)}, u32[]{:S(2)}) collective-permute-start(bf16[16,768]{1,0:T(8,128)(2,1)S(1)} %get-tuple-element.58), channel_id=1, source_target_pairs={{0,4},{4,8},{8,12},{12,16},{16,20},{20,24},{24,28},{1,5},{5,9},{9,... | collective-permute-start | bytes 73736 | tf_op jit(solution)/shard_map/ppermute | solution.py:589
  14.8 5.7 %collective-permute-start.2 = (bf16[208,384]{1,0:T(8,128)(2,1)S(1)}, bf16[208,384]{1,0:T(8,128)(2,1)S(1)}, u32[]{:S(2)}, u32[]{:S(2)}) collective-permute-start(bf16[208,384]{1,0:T(8,128)(2,1)S(1)} %collective-permute-done.1.a2.m2), channel_id=1, source_target_pairs={{0,1},{1,0},{2,3},{3,2},{4,5},{5,4},{6,7},{7,6},{8,9},{9,8},{10,11... | collective-permute-start | bytes 479240 | tf_op jit(solution)/shard_map/ppermute | solution.py:141
  16.5 10.6 %collective-permute-start.6 = (bf16[192,384]{1,0:T(8,128)(2,1)S(1)}, bf16[192,384]{1,0:T(8,128)(2,1)S(1)}, u32[]{:S(2)}, u32[]{:S(2)}) collective-permute-start(bf16[192,384]{1,0:T(8,128)(2,1)S(1)} %get-tuple-element.33.e0), channel_id=1, source_target_pairs={{0,2},{1,3},{2,0},{3,1},{4,6},{5,7},{6,4},{7,5},{8,10},{9,11},{10,... | collective-permute-start | bytes 442376 | tf_op jit(solution)/shard_map/ppermute | solution.py:141
  20.0 10.0 %collective-permute-start.5 = (bf16[192,384]{1,0:T(8,128)(2,1)S(1)}, bf16[192,384]{1,0:T(8,128)(2,1)S(1)}, u32[]{:S(2)}, u32[]{:S(2)}) collective-permute-start(bf16[192,384]{1,0:T(8,128)(2,1)S(1)} %get-tuple-element.33.e0), channel_id=1, source_target_pairs={{0,1},{1,0},{2,3},{3,2},{4,5},{5,4},{6,7},{7,6},{8,9},{9,8},{10,11... | collective-permute-start | bytes 442376 | tf_op jit(solution)/shard_map/ppermute | solution.py:141
  27.1 8.7 %collective-permute-start.10 = (bf16[192,384]{1,0:T(8,128)(2,1)S(1)}, bf16[192,384]{1,0:T(8,128)(2,1)S(1)}, u32[]{:S(2)}, u32[]{:S(2)}) collective-permute-start(bf16[192,384]{1,0:T(8,128)(2,1)S(1)} %get-tuple-element.45.a0), channel_id=1, source_target_pairs={{0,2},{1,3},{2,0},{3,1},{4,6},{5,7},{6,4},{7,5},{8,10},{9,11},{10,... | collective-permute-start | bytes 442376 | tf_op jit(solution)/shard_map/ppermute | solution.py:141
  27.6 10.2 %collective-permute-start.7 = (bf16[192,384]{1,0:T(8,128)(2,1)S(1)}, bf16[192,384]{1,0:T(8,128)(2,1)S(1)}, u32[]{:S(2)}, u32[]{:S(2)}) collective-permute-start(bf16[192,384]{1,0:T(8,128)(2,1)S(1)} %collective-permute-done.6.e2), channel_id=1, source_target_pairs={{0,1},{1,0},{2,3},{3,2},{4,5},{5,4},{6,7},{7,6},{8,9},{9,8},{10,11... | collective-permute-start | bytes 442376 | tf_op jit(solution)/shard_map/ppermute | solution.py:141
  30.0 11.0 %collective-permute-start.8 = (bf16[192,384]{1,0:T(8,128)(2,1)S(1)}, bf16[192,384]{1,0:T(8,128)(2,1)S(1)}, u32[]{:S(2)}, u32[]{:S(2)}) collective-permute-start(bf16[192,384]{1,0:T(8,128)(2,1)S(1)} %get-tuple-element.45.a0), channel_id=1, source_target_pairs={{0,1},{1,0},{2,3},{3,2},{4,5},{5,4},{6,7},{7,6},{8,9},{9,8},{10,11... | collective-permute-start | bytes 442376 | tf_op jit(solution)/shard_map/ppermute | solution.py:141
  35.8 8.3 %collective-permute-start.12 = (bf16[192,384]{1,0:T(8,128)(2,1)S(1)}, bf16[192,384]{1,0:T(8,128)(2,1)S(1)}, u32[]{:S(2)}, u32[]{:S(2)}) collective-permute-start(bf16[192,384]{1,0:T(8,128)(2,1)S(1)} %collective-permute-done.10.a2), channel_id=1, source_target_pairs={{0,1},{1,0},{2,3},{3,2},{4,5},{5,4},{6,7},{7,6},{8,9},{9,8},{10,11... | collective-permute-start | bytes 442376 | tf_op jit(solution)/shard_map/ppermute | solution.py:141
  39.6 8.4 %collective-permute-start.11 = (bf16[192,384]{1,0:T(8,128)(2,1)S(1)}, bf16[192,384]{1,0:T(8,128)(2,1)S(1)}, u32[]{:S(2)}, u32[]{:S(2)}) collective-permute-start(bf16[192,384]{1,0:T(8,128)(2,1)S(1)} %get-tuple-element.44.a0), channel_id=1, source_target_pairs={{0,2},{1,3},{2,0},{3,1},{4,6},{5,7},{6,4},{7,5},{8,10},{9,11},{10,... | collective-permute-start | bytes 442376 | tf_op jit(solution)/shard_map/ppermute | solution.py:141
  46.0 8.7 %collective-permute-start.18 = (bf16[192,768]{1,0:T(8,128)(2,1)S(1)}, bf16[192,768]{1,0:T(8,128)(2,1)S(1)}, u32[]{:S(2)}, u32[]{:S(2)}) collective-permute-start(bf16[192,768]{1,0:T(8,128)(2,1)S(1)} %get-tuple-element.46.refs_2_), channel_id=1, source_target_pairs={{0,8},{4,12},{8,0},{12,4},{16,24},{20,28},{24,16},{28,20},{1,9},{5... | collective-permute-start | bytes 884744 | tf_op jit(solution)/shard_map/ppermute | solution.py:581
  48.0 8.3 %collective-permute-start.9 = (bf16[192,384]{1,0:T(8,128)(2,1)S(1)}, bf16[192,384]{1,0:T(8,128)(2,1)S(1)}, u32[]{:S(2)}, u32[]{:S(2)}) collective-permute-start(bf16[192,384]{1,0:T(8,128)(2,1)S(1)} %get-tuple-element.44.a0), channel_id=1, source_target_pairs={{0,1},{1,0},{2,3},{3,2},{4,5},{5,4},{6,7},{7,6},{8,9},{9,8},{10,11... | collective-permute-start | bytes 442376 | tf_op jit(solution)/shard_map/ppermute | solution.py:141
  48.0 8.3 %collective-permute-start.13 = (bf16[192,384]{1,0:T(8,128)(2,1)S(1)}, bf16[192,384]{1,0:T(8,128)(2,1)S(1)}, u32[]{:S(2)}, u32[]{:S(2)}) collective-permute-start(bf16[192,384]{1,0:T(8,128)(2,1)S(1)} %collective-permute-done.11.a2), channel_id=1, source_target_pairs={{0,1},{1,0},{2,3},{3,2},{4,5},{5,4},{6,7},{7,6},{8,9},{9,8},{10,11... | collective-permute-start | bytes 442376 | tf_op jit(solution)/shard_map/ppermute | solution.py:141
  50.0 10.5 %collective-permute-start.19 = (bf16[192,768]{1,0:T(8,128)(2,1)S(1)}, bf16[192,768]{1,0:T(8,128)(2,1)S(1)}, u32[]{:S(2)}, u32[]{:S(2)}) collective-permute-start(bf16[192,768]{1,0:T(8,128)(2,1)S(1)} %get-tuple-element.46.refs_2_), channel_id=1, source_target_pairs={{0,16},{4,20},{8,24},{12,28},{16,0},{20,4},{24,8},{28,12},{1,17},{... | collective-permute-start | bytes 884744 | tf_op jit(solution)/shard_map/ppermute | solution.py:581
  54.7 7.2 %collective-permute-start.20 = (bf16[192,384]{1,0:T(8,128)(2,1)S(1)}, bf16[192,384]{1,0:T(8,128)(2,1)S(1)}, u32[]{:S(2)}, u32[]{:S(2)}) collective-permute-start(bf16[192,384]{1,0:T(8,128)(2,1)S(1)} %slice.16), channel_id=1, source_target_pairs={{0,16},{4,20},{8,24},{12,28},{16,0},{20,4},{24,8},{28,12},{1,17},{... | collective-permute-start | bytes 442376 | tf_op jit(solution)/shard_map/ppermute | solution.py:581
  58.2 19.0 %collective-permute-start.17 = (bf16[384,384]{1,0:T(8,128)(2,1)S(1)}, bf16[384,384]{1,0:T(8,128)(2,1)S(1)}, u32[]{:S(2)}, u32[]{:S(2)}) collective-permute-start(bf16[384,384]{1,0:T(8,128)(2,1)S(1)} %get-tuple-element.49.refs_0_), channel_id=1, source_target_pairs={{0,4},{4,0},{8,12},{12,8},{16,20},{20,16},{24,28},{28,24},{1,5},{5... | collective-permute-start | bytes 884744 | tf_op jit(solution)/shard_map/ppermute | solution.py:581
  58.3 25.2 %collective-permute-start.14 = (bf16[192,768]{1,0:T(8,128)(2,1)S(1)}, bf16[192,768]{1,0:T(8,128)(2,1)S(1)}, u32[]{:S(2)}, u32[]{:S(2)}) collective-permute-start(bf16[192,768]{1,0:T(8,128)(2,1)S(1)} %get-tuple-element.50.refs_3_), channel_id=1, source_target_pairs={{0,8},{4,12},{8,0},{12,4},{16,24},{20,28},{24,16},{28,20},{1,9},{5... | collective-permute-start | bytes 884744 | tf_op jit(solution)/shard_map/ppermute | solution.py:581
  58.6 24.9 %collective-permute-start.15 = (bf16[192,768]{1,0:T(8,128)(2,1)S(1)}, bf16[192,768]{1,0:T(8,128)(2,1)S(1)}, u32[]{:S(2)}, u32[]{:S(2)}) collective-permute-start(bf16[192,768]{1,0:T(8,128)(2,1)S(1)} %get-tuple-element.50.refs_3_), channel_id=1, source_target_pairs={{0,16},{4,20},{8,24},{12,28},{16,0},{20,4},{24,8},{28,12},{1,17},{... | collective-permute-start | bytes 884744 | tf_op jit(solution)/shard_map/ppermute | solution.py:581
  60.5 23.0 %collective-permute-start.16 = (bf16[192,768]{1,0:T(8,128)(2,1)S(1)}, bf16[192,768]{1,0:T(8,128)(2,1)S(1)}, u32[]{:S(2)}, u32[]{:S(2)}) collective-permute-start(bf16[192,768]{1,0:T(8,128)(2,1)S(1)} %get-tuple-element.50.refs_3_), channel_id=1, source_target_pairs={{0,24},{4,28},{8,16},{12,20},{16,8},{20,12},{24,0},{28,4},{1,25},{... | collective-permute-start | bytes 884744 | tf_op jit(solution)/shard_map/ppermute | solution.py:581
  61.8 15.4 %collective-permute-start.21 = (bf16[192,384]{1,0:T(8,128)(2,1)S(1)}, bf16[192,384]{1,0:T(8,128)(2,1)S(1)}, u32[]{:S(2)}, u32[]{:S(2)}) collective-permute-start(bf16[192,384]{1,0:T(8,128)(2,1)S(1)} %slice.17), channel_id=1, source_target_pairs={{0,8},{4,12},{8,0},{12,4},{16,24},{20,28},{24,16},{28,20},{1,9},{5... | collective-permute-start | bytes 442376 | tf_op jit(solution)/shard_map/ppermute | solution.py:581
  90.5 9.5 %collective-permute-start.23 = (bf16[384,384]{1,0:T(8,128)(2,1)S(1)}, bf16[384,384]{1,0:T(8,128)(2,1)S(1)}, u32[]{:S(2)}, u32[]{:S(2)}) collective-permute-start(bf16[384,384]{1,0:T(8,128)(2,1)S(1)} %get-tuple-element.54), channel_id=1, source_target_pairs={{0,1},{1,0},{2,3},{3,2},{4,5},{5,4},{6,7},{7,6},{8,9},{9,8},{10,11... | collective-permute-start | bytes 884744 | tf_op jit(solution)/shard_map/ppermute | solution.py:141
  100.1 14.3 %collective-permute-start.25 = (bf16[384,384]{1,0:T(8,128)(2,1)S(1)}, bf16[384,384]{1,0:T(8,128)(2,1)S(1)}, u32[]{:S(2)}, u32[]{:S(2)}) collective-permute-start(bf16[384,384]{1,0:T(8,128)(2,1)S(1)} %get-tuple-element.56), channel_id=1, source_target_pairs={{0,1},{1,0},{2,3},{3,2},{4,5},{5,4},{6,7},{7,6},{8,9},{9,8},{10,11... | collective-permute-start | bytes 884744 | tf_op jit(solution)/shard_map/ppermute | solution.py:141
  100.4 15.8 %collective-permute-start.24 = (bf16[384,384]{1,0:T(8,128)(2,1)S(1)}, bf16[384,384]{1,0:T(8,128)(2,1)S(1)}, u32[]{:S(2)}, u32[]{:S(2)}) collective-permute-start(bf16[384,384]{1,0:T(8,128)(2,1)S(1)} %add_convert_fusion.1), channel_id=1, source_target_pairs={{0,2},{1,3},{2,0},{3,1},{4,6},{5,7},{6,4},{7,5},{8,10},{9,11},{10,... | collective-permute-start | bytes 884744 | tf_op jit(solution)/shard_map/ppermute | solution.py:141
  (9 other events, 65.0 us)

commit v12 on v10

--- a/solution.py
+++ b/solution.py
@@ -630,9 +630,9 @@
     own, p1, p2, p3 = mix(state_own, given, w_out, h2)
     inward = swapped(p3, 1)
     joined = (p2.astype(jnp.float32) + inward.astype(jnp.float32)).astype(jnp.bfloat16)
-    total = own
-    for part in (swapped(joined, 2), swapped(after(p1, joined), 1)):
-        total = total + part.astype(jnp.float32)
+    beside = swapped(after(p1, joined), 1)
+    total = own + swapped(joined, 2).astype(jnp.float32)
+    total = after(total) + beside.astype(jnp.float32)
     return total.astype(jnp.bfloat16)
 
 

time: 111 us -> 110 us (level)
  waiting for transfers between devices: 54.7 us -> 53.2 us
    ppermute x15, waiting for transfers between devices: 46.2 us -> 44.7 us  [swapped(): return lax.ppermute(block, 'head', [(i, i ^ mask) for i in range(count)])]
  transfers between devices with their start and end apart: 25 -> 25, of which waited for: 15 -> 14; matrix products, arithmetic and copies ran while one was open for 0% -> 0% of each run, Pallas kernels for 16% -> 16%
where the time goes in v12:
time: 110 us
  waiting for transfers between devices  53.2 us (48%)
  starting transfers between devices  30.8 us (28%)
  Pallas kernels  24.3 us (22%)
    ppermute x15, waiting for transfers between devices, swapped(): return lax.ppermute(block, 'head', [(i, i ^ mask) for i in range(count)])  44.7 us
    ppermute x15, starting transfers between devices, swapped(): return lax.ppermute(block, 'head', [(i, i ^ mask) for i in range(count)])  18 us
    pallas_call x3, Pallas kernels, attend(): pl.pallas_call(kernel, out_shape=out, scratch_shapes=[pltpu.VMEM((2, exte...  12.1 us
    ppermute x8, starting transfers between devices, exchanged(): return lax.ppermute(block, 'seq', [(i, i ^ mask) for i in range(count)])  9.9 us
    ppermute x8, waiting for transfers between devices, exchanged(): return lax.ppermute(block, 'seq', [(i, i ^ mask) for i in range(count)])  8.5 us
    pallas_call x2, Pallas kernels, first_conv(): pl.pallas_call(kernel, out_shape=(kept, sent), in_specs=[pl.BlockSpec(mem...  4.14 us
    pallas_call x2, Pallas kernels, project(): pl.pallas_call(kernel, out_shape=(q, kv), compiler_params=pltpu.CompilerP...  3.7 us
    pallas_call x2, Pallas kernels, second_conv(): pl.pallas_call(kernel, out_shape=(kept, sent), scratch_shapes=[pltpu.VMEM...  3.42 us
  transfers between devices with their start and end apart: 25, of which 14 were waited for; matrix products, arithmetic and copies ran while one was open for 0% of the time, Pallas kernels for 16%

profile of v12, /device:TPU:0, one launch (start us, length us, event | category | flops | bytes accessed | tf_op | source)
XLA Modules:
  0.0 109.5 jit_solution(6132863473559725284)
XLA Ops:
  0.0 3.0 %conv_middle.1 = (f32[208,384]{1,0:T(8,128)S(1)}, bf16[208,384]{1,0:T(8,128)(2,1)S(1)}) custom-call(bf16[768,768]{1,0:T(8,128)(2,1)} %dna_ref.3, bf16[5,384,768]{2,1,0:T(8,128)(2,1)} %weight_ref.5), custom_call_target="tpu_custom_call" | custom-call | flops 613416960 | bytes 4608000 | tf_op jit(solution)/shard_map/conv_middle/pallas_call | solution.py:237
  3.0 4.1 %collective-permute-start.1 = (bf16[208,384]{1,0:T(8,128)(2,1)S(1)}, bf16[208,384]{1,0:T(8,128)(2,1)S(1)}, u32[]{:S(2)}, u32[]{:S(2)}) collective-permute-start(bf16[208,384]{1,0:T(8,128)(2,1)S(1)} %get-tuple-element.31.a0.m0), channel_id=1, source_target_pairs={{0,2},{1,3},{2,0},{3,1},{4,6},{5,7},{6,4},{7,5},{8,10},{9,11},{10,... | collective-permute-start | bytes 479240 | tf_op jit(solution)/shard_map/ppermute | solution.py:141
  11.6 3.2 %collective-permute-done.1.a2.m2 = bf16[208,384]{1,0:T(8,128)(2,1)S(1)} collective-permute-done((bf16[208,384]{1,0:T(8,128)(2,1)S(1)}, bf16[208,384]{1,0:T(8,128)(2,1)S(1)}, u32[]{:S(2)}, u32[]{:S(2)}) %collective-permute-start.1) | collective-permute-done | bytes 159776 | tf_op jit(solution)/shard_map/ppermute | solution.py:141
  16.5 3.4 %collective-permute-start.6 = (bf16[192,384]{1,0:T(8,128)(2,1)S(1)}, bf16[192,384]{1,0:T(8,128)(2,1)S(1)}, u32[]{:S(2)}, u32[]{:S(2)}) collective-permute-start(bf16[192,384]{1,0:T(8,128)(2,1)S(1)} %get-tuple-element.33.e0), channel_id=1, source_target_pairs={{0,2},{1,3},{2,0},{3,1},{4,6},{5,7},{6,4},{7,5},{8,10},{9,11},{10,... | collective-permute-start | bytes 442376 | tf_op jit(solution)/shard_map/ppermute | solution.py:141
  22.2 4.9 %collective-permute-done.6.e2 = bf16[192,384]{1,0:T(8,128)(2,1)S(1)} collective-permute-done((bf16[192,384]{1,0:T(8,128)(2,1)S(1)}, bf16[192,384]{1,0:T(8,128)(2,1)S(1)}, u32[]{:S(2)}, u32[]{:S(2)}) %collective-permute-start.6) | collective-permute-done | bytes 147488 | tf_op jit(solution)/shard_map/ppermute | solution.py:141
  27.6 2.3 %collective-permute-start.7 = (bf16[192,384]{1,0:T(8,128)(2,1)S(1)}, bf16[192,384]{1,0:T(8,128)(2,1)S(1)}, u32[]{:S(2)}, u32[]{:S(2)}) collective-permute-start(bf16[192,384]{1,0:T(8,128)(2,1)S(1)} %collective-permute-done.6.e2), channel_id=1, source_target_pairs={{0,1},{1,0},{2,3},{3,2},{4,5},{5,4},{6,7},{7,6},{8,9},{9,8},{10,11... | collective-permute-start | bytes 442376 | tf_op jit(solution)/shard_map/ppermute | solution.py:141
  30.0 5.8 %collective-permute-done.10.a2 = bf16[192,384]{1,0:T(8,128)(2,1)S(1)} collective-permute-done((bf16[192,384]{1,0:T(8,128)(2,1)S(1)}, bf16[192,384]{1,0:T(8,128)(2,1)S(1)}, u32[]{:S(2)}, u32[]{:S(2)}) %collective-permute-start.10) | collective-permute-done | bytes 147488 | tf_op jit(solution)/shard_map/ppermute | solution.py:141
  35.8 2.0 %collective-permute-done.7.e3 = bf16[192,384]{1,0:T(8,128)(2,1)S(1)} collective-permute-done((bf16[192,384]{1,0:T(8,128)(2,1)S(1)}, bf16[192,384]{1,0:T(8,128)(2,1)S(1)}, u32[]{:S(2)}, u32[]{:S(2)}) %collective-permute-start.7) | collective-permute-done | bytes 147488 | tf_op jit(solution)/shard_map/ppermute | solution.py:141
  41.0 5.3 %collective-permute-done.12.a3 = bf16[192,384]{1,0:T(8,128)(2,1)S(1)} collective-permute-done((bf16[192,384]{1,0:T(8,128)(2,1)S(1)}, bf16[192,384]{1,0:T(8,128)(2,1)S(1)}, u32[]{:S(2)}, u32[]{:S(2)}) %collective-permute-start.12) | collective-permute-done | bytes 147488 | tf_op jit(solution)/shard_map/ppermute | solution.py:141
  46.3 1.9 %project_middle.1 = (bf16[192,384]{1,0:T(8,128)(2,1)S(1)}, bf16[192,768]{1,0:T(8,128)(2,1)S(1)}) custom-call(bf16[192,384]{1,0:T(8,128)(2,1)S(1)} %get-tuple-element.45.a0, bf16[192,384]{1,0:T(8,128)(2,1)S(1)} %collective-permute-done.8.a1, bf16[192,384]{1,0:T(8,128)(2,1)S(1)} %collective-permute-done.10.a2, ...), custom_call_target="tpu_custom_call" | custom-call | flops 679477248 | bytes 4571136 | tf_op jit(solution)/shard_map/project_middle/pallas_call | solution.py:401
  48.2 2.0 %collective-permute-start.18 = (bf16[192,768]{1,0:T(8,128)(2,1)S(1)}, bf16[192,768]{1,0:T(8,128)(2,1)S(1)}, u32[]{:S(2)}, u32[]{:S(2)}) collective-permute-start(bf16[192,768]{1,0:T(8,128)(2,1)S(1)} %get-tuple-element.46.refs_2_), channel_id=1, source_target_pairs={{0,8},{4,12},{8,0},{12,4},{16,24},{20,28},{24,16},{28,20},{1,9},{5... | collective-permute-start | bytes 884744 | tf_op jit(solution)/shard_map/ppermute | solution.py:573
  53.4 1.8 %project_edge.1 = (bf16[384,384]{1,0:T(8,128)(2,1)S(1)}, bf16[192,768]{1,0:T(8,128)(2,1)S(1)}) custom-call(bf16[192,384]{1,0:T(8,128)(2,1)S(1)} %get-tuple-element.44.a0, bf16[192,384]{1,0:T(8,128)(2,1)S(1)} %collective-permute-done.9.a1, bf16[192,384]{1,0:T(8,128)(2,1)S(1)} %collective-permute-done.11.a2, bf16[192,384]{1,0:T(8,128)(2,1)S(1)} %collective-permute-done.13.a3, ...), custom_call_target="tpu_custom_call" | custom-call | flops 679477248 | bytes 4866048 | tf_op jit(solution)/shard_map/project_edge/pallas_call | solution.py:401
  55.3 2.1 %collective-permute-start.14 = (bf16[192,768]{1,0:T(8,128)(2,1)S(1)}, bf16[192,768]{1,0:T(8,128)(2,1)S(1)}, u32[]{:S(2)}, u32[]{:S(2)}) collective-permute-start(bf16[192,768]{1,0:T(8,128)(2,1)S(1)} %get-tuple-element.50.refs_3_), channel_id=1, source_target_pairs={{0,8},{4,12},{8,0},{12,4},{16,24},{20,28},{24,16},{28,20},{1,9},{5... | collective-permute-start | bytes 884744 | tf_op jit(solution)/shard_map/ppermute | solution.py:573
  58.3 2.1 %collective-permute-start.15 = (bf16[192,768]{1,0:T(8,128)(2,1)S(1)}, bf16[192,768]{1,0:T(8,128)(2,1)S(1)}, u32[]{:S(2)}, u32[]{:S(2)}) collective-permute-start(bf16[192,768]{1,0:T(8,128)(2,1)S(1)} %get-tuple-element.50.refs_3_), channel_id=1, source_target_pairs={{0,16},{4,20},{8,24},{12,28},{16,0},{20,4},{24,8},{28,12},{1,17},{... | collective-permute-start | bytes 884744 | tf_op jit(solution)/shard_map/ppermute | solution.py:573
  61.0 2.0 %collective-permute-start.16 = (bf16[192,768]{1,0:T(8,128)(2,1)S(1)}, bf16[192,768]{1,0:T(8,128)(2,1)S(1)}, u32[]{:S(2)}, u32[]{:S(2)}) collective-permute-start(bf16[192,768]{1,0:T(8,128)(2,1)S(1)} %get-tuple-element.50.refs_3_), channel_id=1, source_target_pairs={{0,24},{4,28},{8,16},{12,20},{16,8},{20,12},{24,0},{28,4},{1,25},{... | collective-permute-start | bytes 884744 | tf_op jit(solution)/shard_map/ppermute | solution.py:573
  63.0 3.1 %collective-permute-done.20.refs_6_ = bf16[192,768]{1,0:T(8,128)(2,1)S(1)} collective-permute-done((bf16[192,768]{1,0:T(8,128)(2,1)S(1)}, bf16[192,768]{1,0:T(8,128)(2,1)S(1)}, u32[]{:S(2)}, u32[]{:S(2)}) %collective-permute-start.20) | collective-permute-done | bytes 294944 | tf_op jit(solution)/shard_map/ppermute | solution.py:573
  66.1 6.2 %attend_m.1.refs_4_ = f32[400,768]{1,0:T(8,128)S(1)} custom-call(bf16[384,384]{1,0:T(8,128)(2,1)S(1)} %get-tuple-element.49.refs_0_, bf16[384,384]{1,0:T(8,128)(2,1)S(1)} %collective-permute-done.17.refs_1_.refs_0_, bf16[192,768]{1,0:T(8,128)(2,1)S(1)} %get-tuple-element.46.refs_2_, bf16[192,768]{1,0:T(8,128)(2,1)S(1)} %get-tuple-element.50.refs_3_, ...), custom_call_target="tpu_custom_call" | custom-call | flops 1132462080 | bytes 3293184 | tf_op jit(solution)/shard_map/attend_m/pallas_call | solution.py:516
  72.3 3.8 %collective-permute-done.15.refs_2_ = bf16[192,768]{1,0:T(8,128)(2,1)S(1)} collective-permute-done((bf16[192,768]{1,0:T(8,128)(2,1)S(1)}, bf16[192,768]{1,0:T(8,128)(2,1)S(1)}, u32[]{:S(2)}, u32[]{:S(2)}) %collective-permute-start.15) | collective-permute-done | bytes 294944 | tf_op jit(solution)/shard_map/ppermute | solution.py:573
  76.1 3.0 %attend_other.1 = f32[400,384]{1,0:T(8,128)S(1)} custom-call(bf16[384,384]{1,0:T(8,128)(2,1)S(1)} %collective-permute-done.17.refs_1_.refs_0_, bf16[192,768]{1,0:T(8,128)(2,1)S(1)} %collective-permute-done.14.refs_1_, bf16[192,768]{1,0:T(8,128)(2,1)S(1)} %collective-permute-done.15.refs_2_, bf16[192,768]{1,0:T(8,128)(2,1)S(1)} %collective-permute-done.16.refs_3_, ...), custom_call_target="tpu_custom_call" | custom-call | flops 339738624 | bytes 3022848 | tf_op jit(solution)/shard_map/attend_other/pallas_call | solution.py:516
  79.2 3.0 %attend_own.1.own_state = f32[400,384]{1,0:T(8,128)S(1)} custom-call(bf16[384,384]{1,0:T(8,128)(2,1)S(1)} %get-tuple-element.49.refs_0_, bf16[192,768]{1,0:T(8,128)(2,1)S(1)} %collective-permute-done.14.refs_1_, bf16[192,768]{1,0:T(8,128)(2,1)S(1)} %collective-permute-done.15.refs_2_, bf16[192,768]{1,0:T(8,128)(2,1)S(1)} %collective-permute-done.16.refs_3_, ...), custom_call_target="tpu_custom_call" | custom-call | flops 339738624 | bytes 3022848 | tf_op jit(solution)/shard_map/attend_own/pallas_call | solution.py:516
  83.2 1.8 %collective-permute-start.22 = (bf16[384,384]{1,0:T(8,128)(2,1)S(1)}, bf16[384,384]{1,0:T(8,128)(2,1)S(1)}, u32[]{:S(2)}, u32[]{:S(2)}) collective-permute-start(bf16[384,384]{1,0:T(8,128)(2,1)S(1)} %get-tuple-element.54), channel_id=1, source_target_pairs={{0,1},{1,0},{2,3},{3,2},{4,5},{5,4},{6,7},{7,6},{8,9},{9,8},{10,11... | collective-permute-start | bytes 884744 | tf_op jit(solution)/shard_map/ppermute | solution.py:141
  85.0 7.7 %collective-permute-done.22 = bf16[384,384]{1,0:T(8,128)(2,1)S(1)} collective-permute-done((bf16[384,384]{1,0:T(8,128)(2,1)S(1)}, bf16[384,384]{1,0:T(8,128)(2,1)S(1)}, u32[]{:S(2)}, u32[]{:S(2)}) %collective-permute-start.22) | collective-permute-done | bytes 294944 | tf_op jit(solution)/shard_map/ppermute | solution.py:141
  92.7 2.2 %collective-permute-start.23 = (bf16[384,384]{1,0:T(8,128)(2,1)S(1)}, bf16[384,384]{1,0:T(8,128)(2,1)S(1)}, u32[]{:S(2)}, u32[]{:S(2)}) collective-permute-start(bf16[384,384]{1,0:T(8,128)(2,1)S(1)} %add_convert_fusion.1), channel_id=1, source_target_pairs={{0,2},{1,3},{2,0},{3,1},{4,6},{5,7},{6,4},{7,5},{8,10},{9,11},{10,... | collective-permute-start | bytes 884744 | tf_op jit(solution)/shard_map/ppermute | solution.py:141
  95.2 13.5 %collective-permute-done.23 = bf16[384,384]{1,0:T(8,128)(2,1)S(1)} collective-permute-done((bf16[384,384]{1,0:T(8,128)(2,1)S(1)}, bf16[384,384]{1,0:T(8,128)(2,1)S(1)}, u32[]{:S(2)}, u32[]{:S(2)}) %collective-permute-start.23) | collective-permute-done | bytes 294944 | tf_op jit(solution)/shard_map/ppermute | solution.py:141
  (54 shorter events, 19.2 us)
Async XLA Ops:
  3.0 11.7 %collective-permute-start.1 = (bf16[208,384]{1,0:T(8,128)(2,1)S(1)}, bf16[208,384]{1,0:T(8,128)(2,1)S(1)}, u32[]{:S(2)}, u32[]{:S(2)}) collective-permute-start(bf16[208,384]{1,0:T(8,128)(2,1)S(1)} %get-tuple-element.31.a0.m0), channel_id=1, source_target_pairs={{0,2},{1,3},{2,0},{3,1},{4,6},{5,7},{6,4},{7,5},{8,10},{9,11},{10,... | collective-permute-start | bytes 479240 | tf_op jit(solution)/shard_map/ppermute | solution.py:141
  7.1 8.3 %collective-permute-start = (bf16[208,384]{1,0:T(8,128)(2,1)S(1)}, bf16[208,384]{1,0:T(8,128)(2,1)S(1)}, u32[]{:S(2)}, u32[]{:S(2)}) collective-permute-start(bf16[208,384]{1,0:T(8,128)(2,1)S(1)} %get-tuple-element.31.a0.m0), channel_id=1, source_target_pairs={{0,1},{1,0},{2,3},{3,2},{4,5},{5,4},{6,7},{7,6},{8,9},{9,8},{10,11... | collective-permute-start | bytes 479240 | tf_op jit(solution)/shard_map/ppermute | solution.py:141
  8.7 6.7 %collective-permute-start.3 = (bf16[16,768]{1,0:T(8,128)(2,1)S(1)}, bf16[16,768]{1,0:T(8,128)(2,1)S(1)}, u32[]{:S(2)}, u32[]{:S(2)}) collective-permute-start(bf16[16,768]{1,0:T(8,128)(2,1)S(1)} %get-tuple-element.58), channel_id=1, source_target_pairs={{0,4},{4,8},{8,12},{12,16},{16,20},{20,24},{24,28},{1,5},{5,9},{9,... | collective-permute-start | bytes 73736 | tf_op jit(solution)/shard_map/ppermute | solution.py:581
  10.0 5.4 %collective-permute-start.4 = (bf16[16,768]{1,0:T(8,128)(2,1)S(1)}, bf16[16,768]{1,0:T(8,128)(2,1)S(1)}, u32[]{:S(2)}, u32[]{:S(2)}) collective-permute-start(bf16[16,768]{1,0:T(8,128)(2,1)S(1)} %get-tuple-element.57), channel_id=1, source_target_pairs={{4,0},{8,4},{12,8},{16,12},{20,16},{24,20},{28,24},{5,1},{9,5},{13... | collective-permute-start | bytes 73736 | tf_op jit(solution)/shard_map/ppermute | solution.py:582
  14.8 5.7 %collective-permute-start.2 = (bf16[208,384]{1,0:T(8,128)(2,1)S(1)}, bf16[208,384]{1,0:T(8,128)(2,1)S(1)}, u32[]{:S(2)}, u32[]{:S(2)}) collective-permute-start(bf16[208,384]{1,0:T(8,128)(2,1)S(1)} %collective-permute-done.1.a2.m2), channel_id=1, source_target_pairs={{0,1},{1,0},{2,3},{3,2},{4,5},{5,4},{6,7},{7,6},{8,9},{9,8},{10,11... | collective-permute-start | bytes 479240 | tf_op jit(solution)/shard_map/ppermute | solution.py:141
  16.5 10.6 %collective-permute-start.6 = (bf16[192,384]{1,0:T(8,128)(2,1)S(1)}, bf16[192,384]{1,0:T(8,128)(2,1)S(1)}, u32[]{:S(2)}, u32[]{:S(2)}) collective-permute-start(bf16[192,384]{1,0:T(8,128)(2,1)S(1)} %get-tuple-element.33.e0), channel_id=1, source_target_pairs={{0,2},{1,3},{2,0},{3,1},{4,6},{5,7},{6,4},{7,5},{8,10},{9,11},{10,... | collective-permute-start | bytes 442376 | tf_op jit(solution)/shard_map/ppermute | solution.py:141
  20.0 10.0 %collective-permute-start.5 = (bf16[192,384]{1,0:T(8,128)(2,1)S(1)}, bf16[192,384]{1,0:T(8,128)(2,1)S(1)}, u32[]{:S(2)}, u32[]{:S(2)}) collective-permute-start(bf16[192,384]{1,0:T(8,128)(2,1)S(1)} %get-tuple-element.33.e0), channel_id=1, source_target_pairs={{0,1},{1,0},{2,3},{3,2},{4,5},{5,4},{6,7},{7,6},{8,9},{9,8},{10,11... | collective-permute-start | bytes 442376 | tf_op jit(solution)/shard_map/ppermute | solution.py:141
  27.1 8.7 %collective-permute-start.10 = (bf16[192,384]{1,0:T(8,128)(2,1)S(1)}, bf16[192,384]{1,0:T(8,128)(2,1)S(1)}, u32[]{:S(2)}, u32[]{:S(2)}) collective-permute-start(bf16[192,384]{1,0:T(8,128)(2,1)S(1)} %get-tuple-element.45.a0), channel_id=1, source_target_pairs={{0,2},{1,3},{2,0},{3,1},{4,6},{5,7},{6,4},{7,5},{8,10},{9,11},{10,... | collective-permute-start | bytes 442376 | tf_op jit(solution)/shard_map/ppermute | solution.py:141
  27.6 10.2 %collective-permute-start.7 = (bf16[192,384]{1,0:T(8,128)(2,1)S(1)}, bf16[192,384]{1,0:T(8,128)(2,1)S(1)}, u32[]{:S(2)}, u32[]{:S(2)}) collective-permute-start(bf16[192,384]{1,0:T(8,128)(2,1)S(1)} %collective-permute-done.6.e2), channel_id=1, source_target_pairs={{0,1},{1,0},{2,3},{3,2},{4,5},{5,4},{6,7},{7,6},{8,9},{9,8},{10,11... | collective-permute-start | bytes 442376 | tf_op jit(solution)/shard_map/ppermute | solution.py:141
  30.0 11.0 %collective-permute-start.8 = (bf16[192,384]{1,0:T(8,128)(2,1)S(1)}, bf16[192,384]{1,0:T(8,128)(2,1)S(1)}, u32[]{:S(2)}, u32[]{:S(2)}) collective-permute-start(bf16[192,384]{1,0:T(8,128)(2,1)S(1)} %get-tuple-element.45.a0), channel_id=1, source_target_pairs={{0,1},{1,0},{2,3},{3,2},{4,5},{5,4},{6,7},{7,6},{8,9},{9,8},{10,11... | collective-permute-start | bytes 442376 | tf_op jit(solution)/shard_map/ppermute | solution.py:141
  35.8 10.5 %collective-permute-start.12 = (bf16[192,384]{1,0:T(8,128)(2,1)S(1)}, bf16[192,384]{1,0:T(8,128)(2,1)S(1)}, u32[]{:S(2)}, u32[]{:S(2)}) collective-permute-start(bf16[192,384]{1,0:T(8,128)(2,1)S(1)} %collective-permute-done.10.a2), channel_id=1, source_target_pairs={{0,1},{1,0},{2,3},{3,2},{4,5},{5,4},{6,7},{7,6},{8,9},{9,8},{10,11... | collective-permute-start | bytes 442376 | tf_op jit(solution)/shard_map/ppermute | solution.py:141
  39.6 8.6 %collective-permute-start.11 = (bf16[192,384]{1,0:T(8,128)(2,1)S(1)}, bf16[192,384]{1,0:T(8,128)(2,1)S(1)}, u32[]{:S(2)}, u32[]{:S(2)}) collective-permute-start(bf16[192,384]{1,0:T(8,128)(2,1)S(1)} %get-tuple-element.44.a0), channel_id=1, source_target_pairs={{0,2},{1,3},{2,0},{3,1},{4,6},{5,7},{6,4},{7,5},{8,10},{9,11},{10,... | collective-permute-start | bytes 442376 | tf_op jit(solution)/shard_map/ppermute | solution.py:141
  41.0 10.9 %collective-permute-start.9 = (bf16[192,384]{1,0:T(8,128)(2,1)S(1)}, bf16[192,384]{1,0:T(8,128)(2,1)S(1)}, u32[]{:S(2)}, u32[]{:S(2)}) collective-permute-start(bf16[192,384]{1,0:T(8,128)(2,1)S(1)} %get-tuple-element.44.a0), channel_id=1, source_target_pairs={{0,1},{1,0},{2,3},{3,2},{4,5},{5,4},{6,7},{7,6},{8,9},{9,8},{10,11... | collective-permute-start | bytes 442376 | tf_op jit(solution)/shard_map/ppermute | solution.py:141
  48.2 5.2 %collective-permute-start.13 = (bf16[192,384]{1,0:T(8,128)(2,1)S(1)}, bf16[192,384]{1,0:T(8,128)(2,1)S(1)}, u32[]{:S(2)}, u32[]{:S(2)}) collective-permute-start(bf16[192,384]{1,0:T(8,128)(2,1)S(1)} %collective-permute-done.11.a2), channel_id=1, source_target_pairs={{0,1},{1,0},{2,3},{3,2},{4,5},{5,4},{6,7},{7,6},{8,9},{9,8},{10,11... | collective-permute-start | bytes 442376 | tf_op jit(solution)/shard_map/ppermute | solution.py:141
  48.2 10.0 %collective-permute-start.18 = (bf16[192,768]{1,0:T(8,128)(2,1)S(1)}, bf16[192,768]{1,0:T(8,128)(2,1)S(1)}, u32[]{:S(2)}, u32[]{:S(2)}) collective-permute-start(bf16[192,768]{1,0:T(8,128)(2,1)S(1)} %get-tuple-element.46.refs_2_), channel_id=1, source_target_pairs={{0,8},{4,12},{8,0},{12,4},{16,24},{20,28},{24,16},{28,20},{1,9},{5... | collective-permute-start | bytes 884744 | tf_op jit(solution)/shard_map/ppermute | solution.py:573
  50.2 10.7 %collective-permute-start.19 = (bf16[192,768]{1,0:T(8,128)(2,1)S(1)}, bf16[192,768]{1,0:T(8,128)(2,1)S(1)}, u32[]{:S(2)}, u32[]{:S(2)}) collective-permute-start(bf16[192,768]{1,0:T(8,128)(2,1)S(1)} %get-tuple-element.46.refs_2_), channel_id=1, source_target_pairs={{0,16},{4,20},{8,24},{12,28},{16,0},{20,4},{24,8},{28,12},{1,17},{... | collective-permute-start | bytes 884744 | tf_op jit(solution)/shard_map/ppermute | solution.py:573
  50.5 15.6 %collective-permute-start.20 = (bf16[192,768]{1,0:T(8,128)(2,1)S(1)}, bf16[192,768]{1,0:T(8,128)(2,1)S(1)}, u32[]{:S(2)}, u32[]{:S(2)}) collective-permute-start(bf16[192,768]{1,0:T(8,128)(2,1)S(1)} %get-tuple-element.46.refs_2_), channel_id=1, source_target_pairs={{0,24},{4,28},{8,16},{12,20},{16,8},{20,12},{24,0},{28,4},{1,25},{... | collective-permute-start | bytes 884744 | tf_op jit(solution)/shard_map/ppermute | solution.py:573
  55.2 10.9 %collective-permute-start.17 = (bf16[384,384]{1,0:T(8,128)(2,1)S(1)}, bf16[384,384]{1,0:T(8,128)(2,1)S(1)}, u32[]{:S(2)}, u32[]{:S(2)}) collective-permute-start(bf16[384,384]{1,0:T(8,128)(2,1)S(1)} %get-tuple-element.49.refs_0_), channel_id=1, source_target_pairs={{0,4},{4,0},{8,12},{12,8},{16,20},{20,16},{24,28},{28,24},{1,5},{5... | collective-permute-start | bytes 884744 | tf_op jit(solution)/shard_map/ppermute | solution.py:573
  55.3 17.0 %collective-permute-start.14 = (bf16[192,768]{1,0:T(8,128)(2,1)S(1)}, bf16[192,768]{1,0:T(8,128)(2,1)S(1)}, u32[]{:S(2)}, u32[]{:S(2)}) collective-permute-start(bf16[192,768]{1,0:T(8,128)(2,1)S(1)} %get-tuple-element.50.refs_3_), channel_id=1, source_target_pairs={{0,8},{4,12},{8,0},{12,4},{16,24},{20,28},{24,16},{28,20},{1,9},{5... | collective-permute-start | bytes 884744 | tf_op jit(solution)/shard_map/ppermute | solution.py:573
  58.3 17.9 %collective-permute-start.15 = (bf16[192,768]{1,0:T(8,128)(2,1)S(1)}, bf16[192,768]{1,0:T(8,128)(2,1)S(1)}, u32[]{:S(2)}, u32[]{:S(2)}) collective-permute-start(bf16[192,768]{1,0:T(8,128)(2,1)S(1)} %get-tuple-element.50.refs_3_), channel_id=1, source_target_pairs={{0,16},{4,20},{8,24},{12,28},{16,0},{20,4},{24,8},{28,12},{1,17},{... | collective-permute-start | bytes 884744 | tf_op jit(solution)/shard_map/ppermute | solution.py:573
  61.0 15.2 %collective-permute-start.16 = (bf16[192,768]{1,0:T(8,128)(2,1)S(1)}, bf16[192,768]{1,0:T(8,128)(2,1)S(1)}, u32[]{:S(2)}, u32[]{:S(2)}) collective-permute-start(bf16[192,768]{1,0:T(8,128)(2,1)S(1)} %get-tuple-element.50.refs_3_), channel_id=1, source_target_pairs={{0,24},{4,28},{8,16},{12,20},{16,8},{20,12},{24,0},{28,4},{1,25},{... | collective-permute-start | bytes 884744 | tf_op jit(solution)/shard_map/ppermute | solution.py:573
  83.2 9.5 %collective-permute-start.22 = (bf16[384,384]{1,0:T(8,128)(2,1)S(1)}, bf16[384,384]{1,0:T(8,128)(2,1)S(1)}, u32[]{:S(2)}, u32[]{:S(2)}) collective-permute-start(bf16[384,384]{1,0:T(8,128)(2,1)S(1)} %get-tuple-element.54), channel_id=1, source_target_pairs={{0,1},{1,0},{2,3},{3,2},{4,5},{5,4},{6,7},{7,6},{8,9},{9,8},{10,11... | collective-permute-start | bytes 884744 | tf_op jit(solution)/shard_map/ppermute | solution.py:141
  92.7 15.9 %collective-permute-start.23 = (bf16[384,384]{1,0:T(8,128)(2,1)S(1)}, bf16[384,384]{1,0:T(8,128)(2,1)S(1)}, u32[]{:S(2)}, u32[]{:S(2)}) collective-permute-start(bf16[384,384]{1,0:T(8,128)(2,1)S(1)} %add_convert_fusion.1), channel_id=1, source_target_pairs={{0,2},{1,3},{2,0},{3,1},{4,6},{5,7},{6,4},{7,5},{8,10},{9,11},{10,... | collective-permute-start | bytes 884744 | tf_op jit(solution)/shard_map/ppermute | solution.py:141
  94.9 13.8 %collective-permute-start.24 = (bf16[384,384]{1,0:T(8,128)(2,1)S(1)}, bf16[384,384]{1,0:T(8,128)(2,1)S(1)}, u32[]{:S(2)}, u32[]{:S(2)}) collective-permute-start(bf16[384,384]{1,0:T(8,128)(2,1)S(1)} %get-tuple-element.56), channel_id=1, source_target_pairs={{0,1},{1,0},{2,3},{3,2},{4,5},{5,4},{6,7},{7,6},{8,9},{9,8},{10,11... | collective-permute-start | bytes 884744 | tf_op jit(solution)/shard_map/ppermute | solution.py:141
  (8 other events, 66.1 us)

commit v13 on v12

--- a/solution.py
+++ b/solution.py
@@ -623,7 +623,8 @@
     q, kv_e = project(project_edge_kernel, (*normed_e, q_m), weights, rows, "project_edge")
     q_other, x_e, y_e, d_e = exchanged(q, 1), *(exchanged(kv_e, mask) for mask in (2, 4, 6))
     state = attend((q, q_other), (kv_m, kv_e, x_m, y_m, d_m), None, 0, "attend_m")
-    late = (x_e, y_e, d_e)
+    state = attend((q, q_other), (x_e,), state, 0, "attend_x")
+    late = (y_e, d_e)
     state_other = attend((q_other,), late, state, rows, "attend_other")
     given = exchanged(state_other, 1)
     state_own = attend((q,), late, state, 0, "attend_own")

time: 110 us -> 109 us (level)
  waiting for transfers between devices: 53.2 us -> 51.1 us
    ppermute x8, waiting for transfers between devices: 8.5 us -> 6.37 us  [exchanged(): return lax.ppermute(block, 'seq', [(i, i ^ mask) for i in range(count)])]
    pallas_call x3 -> x4, Pallas kernels: 12.1 us -> 13 us  [attend(): pl.pallas_call(kernel, out_shape=out, scratch_shapes=[pltpu.VMEM((2, exte...]
  transfers between devices with their start and end apart: 25 -> 25, of which waited for: 14 -> 14; matrix products, arithmetic and copies ran while one was open for 0% -> 0% of each run, Pallas kernels for 16% -> 17%
where the time goes in v13:
time: 109 us; the launch traced here: 108 us
  waiting for transfers between devices  51.1 us (47%)
  starting transfers between devices  30.8 us (28%)
  Pallas kernels  25.3 us (23%)
    ppermute x15, waiting for transfers between devices, swapped(): return lax.ppermute(block, 'head', [(i, i ^ mask) for i in range(count)])  44.7 us
    ppermute x15, starting transfers between devices, swapped(): return lax.ppermute(block, 'head', [(i, i ^ mask) for i in range(count)])  18 us
    pallas_call x4, Pallas kernels, attend(): pl.pallas_call(kernel, out_shape=out, scratch_shapes=[pltpu.VMEM((2, exte...  13 us
    ppermute x8, starting transfers between devices, exchanged(): return lax.ppermute(block, 'seq', [(i, i ^ mask) for i in range(count)])  9.9 us
    ppermute x8, waiting for transfers between devices, exchanged(): return lax.ppermute(block, 'seq', [(i, i ^ mask) for i in range(count)])  6.37 us
    pallas_call x2, Pallas kernels, first_conv(): pl.pallas_call(kernel, out_shape=(kept, sent), in_specs=[pl.BlockSpec(mem...  4.14 us
    pallas_call x2, Pallas kernels, project(): pl.pallas_call(kernel, out_shape=(q, kv), compiler_params=pltpu.CompilerP...  3.7 us
    pallas_call x2, Pallas kernels, second_conv(): pl.pallas_call(kernel, out_shape=(kept, sent), scratch_shapes=[pltpu.VMEM...  3.42 us
  transfers between devices with their start and end apart: 25, of which 14 were waited for; matrix products, arithmetic and copies ran while one was open for 0% of the time, Pallas kernels for 17%

profile of v13, /device:TPU:0, one launch (start us, length us, event | category | flops | bytes accessed | tf_op | source)
XLA Modules:
  0.0 108.4 jit_solution(3474300537358462622)
XLA Ops:
  0.0 3.0 %conv_middle.1 = (f32[208,384]{1,0:T(8,128)S(1)}, bf16[208,384]{1,0:T(8,128)(2,1)S(1)}) custom-call(bf16[768,768]{1,0:T(8,128)(2,1)} %dna_ref.3, bf16[5,384,768]{2,1,0:T(8,128)(2,1)} %weight_ref.5), custom_call_target="tpu_custom_call" | custom-call | flops 613416960 | bytes 4608000 | tf_op jit(solution)/shard_map/conv_middle/pallas_call | solution.py:237
  3.0 4.1 %collective-permute-start.1 = (bf16[208,384]{1,0:T(8,128)(2,1)S(1)}, bf16[208,384]{1,0:T(8,128)(2,1)S(1)}, u32[]{:S(2)}, u32[]{:S(2)}) collective-permute-start(bf16[208,384]{1,0:T(8,128)(2,1)S(1)} %get-tuple-element.31.a0.m0), channel_id=1, source_target_pairs={{0,2},{1,3},{2,0},{3,1},{4,6},{5,7},{6,4},{7,5},{8,10},{9,11},{10,... | collective-permute-start | bytes 479240 | tf_op jit(solution)/shard_map/ppermute | solution.py:141
  11.6 3.2 %collective-permute-done.1.a2.m2 = bf16[208,384]{1,0:T(8,128)(2,1)S(1)} collective-permute-done((bf16[208,384]{1,0:T(8,128)(2,1)S(1)}, bf16[208,384]{1,0:T(8,128)(2,1)S(1)}, u32[]{:S(2)}, u32[]{:S(2)}) %collective-permute-start.1) | collective-permute-done | bytes 159776 | tf_op jit(solution)/shard_map/ppermute | solution.py:141
  16.5 3.4 %collective-permute-start.6 = (bf16[192,384]{1,0:T(8,128)(2,1)S(1)}, bf16[192,384]{1,0:T(8,128)(2,1)S(1)}, u32[]{:S(2)}, u32[]{:S(2)}) collective-permute-start(bf16[192,384]{1,0:T(8,128)(2,1)S(1)} %get-tuple-element.33.e0), channel_id=1, source_target_pairs={{0,2},{1,3},{2,0},{3,1},{4,6},{5,7},{6,4},{7,5},{8,10},{9,11},{10,... | collective-permute-start | bytes 442376 | tf_op jit(solution)/shard_map/ppermute | solution.py:141
  22.2 4.9 %collective-permute-done.6.e2 = bf16[192,384]{1,0:T(8,128)(2,1)S(1)} collective-permute-done((bf16[192,384]{1,0:T(8,128)(2,1)S(1)}, bf16[192,384]{1,0:T(8,128)(2,1)S(1)}, u32[]{:S(2)}, u32[]{:S(2)}) %collective-permute-start.6) | collective-permute-done | bytes 147488 | tf_op jit(solution)/shard_map/ppermute | solution.py:141
  27.6 2.3 %collective-permute-start.7 = (bf16[192,384]{1,0:T(8,128)(2,1)S(1)}, bf16[192,384]{1,0:T(8,128)(2,1)S(1)}, u32[]{:S(2)}, u32[]{:S(2)}) collective-permute-start(bf16[192,384]{1,0:T(8,128)(2,1)S(1)} %collective-permute-done.6.e2), channel_id=1, source_target_pairs={{0,1},{1,0},{2,3},{3,2},{4,5},{5,4},{6,7},{7,6},{8,9},{9,8},{10,11... | collective-permute-start | bytes 442376 | tf_op jit(solution)/shard_map/ppermute | solution.py:141
  30.0 5.8 %collective-permute-done.10.a2 = bf16[192,384]{1,0:T(8,128)(2,1)S(1)} collective-permute-done((bf16[192,384]{1,0:T(8,128)(2,1)S(1)}, bf16[192,384]{1,0:T(8,128)(2,1)S(1)}, u32[]{:S(2)}, u32[]{:S(2)}) %collective-permute-start.10) | collective-permute-done | bytes 147488 | tf_op jit(solution)/shard_map/ppermute | solution.py:141
  35.8 2.0 %collective-permute-done.7.e3 = bf16[192,384]{1,0:T(8,128)(2,1)S(1)} collective-permute-done((bf16[192,384]{1,0:T(8,128)(2,1)S(1)}, bf16[192,384]{1,0:T(8,128)(2,1)S(1)}, u32[]{:S(2)}, u32[]{:S(2)}) %collective-permute-start.7) | collective-permute-done | bytes 147488 | tf_op jit(solution)/shard_map/ppermute | solution.py:141
  41.0 5.3 %collective-permute-done.12.a3 = bf16[192,384]{1,0:T(8,128)(2,1)S(1)} collective-permute-done((bf16[192,384]{1,0:T(8,128)(2,1)S(1)}, bf16[192,384]{1,0:T(8,128)(2,1)S(1)}, u32[]{:S(2)}, u32[]{:S(2)}) %collective-permute-start.12) | collective-permute-done | bytes 147488 | tf_op jit(solution)/shard_map/ppermute | solution.py:141
  46.3 1.9 %project_middle.1 = (bf16[192,384]{1,0:T(8,128)(2,1)S(1)}, bf16[192,768]{1,0:T(8,128)(2,1)S(1)}) custom-call(bf16[192,384]{1,0:T(8,128)(2,1)S(1)} %get-tuple-element.45.a0, bf16[192,384]{1,0:T(8,128)(2,1)S(1)} %collective-permute-done.8.a1, bf16[192,384]{1,0:T(8,128)(2,1)S(1)} %collective-permute-done.10.a2, ...), custom_call_target="tpu_custom_call" | custom-call | flops 679477248 | bytes 4571136 | tf_op jit(solution)/shard_map/project_middle/pallas_call | solution.py:401
  48.2 2.0 %collective-permute-start.18 = (bf16[192,768]{1,0:T(8,128)(2,1)S(1)}, bf16[192,768]{1,0:T(8,128)(2,1)S(1)}, u32[]{:S(2)}, u32[]{:S(2)}) collective-permute-start(bf16[192,768]{1,0:T(8,128)(2,1)S(1)} %get-tuple-element.46.refs_2_), channel_id=1, source_target_pairs={{0,8},{4,12},{8,0},{12,4},{16,24},{20,28},{24,16},{28,20},{1,9},{5... | collective-permute-start | bytes 884744 | tf_op jit(solution)/shard_map/ppermute | solution.py:573
  53.4 1.8 %project_edge.1 = (bf16[384,384]{1,0:T(8,128)(2,1)S(1)}, bf16[192,768]{1,0:T(8,128)(2,1)S(1)}) custom-call(bf16[192,384]{1,0:T(8,128)(2,1)S(1)} %get-tuple-element.44.a0, bf16[192,384]{1,0:T(8,128)(2,1)S(1)} %collective-permute-done.9.a1, bf16[192,384]{1,0:T(8,128)(2,1)S(1)} %collective-permute-done.11.a2, bf16[192,384]{1,0:T(8,128)(2,1)S(1)} %collective-permute-done.13.a3, ...), custom_call_target="tpu_custom_call" | custom-call | flops 679477248 | bytes 4866048 | tf_op jit(solution)/shard_map/project_edge/pallas_call | solution.py:401
  55.3 2.1 %collective-permute-start.17 = (bf16[192,768]{1,0:T(8,128)(2,1)S(1)}, bf16[192,768]{1,0:T(8,128)(2,1)S(1)}, u32[]{:S(2)}, u32[]{:S(2)}) collective-permute-start(bf16[192,768]{1,0:T(8,128)(2,1)S(1)} %get-tuple-element.50.refs_3_), channel_id=1, source_target_pairs={{0,8},{4,12},{8,0},{12,4},{16,24},{20,28},{24,16},{28,20},{1,9},{5... | collective-permute-start | bytes 884744 | tf_op jit(solution)/shard_map/ppermute | solution.py:573
  58.3 2.1 %collective-permute-start.14 = (bf16[192,768]{1,0:T(8,128)(2,1)S(1)}, bf16[192,768]{1,0:T(8,128)(2,1)S(1)}, u32[]{:S(2)}, u32[]{:S(2)}) collective-permute-start(bf16[192,768]{1,0:T(8,128)(2,1)S(1)} %get-tuple-element.50.refs_3_), channel_id=1, source_target_pairs={{0,16},{4,20},{8,24},{12,28},{16,0},{20,4},{24,8},{28,12},{1,17},{... | collective-permute-start | bytes 884744 | tf_op jit(solution)/shard_map/ppermute | solution.py:573
  61.0 2.0 %collective-permute-start.15 = (bf16[192,768]{1,0:T(8,128)(2,1)S(1)}, bf16[192,768]{1,0:T(8,128)(2,1)S(1)}, u32[]{:S(2)}, u32[]{:S(2)}) collective-permute-start(bf16[192,768]{1,0:T(8,128)(2,1)S(1)} %get-tuple-element.50.refs_3_), channel_id=1, source_target_pairs={{0,24},{4,28},{8,16},{12,20},{16,8},{20,12},{24,0},{28,4},{1,25},{... | collective-permute-start | bytes 884744 | tf_op jit(solution)/shard_map/ppermute | solution.py:573
  63.0 3.1 %collective-permute-done.20.refs_6_ = bf16[192,768]{1,0:T(8,128)(2,1)S(1)} collective-permute-done((bf16[192,768]{1,0:T(8,128)(2,1)S(1)}, bf16[192,768]{1,0:T(8,128)(2,1)S(1)}, u32[]{:S(2)}, u32[]{:S(2)}) %collective-permute-start.20) | collective-permute-done | bytes 294944 | tf_op jit(solution)/shard_map/ppermute | solution.py:573
  66.1 6.2 %attend_m.1.refs_3_ = f32[400,768]{1,0:T(8,128)S(1)} custom-call(bf16[384,384]{1,0:T(8,128)(2,1)S(1)} %get-tuple-element.49.refs_0_, bf16[384,384]{1,0:T(8,128)(2,1)S(1)} %collective-permute-done.16.refs_1_.refs_0_, bf16[192,768]{1,0:T(8,128)(2,1)S(1)} %get-tuple-element.46.refs_2_, bf16[192,768]{1,0:T(8,128)(2,1)S(1)} %get-tuple-element.50.refs_3_, ...), custom_call_target="tpu_custom_call" | custom-call | flops 1132462080 | bytes 3293184 | tf_op jit(solution)/shard_map/attend_m/pallas_call | solution.py:516
  72.3 2.1 %attend_x.1.refs_3_ = f32[400,768]{1,0:T(8,128)S(1)} custom-call(bf16[384,384]{1,0:T(8,128)(2,1)S(1)} %get-tuple-element.49.refs_0_, bf16[384,384]{1,0:T(8,128)(2,1)S(1)} %collective-permute-done.16.refs_1_.refs_0_, bf16[192,768]{1,0:T(8,128)(2,1)S(1)} %collective-permute-done.17.refs_2_, f32[400,768]{1,0:T(8,128)S(1)} %attend_m.1.refs_3_), custom_call_target="tpu_custom_call" | custom-call | flops 226492416 | bytes 3342336 | tf_op jit(solution)/shard_map/attend_x/pallas_call | solution.py:516
  76.1 2.4 %attend_other.1 = f32[400,384]{1,0:T(8,128)S(1)} custom-call(bf16[384,384]{1,0:T(8,128)(2,1)S(1)} %collective-permute-done.16.refs_1_.refs_0_, bf16[192,768]{1,0:T(8,128)(2,1)S(1)} %collective-permute-done.14.refs_1_, bf16[192,768]{1,0:T(8,128)(2,1)S(1)} %collective-permute-done.15.refs_2_, f32[400,768]{1,0:T(8,128)S(1)} %attend_x.1.refs_3_), custom_call_target="tpu_custom_call" | custom-call | flops 226492416 | bytes 2727936 | tf_op jit(solution)/shard_map/attend_other/pallas_call | solution.py:516
  78.6 2.4 %attend_own.1.own_state = f32[400,384]{1,0:T(8,128)S(1)} custom-call(bf16[384,384]{1,0:T(8,128)(2,1)S(1)} %get-tuple-element.49.refs_0_, bf16[192,768]{1,0:T(8,128)(2,1)S(1)} %collective-permute-done.14.refs_1_, bf16[192,768]{1,0:T(8,128)(2,1)S(1)} %collective-permute-done.15.refs_2_, f32[400,768]{1,0:T(8,128)S(1)} %attend_x.1.refs_3_), custom_call_target="tpu_custom_call" | custom-call | flops 226492416 | bytes 2727936 | tf_op jit(solution)/shard_map/attend_own/pallas_call | solution.py:516
  82.0 1.8 %collective-permute-start.22 = (bf16[384,384]{1,0:T(8,128)(2,1)S(1)}, bf16[384,384]{1,0:T(8,128)(2,1)S(1)}, u32[]{:S(2)}, u32[]{:S(2)}) collective-permute-start(bf16[384,384]{1,0:T(8,128)(2,1)S(1)} %get-tuple-element.54), channel_id=1, source_target_pairs={{0,1},{1,0},{2,3},{3,2},{4,5},{5,4},{6,7},{7,6},{8,9},{9,8},{10,11... | collective-permute-start | bytes 884744 | tf_op jit(solution)/shard_map/ppermute | solution.py:141
  83.8 7.7 %collective-permute-done.22 = bf16[384,384]{1,0:T(8,128)(2,1)S(1)} collective-permute-done((bf16[384,384]{1,0:T(8,128)(2,1)S(1)}, bf16[384,384]{1,0:T(8,128)(2,1)S(1)}, u32[]{:S(2)}, u32[]{:S(2)}) %collective-permute-start.22) | collective-permute-done | bytes 294944 | tf_op jit(solution)/shard_map/ppermute | solution.py:141
  91.6 2.2 %collective-permute-start.23 = (bf16[384,384]{1,0:T(8,128)(2,1)S(1)}, bf16[384,384]{1,0:T(8,128)(2,1)S(1)}, u32[]{:S(2)}, u32[]{:S(2)}) collective-permute-start(bf16[384,384]{1,0:T(8,128)(2,1)S(1)} %add_convert_fusion.1), channel_id=1, source_target_pairs={{0,2},{1,3},{2,0},{3,1},{4,6},{5,7},{6,4},{7,5},{8,10},{9,11},{10,... | collective-permute-start | bytes 884744 | tf_op jit(solution)/shard_map/ppermute | solution.py:141
  94.0 13.5 %collective-permute-done.23 = bf16[384,384]{1,0:T(8,128)(2,1)S(1)} collective-permute-done((bf16[384,384]{1,0:T(8,128)(2,1)S(1)}, bf16[384,384]{1,0:T(8,128)(2,1)S(1)}, u32[]{:S(2)}, u32[]{:S(2)}) %collective-permute-start.23) | collective-permute-done | bytes 294944 | tf_op jit(solution)/shard_map/ppermute | solution.py:141
  (55 shorter events, 20.9 us)
Async XLA Ops:
  3.0 11.7 %collective-permute-start.1 = (bf16[208,384]{1,0:T(8,128)(2,1)S(1)}, bf16[208,384]{1,0:T(8,128)(2,1)S(1)}, u32[]{:S(2)}, u32[]{:S(2)}) collective-permute-start(bf16[208,384]{1,0:T(8,128)(2,1)S(1)} %get-tuple-element.31.a0.m0), channel_id=1, source_target_pairs={{0,2},{1,3},{2,0},{3,1},{4,6},{5,7},{6,4},{7,5},{8,10},{9,11},{10,... | collective-permute-start | bytes 479240 | tf_op jit(solution)/shard_map/ppermute | solution.py:141
  7.1 8.3 %collective-permute-start = (bf16[208,384]{1,0:T(8,128)(2,1)S(1)}, bf16[208,384]{1,0:T(8,128)(2,1)S(1)}, u32[]{:S(2)}, u32[]{:S(2)}) collective-permute-start(bf16[208,384]{1,0:T(8,128)(2,1)S(1)} %get-tuple-element.31.a0.m0), channel_id=1, source_target_pairs={{0,1},{1,0},{2,3},{3,2},{4,5},{5,4},{6,7},{7,6},{8,9},{9,8},{10,11... | collective-permute-start | bytes 479240 | tf_op jit(solution)/shard_map/ppermute | solution.py:141
  8.7 6.7 %collective-permute-start.3 = (bf16[16,768]{1,0:T(8,128)(2,1)S(1)}, bf16[16,768]{1,0:T(8,128)(2,1)S(1)}, u32[]{:S(2)}, u32[]{:S(2)}) collective-permute-start(bf16[16,768]{1,0:T(8,128)(2,1)S(1)} %get-tuple-element.58), channel_id=1, source_target_pairs={{0,4},{4,8},{8,12},{12,16},{16,20},{20,24},{24,28},{1,5},{5,9},{9,... | collective-permute-start | bytes 73736 | tf_op jit(solution)/shard_map/ppermute | solution.py:581
  10.0 5.4 %collective-permute-start.4 = (bf16[16,768]{1,0:T(8,128)(2,1)S(1)}, bf16[16,768]{1,0:T(8,128)(2,1)S(1)}, u32[]{:S(2)}, u32[]{:S(2)}) collective-permute-start(bf16[16,768]{1,0:T(8,128)(2,1)S(1)} %get-tuple-element.57), channel_id=1, source_target_pairs={{4,0},{8,4},{12,8},{16,12},{20,16},{24,20},{28,24},{5,1},{9,5},{13... | collective-permute-start | bytes 73736 | tf_op jit(solution)/shard_map/ppermute | solution.py:582
  14.8 5.7 %collective-permute-start.2 = (bf16[208,384]{1,0:T(8,128)(2,1)S(1)}, bf16[208,384]{1,0:T(8,128)(2,1)S(1)}, u32[]{:S(2)}, u32[]{:S(2)}) collective-permute-start(bf16[208,384]{1,0:T(8,128)(2,1)S(1)} %collective-permute-done.1.a2.m2), channel_id=1, source_target_pairs={{0,1},{1,0},{2,3},{3,2},{4,5},{5,4},{6,7},{7,6},{8,9},{9,8},{10,11... | collective-permute-start | bytes 479240 | tf_op jit(solution)/shard_map/ppermute | solution.py:141
  16.5 10.6 %collective-permute-start.6 = (bf16[192,384]{1,0:T(8,128)(2,1)S(1)}, bf16[192,384]{1,0:T(8,128)(2,1)S(1)}, u32[]{:S(2)}, u32[]{:S(2)}) collective-permute-start(bf16[192,384]{1,0:T(8,128)(2,1)S(1)} %get-tuple-element.33.e0), channel_id=1, source_target_pairs={{0,2},{1,3},{2,0},{3,1},{4,6},{5,7},{6,4},{7,5},{8,10},{9,11},{10,... | collective-permute-start | bytes 442376 | tf_op jit(solution)/shard_map/ppermute | solution.py:141
  20.0 10.0 %collective-permute-start.5 = (bf16[192,384]{1,0:T(8,128)(2,1)S(1)}, bf16[192,384]{1,0:T(8,128)(2,1)S(1)}, u32[]{:S(2)}, u32[]{:S(2)}) collective-permute-start(bf16[192,384]{1,0:T(8,128)(2,1)S(1)} %get-tuple-element.33.e0), channel_id=1, source_target_pairs={{0,1},{1,0},{2,3},{3,2},{4,5},{5,4},{6,7},{7,6},{8,9},{9,8},{10,11... | collective-permute-start | bytes 442376 | tf_op jit(solution)/shard_map/ppermute | solution.py:141
  27.1 8.7 %collective-permute-start.10 = (bf16[192,384]{1,0:T(8,128)(2,1)S(1)}, bf16[192,384]{1,0:T(8,128)(2,1)S(1)}, u32[]{:S(2)}, u32[]{:S(2)}) collective-permute-start(bf16[192,384]{1,0:T(8,128)(2,1)S(1)} %get-tuple-element.45.a0), channel_id=1, source_target_pairs={{0,2},{1,3},{2,0},{3,1},{4,6},{5,7},{6,4},{7,5},{8,10},{9,11},{10,... | collective-permute-start | bytes 442376 | tf_op jit(solution)/shard_map/ppermute | solution.py:141
  27.6 10.2 %collective-permute-start.7 = (bf16[192,384]{1,0:T(8,128)(2,1)S(1)}, bf16[192,384]{1,0:T(8,128)(2,1)S(1)}, u32[]{:S(2)}, u32[]{:S(2)}) collective-permute-start(bf16[192,384]{1,0:T(8,128)(2,1)S(1)} %collective-permute-done.6.e2), channel_id=1, source_target_pairs={{0,1},{1,0},{2,3},{3,2},{4,5},{5,4},{6,7},{7,6},{8,9},{9,8},{10,11... | collective-permute-start | bytes 442376 | tf_op jit(solution)/shard_map/ppermute | solution.py:141
  30.0 11.0 %collective-permute-start.8 = (bf16[192,384]{1,0:T(8,128)(2,1)S(1)}, bf16[192,384]{1,0:T(8,128)(2,1)S(1)}, u32[]{:S(2)}, u32[]{:S(2)}) collective-permute-start(bf16[192,384]{1,0:T(8,128)(2,1)S(1)} %get-tuple-element.45.a0), channel_id=1, source_target_pairs={{0,1},{1,0},{2,3},{3,2},{4,5},{5,4},{6,7},{7,6},{8,9},{9,8},{10,11... | collective-permute-start | bytes 442376 | tf_op jit(solution)/shard_map/ppermute | solution.py:141
  35.8 10.5 %collective-permute-start.12 = (bf16[192,384]{1,0:T(8,128)(2,1)S(1)}, bf16[192,384]{1,0:T(8,128)(2,1)S(1)}, u32[]{:S(2)}, u32[]{:S(2)}) collective-permute-start(bf16[192,384]{1,0:T(8,128)(2,1)S(1)} %collective-permute-done.10.a2), channel_id=1, source_target_pairs={{0,1},{1,0},{2,3},{3,2},{4,5},{5,4},{6,7},{7,6},{8,9},{9,8},{10,11... | collective-permute-start | bytes 442376 | tf_op jit(solution)/shard_map/ppermute | solution.py:141
  39.6 8.6 %collective-permute-start.11 = (bf16[192,384]{1,0:T(8,128)(2,1)S(1)}, bf16[192,384]{1,0:T(8,128)(2,1)S(1)}, u32[]{:S(2)}, u32[]{:S(2)}) collective-permute-start(bf16[192,384]{1,0:T(8,128)(2,1)S(1)} %get-tuple-element.44.a0), channel_id=1, source_target_pairs={{0,2},{1,3},{2,0},{3,1},{4,6},{5,7},{6,4},{7,5},{8,10},{9,11},{10,... | collective-permute-start | bytes 442376 | tf_op jit(solution)/shard_map/ppermute | solution.py:141
  41.0 10.9 %collective-permute-start.9 = (bf16[192,384]{1,0:T(8,128)(2,1)S(1)}, bf16[192,384]{1,0:T(8,128)(2,1)S(1)}, u32[]{:S(2)}, u32[]{:S(2)}) collective-permute-start(bf16[192,384]{1,0:T(8,128)(2,1)S(1)} %get-tuple-element.44.a0), channel_id=1, source_target_pairs={{0,1},{1,0},{2,3},{3,2},{4,5},{5,4},{6,7},{7,6},{8,9},{9,8},{10,11... | collective-permute-start | bytes 442376 | tf_op jit(solution)/shard_map/ppermute | solution.py:141
  48.2 5.2 %collective-permute-start.13 = (bf16[192,384]{1,0:T(8,128)(2,1)S(1)}, bf16[192,384]{1,0:T(8,128)(2,1)S(1)}, u32[]{:S(2)}, u32[]{:S(2)}) collective-permute-start(bf16[192,384]{1,0:T(8,128)(2,1)S(1)} %collective-permute-done.11.a2), channel_id=1, source_target_pairs={{0,1},{1,0},{2,3},{3,2},{4,5},{5,4},{6,7},{7,6},{8,9},{9,8},{10,11... | collective-permute-start | bytes 442376 | tf_op jit(solution)/shard_map/ppermute | solution.py:141
  48.2 10.0 %collective-permute-start.18 = (bf16[192,768]{1,0:T(8,128)(2,1)S(1)}, bf16[192,768]{1,0:T(8,128)(2,1)S(1)}, u32[]{:S(2)}, u32[]{:S(2)}) collective-permute-start(bf16[192,768]{1,0:T(8,128)(2,1)S(1)} %get-tuple-element.46.refs_2_), channel_id=1, source_target_pairs={{0,8},{4,12},{8,0},{12,4},{16,24},{20,28},{24,16},{28,20},{1,9},{5... | collective-permute-start | bytes 884744 | tf_op jit(solution)/shard_map/ppermute | solution.py:573
  50.2 10.7 %collective-permute-start.19 = (bf16[192,768]{1,0:T(8,128)(2,1)S(1)}, bf16[192,768]{1,0:T(8,128)(2,1)S(1)}, u32[]{:S(2)}, u32[]{:S(2)}) collective-permute-start(bf16[192,768]{1,0:T(8,128)(2,1)S(1)} %get-tuple-element.46.refs_2_), channel_id=1, source_target_pairs={{0,16},{4,20},{8,24},{12,28},{16,0},{20,4},{24,8},{28,12},{1,17},{... | collective-permute-start | bytes 884744 | tf_op jit(solution)/shard_map/ppermute | solution.py:573
  50.5 15.6 %collective-permute-start.20 = (bf16[192,768]{1,0:T(8,128)(2,1)S(1)}, bf16[192,768]{1,0:T(8,128)(2,1)S(1)}, u32[]{:S(2)}, u32[]{:S(2)}) collective-permute-start(bf16[192,768]{1,0:T(8,128)(2,1)S(1)} %get-tuple-element.46.refs_2_), channel_id=1, source_target_pairs={{0,24},{4,28},{8,16},{12,20},{16,8},{20,12},{24,0},{28,4},{1,25},{... | collective-permute-start | bytes 884744 | tf_op jit(solution)/shard_map/ppermute | solution.py:573
  55.2 10.9 %collective-permute-start.16 = (bf16[384,384]{1,0:T(8,128)(2,1)S(1)}, bf16[384,384]{1,0:T(8,128)(2,1)S(1)}, u32[]{:S(2)}, u32[]{:S(2)}) collective-permute-start(bf16[384,384]{1,0:T(8,128)(2,1)S(1)} %get-tuple-element.49.refs_0_), channel_id=1, source_target_pairs={{0,4},{4,0},{8,12},{12,8},{16,20},{20,16},{24,28},{28,24},{1,5},{5... | collective-permute-start | bytes 884744 | tf_op jit(solution)/shard_map/ppermute | solution.py:573
  55.3 17.0 %collective-permute-start.17 = (bf16[192,768]{1,0:T(8,128)(2,1)S(1)}, bf16[192,768]{1,0:T(8,128)(2,1)S(1)}, u32[]{:S(2)}, u32[]{:S(2)}) collective-permute-start(bf16[192,768]{1,0:T(8,128)(2,1)S(1)} %get-tuple-element.50.refs_3_), channel_id=1, source_target_pairs={{0,8},{4,12},{8,0},{12,4},{16,24},{20,28},{24,16},{28,20},{1,9},{5... | collective-permute-start | bytes 884744 | tf_op jit(solution)/shard_map/ppermute | solution.py:573
  58.3 17.9 %collective-permute-start.14 = (bf16[192,768]{1,0:T(8,128)(2,1)S(1)}, bf16[192,768]{1,0:T(8,128)(2,1)S(1)}, u32[]{:S(2)}, u32[]{:S(2)}) collective-permute-start(bf16[192,768]{1,0:T(8,128)(2,1)S(1)} %get-tuple-element.50.refs_3_), channel_id=1, source_target_pairs={{0,16},{4,20},{8,24},{12,28},{16,0},{20,4},{24,8},{28,12},{1,17},{... | collective-permute-start | bytes 884744 | tf_op jit(solution)/shard_map/ppermute | solution.py:573
  61.0 15.2 %collective-permute-start.15 = (bf16[192,768]{1,0:T(8,128)(2,1)S(1)}, bf16[192,768]{1,0:T(8,128)(2,1)S(1)}, u32[]{:S(2)}, u32[]{:S(2)}) collective-permute-start(bf16[192,768]{1,0:T(8,128)(2,1)S(1)} %get-tuple-element.50.refs_3_), channel_id=1, source_target_pairs={{0,24},{4,28},{8,16},{12,20},{16,8},{20,12},{24,0},{28,4},{1,25},{... | collective-permute-start | bytes 884744 | tf_op jit(solution)/shard_map/ppermute | solution.py:573
  82.0 9.5 %collective-permute-start.22 = (bf16[384,384]{1,0:T(8,128)(2,1)S(1)}, bf16[384,384]{1,0:T(8,128)(2,1)S(1)}, u32[]{:S(2)}, u32[]{:S(2)}) collective-permute-start(bf16[384,384]{1,0:T(8,128)(2,1)S(1)} %get-tuple-element.54), channel_id=1, source_target_pairs={{0,1},{1,0},{2,3},{3,2},{4,5},{5,4},{6,7},{7,6},{8,9},{9,8},{10,11... | collective-permute-start | bytes 884744 | tf_op jit(solution)/shard_map/ppermute | solution.py:141
  91.6 15.9 %collective-permute-start.23 = (bf16[384,384]{1,0:T(8,128)(2,1)S(1)}, bf16[384,384]{1,0:T(8,128)(2,1)S(1)}, u32[]{:S(2)}, u32[]{:S(2)}) collective-permute-start(bf16[384,384]{1,0:T(8,128)(2,1)S(1)} %add_convert_fusion.1), channel_id=1, source_target_pairs={{0,2},{1,3},{2,0},{3,1},{4,6},{5,7},{6,4},{7,5},{8,10},{9,11},{10,... | collective-permute-start | bytes 884744 | tf_op jit(solution)/shard_map/ppermute | solution.py:141
  93.7 13.8 %collective-permute-start.24 = (bf16[384,384]{1,0:T(8,128)(2,1)S(1)}, bf16[384,384]{1,0:T(8,128)(2,1)S(1)}, u32[]{:S(2)}, u32[]{:S(2)}) collective-permute-start(bf16[384,384]{1,0:T(8,128)(2,1)S(1)} %get-tuple-element.56), channel_id=1, source_target_pairs={{0,1},{1,0},{2,3},{3,2},{4,5},{5,4},{6,7},{7,6},{8,9},{9,8},{10,11... | collective-permute-start | bytes 884744 | tf_op jit(solution)/shard_map/ppermute | solution.py:141
  (8 other events, 65.0 us)

commit v14 on v13

--- a/solution.py
+++ b/solution.py
@@ -407,7 +407,7 @@
     )(*operands, *weights)
 
 
-TILE = 64
+TILE = 32
 
 
 def split_rows(block):
@@ -576,7 +576,7 @@
 def on_device(dna, conv_in, dilated_kernel_weight, w_query, w_key, w_value, w_out):
     count = lax.axis_size("seq")
     rows = dna.shape[0] // 2
-    inner = rows // 2
+    inner = rows // 2 - 2 * EDGE
     outer = rows - inner
     low = lax.ppermute(dna[-EDGE:], "seq", [(i, i + 1) for i in range(count - 1)])
     high = lax.ppermute(dna[:EDGE], "seq", [(i + 1, i) for i in range(count - 1)])

time: 109 us -> 115 us (1.055)
  starting transfers between devices: 30.8 us -> 34.7 us
  waiting for transfers between devices: 51.1 us -> 53.5 us
    ppermute x8, waiting for transfers between devices: 6.37 us -> 10.8 us  [exchanged(): return lax.ppermute(block, 'seq', [(i, i ^ mask) for i in range(count)])]
    ppermute x15, starting transfers between devices: 18 us -> 21.6 us  [swapped(): return lax.ppermute(block, 'head', [(i, i ^ mask) for i in range(count)])]
    ppermute x15, waiting for transfers between devices: 44.7 us -> 42.8 us  [swapped(): return lax.ppermute(block, 'head', [(i, i ^ mask) for i in range(count)])]
  transfers between devices with their start and end apart: 25 -> 25, of which waited for: 14 -> 13; matrix products, arithmetic and copies ran while one was open for 0% -> 0% of each run, Pallas kernels for 17% -> 16%
where the time goes in v14:
time: 115 us
  waiting for transfers between devices  53.5 us (47%)
  starting transfers between devices  34.7 us (30%)
  Pallas kernels  25.2 us (22%)
    ppermute x15, waiting for transfers between devices, swapped(): return lax.ppermute(block, 'head', [(i, i ^ mask) for i in range(count)])  42.8 us
    ppermute x15, starting transfers between devices, swapped(): return lax.ppermute(block, 'head', [(i, i ^ mask) for i in range(count)])  21.6 us
    pallas_call x4, Pallas kernels, attend(): pl.pallas_call(kernel, out_shape=out, scratch_shapes=[pltpu.VMEM((2, exte...  12.9 us
    ppermute x8, waiting for transfers between devices, exchanged(): return lax.ppermute(block, 'seq', [(i, i ^ mask) for i in range(count)])  10.8 us
    ppermute x8, starting transfers between devices, exchanged(): return lax.ppermute(block, 'seq', [(i, i ^ mask) for i in range(count)])  10.2 us
    pallas_call x2, Pallas kernels, first_conv(): pl.pallas_call(kernel, out_shape=(kept, sent), in_specs=[pl.BlockSpec(mem...  4.14 us
    pallas_call x2, Pallas kernels, project(): pl.pallas_call(kernel, out_shape=(q, kv), compiler_params=pltpu.CompilerP...  3.67 us
    pallas_call x2, Pallas kernels, second_conv(): pl.pallas_call(kernel, out_shape=(kept, sent), scratch_shapes=[pltpu.VMEM...  3.56 us
  transfers between devices with their start and end apart: 25, of which 13 were waited for; matrix products, arithmetic and copies ran while one was open for 0% of the time, Pallas kernels for 16%

profile of v14, /device:TPU:0, one launch (start us, length us, event | category | flops | bytes accessed | tf_op | source)
XLA Modules:
  0.0 114.6 jit_solution(8315010655824565414)
XLA Ops:
  0.0 3.0 %conv_middle.1 = (f32[176,384]{1,0:T(8,128)S(1)}, bf16[176,384]{1,0:T(8,128)(2,1)S(1)}) custom-call(bf16[768,768]{1,0:T(8,128)(2,1)} %dna_ref.3, bf16[5,384,768]{2,1,0:T(8,128)(2,1)} %weight_ref.5), custom_call_target="tpu_custom_call" | custom-call | flops 519045120 | bytes 4534272 | tf_op jit(solution)/shard_map/conv_middle/pallas_call | solution.py:237
  3.0 4.1 %collective-permute-start.1 = (bf16[176,384]{1,0:T(8,128)(2,1)S(1)}, bf16[176,384]{1,0:T(8,128)(2,1)S(1)}, u32[]{:S(2)}, u32[]{:S(2)}) collective-permute-start(bf16[176,384]{1,0:T(8,128)(2,1)S(1)} %get-tuple-element.31.a0.m0), channel_id=1, source_target_pairs={{0,2},{1,3},{2,0},{3,1},{4,6},{5,7},{6,4},{7,5},{8,10},{9,11},{10,... | collective-permute-start | bytes 405512 | tf_op jit(solution)/shard_map/ppermute | solution.py:141
  11.6 2.1 %collective-permute-done.1.a2.m2 = bf16[176,384]{1,0:T(8,128)(2,1)S(1)} collective-permute-done((bf16[176,384]{1,0:T(8,128)(2,1)S(1)}, bf16[176,384]{1,0:T(8,128)(2,1)S(1)}, u32[]{:S(2)}, u32[]{:S(2)}) %collective-permute-start.1) | collective-permute-done | bytes 135200 | tf_op jit(solution)/shard_map/ppermute | solution.py:141
  16.5 2.4 %collective-permute-start.6 = (bf16[224,384]{1,0:T(8,128)(2,1)S(1)}, bf16[224,384]{1,0:T(8,128)(2,1)S(1)}, u32[]{:S(2)}, u32[]{:S(2)}) collective-permute-start(bf16[224,384]{1,0:T(8,128)(2,1)S(1)} %get-tuple-element.33.e0), channel_id=1, source_target_pairs={{0,2},{1,3},{2,0},{3,1},{4,6},{5,7},{6,4},{7,5},{8,10},{9,11},{10,... | collective-permute-start | bytes 516104 | tf_op jit(solution)/shard_map/ppermute | solution.py:141
  21.6 6.8 %collective-permute-done.6.e2 = bf16[224,384]{1,0:T(8,128)(2,1)S(1)} collective-permute-done((bf16[224,384]{1,0:T(8,128)(2,1)S(1)}, bf16[224,384]{1,0:T(8,128)(2,1)S(1)}, u32[]{:S(2)}, u32[]{:S(2)}) %collective-permute-start.6) | collective-permute-done | bytes 172064 | tf_op jit(solution)/shard_map/ppermute | solution.py:141
  28.4 2.2 %collective-permute-start.10 = (bf16[160,384]{1,0:T(8,128)(2,1)S(1)}, bf16[160,384]{1,0:T(8,128)(2,1)S(1)}, u32[]{:S(2)}, u32[]{:S(2)}) collective-permute-start(bf16[160,384]{1,0:T(8,128)(2,1)S(1)} %get-tuple-element.45.a0), channel_id=1, source_target_pairs={{0,2},{1,3},{2,0},{3,1},{4,6},{5,7},{6,4},{7,5},{8,10},{9,11},{10,... | collective-permute-start | bytes 368648 | tf_op jit(solution)/shard_map/ppermute | solution.py:141
  30.6 6.1 %collective-permute-done.10.a2 = bf16[160,384]{1,0:T(8,128)(2,1)S(1)} collective-permute-done((bf16[160,384]{1,0:T(8,128)(2,1)S(1)}, bf16[160,384]{1,0:T(8,128)(2,1)S(1)}, u32[]{:S(2)}, u32[]{:S(2)}) %collective-permute-start.10) | collective-permute-done | bytes 122912 | tf_op jit(solution)/shard_map/ppermute | solution.py:141
  38.4 1.9 %dilated_edge.1 = (f32[384,384]{1,0:T(8,128)S(1)}, bf16[224,384]{1,0:T(8,128)(2,1)S(1)}) custom-call(bf16[176,384]{1,0:T(8,128)(2,1)S(1)} %get-tuple-element.31.a0.m0, bf16[176,384]{1,0:T(8,128)(2,1)S(1)} %collective-permute-done.a1.m1, bf16[176,384]{1,0:T(8,128)(2,1)S(1)} %collective-permute-done.1.a2.m2, ...), custom_call_target="tpu_custom_call" | custom-call | flops 792723456 | bytes 6389760 | tf_op jit(solution)/shard_map/dilated_edge/pallas_call | solution.py:339
  41.2 2.0 %collective-permute-start.9 = (bf16[224,384]{1,0:T(8,128)(2,1)S(1)}, bf16[224,384]{1,0:T(8,128)(2,1)S(1)}, u32[]{:S(2)}, u32[]{:S(2)}) collective-permute-start(bf16[224,384]{1,0:T(8,128)(2,1)S(1)} %get-tuple-element.44.a0), channel_id=1, source_target_pairs={{0,1},{1,0},{2,3},{3,2},{4,5},{5,4},{6,7},{7,6},{8,9},{9,8},{10,11... | collective-permute-start | bytes 516104 | tf_op jit(solution)/shard_map/ppermute | solution.py:141
  46.0 3.5 %collective-permute-done.11.a2 = bf16[224,384]{1,0:T(8,128)(2,1)S(1)} collective-permute-done((bf16[224,384]{1,0:T(8,128)(2,1)S(1)}, bf16[224,384]{1,0:T(8,128)(2,1)S(1)}, u32[]{:S(2)}, u32[]{:S(2)}) %collective-permute-start.11) | collective-permute-done | bytes 172064 | tf_op jit(solution)/shard_map/ppermute | solution.py:141
  50.1 3.1 %collective-permute-start.19 = (bf16[160,768]{1,0:T(8,128)(2,1)S(1)}, bf16[160,768]{1,0:T(8,128)(2,1)S(1)}, u32[]{:S(2)}, u32[]{:S(2)}) collective-permute-start(bf16[160,768]{1,0:T(8,128)(2,1)S(1)} %get-tuple-element.46.refs_2_), channel_id=1, source_target_pairs={{0,16},{4,20},{8,24},{12,28},{16,0},{20,4},{24,8},{28,12},{1,17},{... | collective-permute-start | bytes 737288 | tf_op jit(solution)/shard_map/ppermute | solution.py:573
  53.1 1.8 %collective-permute-done.13.a3 = bf16[224,384]{1,0:T(8,128)(2,1)S(1)} collective-permute-done((bf16[224,384]{1,0:T(8,128)(2,1)S(1)}, bf16[224,384]{1,0:T(8,128)(2,1)S(1)}, u32[]{:S(2)}, u32[]{:S(2)}) %collective-permute-start.13) | collective-permute-done | bytes 172064 | tf_op jit(solution)/shard_map/ppermute | solution.py:141
  54.9 1.9 %project_edge.1 = (bf16[384,384]{1,0:T(8,128)(2,1)S(1)}, bf16[224,768]{1,0:T(8,128)(2,1)S(1)}) custom-call(bf16[224,384]{1,0:T(8,128)(2,1)S(1)} %get-tuple-element.44.a0, bf16[224,384]{1,0:T(8,128)(2,1)S(1)} %collective-permute-done.9.a1, bf16[224,384]{1,0:T(8,128)(2,1)S(1)} %collective-permute-done.11.a2, bf16[224,384]{1,0:T(8,128)(2,1)S(1)} %collective-permute-done.13.a3, ...), custom_call_target="tpu_custom_call" | custom-call | flops 792723456 | bytes 4988928 | tf_op jit(solution)/shard_map/project_edge/pallas_call | solution.py:401
  56.9 2.1 %collective-permute-start.17 = (bf16[224,768]{1,0:T(8,128)(2,1)S(1)}, bf16[224,768]{1,0:T(8,128)(2,1)S(1)}, u32[]{:S(2)}, u32[]{:S(2)}) collective-permute-start(bf16[224,768]{1,0:T(8,128)(2,1)S(1)} %get-tuple-element.50.refs_3_), channel_id=1, source_target_pairs={{0,8},{4,12},{8,0},{12,4},{16,24},{20,28},{24,16},{28,20},{1,9},{5... | collective-permute-start | bytes 1032200 | tf_op jit(solution)/shard_map/ppermute | solution.py:573
  60.9 1.9 %collective-permute-done.19.refs_5_ = bf16[160,768]{1,0:T(8,128)(2,1)S(1)} collective-permute-done((bf16[160,768]{1,0:T(8,128)(2,1)S(1)}, bf16[160,768]{1,0:T(8,128)(2,1)S(1)}, u32[]{:S(2)}, u32[]{:S(2)}) %collective-permute-start.19) | collective-permute-done | bytes 245792 | tf_op jit(solution)/shard_map/ppermute | solution.py:573
  62.8 2.5 %collective-permute-start.14 = (bf16[224,768]{1,0:T(8,128)(2,1)S(1)}, bf16[224,768]{1,0:T(8,128)(2,1)S(1)}, u32[]{:S(2)}, u32[]{:S(2)}) collective-permute-start(bf16[224,768]{1,0:T(8,128)(2,1)S(1)} %get-tuple-element.50.refs_3_), channel_id=1, source_target_pairs={{0,16},{4,20},{8,24},{12,28},{16,0},{20,4},{24,8},{28,12},{1,17},{... | collective-permute-start | bytes 1032200 | tf_op jit(solution)/shard_map/ppermute | solution.py:573
  65.3 8.0 %collective-permute-done.18.refs_4_ = bf16[160,768]{1,0:T(8,128)(2,1)S(1)} collective-permute-done((bf16[160,768]{1,0:T(8,128)(2,1)S(1)}, bf16[160,768]{1,0:T(8,128)(2,1)S(1)}, u32[]{:S(2)}, u32[]{:S(2)}) %collective-permute-start.18) | collective-permute-done | bytes 245792 | tf_op jit(solution)/shard_map/ppermute | solution.py:573
  73.2 5.5 %attend_m.1.refs_3_ = f32[400,768]{1,0:T(8,128)S(1)} custom-call(bf16[384,384]{1,0:T(8,128)(2,1)S(1)} %get-tuple-element.49.refs_0_, bf16[384,384]{1,0:T(8,128)(2,1)S(1)} %collective-permute-done.16.refs_1_.refs_0_, bf16[160,768]{1,0:T(8,128)(2,1)S(1)} %get-tuple-element.46.refs_2_, bf16[224,768]{1,0:T(8,128)(2,1)S(1)} %get-tuple-element.50.refs_3_, ...), custom_call_target="tpu_custom_call" | custom-call | flops 1019215872 | bytes 3145728 | tf_op jit(solution)/shard_map/attend_m/pallas_call | solution.py:516
  78.8 2.2 %attend_x.1.refs_3_ = f32[400,768]{1,0:T(8,128)S(1)} custom-call(bf16[384,384]{1,0:T(8,128)(2,1)S(1)} %get-tuple-element.49.refs_0_, bf16[384,384]{1,0:T(8,128)(2,1)S(1)} %collective-permute-done.16.refs_1_.refs_0_, bf16[224,768]{1,0:T(8,128)(2,1)S(1)} %collective-permute-done.17.refs_2_, f32[400,768]{1,0:T(8,128)S(1)} %attend_m.1.refs_3_), custom_call_target="tpu_custom_call" | custom-call | flops 264241152 | bytes 3391488 | tf_op jit(solution)/shard_map/attend_x/pallas_call | solution.py:516
  81.9 2.6 %attend_other.1 = f32[400,384]{1,0:T(8,128)S(1)} custom-call(bf16[384,384]{1,0:T(8,128)(2,1)S(1)} %collective-permute-done.16.refs_1_.refs_0_, bf16[224,768]{1,0:T(8,128)(2,1)S(1)} %collective-permute-done.14.refs_1_, bf16[224,768]{1,0:T(8,128)(2,1)S(1)} %collective-permute-done.15.refs_2_, f32[400,768]{1,0:T(8,128)S(1)} %attend_x.1.refs_3_), custom_call_target="tpu_custom_call" | custom-call | flops 264241152 | bytes 2826240 | tf_op jit(solution)/shard_map/attend_other/pallas_call | solution.py:516
  84.5 2.6 %attend_own.1.own_state = f32[400,384]{1,0:T(8,128)S(1)} custom-call(bf16[384,384]{1,0:T(8,128)(2,1)S(1)} %get-tuple-element.49.refs_0_, bf16[224,768]{1,0:T(8,128)(2,1)S(1)} %collective-permute-done.14.refs_1_, bf16[224,768]{1,0:T(8,128)(2,1)S(1)} %collective-permute-done.15.refs_2_, f32[400,768]{1,0:T(8,128)S(1)} %attend_x.1.refs_3_), custom_call_target="tpu_custom_call" | custom-call | flops 264241152 | bytes 2826240 | tf_op jit(solution)/shard_map/attend_own/pallas_call | solution.py:516
  89.1 8.5 %collective-permute-done.22 = bf16[384,384]{1,0:T(8,128)(2,1)S(1)} collective-permute-done((bf16[384,384]{1,0:T(8,128)(2,1)S(1)}, bf16[384,384]{1,0:T(8,128)(2,1)S(1)}, u32[]{:S(2)}, u32[]{:S(2)}) %collective-permute-start.22) | collective-permute-done | bytes 294944 | tf_op jit(solution)/shard_map/ppermute | solution.py:141
  97.7 2.6 %collective-permute-start.23 = (bf16[384,384]{1,0:T(8,128)(2,1)S(1)}, bf16[384,384]{1,0:T(8,128)(2,1)S(1)}, u32[]{:S(2)}, u32[]{:S(2)}) collective-permute-start(bf16[384,384]{1,0:T(8,128)(2,1)S(1)} %add_convert_fusion.1), channel_id=1, source_target_pairs={{0,2},{1,3},{2,0},{3,1},{4,6},{5,7},{6,4},{7,5},{8,10},{9,11},{10,... | collective-permute-start | bytes 884744 | tf_op jit(solution)/shard_map/ppermute | solution.py:141
  102.1 11.7 %collective-permute-done.23 = bf16[384,384]{1,0:T(8,128)(2,1)S(1)} collective-permute-done((bf16[384,384]{1,0:T(8,128)(2,1)S(1)}, bf16[384,384]{1,0:T(8,128)(2,1)S(1)}, u32[]{:S(2)}, u32[]{:S(2)}) %collective-permute-start.23) | collective-permute-done | bytes 294944 | tf_op jit(solution)/shard_map/ppermute | solution.py:141
  (55 shorter events, 23.4 us)
Async XLA Ops:
  3.0 10.7 %collective-permute-start.1 = (bf16[176,384]{1,0:T(8,128)(2,1)S(1)}, bf16[176,384]{1,0:T(8,128)(2,1)S(1)}, u32[]{:S(2)}, u32[]{:S(2)}) collective-permute-start(bf16[176,384]{1,0:T(8,128)(2,1)S(1)} %get-tuple-element.31.a0.m0), channel_id=1, source_target_pairs={{0,2},{1,3},{2,0},{3,1},{4,6},{5,7},{6,4},{7,5},{8,10},{9,11},{10,... | collective-permute-start | bytes 405512 | tf_op jit(solution)/shard_map/ppermute | solution.py:141
  7.1 6.8 %collective-permute-start = (bf16[176,384]{1,0:T(8,128)(2,1)S(1)}, bf16[176,384]{1,0:T(8,128)(2,1)S(1)}, u32[]{:S(2)}, u32[]{:S(2)}) collective-permute-start(bf16[176,384]{1,0:T(8,128)(2,1)S(1)} %get-tuple-element.31.a0.m0), channel_id=1, source_target_pairs={{0,1},{1,0},{2,3},{3,2},{4,5},{5,4},{6,7},{7,6},{8,9},{9,8},{10,11... | collective-permute-start | bytes 405512 | tf_op jit(solution)/shard_map/ppermute | solution.py:141
  8.7 2.9 %collective-permute-start.3 = (bf16[16,768]{1,0:T(8,128)(2,1)S(1)}, bf16[16,768]{1,0:T(8,128)(2,1)S(1)}, u32[]{:S(2)}, u32[]{:S(2)}) collective-permute-start(bf16[16,768]{1,0:T(8,128)(2,1)S(1)} %get-tuple-element.58), channel_id=1, source_target_pairs={{0,4},{4,8},{8,12},{12,16},{16,20},{20,24},{24,28},{1,5},{5,9},{9,... | collective-permute-start | bytes 73736 | tf_op jit(solution)/shard_map/ppermute | solution.py:581
  10.0 5.4 %collective-permute-start.4 = (bf16[16,768]{1,0:T(8,128)(2,1)S(1)}, bf16[16,768]{1,0:T(8,128)(2,1)S(1)}, u32[]{:S(2)}, u32[]{:S(2)}) collective-permute-start(bf16[16,768]{1,0:T(8,128)(2,1)S(1)} %get-tuple-element.57), channel_id=1, source_target_pairs={{4,0},{8,4},{12,8},{16,12},{20,16},{24,20},{28,24},{5,1},{9,5},{13... | collective-permute-start | bytes 73736 | tf_op jit(solution)/shard_map/ppermute | solution.py:582
  13.9 6.1 %collective-permute-start.2 = (bf16[176,384]{1,0:T(8,128)(2,1)S(1)}, bf16[176,384]{1,0:T(8,128)(2,1)S(1)}, u32[]{:S(2)}, u32[]{:S(2)}) collective-permute-start(bf16[176,384]{1,0:T(8,128)(2,1)S(1)} %collective-permute-done.1.a2.m2), channel_id=1, source_target_pairs={{0,1},{1,0},{2,3},{3,2},{4,5},{5,4},{6,7},{7,6},{8,9},{9,8},{10,11... | collective-permute-start | bytes 405512 | tf_op jit(solution)/shard_map/ppermute | solution.py:141
  16.5 11.9 %collective-permute-start.6 = (bf16[224,384]{1,0:T(8,128)(2,1)S(1)}, bf16[224,384]{1,0:T(8,128)(2,1)S(1)}, u32[]{:S(2)}, u32[]{:S(2)}) collective-permute-start(bf16[224,384]{1,0:T(8,128)(2,1)S(1)} %get-tuple-element.33.e0), channel_id=1, source_target_pairs={{0,2},{1,3},{2,0},{3,1},{4,6},{5,7},{6,4},{7,5},{8,10},{9,11},{10,... | collective-permute-start | bytes 516104 | tf_op jit(solution)/shard_map/ppermute | solution.py:141
  18.9 11.7 %collective-permute-start.5 = (bf16[224,384]{1,0:T(8,128)(2,1)S(1)}, bf16[224,384]{1,0:T(8,128)(2,1)S(1)}, u32[]{:S(2)}, u32[]{:S(2)}) collective-permute-start(bf16[224,384]{1,0:T(8,128)(2,1)S(1)} %get-tuple-element.33.e0), channel_id=1, source_target_pairs={{0,1},{1,0},{2,3},{3,2},{4,5},{5,4},{6,7},{7,6},{8,9},{9,8},{10,11... | collective-permute-start | bytes 516104 | tf_op jit(solution)/shard_map/ppermute | solution.py:141
  28.4 10.0 %collective-permute-start.7 = (bf16[224,384]{1,0:T(8,128)(2,1)S(1)}, bf16[224,384]{1,0:T(8,128)(2,1)S(1)}, u32[]{:S(2)}, u32[]{:S(2)}) collective-permute-start(bf16[224,384]{1,0:T(8,128)(2,1)S(1)} %collective-permute-done.6.e2), channel_id=1, source_target_pairs={{0,1},{1,0},{2,3},{3,2},{4,5},{5,4},{6,7},{7,6},{8,9},{9,8},{10,11... | collective-permute-start | bytes 516104 | tf_op jit(solution)/shard_map/ppermute | solution.py:141
  28.4 8.3 %collective-permute-start.10 = (bf16[160,384]{1,0:T(8,128)(2,1)S(1)}, bf16[160,384]{1,0:T(8,128)(2,1)S(1)}, u32[]{:S(2)}, u32[]{:S(2)}) collective-permute-start(bf16[160,384]{1,0:T(8,128)(2,1)S(1)} %get-tuple-element.45.a0), channel_id=1, source_target_pairs={{0,2},{1,3},{2,0},{3,1},{4,6},{5,7},{6,4},{7,5},{8,10},{9,11},{10,... | collective-permute-start | bytes 368648 | tf_op jit(solution)/shard_map/ppermute | solution.py:141
  30.6 10.6 %collective-permute-start.8 = (bf16[160,384]{1,0:T(8,128)(2,1)S(1)}, bf16[160,384]{1,0:T(8,128)(2,1)S(1)}, u32[]{:S(2)}, u32[]{:S(2)}) collective-permute-start(bf16[160,384]{1,0:T(8,128)(2,1)S(1)} %get-tuple-element.45.a0), channel_id=1, source_target_pairs={{0,1},{1,0},{2,3},{3,2},{4,5},{5,4},{6,7},{7,6},{8,9},{9,8},{10,11... | collective-permute-start | bytes 368648 | tf_op jit(solution)/shard_map/ppermute | solution.py:141
  36.7 7.5 %collective-permute-start.12 = (bf16[160,384]{1,0:T(8,128)(2,1)S(1)}, bf16[160,384]{1,0:T(8,128)(2,1)S(1)}, u32[]{:S(2)}, u32[]{:S(2)}) collective-permute-start(bf16[160,384]{1,0:T(8,128)(2,1)S(1)} %collective-permute-done.10.a2), channel_id=1, source_target_pairs={{0,1},{1,0},{2,3},{3,2},{4,5},{5,4},{6,7},{7,6},{8,9},{9,8},{10,11... | collective-permute-start | bytes 368648 | tf_op jit(solution)/shard_map/ppermute | solution.py:141
  40.4 9.1 %collective-permute-start.11 = (bf16[224,384]{1,0:T(8,128)(2,1)S(1)}, bf16[224,384]{1,0:T(8,128)(2,1)S(1)}, u32[]{:S(2)}, u32[]{:S(2)}) collective-permute-start(bf16[224,384]{1,0:T(8,128)(2,1)S(1)} %get-tuple-element.44.a0), channel_id=1, source_target_pairs={{0,2},{1,3},{2,0},{3,1},{4,6},{5,7},{6,4},{7,5},{8,10},{9,11},{10,... | collective-permute-start | bytes 516104 | tf_op jit(solution)/shard_map/ppermute | solution.py:141
  41.2 11.9 %collective-permute-start.9 = (bf16[224,384]{1,0:T(8,128)(2,1)S(1)}, bf16[224,384]{1,0:T(8,128)(2,1)S(1)}, u32[]{:S(2)}, u32[]{:S(2)}) collective-permute-start(bf16[224,384]{1,0:T(8,128)(2,1)S(1)} %get-tuple-element.44.a0), channel_id=1, source_target_pairs={{0,1},{1,0},{2,3},{3,2},{4,5},{5,4},{6,7},{7,6},{8,9},{9,8},{10,11... | collective-permute-start | bytes 516104 | tf_op jit(solution)/shard_map/ppermute | solution.py:141
  49.5 5.4 %collective-permute-start.13 = (bf16[224,384]{1,0:T(8,128)(2,1)S(1)}, bf16[224,384]{1,0:T(8,128)(2,1)S(1)}, u32[]{:S(2)}, u32[]{:S(2)}) collective-permute-start(bf16[224,384]{1,0:T(8,128)(2,1)S(1)} %collective-permute-done.11.a2), channel_id=1, source_target_pairs={{0,1},{1,0},{2,3},{3,2},{4,5},{5,4},{6,7},{7,6},{8,9},{9,8},{10,11... | collective-permute-start | bytes 516104 | tf_op jit(solution)/shard_map/ppermute | solution.py:141
  49.5 9.7 %collective-permute-start.20 = (bf16[160,768]{1,0:T(8,128)(2,1)S(1)}, bf16[160,768]{1,0:T(8,128)(2,1)S(1)}, u32[]{:S(2)}, u32[]{:S(2)}) collective-permute-start(bf16[160,768]{1,0:T(8,128)(2,1)S(1)} %get-tuple-element.46.refs_2_), channel_id=1, source_target_pairs={{0,24},{4,28},{8,16},{12,20},{16,8},{20,12},{24,0},{28,4},{1,25},{... | collective-permute-start | bytes 737288 | tf_op jit(solution)/shard_map/ppermute | solution.py:573
  50.1 12.7 %collective-permute-start.19 = (bf16[160,768]{1,0:T(8,128)(2,1)S(1)}, bf16[160,768]{1,0:T(8,128)(2,1)S(1)}, u32[]{:S(2)}, u32[]{:S(2)}) collective-permute-start(bf16[160,768]{1,0:T(8,128)(2,1)S(1)} %get-tuple-element.46.refs_2_), channel_id=1, source_target_pairs={{0,16},{4,20},{8,24},{12,28},{16,0},{20,4},{24,8},{28,12},{1,17},{... | collective-permute-start | bytes 737288 | tf_op jit(solution)/shard_map/ppermute | solution.py:573
  56.9 16.4 %collective-permute-start.16 = (bf16[384,384]{1,0:T(8,128)(2,1)S(1)}, bf16[384,384]{1,0:T(8,128)(2,1)S(1)}, u32[]{:S(2)}, u32[]{:S(2)}) collective-permute-start(bf16[384,384]{1,0:T(8,128)(2,1)S(1)} %get-tuple-element.49.refs_0_), channel_id=1, source_target_pairs={{0,4},{4,0},{8,12},{12,8},{16,20},{20,16},{24,28},{28,24},{1,5},{5... | collective-permute-start | bytes 884744 | tf_op jit(solution)/shard_map/ppermute | solution.py:573
  56.9 21.8 %collective-permute-start.17 = (bf16[224,768]{1,0:T(8,128)(2,1)S(1)}, bf16[224,768]{1,0:T(8,128)(2,1)S(1)}, u32[]{:S(2)}, u32[]{:S(2)}) collective-permute-start(bf16[224,768]{1,0:T(8,128)(2,1)S(1)} %get-tuple-element.50.refs_3_), channel_id=1, source_target_pairs={{0,8},{4,12},{8,0},{12,4},{16,24},{20,28},{24,16},{28,20},{1,9},{5... | collective-permute-start | bytes 1032200 | tf_op jit(solution)/shard_map/ppermute | solution.py:573
  59.1 14.2 %collective-permute-start.18 = (bf16[160,768]{1,0:T(8,128)(2,1)S(1)}, bf16[160,768]{1,0:T(8,128)(2,1)S(1)}, u32[]{:S(2)}, u32[]{:S(2)}) collective-permute-start(bf16[160,768]{1,0:T(8,128)(2,1)S(1)} %get-tuple-element.46.refs_2_), channel_id=1, source_target_pairs={{0,8},{4,12},{8,0},{12,4},{16,24},{20,28},{24,16},{28,20},{1,9},{5... | collective-permute-start | bytes 737288 | tf_op jit(solution)/shard_map/ppermute | solution.py:573
  59.2 22.7 %collective-permute-start.15 = (bf16[224,768]{1,0:T(8,128)(2,1)S(1)}, bf16[224,768]{1,0:T(8,128)(2,1)S(1)}, u32[]{:S(2)}, u32[]{:S(2)}) collective-permute-start(bf16[224,768]{1,0:T(8,128)(2,1)S(1)} %get-tuple-element.50.refs_3_), channel_id=1, source_target_pairs={{0,24},{4,28},{8,16},{12,20},{16,8},{20,12},{24,0},{28,4},{1,25},{... | collective-permute-start | bytes 1032200 | tf_op jit(solution)/shard_map/ppermute | solution.py:573
  62.8 19.1 %collective-permute-start.14 = (bf16[224,768]{1,0:T(8,128)(2,1)S(1)}, bf16[224,768]{1,0:T(8,128)(2,1)S(1)}, u32[]{:S(2)}, u32[]{:S(2)}) collective-permute-start(bf16[224,768]{1,0:T(8,128)(2,1)S(1)} %get-tuple-element.50.refs_3_), channel_id=1, source_target_pairs={{0,16},{4,20},{8,24},{12,28},{16,0},{20,4},{24,8},{28,12},{1,17},{... | collective-permute-start | bytes 1032200 | tf_op jit(solution)/shard_map/ppermute | solution.py:573
  88.1 9.5 %collective-permute-start.22 = (bf16[384,384]{1,0:T(8,128)(2,1)S(1)}, bf16[384,384]{1,0:T(8,128)(2,1)S(1)}, u32[]{:S(2)}, u32[]{:S(2)}) collective-permute-start(bf16[384,384]{1,0:T(8,128)(2,1)S(1)} %get-tuple-element.54), channel_id=1, source_target_pairs={{0,1},{1,0},{2,3},{3,2},{4,5},{5,4},{6,7},{7,6},{8,9},{9,8},{10,11... | collective-permute-start | bytes 884744 | tf_op jit(solution)/shard_map/ppermute | solution.py:141
  97.7 16.0 %collective-permute-start.23 = (bf16[384,384]{1,0:T(8,128)(2,1)S(1)}, bf16[384,384]{1,0:T(8,128)(2,1)S(1)}, u32[]{:S(2)}, u32[]{:S(2)}) collective-permute-start(bf16[384,384]{1,0:T(8,128)(2,1)S(1)} %add_convert_fusion.1), channel_id=1, source_target_pairs={{0,2},{1,3},{2,0},{3,1},{4,6},{5,7},{6,4},{7,5},{8,10},{9,11},{10,... | collective-permute-start | bytes 884744 | tf_op jit(solution)/shard_map/ppermute | solution.py:141
  100.3 13.5 %collective-permute-start.24 = (bf16[384,384]{1,0:T(8,128)(2,1)S(1)}, bf16[384,384]{1,0:T(8,128)(2,1)S(1)}, u32[]{:S(2)}, u32[]{:S(2)}) collective-permute-start(bf16[384,384]{1,0:T(8,128)(2,1)S(1)} %get-tuple-element.56), channel_id=1, source_target_pairs={{0,1},{1,0},{2,3},{3,2},{4,5},{5,4},{6,7},{7,6},{8,9},{9,8},{10,11... | collective-permute-start | bytes 884744 | tf_op jit(solution)/shard_map/ppermute | solution.py:141
  (8 other events, 56.8 us)

commit v15 on v13

--- a/solution.py
+++ b/solution.py
@@ -603,7 +603,7 @@
         inner + EDGE,
         "dilated_middle",
     )
-    normed_m = forwarded(shared(sent, wide_e))
+    normed_m = forwarded(shared(sent))
     wide_e = forwarded(wide_e, sent)
     h2, sent = second_conv(
         dilated_edge_kernel,

time: 109 us -> 109 us (level)
  starting transfers between devices: 30.8 us -> 36.4 us
  waiting for transfers between devices: 51.1 us -> 45.8 us
    ppermute x15, waiting for transfers between devices: 44.7 us -> 40 us  [swapped(): return lax.ppermute(block, 'head', [(i, i ^ mask) for i in range(count)])]
    ppermute x15, starting transfers between devices: 18 us -> 22.3 us  [swapped(): return lax.ppermute(block, 'head', [(i, i ^ mask) for i in range(count)])]
    ppermute x8, starting transfers between devices: 9.9 us -> 11.3 us  [exchanged(): return lax.ppermute(block, 'seq', [(i, i ^ mask) for i in range(count)])]
  transfers between devices with their start and end apart: 25 -> 25, of which waited for: 14 -> 15; matrix products, arithmetic and copies ran while one was open for 0% -> 0% of each run, Pallas kernels for 17% -> 17%
where the time goes in v15:
time: 109 us
  waiting for transfers between devices  45.8 us (42%)
  starting transfers between devices  36.4 us (33%)
  Pallas kernels  25.3 us (23%)
    ppermute x15, waiting for transfers between devices, swapped(): return lax.ppermute(block, 'head', [(i, i ^ mask) for i in range(count)])  40 us
    ppermute x15, starting transfers between devices, swapped(): return lax.ppermute(block, 'head', [(i, i ^ mask) for i in range(count)])  22.3 us
    pallas_call x4, Pallas kernels, attend(): pl.pallas_call(kernel, out_shape=out, scratch_shapes=[pltpu.VMEM((2, exte...  13.1 us
    ppermute x8, starting transfers between devices, exchanged(): return lax.ppermute(block, 'seq', [(i, i ^ mask) for i in range(count)])  11.3 us
    ppermute x8, waiting for transfers between devices, exchanged(): return lax.ppermute(block, 'seq', [(i, i ^ mask) for i in range(count)])  5.71 us
    pallas_call x2, Pallas kernels, first_conv(): pl.pallas_call(kernel, out_shape=(kept, sent), in_specs=[pl.BlockSpec(mem...  4.15 us
    pallas_call x2, Pallas kernels, project(): pl.pallas_call(kernel, out_shape=(q, kv), compiler_params=pltpu.CompilerP...  3.71 us
    pallas_call x2, Pallas kernels, second_conv(): pl.pallas_call(kernel, out_shape=(kept, sent), scratch_shapes=[pltpu.VMEM...  3.42 us
  transfers between devices with their start and end apart: 25, of which 15 were waited for; matrix products, arithmetic and copies ran while one was open for 0% of the time, Pallas kernels for 17%

profile of v15, /device:TPU:0, one launch (start us, length us, event | category | flops | bytes accessed | tf_op | source)
XLA Modules:
  0.0 108.7 jit_solution(4799262420662071663)
XLA Ops:
  0.0 3.0 %conv_middle.1 = (f32[208,384]{1,0:T(8,128)S(1)}, bf16[208,384]{1,0:T(8,128)(2,1)S(1)}) custom-call(bf16[768,768]{1,0:T(8,128)(2,1)} %dna_ref.3, bf16[5,384,768]{2,1,0:T(8,128)(2,1)} %weight_ref.5), custom_call_target="tpu_custom_call" | custom-call | flops 613416960 | bytes 4608000 | tf_op jit(solution)/shard_map/conv_middle/pallas_call | solution.py:237
  3.0 4.1 %collective-permute-start.1 = (bf16[208,384]{1,0:T(8,128)(2,1)S(1)}, bf16[208,384]{1,0:T(8,128)(2,1)S(1)}, u32[]{:S(2)}, u32[]{:S(2)}) collective-permute-start(bf16[208,384]{1,0:T(8,128)(2,1)S(1)} %get-tuple-element.29.a0.m0), channel_id=1, source_target_pairs={{0,2},{1,3},{2,0},{3,1},{4,6},{5,7},{6,4},{7,5},{8,10},{9,11},{10,... | collective-permute-start | bytes 479240 | tf_op jit(solution)/shard_map/ppermute | solution.py:141
  11.6 3.2 %collective-permute-done.1.a2.m2 = bf16[208,384]{1,0:T(8,128)(2,1)S(1)} collective-permute-done((bf16[208,384]{1,0:T(8,128)(2,1)S(1)}, bf16[208,384]{1,0:T(8,128)(2,1)S(1)}, u32[]{:S(2)}, u32[]{:S(2)}) %collective-permute-start.1) | collective-permute-done | bytes 159776 | tf_op jit(solution)/shard_map/ppermute | solution.py:141
  16.5 3.4 %collective-permute-start.6 = (bf16[192,384]{1,0:T(8,128)(2,1)S(1)}, bf16[192,384]{1,0:T(8,128)(2,1)S(1)}, u32[]{:S(2)}, u32[]{:S(2)}) collective-permute-start(bf16[192,384]{1,0:T(8,128)(2,1)S(1)} %get-tuple-element.31.e0), channel_id=1, source_target_pairs={{0,2},{1,3},{2,0},{3,1},{4,6},{5,7},{6,4},{7,5},{8,10},{9,11},{10,... | collective-permute-start | bytes 442376 | tf_op jit(solution)/shard_map/ppermute | solution.py:141
  22.2 4.0 %collective-permute-start.10 = (bf16[192,384]{1,0:T(8,128)(2,1)S(1)}, bf16[192,384]{1,0:T(8,128)(2,1)S(1)}, u32[]{:S(2)}, u32[]{:S(2)}) collective-permute-start(bf16[192,384]{1,0:T(8,128)(2,1)S(1)} %get-tuple-element.41.a0), channel_id=1, source_target_pairs={{0,2},{1,3},{2,0},{3,1},{4,6},{5,7},{6,4},{7,5},{8,10},{9,11},{10,... | collective-permute-start | bytes 442376 | tf_op jit(solution)/shard_map/ppermute | solution.py:141
  27.1 1.8 %collective-permute-start.7 = (bf16[192,384]{1,0:T(8,128)(2,1)S(1)}, bf16[192,384]{1,0:T(8,128)(2,1)S(1)}, u32[]{:S(2)}, u32[]{:S(2)}) collective-permute-start(bf16[192,384]{1,0:T(8,128)(2,1)S(1)} %collective-permute-done.6.e2), channel_id=1, source_target_pairs={{0,1},{1,0},{2,3},{3,2},{4,5},{5,4},{6,7},{7,6},{8,9},{9,8},{10,11... | collective-permute-start | bytes 442376 | tf_op jit(solution)/shard_map/ppermute | solution.py:141
  29.1 5.1 %collective-permute-done.10.a2 = bf16[192,384]{1,0:T(8,128)(2,1)S(1)} collective-permute-done((bf16[192,384]{1,0:T(8,128)(2,1)S(1)}, bf16[192,384]{1,0:T(8,128)(2,1)S(1)}, u32[]{:S(2)}, u32[]{:S(2)}) %collective-permute-start.10) | collective-permute-done | bytes 147488 | tf_op jit(solution)/shard_map/ppermute | solution.py:141
  40.7 2.1 %collective-permute-done.12.a3 = bf16[192,384]{1,0:T(8,128)(2,1)S(1)} collective-permute-done((bf16[192,384]{1,0:T(8,128)(2,1)S(1)}, bf16[192,384]{1,0:T(8,128)(2,1)S(1)}, u32[]{:S(2)}, u32[]{:S(2)}) %collective-permute-start.12) | collective-permute-done | bytes 147488 | tf_op jit(solution)/shard_map/ppermute | solution.py:141
  42.8 1.9 %project_middle.1 = (bf16[192,384]{1,0:T(8,128)(2,1)S(1)}, bf16[192,768]{1,0:T(8,128)(2,1)S(1)}) custom-call(bf16[192,384]{1,0:T(8,128)(2,1)S(1)} %get-tuple-element.41.a0, bf16[192,384]{1,0:T(8,128)(2,1)S(1)} %collective-permute-done.8.a1, bf16[192,384]{1,0:T(8,128)(2,1)S(1)} %collective-permute-done.10.a2, ...), custom_call_target="tpu_custom_call" | custom-call | flops 679477248 | bytes 4571136 | tf_op jit(solution)/shard_map/project_middle/pallas_call | solution.py:401
  44.7 2.8 %collective-permute-done.11.a2 = bf16[192,384]{1,0:T(8,128)(2,1)S(1)} collective-permute-done((bf16[192,384]{1,0:T(8,128)(2,1)S(1)}, bf16[192,384]{1,0:T(8,128)(2,1)S(1)}, u32[]{:S(2)}, u32[]{:S(2)}) %collective-permute-start.11) | collective-permute-done | bytes 147488 | tf_op jit(solution)/shard_map/ppermute | solution.py:141
  51.0 1.8 %collective-permute-done.13.a3 = bf16[192,384]{1,0:T(8,128)(2,1)S(1)} collective-permute-done((bf16[192,384]{1,0:T(8,128)(2,1)S(1)}, bf16[192,384]{1,0:T(8,128)(2,1)S(1)}, u32[]{:S(2)}, u32[]{:S(2)}) %collective-permute-start.13) | collective-permute-done | bytes 147488 | tf_op jit(solution)/shard_map/ppermute | solution.py:141
  52.7 1.9 %project_edge.1 = (bf16[384,384]{1,0:T(8,128)(2,1)S(1)}, bf16[192,768]{1,0:T(8,128)(2,1)S(1)}) custom-call(bf16[192,384]{1,0:T(8,128)(2,1)S(1)} %get-tuple-element.40.a0, bf16[192,384]{1,0:T(8,128)(2,1)S(1)} %collective-permute-done.9.a1, bf16[192,384]{1,0:T(8,128)(2,1)S(1)} %collective-permute-done.11.a2, bf16[192,384]{1,0:T(8,128)(2,1)S(1)} %collective-permute-done.13.a3, ...), custom_call_target="tpu_custom_call" | custom-call | flops 679477248 | bytes 4866048 | tf_op jit(solution)/shard_map/project_edge/pallas_call | solution.py:401
  55.3 2.0 %collective-permute-done.18.refs_4_ = bf16[192,768]{1,0:T(8,128)(2,1)S(1)} collective-permute-done((bf16[192,768]{1,0:T(8,128)(2,1)S(1)}, bf16[192,768]{1,0:T(8,128)(2,1)S(1)}, u32[]{:S(2)}, u32[]{:S(2)}) %collective-permute-start.18) | collective-permute-done | bytes 294944 | tf_op jit(solution)/shard_map/ppermute | solution.py:573
  57.4 2.0 %collective-permute-start.14 = (bf16[192,768]{1,0:T(8,128)(2,1)S(1)}, bf16[192,768]{1,0:T(8,128)(2,1)S(1)}, u32[]{:S(2)}, u32[]{:S(2)}) collective-permute-start(bf16[192,768]{1,0:T(8,128)(2,1)S(1)} %get-tuple-element.46.refs_3_), channel_id=1, source_target_pairs={{0,16},{4,20},{8,24},{12,28},{16,0},{20,4},{24,8},{28,12},{1,17},{... | collective-permute-start | bytes 884744 | tf_op jit(solution)/shard_map/ppermute | solution.py:573
  61.0 4.9 %collective-permute-start.15 = (bf16[192,768]{1,0:T(8,128)(2,1)S(1)}, bf16[192,768]{1,0:T(8,128)(2,1)S(1)}, u32[]{:S(2)}, u32[]{:S(2)}) collective-permute-start(bf16[192,768]{1,0:T(8,128)(2,1)S(1)} %get-tuple-element.46.refs_3_), channel_id=1, source_target_pairs={{0,24},{4,28},{8,16},{12,20},{16,8},{20,12},{24,0},{28,4},{1,25},{... | collective-permute-start | bytes 884744 | tf_op jit(solution)/shard_map/ppermute | solution.py:573
  66.0 6.2 %attend_m.1.refs_3_ = f32[400,768]{1,0:T(8,128)S(1)} custom-call(bf16[384,384]{1,0:T(8,128)(2,1)S(1)} %get-tuple-element.45.refs_0_, bf16[384,384]{1,0:T(8,128)(2,1)S(1)} %collective-permute-done.16.refs_1_.refs_0_, bf16[192,768]{1,0:T(8,128)(2,1)S(1)} %get-tuple-element.42.refs_2_, bf16[192,768]{1,0:T(8,128)(2,1)S(1)} %get-tuple-element.46.refs_3_, ...), custom_call_target="tpu_custom_call" | custom-call | flops 1132462080 | bytes 3293184 | tf_op jit(solution)/shard_map/attend_m/pallas_call | solution.py:516
  72.2 2.1 %attend_x.1.refs_3_ = f32[400,768]{1,0:T(8,128)S(1)} custom-call(bf16[384,384]{1,0:T(8,128)(2,1)S(1)} %get-tuple-element.45.refs_0_, bf16[384,384]{1,0:T(8,128)(2,1)S(1)} %collective-permute-done.16.refs_1_.refs_0_, bf16[192,768]{1,0:T(8,128)(2,1)S(1)} %collective-permute-done.17.refs_2_, f32[400,768]{1,0:T(8,128)S(1)} %attend_m.1.refs_3_), custom_call_target="tpu_custom_call" | custom-call | flops 226492416 | bytes 3342336 | tf_op jit(solution)/shard_map/attend_x/pallas_call | solution.py:516
  74.4 1.9 %collective-permute-done.15.refs_2_ = bf16[192,768]{1,0:T(8,128)(2,1)S(1)} collective-permute-done((bf16[192,768]{1,0:T(8,128)(2,1)S(1)}, bf16[192,768]{1,0:T(8,128)(2,1)S(1)}, u32[]{:S(2)}, u32[]{:S(2)}) %collective-permute-start.15) | collective-permute-done | bytes 294944 | tf_op jit(solution)/shard_map/ppermute | solution.py:573
  76.4 2.4 %attend_other.1 = f32[400,384]{1,0:T(8,128)S(1)} custom-call(bf16[384,384]{1,0:T(8,128)(2,1)S(1)} %collective-permute-done.16.refs_1_.refs_0_, bf16[192,768]{1,0:T(8,128)(2,1)S(1)} %collective-permute-done.14.refs_1_, bf16[192,768]{1,0:T(8,128)(2,1)S(1)} %collective-permute-done.15.refs_2_, f32[400,768]{1,0:T(8,128)S(1)} %attend_x.1.refs_3_), custom_call_target="tpu_custom_call" | custom-call | flops 226492416 | bytes 2727936 | tf_op jit(solution)/shard_map/attend_other/pallas_call | solution.py:516
  78.8 2.4 %attend_own.1.own_state = f32[400,384]{1,0:T(8,128)S(1)} custom-call(bf16[384,384]{1,0:T(8,128)(2,1)S(1)} %get-tuple-element.45.refs_0_, bf16[192,768]{1,0:T(8,128)(2,1)S(1)} %collective-permute-done.14.refs_1_, bf16[192,768]{1,0:T(8,128)(2,1)S(1)} %collective-permute-done.15.refs_2_, f32[400,768]{1,0:T(8,128)S(1)} %attend_x.1.refs_3_), custom_call_target="tpu_custom_call" | custom-call | flops 226492416 | bytes 2727936 | tf_op jit(solution)/shard_map/attend_own/pallas_call | solution.py:516
  82.2 1.8 %collective-permute-start.22 = (bf16[384,384]{1,0:T(8,128)(2,1)S(1)}, bf16[384,384]{1,0:T(8,128)(2,1)S(1)}, u32[]{:S(2)}, u32[]{:S(2)}) collective-permute-start(bf16[384,384]{1,0:T(8,128)(2,1)S(1)} %get-tuple-element.50), channel_id=1, source_target_pairs={{0,1},{1,0},{2,3},{3,2},{4,5},{5,4},{6,7},{7,6},{8,9},{9,8},{10,11... | collective-permute-start | bytes 884744 | tf_op jit(solution)/shard_map/ppermute | solution.py:141
  84.0 7.7 %collective-permute-done.22 = bf16[384,384]{1,0:T(8,128)(2,1)S(1)} collective-permute-done((bf16[384,384]{1,0:T(8,128)(2,1)S(1)}, bf16[384,384]{1,0:T(8,128)(2,1)S(1)}, u32[]{:S(2)}, u32[]{:S(2)}) %collective-permute-start.22) | collective-permute-done | bytes 294944 | tf_op jit(solution)/shard_map/ppermute | solution.py:141
  91.9 1.8 %collective-permute-start.24 = (bf16[384,384]{1,0:T(8,128)(2,1)S(1)}, bf16[384,384]{1,0:T(8,128)(2,1)S(1)}, u32[]{:S(2)}, u32[]{:S(2)}) collective-permute-start(bf16[384,384]{1,0:T(8,128)(2,1)S(1)} %get-tuple-element.52), channel_id=1, source_target_pairs={{0,1},{1,0},{2,3},{3,2},{4,5},{5,4},{6,7},{7,6},{8,9},{9,8},{10,11... | collective-permute-start | bytes 884744 | tf_op jit(solution)/shard_map/ppermute | solution.py:141
  93.7 14.1 %collective-permute-done.23 = bf16[384,384]{1,0:T(8,128)(2,1)S(1)} collective-permute-done((bf16[384,384]{1,0:T(8,128)(2,1)S(1)}, bf16[384,384]{1,0:T(8,128)(2,1)S(1)}, u32[]{:S(2)}, u32[]{:S(2)}) %collective-permute-start.23) | collective-permute-done | bytes 294944 | tf_op jit(solution)/shard_map/ppermute | solution.py:141
  (55 shorter events, 23.9 us)
Async XLA Ops:
  3.0 11.7 %collective-permute-start.1 = (bf16[208,384]{1,0:T(8,128)(2,1)S(1)}, bf16[208,384]{1,0:T(8,128)(2,1)S(1)}, u32[]{:S(2)}, u32[]{:S(2)}) collective-permute-start(bf16[208,384]{1,0:T(8,128)(2,1)S(1)} %get-tuple-element.29.a0.m0), channel_id=1, source_target_pairs={{0,2},{1,3},{2,0},{3,1},{4,6},{5,7},{6,4},{7,5},{8,10},{9,11},{10,... | collective-permute-start | bytes 479240 | tf_op jit(solution)/shard_map/ppermute | solution.py:141
  7.1 8.3 %collective-permute-start = (bf16[208,384]{1,0:T(8,128)(2,1)S(1)}, bf16[208,384]{1,0:T(8,128)(2,1)S(1)}, u32[]{:S(2)}, u32[]{:S(2)}) collective-permute-start(bf16[208,384]{1,0:T(8,128)(2,1)S(1)} %get-tuple-element.29.a0.m0), channel_id=1, source_target_pairs={{0,1},{1,0},{2,3},{3,2},{4,5},{5,4},{6,7},{7,6},{8,9},{9,8},{10,11... | collective-permute-start | bytes 479240 | tf_op jit(solution)/shard_map/ppermute | solution.py:141
  8.7 6.7 %collective-permute-start.3 = (bf16[16,768]{1,0:T(8,128)(2,1)S(1)}, bf16[16,768]{1,0:T(8,128)(2,1)S(1)}, u32[]{:S(2)}, u32[]{:S(2)}) collective-permute-start(bf16[16,768]{1,0:T(8,128)(2,1)S(1)} %get-tuple-element.54), channel_id=1, source_target_pairs={{0,4},{4,8},{8,12},{12,16},{16,20},{20,24},{24,28},{1,5},{5,9},{9,... | collective-permute-start | bytes 73736 | tf_op jit(solution)/shard_map/ppermute | solution.py:581
  10.0 5.4 %collective-permute-start.4 = (bf16[16,768]{1,0:T(8,128)(2,1)S(1)}, bf16[16,768]{1,0:T(8,128)(2,1)S(1)}, u32[]{:S(2)}, u32[]{:S(2)}) collective-permute-start(bf16[16,768]{1,0:T(8,128)(2,1)S(1)} %get-tuple-element.53), channel_id=1, source_target_pairs={{4,0},{8,4},{12,8},{16,12},{20,16},{24,20},{28,24},{5,1},{9,5},{13... | collective-permute-start | bytes 73736 | tf_op jit(solution)/shard_map/ppermute | solution.py:582
  14.8 5.7 %collective-permute-start.2 = (bf16[208,384]{1,0:T(8,128)(2,1)S(1)}, bf16[208,384]{1,0:T(8,128)(2,1)S(1)}, u32[]{:S(2)}, u32[]{:S(2)}) collective-permute-start(bf16[208,384]{1,0:T(8,128)(2,1)S(1)} %collective-permute-done.1.a2.m2), channel_id=1, source_target_pairs={{0,1},{1,0},{2,3},{3,2},{4,5},{5,4},{6,7},{7,6},{8,9},{9,8},{10,11... | collective-permute-start | bytes 479240 | tf_op jit(solution)/shard_map/ppermute | solution.py:141
  16.5 10.5 %collective-permute-start.6 = (bf16[192,384]{1,0:T(8,128)(2,1)S(1)}, bf16[192,384]{1,0:T(8,128)(2,1)S(1)}, u32[]{:S(2)}, u32[]{:S(2)}) collective-permute-start(bf16[192,384]{1,0:T(8,128)(2,1)S(1)} %get-tuple-element.31.e0), channel_id=1, source_target_pairs={{0,2},{1,3},{2,0},{3,1},{4,6},{5,7},{6,4},{7,5},{8,10},{9,11},{10,... | collective-permute-start | bytes 442376 | tf_op jit(solution)/shard_map/ppermute | solution.py:141
  20.0 14.3 %collective-permute-start.5 = (bf16[192,384]{1,0:T(8,128)(2,1)S(1)}, bf16[192,384]{1,0:T(8,128)(2,1)S(1)}, u32[]{:S(2)}, u32[]{:S(2)}) collective-permute-start(bf16[192,384]{1,0:T(8,128)(2,1)S(1)} %get-tuple-element.31.e0), channel_id=1, source_target_pairs={{0,1},{1,0},{2,3},{3,2},{4,5},{5,4},{6,7},{7,6},{8,9},{9,8},{10,11... | collective-permute-start | bytes 442376 | tf_op jit(solution)/shard_map/ppermute | solution.py:141
  22.2 12.1 %collective-permute-start.10 = (bf16[192,384]{1,0:T(8,128)(2,1)S(1)}, bf16[192,384]{1,0:T(8,128)(2,1)S(1)}, u32[]{:S(2)}, u32[]{:S(2)}) collective-permute-start(bf16[192,384]{1,0:T(8,128)(2,1)S(1)} %get-tuple-element.41.a0), channel_id=1, source_target_pairs={{0,2},{1,3},{2,0},{3,1},{4,6},{5,7},{6,4},{7,5},{8,10},{9,11},{10,... | collective-permute-start | bytes 442376 | tf_op jit(solution)/shard_map/ppermute | solution.py:141
  27.1 8.8 %collective-permute-start.7 = (bf16[192,384]{1,0:T(8,128)(2,1)S(1)}, bf16[192,384]{1,0:T(8,128)(2,1)S(1)}, u32[]{:S(2)}, u32[]{:S(2)}) collective-permute-start(bf16[192,384]{1,0:T(8,128)(2,1)S(1)} %collective-permute-done.6.e2), channel_id=1, source_target_pairs={{0,1},{1,0},{2,3},{3,2},{4,5},{5,4},{6,7},{7,6},{8,9},{9,8},{10,11... | collective-permute-start | bytes 442376 | tf_op jit(solution)/shard_map/ppermute | solution.py:141
  28.9 10.1 %collective-permute-start.8 = (bf16[192,384]{1,0:T(8,128)(2,1)S(1)}, bf16[192,384]{1,0:T(8,128)(2,1)S(1)}, u32[]{:S(2)}, u32[]{:S(2)}) collective-permute-start(bf16[192,384]{1,0:T(8,128)(2,1)S(1)} %get-tuple-element.41.a0), channel_id=1, source_target_pairs={{0,1},{1,0},{2,3},{3,2},{4,5},{5,4},{6,7},{7,6},{8,9},{9,8},{10,11... | collective-permute-start | bytes 442376 | tf_op jit(solution)/shard_map/ppermute | solution.py:141
  34.3 8.5 %collective-permute-start.12 = (bf16[192,384]{1,0:T(8,128)(2,1)S(1)}, bf16[192,384]{1,0:T(8,128)(2,1)S(1)}, u32[]{:S(2)}, u32[]{:S(2)}) collective-permute-start(bf16[192,384]{1,0:T(8,128)(2,1)S(1)} %collective-permute-done.10.a2), channel_id=1, source_target_pairs={{0,1},{1,0},{2,3},{3,2},{4,5},{5,4},{6,7},{7,6},{8,9},{9,8},{10,11... | collective-permute-start | bytes 442376 | tf_op jit(solution)/shard_map/ppermute | solution.py:141
  37.6 9.8 %collective-permute-start.11 = (bf16[192,384]{1,0:T(8,128)(2,1)S(1)}, bf16[192,384]{1,0:T(8,128)(2,1)S(1)}, u32[]{:S(2)}, u32[]{:S(2)}) collective-permute-start(bf16[192,384]{1,0:T(8,128)(2,1)S(1)} %get-tuple-element.40.a0), channel_id=1, source_target_pairs={{0,2},{1,3},{2,0},{3,1},{4,6},{5,7},{6,4},{7,5},{8,10},{9,11},{10,... | collective-permute-start | bytes 442376 | tf_op jit(solution)/shard_map/ppermute | solution.py:141
  39.0 12.0 %collective-permute-start.9 = (bf16[192,384]{1,0:T(8,128)(2,1)S(1)}, bf16[192,384]{1,0:T(8,128)(2,1)S(1)}, u32[]{:S(2)}, u32[]{:S(2)}) collective-permute-start(bf16[192,384]{1,0:T(8,128)(2,1)S(1)} %get-tuple-element.40.a0), channel_id=1, source_target_pairs={{0,1},{1,0},{2,3},{3,2},{4,5},{5,4},{6,7},{7,6},{8,9},{9,8},{10,11... | collective-permute-start | bytes 442376 | tf_op jit(solution)/shard_map/ppermute | solution.py:141
  47.5 5.3 %collective-permute-start.13 = (bf16[192,384]{1,0:T(8,128)(2,1)S(1)}, bf16[192,384]{1,0:T(8,128)(2,1)S(1)}, u32[]{:S(2)}, u32[]{:S(2)}) collective-permute-start(bf16[192,384]{1,0:T(8,128)(2,1)S(1)} %collective-permute-done.11.a2), channel_id=1, source_target_pairs={{0,1},{1,0},{2,3},{3,2},{4,5},{5,4},{6,7},{7,6},{8,9},{9,8},{10,11... | collective-permute-start | bytes 442376 | tf_op jit(solution)/shard_map/ppermute | solution.py:141
  47.5 9.9 %collective-permute-start.18 = (bf16[192,768]{1,0:T(8,128)(2,1)S(1)}, bf16[192,768]{1,0:T(8,128)(2,1)S(1)}, u32[]{:S(2)}, u32[]{:S(2)}) collective-permute-start(bf16[192,768]{1,0:T(8,128)(2,1)S(1)} %get-tuple-element.42.refs_2_), channel_id=1, source_target_pairs={{0,8},{4,12},{8,0},{12,4},{16,24},{20,28},{24,16},{28,20},{1,9},{5... | collective-permute-start | bytes 884744 | tf_op jit(solution)/shard_map/ppermute | solution.py:573
  48.1 13.0 %collective-permute-start.19 = (bf16[192,768]{1,0:T(8,128)(2,1)S(1)}, bf16[192,768]{1,0:T(8,128)(2,1)S(1)}, u32[]{:S(2)}, u32[]{:S(2)}) collective-permute-start(bf16[192,768]{1,0:T(8,128)(2,1)S(1)} %get-tuple-element.42.refs_2_), channel_id=1, source_target_pairs={{0,16},{4,20},{8,24},{12,28},{16,0},{20,4},{24,8},{28,12},{1,17},{... | collective-permute-start | bytes 884744 | tf_op jit(solution)/shard_map/ppermute | solution.py:573
  49.5 16.5 %collective-permute-start.20 = (bf16[192,768]{1,0:T(8,128)(2,1)S(1)}, bf16[192,768]{1,0:T(8,128)(2,1)S(1)}, u32[]{:S(2)}, u32[]{:S(2)}) collective-permute-start(bf16[192,768]{1,0:T(8,128)(2,1)S(1)} %get-tuple-element.42.refs_2_), channel_id=1, source_target_pairs={{0,24},{4,28},{8,16},{12,20},{16,8},{20,12},{24,0},{28,4},{1,25},{... | collective-permute-start | bytes 884744 | tf_op jit(solution)/shard_map/ppermute | solution.py:573
  54.6 11.4 %collective-permute-start.16 = (bf16[384,384]{1,0:T(8,128)(2,1)S(1)}, bf16[384,384]{1,0:T(8,128)(2,1)S(1)}, u32[]{:S(2)}, u32[]{:S(2)}) collective-permute-start(bf16[384,384]{1,0:T(8,128)(2,1)S(1)} %get-tuple-element.45.refs_0_), channel_id=1, source_target_pairs={{0,4},{4,0},{8,12},{12,8},{16,20},{20,16},{24,28},{28,24},{1,5},{5... | collective-permute-start | bytes 884744 | tf_op jit(solution)/shard_map/ppermute | solution.py:573
  54.7 17.5 %collective-permute-start.17 = (bf16[192,768]{1,0:T(8,128)(2,1)S(1)}, bf16[192,768]{1,0:T(8,128)(2,1)S(1)}, u32[]{:S(2)}, u32[]{:S(2)}) collective-permute-start(bf16[192,768]{1,0:T(8,128)(2,1)S(1)} %get-tuple-element.46.refs_3_), channel_id=1, source_target_pairs={{0,8},{4,12},{8,0},{12,4},{16,24},{20,28},{24,16},{28,20},{1,9},{5... | collective-permute-start | bytes 884744 | tf_op jit(solution)/shard_map/ppermute | solution.py:573
  57.4 17.0 %collective-permute-start.14 = (bf16[192,768]{1,0:T(8,128)(2,1)S(1)}, bf16[192,768]{1,0:T(8,128)(2,1)S(1)}, u32[]{:S(2)}, u32[]{:S(2)}) collective-permute-start(bf16[192,768]{1,0:T(8,128)(2,1)S(1)} %get-tuple-element.46.refs_3_), channel_id=1, source_target_pairs={{0,16},{4,20},{8,24},{12,28},{16,0},{20,4},{24,8},{28,12},{1,17},{... | collective-permute-start | bytes 884744 | tf_op jit(solution)/shard_map/ppermute | solution.py:573
  61.0 15.3 %collective-permute-start.15 = (bf16[192,768]{1,0:T(8,128)(2,1)S(1)}, bf16[192,768]{1,0:T(8,128)(2,1)S(1)}, u32[]{:S(2)}, u32[]{:S(2)}) collective-permute-start(bf16[192,768]{1,0:T(8,128)(2,1)S(1)} %get-tuple-element.46.refs_3_), channel_id=1, source_target_pairs={{0,24},{4,28},{8,16},{12,20},{16,8},{20,12},{24,0},{28,4},{1,25},{... | collective-permute-start | bytes 884744 | tf_op jit(solution)/shard_map/ppermute | solution.py:573
  82.2 9.5 %collective-permute-start.22 = (bf16[384,384]{1,0:T(8,128)(2,1)S(1)}, bf16[384,384]{1,0:T(8,128)(2,1)S(1)}, u32[]{:S(2)}, u32[]{:S(2)}) collective-permute-start(bf16[384,384]{1,0:T(8,128)(2,1)S(1)} %get-tuple-element.50), channel_id=1, source_target_pairs={{0,1},{1,0},{2,3},{3,2},{4,5},{5,4},{6,7},{7,6},{8,9},{9,8},{10,11... | collective-permute-start | bytes 884744 | tf_op jit(solution)/shard_map/ppermute | solution.py:141
  91.8 16.0 %collective-permute-start.23 = (bf16[384,384]{1,0:T(8,128)(2,1)S(1)}, bf16[384,384]{1,0:T(8,128)(2,1)S(1)}, u32[]{:S(2)}, u32[]{:S(2)}) collective-permute-start(bf16[384,384]{1,0:T(8,128)(2,1)S(1)} %add_convert_fusion.1), channel_id=1, source_target_pairs={{0,2},{1,3},{2,0},{3,1},{4,6},{5,7},{6,4},{7,5},{8,10},{9,11},{10,... | collective-permute-start | bytes 884744 | tf_op jit(solution)/shard_map/ppermute | solution.py:141
  91.9 16.0 %collective-permute-start.24 = (bf16[384,384]{1,0:T(8,128)(2,1)S(1)}, bf16[384,384]{1,0:T(8,128)(2,1)S(1)}, u32[]{:S(2)}, u32[]{:S(2)}) collective-permute-start(bf16[384,384]{1,0:T(8,128)(2,1)S(1)} %get-tuple-element.52), channel_id=1, source_target_pairs={{0,1},{1,0},{2,3},{3,2},{4,5},{5,4},{6,7},{7,6},{8,9},{9,8},{10,11... | collective-permute-start | bytes 884744 | tf_op jit(solution)/shard_map/ppermute | solution.py:141
  (8 other events, 60.4 us)

commit v16 on v15

--- a/solution.py
+++ b/solution.py
@@ -603,7 +603,7 @@
         inner + EDGE,
         "dilated_middle",
     )
-    normed_m = forwarded(shared(sent))
+    normed_m = shared(sent)
     wide_e = forwarded(wide_e, sent)
     h2, sent = second_conv(
         dilated_edge_kernel,
@@ -615,7 +615,7 @@
         "dilated_edge",
     )
     normed_e = shared(sent, normed_m)
-    normed_m[0] = after(normed_m[0], sent)
+    normed_m = forwarded(normed_m, sent)
     weights = (w_query, w_key, w_value)
     q_m, kv_m = project(project_middle_kernel, normed_m, weights, inner, "project_middle")
     x_m, y_m, d_m = (exchanged(kv_m, mask) for mask in (2, 4, 6))

time: 109 us -> 108 us (level)
  starting transfers between devices: 36.4 us -> 34.7 us
  waiting for transfers between devices: 45.8 us -> 46.9 us
    ppermute x15, waiting for transfers between devices: 40 us -> 44 us  [swapped(): return lax.ppermute(block, 'head', [(i, i ^ mask) for i in range(count)])]
    ppermute x8, waiting for transfers between devices: 5.71 us -> 2.87 us  [exchanged(): return lax.ppermute(block, 'seq', [(i, i ^ mask) for i in range(count)])]
    ppermute x15, starting transfers between devices: 22.3 us -> 19.8 us  [swapped(): return lax.ppermute(block, 'head', [(i, i ^ mask) for i in range(count)])]
  transfers between devices with their start and end apart: 25 -> 25, of which waited for: 15 -> 12; matrix products, arithmetic and copies ran while one was open for 0% -> 0% of each run, Pallas kernels for 17% -> 18%
where the time goes in v16:
time: 108 us
  waiting for transfers between devices  46.9 us (43%)
  starting transfers between devices  34.7 us (32%)
  Pallas kernels  25.3 us (23%)
    ppermute x15, waiting for transfers between devices, swapped(): return lax.ppermute(block, 'head', [(i, i ^ mask) for i in range(count)])  44 us
    ppermute x15, starting transfers between devices, swapped(): return lax.ppermute(block, 'head', [(i, i ^ mask) for i in range(count)])  19.8 us
    pallas_call x4, Pallas kernels, attend(): pl.pallas_call(kernel, out_shape=out, scratch_shapes=[pltpu.VMEM((2, exte...  13.1 us
    ppermute x8, starting transfers between devices, exchanged(): return lax.ppermute(block, 'seq', [(i, i ^ mask) for i in range(count)])  12.1 us
    pallas_call x2, Pallas kernels, first_conv(): pl.pallas_call(kernel, out_shape=(kept, sent), in_specs=[pl.BlockSpec(mem...  4.15 us
    pallas_call x2, Pallas kernels, project(): pl.pallas_call(kernel, out_shape=(q, kv), compiler_params=pltpu.CompilerP...  3.7 us
    pallas_call x2, Pallas kernels, second_conv(): pl.pallas_call(kernel, out_shape=(kept, sent), scratch_shapes=[pltpu.VMEM...  3.42 us
    ppermute x8, waiting for transfers between devices, exchanged(): return lax.ppermute(block, 'seq', [(i, i ^ mask) for i in range(count)])  2.87 us
  transfers between devices with their start and end apart: 25, of which 12 were waited for; matrix products, arithmetic and copies ran while one was open for 0% of the time, Pallas kernels for 18%

profile of v16, /device:TPU:0, one launch (start us, length us, event | category | flops | bytes accessed | tf_op | source)
XLA Modules:
  0.0 108.0 jit_solution(2843420362514163903)
XLA Ops:
  0.0 3.0 %conv_middle.1 = (f32[208,384]{1,0:T(8,128)S(1)}, bf16[208,384]{1,0:T(8,128)(2,1)S(1)}) custom-call(bf16[768,768]{1,0:T(8,128)(2,1)} %dna_ref.3, bf16[5,384,768]{2,1,0:T(8,128)(2,1)} %weight_ref.5), custom_call_target="tpu_custom_call" | custom-call | flops 613416960 | bytes 4608000 | tf_op jit(solution)/shard_map/conv_middle/pallas_call | solution.py:237
  3.0 4.1 %collective-permute-start.1 = (bf16[208,384]{1,0:T(8,128)(2,1)S(1)}, bf16[208,384]{1,0:T(8,128)(2,1)S(1)}, u32[]{:S(2)}, u32[]{:S(2)}) collective-permute-start(bf16[208,384]{1,0:T(8,128)(2,1)S(1)} %get-tuple-element.29.a0.m0), channel_id=1, source_target_pairs={{0,2},{1,3},{2,0},{3,1},{4,6},{5,7},{6,4},{7,5},{8,10},{9,11},{10,... | collective-permute-start | bytes 479240 | tf_op jit(solution)/shard_map/ppermute | solution.py:141
  11.6 3.2 %collective-permute-done.1.a2.m2 = bf16[208,384]{1,0:T(8,128)(2,1)S(1)} collective-permute-done((bf16[208,384]{1,0:T(8,128)(2,1)S(1)}, bf16[208,384]{1,0:T(8,128)(2,1)S(1)}, u32[]{:S(2)}, u32[]{:S(2)}) %collective-permute-start.1) | collective-permute-done | bytes 159776 | tf_op jit(solution)/shard_map/ppermute | solution.py:141
  16.5 3.4 %collective-permute-start.6 = (bf16[192,384]{1,0:T(8,128)(2,1)S(1)}, bf16[192,384]{1,0:T(8,128)(2,1)S(1)}, u32[]{:S(2)}, u32[]{:S(2)}) collective-permute-start(bf16[192,384]{1,0:T(8,128)(2,1)S(1)} %get-tuple-element.31.e0), channel_id=1, source_target_pairs={{0,2},{1,3},{2,0},{3,1},{4,6},{5,7},{6,4},{7,5},{8,10},{9,11},{10,... | collective-permute-start | bytes 442376 | tf_op jit(solution)/shard_map/ppermute | solution.py:141
  22.2 4.9 %collective-permute-done.6.e2 = bf16[192,384]{1,0:T(8,128)(2,1)S(1)} collective-permute-done((bf16[192,384]{1,0:T(8,128)(2,1)S(1)}, bf16[192,384]{1,0:T(8,128)(2,1)S(1)}, u32[]{:S(2)}, u32[]{:S(2)}) %collective-permute-start.6) | collective-permute-done | bytes 147488 | tf_op jit(solution)/shard_map/ppermute | solution.py:141
  27.1 2.9 %collective-permute-start.10 = (bf16[192,384]{1,0:T(8,128)(2,1)S(1)}, bf16[192,384]{1,0:T(8,128)(2,1)S(1)}, u32[]{:S(2)}, u32[]{:S(2)}) collective-permute-start(bf16[192,384]{1,0:T(8,128)(2,1)S(1)} %get-tuple-element.34.a0), channel_id=1, source_target_pairs={{0,2},{1,3},{2,0},{3,1},{4,6},{5,7},{6,4},{7,5},{8,10},{9,11},{10,... | collective-permute-start | bytes 442376 | tf_op jit(solution)/shard_map/ppermute | solution.py:141
  30.0 5.3 %collective-permute-done.7.e3 = bf16[192,384]{1,0:T(8,128)(2,1)S(1)} collective-permute-done((bf16[192,384]{1,0:T(8,128)(2,1)S(1)}, bf16[192,384]{1,0:T(8,128)(2,1)S(1)}, u32[]{:S(2)}, u32[]{:S(2)}) %collective-permute-start.7) | collective-permute-done | bytes 147488 | tf_op jit(solution)/shard_map/ppermute | solution.py:141
  35.3 1.8 %dilated_edge.1 = (f32[384,384]{1,0:T(8,128)S(1)}, bf16[192,384]{1,0:T(8,128)(2,1)S(1)}) custom-call(bf16[208,384]{1,0:T(8,128)(2,1)S(1)} %get-tuple-element.29.a0.m0, bf16[208,384]{1,0:T(8,128)(2,1)S(1)} %collective-permute-done.a1.m1, bf16[208,384]{1,0:T(8,128)(2,1)S(1)} %collective-permute-done.1.a2.m2, ...), custom_call_target="tpu_custom_call" | custom-call | flops 679477248 | bytes 6414336 | tf_op jit(solution)/shard_map/dilated_edge/pallas_call | solution.py:339
  37.6 3.4 %collective-permute-start.11 = (bf16[192,384]{1,0:T(8,128)(2,1)S(1)}, bf16[192,384]{1,0:T(8,128)(2,1)S(1)}, u32[]{:S(2)}, u32[]{:S(2)}) collective-permute-start(bf16[192,384]{1,0:T(8,128)(2,1)S(1)} %get-tuple-element.40.a0), channel_id=1, source_target_pairs={{0,2},{1,3},{2,0},{3,1},{4,6},{5,7},{6,4},{7,5},{8,10},{9,11},{10,... | collective-permute-start | bytes 442376 | tf_op jit(solution)/shard_map/ppermute | solution.py:141
  41.1 6.2 %collective-permute-done.12.a3 = bf16[192,384]{1,0:T(8,128)(2,1)S(1)} collective-permute-done((bf16[192,384]{1,0:T(8,128)(2,1)S(1)}, bf16[192,384]{1,0:T(8,128)(2,1)S(1)}, u32[]{:S(2)}, u32[]{:S(2)}) %collective-permute-start.12) | collective-permute-done | bytes 147488 | tf_op jit(solution)/shard_map/ppermute | solution.py:141
  47.3 1.8 %project_middle.1 = (bf16[192,384]{1,0:T(8,128)(2,1)S(1)}, bf16[192,768]{1,0:T(8,128)(2,1)S(1)}) custom-call(bf16[192,384]{1,0:T(8,128)(2,1)S(1)} %get-tuple-element.34.a0, bf16[192,384]{1,0:T(8,128)(2,1)S(1)} %collective-permute-done.8.a1, bf16[192,384]{1,0:T(8,128)(2,1)S(1)} %collective-permute-done.10.a2, ...), custom_call_target="tpu_custom_call" | custom-call | flops 679477248 | bytes 4571136 | tf_op jit(solution)/shard_map/project_middle/pallas_call | solution.py:401
  49.3 2.0 %collective-permute-start.18 = (bf16[192,768]{1,0:T(8,128)(2,1)S(1)}, bf16[192,768]{1,0:T(8,128)(2,1)S(1)}, u32[]{:S(2)}, u32[]{:S(2)}) collective-permute-start(bf16[192,768]{1,0:T(8,128)(2,1)S(1)} %get-tuple-element.42.refs_2_), channel_id=1, source_target_pairs={{0,8},{4,12},{8,0},{12,4},{16,24},{20,28},{24,16},{28,20},{1,9},{5... | collective-permute-start | bytes 884744 | tf_op jit(solution)/shard_map/ppermute | solution.py:573
  54.4 1.9 %project_edge.1 = (bf16[384,384]{1,0:T(8,128)(2,1)S(1)}, bf16[192,768]{1,0:T(8,128)(2,1)S(1)}) custom-call(bf16[192,384]{1,0:T(8,128)(2,1)S(1)} %get-tuple-element.40.a0, bf16[192,384]{1,0:T(8,128)(2,1)S(1)} %collective-permute-done.9.a1, bf16[192,384]{1,0:T(8,128)(2,1)S(1)} %collective-permute-done.11.a2, bf16[192,384]{1,0:T(8,128)(2,1)S(1)} %collective-permute-done.13.a3, ...), custom_call_target="tpu_custom_call" | custom-call | flops 679477248 | bytes 4866048 | tf_op jit(solution)/shard_map/project_edge/pallas_call | solution.py:401
  56.4 1.9 %collective-permute-start.17 = (bf16[192,768]{1,0:T(8,128)(2,1)S(1)}, bf16[192,768]{1,0:T(8,128)(2,1)S(1)}, u32[]{:S(2)}, u32[]{:S(2)}) collective-permute-start(bf16[192,768]{1,0:T(8,128)(2,1)S(1)} %get-tuple-element.46.refs_3_), channel_id=1, source_target_pairs={{0,8},{4,12},{8,0},{12,4},{16,24},{20,28},{24,16},{28,20},{1,9},{5... | collective-permute-start | bytes 884744 | tf_op jit(solution)/shard_map/ppermute | solution.py:573
  58.6 1.8 %collective-permute-start.14 = (bf16[192,768]{1,0:T(8,128)(2,1)S(1)}, bf16[192,768]{1,0:T(8,128)(2,1)S(1)}, u32[]{:S(2)}, u32[]{:S(2)}) collective-permute-start(bf16[192,768]{1,0:T(8,128)(2,1)S(1)} %get-tuple-element.46.refs_3_), channel_id=1, source_target_pairs={{0,16},{4,20},{8,24},{12,28},{16,0},{20,4},{24,8},{28,12},{1,17},{... | collective-permute-start | bytes 884744 | tf_op jit(solution)/shard_map/ppermute | solution.py:573
  60.4 4.5 %collective-permute-start.15 = (bf16[192,768]{1,0:T(8,128)(2,1)S(1)}, bf16[192,768]{1,0:T(8,128)(2,1)S(1)}, u32[]{:S(2)}, u32[]{:S(2)}) collective-permute-start(bf16[192,768]{1,0:T(8,128)(2,1)S(1)} %get-tuple-element.46.refs_3_), channel_id=1, source_target_pairs={{0,24},{4,28},{8,16},{12,20},{16,8},{20,12},{24,0},{28,4},{1,25},{... | collective-permute-start | bytes 884744 | tf_op jit(solution)/shard_map/ppermute | solution.py:573
  64.9 6.2 %attend_m.1.refs_3_ = f32[400,768]{1,0:T(8,128)S(1)} custom-call(bf16[384,384]{1,0:T(8,128)(2,1)S(1)} %get-tuple-element.45.refs_0_, bf16[384,384]{1,0:T(8,128)(2,1)S(1)} %collective-permute-done.16.refs_1_.refs_0_, bf16[192,768]{1,0:T(8,128)(2,1)S(1)} %get-tuple-element.42.refs_2_, bf16[192,768]{1,0:T(8,128)(2,1)S(1)} %get-tuple-element.46.refs_3_, ...), custom_call_target="tpu_custom_call" | custom-call | flops 1132462080 | bytes 3293184 | tf_op jit(solution)/shard_map/attend_m/pallas_call | solution.py:516
  71.2 2.1 %attend_x.1.refs_3_ = f32[400,768]{1,0:T(8,128)S(1)} custom-call(bf16[384,384]{1,0:T(8,128)(2,1)S(1)} %get-tuple-element.45.refs_0_, bf16[384,384]{1,0:T(8,128)(2,1)S(1)} %collective-permute-done.16.refs_1_.refs_0_, bf16[192,768]{1,0:T(8,128)(2,1)S(1)} %collective-permute-done.17.refs_2_, f32[400,768]{1,0:T(8,128)S(1)} %attend_m.1.refs_3_), custom_call_target="tpu_custom_call" | custom-call | flops 226492416 | bytes 3342336 | tf_op jit(solution)/shard_map/attend_x/pallas_call | solution.py:516
  73.8 1.9 %collective-permute-done.15.refs_2_ = bf16[192,768]{1,0:T(8,128)(2,1)S(1)} collective-permute-done((bf16[192,768]{1,0:T(8,128)(2,1)S(1)}, bf16[192,768]{1,0:T(8,128)(2,1)S(1)}, u32[]{:S(2)}, u32[]{:S(2)}) %collective-permute-start.15) | collective-permute-done | bytes 294944 | tf_op jit(solution)/shard_map/ppermute | solution.py:573
  75.7 2.4 %attend_other.1 = f32[400,384]{1,0:T(8,128)S(1)} custom-call(bf16[384,384]{1,0:T(8,128)(2,1)S(1)} %collective-permute-done.16.refs_1_.refs_0_, bf16[192,768]{1,0:T(8,128)(2,1)S(1)} %collective-permute-done.14.refs_1_, bf16[192,768]{1,0:T(8,128)(2,1)S(1)} %collective-permute-done.15.refs_2_, f32[400,768]{1,0:T(8,128)S(1)} %attend_x.1.refs_3_), custom_call_target="tpu_custom_call" | custom-call | flops 226492416 | bytes 2727936 | tf_op jit(solution)/shard_map/attend_other/pallas_call | solution.py:516
  78.2 2.4 %attend_own.1.own_state = f32[400,384]{1,0:T(8,128)S(1)} custom-call(bf16[384,384]{1,0:T(8,128)(2,1)S(1)} %get-tuple-element.45.refs_0_, bf16[192,768]{1,0:T(8,128)(2,1)S(1)} %collective-permute-done.14.refs_1_, bf16[192,768]{1,0:T(8,128)(2,1)S(1)} %collective-permute-done.15.refs_2_, f32[400,768]{1,0:T(8,128)S(1)} %attend_x.1.refs_3_), custom_call_target="tpu_custom_call" | custom-call | flops 226492416 | bytes 2727936 | tf_op jit(solution)/shard_map/attend_own/pallas_call | solution.py:516
  81.6 1.7 %collective-permute-start.22 = (bf16[384,384]{1,0:T(8,128)(2,1)S(1)}, bf16[384,384]{1,0:T(8,128)(2,1)S(1)}, u32[]{:S(2)}, u32[]{:S(2)}) collective-permute-start(bf16[384,384]{1,0:T(8,128)(2,1)S(1)} %get-tuple-element.50), channel_id=1, source_target_pairs={{0,1},{1,0},{2,3},{3,2},{4,5},{5,4},{6,7},{7,6},{8,9},{9,8},{10,11... | collective-permute-start | bytes 884744 | tf_op jit(solution)/shard_map/ppermute | solution.py:141
  83.3 7.7 %collective-permute-done.22 = bf16[384,384]{1,0:T(8,128)(2,1)S(1)} collective-permute-done((bf16[384,384]{1,0:T(8,128)(2,1)S(1)}, bf16[384,384]{1,0:T(8,128)(2,1)S(1)}, u32[]{:S(2)}, u32[]{:S(2)}) %collective-permute-start.22) | collective-permute-done | bytes 294944 | tf_op jit(solution)/shard_map/ppermute | solution.py:141
  93.0 14.1 %collective-permute-done.23 = bf16[384,384]{1,0:T(8,128)(2,1)S(1)} collective-permute-done((bf16[384,384]{1,0:T(8,128)(2,1)S(1)}, bf16[384,384]{1,0:T(8,128)(2,1)S(1)}, u32[]{:S(2)}, u32[]{:S(2)}) %collective-permute-start.23) | collective-permute-done | bytes 294944 | tf_op jit(solution)/shard_map/ppermute | solution.py:141
  (55 shorter events, 17.1 us)
Async XLA Ops:
  3.0 11.7 %collective-permute-start.1 = (bf16[208,384]{1,0:T(8,128)(2,1)S(1)}, bf16[208,384]{1,0:T(8,128)(2,1)S(1)}, u32[]{:S(2)}, u32[]{:S(2)}) collective-permute-start(bf16[208,384]{1,0:T(8,128)(2,1)S(1)} %get-tuple-element.29.a0.m0), channel_id=1, source_target_pairs={{0,2},{1,3},{2,0},{3,1},{4,6},{5,7},{6,4},{7,5},{8,10},{9,11},{10,... | collective-permute-start | bytes 479240 | tf_op jit(solution)/shard_map/ppermute | solution.py:141
  7.1 8.3 %collective-permute-start = (bf16[208,384]{1,0:T(8,128)(2,1)S(1)}, bf16[208,384]{1,0:T(8,128)(2,1)S(1)}, u32[]{:S(2)}, u32[]{:S(2)}) collective-permute-start(bf16[208,384]{1,0:T(8,128)(2,1)S(1)} %get-tuple-element.29.a0.m0), channel_id=1, source_target_pairs={{0,1},{1,0},{2,3},{3,2},{4,5},{5,4},{6,7},{7,6},{8,9},{9,8},{10,11... | collective-permute-start | bytes 479240 | tf_op jit(solution)/shard_map/ppermute | solution.py:141
  8.7 6.7 %collective-permute-start.3 = (bf16[16,768]{1,0:T(8,128)(2,1)S(1)}, bf16[16,768]{1,0:T(8,128)(2,1)S(1)}, u32[]{:S(2)}, u32[]{:S(2)}) collective-permute-start(bf16[16,768]{1,0:T(8,128)(2,1)S(1)} %get-tuple-element.54), channel_id=1, source_target_pairs={{0,4},{4,8},{8,12},{12,16},{16,20},{20,24},{24,28},{1,5},{5,9},{9,... | collective-permute-start | bytes 73736 | tf_op jit(solution)/shard_map/ppermute | solution.py:581
  10.0 5.4 %collective-permute-start.4 = (bf16[16,768]{1,0:T(8,128)(2,1)S(1)}, bf16[16,768]{1,0:T(8,128)(2,1)S(1)}, u32[]{:S(2)}, u32[]{:S(2)}) collective-permute-start(bf16[16,768]{1,0:T(8,128)(2,1)S(1)} %get-tuple-element.53), channel_id=1, source_target_pairs={{4,0},{8,4},{12,8},{16,12},{20,16},{24,20},{28,24},{5,1},{9,5},{13... | collective-permute-start | bytes 73736 | tf_op jit(solution)/shard_map/ppermute | solution.py:582
  14.8 5.7 %collective-permute-start.2 = (bf16[208,384]{1,0:T(8,128)(2,1)S(1)}, bf16[208,384]{1,0:T(8,128)(2,1)S(1)}, u32[]{:S(2)}, u32[]{:S(2)}) collective-permute-start(bf16[208,384]{1,0:T(8,128)(2,1)S(1)} %collective-permute-done.1.a2.m2), channel_id=1, source_target_pairs={{0,1},{1,0},{2,3},{3,2},{4,5},{5,4},{6,7},{7,6},{8,9},{9,8},{10,11... | collective-permute-start | bytes 479240 | tf_op jit(solution)/shard_map/ppermute | solution.py:141
  16.5 10.5 %collective-permute-start.6 = (bf16[192,384]{1,0:T(8,128)(2,1)S(1)}, bf16[192,384]{1,0:T(8,128)(2,1)S(1)}, u32[]{:S(2)}, u32[]{:S(2)}) collective-permute-start(bf16[192,384]{1,0:T(8,128)(2,1)S(1)} %get-tuple-element.31.e0), channel_id=1, source_target_pairs={{0,2},{1,3},{2,0},{3,1},{4,6},{5,7},{6,4},{7,5},{8,10},{9,11},{10,... | collective-permute-start | bytes 442376 | tf_op jit(solution)/shard_map/ppermute | solution.py:141
  20.0 10.0 %collective-permute-start.5 = (bf16[192,384]{1,0:T(8,128)(2,1)S(1)}, bf16[192,384]{1,0:T(8,128)(2,1)S(1)}, u32[]{:S(2)}, u32[]{:S(2)}) collective-permute-start(bf16[192,384]{1,0:T(8,128)(2,1)S(1)} %get-tuple-element.31.e0), channel_id=1, source_target_pairs={{0,1},{1,0},{2,3},{3,2},{4,5},{5,4},{6,7},{7,6},{8,9},{9,8},{10,11... | collective-permute-start | bytes 442376 | tf_op jit(solution)/shard_map/ppermute | solution.py:141
  27.1 8.2 %collective-permute-start.7 = (bf16[192,384]{1,0:T(8,128)(2,1)S(1)}, bf16[192,384]{1,0:T(8,128)(2,1)S(1)}, u32[]{:S(2)}, u32[]{:S(2)}) collective-permute-start(bf16[192,384]{1,0:T(8,128)(2,1)S(1)} %collective-permute-done.6.e2), channel_id=1, source_target_pairs={{0,1},{1,0},{2,3},{3,2},{4,5},{5,4},{6,7},{7,6},{8,9},{9,8},{10,11... | collective-permute-start | bytes 442376 | tf_op jit(solution)/shard_map/ppermute | solution.py:141
  27.1 10.5 %collective-permute-start.10 = (bf16[192,384]{1,0:T(8,128)(2,1)S(1)}, bf16[192,384]{1,0:T(8,128)(2,1)S(1)}, u32[]{:S(2)}, u32[]{:S(2)}) collective-permute-start(bf16[192,384]{1,0:T(8,128)(2,1)S(1)} %get-tuple-element.34.a0), channel_id=1, source_target_pairs={{0,2},{1,3},{2,0},{3,1},{4,6},{5,7},{6,4},{7,5},{8,10},{9,11},{10,... | collective-permute-start | bytes 442376 | tf_op jit(solution)/shard_map/ppermute | solution.py:141
  30.0 11.1 %collective-permute-start.8 = (bf16[192,384]{1,0:T(8,128)(2,1)S(1)}, bf16[192,384]{1,0:T(8,128)(2,1)S(1)}, u32[]{:S(2)}, u32[]{:S(2)}) collective-permute-start(bf16[192,384]{1,0:T(8,128)(2,1)S(1)} %get-tuple-element.34.a0), channel_id=1, source_target_pairs={{0,1},{1,0},{2,3},{3,2},{4,5},{5,4},{6,7},{7,6},{8,9},{9,8},{10,11... | collective-permute-start | bytes 442376 | tf_op jit(solution)/shard_map/ppermute | solution.py:141
  37.6 9.7 %collective-permute-start.12 = (bf16[192,384]{1,0:T(8,128)(2,1)S(1)}, bf16[192,384]{1,0:T(8,128)(2,1)S(1)}, u32[]{:S(2)}, u32[]{:S(2)}) collective-permute-start(bf16[192,384]{1,0:T(8,128)(2,1)S(1)} %collective-permute-done.10.a2), channel_id=1, source_target_pairs={{0,1},{1,0},{2,3},{3,2},{4,5},{5,4},{6,7},{7,6},{8,9},{9,8},{10,11... | collective-permute-start | bytes 442376 | tf_op jit(solution)/shard_map/ppermute | solution.py:141
  37.6 11.6 %collective-permute-start.11 = (bf16[192,384]{1,0:T(8,128)(2,1)S(1)}, bf16[192,384]{1,0:T(8,128)(2,1)S(1)}, u32[]{:S(2)}, u32[]{:S(2)}) collective-permute-start(bf16[192,384]{1,0:T(8,128)(2,1)S(1)} %get-tuple-element.40.a0), channel_id=1, source_target_pairs={{0,2},{1,3},{2,0},{3,1},{4,6},{5,7},{6,4},{7,5},{8,10},{9,11},{10,... | collective-permute-start | bytes 442376 | tf_op jit(solution)/shard_map/ppermute | solution.py:141
  41.0 12.0 %collective-permute-start.9 = (bf16[192,384]{1,0:T(8,128)(2,1)S(1)}, bf16[192,384]{1,0:T(8,128)(2,1)S(1)}, u32[]{:S(2)}, u32[]{:S(2)}) collective-permute-start(bf16[192,384]{1,0:T(8,128)(2,1)S(1)} %get-tuple-element.40.a0), channel_id=1, source_target_pairs={{0,1},{1,0},{2,3},{3,2},{4,5},{5,4},{6,7},{7,6},{8,9},{9,8},{10,11... | collective-permute-start | bytes 442376 | tf_op jit(solution)/shard_map/ppermute | solution.py:141
  49.2 5.2 %collective-permute-start.13 = (bf16[192,384]{1,0:T(8,128)(2,1)S(1)}, bf16[192,384]{1,0:T(8,128)(2,1)S(1)}, u32[]{:S(2)}, u32[]{:S(2)}) collective-permute-start(bf16[192,384]{1,0:T(8,128)(2,1)S(1)} %collective-permute-done.11.a2), channel_id=1, source_target_pairs={{0,1},{1,0},{2,3},{3,2},{4,5},{5,4},{6,7},{7,6},{8,9},{9,8},{10,11... | collective-permute-start | bytes 442376 | tf_op jit(solution)/shard_map/ppermute | solution.py:141
  49.3 9.4 %collective-permute-start.18 = (bf16[192,768]{1,0:T(8,128)(2,1)S(1)}, bf16[192,768]{1,0:T(8,128)(2,1)S(1)}, u32[]{:S(2)}, u32[]{:S(2)}) collective-permute-start(bf16[192,768]{1,0:T(8,128)(2,1)S(1)} %get-tuple-element.42.refs_2_), channel_id=1, source_target_pairs={{0,8},{4,12},{8,0},{12,4},{16,24},{20,28},{24,16},{28,20},{1,9},{5... | collective-permute-start | bytes 884744 | tf_op jit(solution)/shard_map/ppermute | solution.py:573
  51.2 9.2 %collective-permute-start.19 = (bf16[192,768]{1,0:T(8,128)(2,1)S(1)}, bf16[192,768]{1,0:T(8,128)(2,1)S(1)}, u32[]{:S(2)}, u32[]{:S(2)}) collective-permute-start(bf16[192,768]{1,0:T(8,128)(2,1)S(1)} %get-tuple-element.42.refs_2_), channel_id=1, source_target_pairs={{0,16},{4,20},{8,24},{12,28},{16,0},{20,4},{24,8},{28,12},{1,17},{... | collective-permute-start | bytes 884744 | tf_op jit(solution)/shard_map/ppermute | solution.py:573
  51.6 13.3 %collective-permute-start.20 = (bf16[192,768]{1,0:T(8,128)(2,1)S(1)}, bf16[192,768]{1,0:T(8,128)(2,1)S(1)}, u32[]{:S(2)}, u32[]{:S(2)}) collective-permute-start(bf16[192,768]{1,0:T(8,128)(2,1)S(1)} %get-tuple-element.42.refs_2_), channel_id=1, source_target_pairs={{0,24},{4,28},{8,16},{12,20},{16,8},{20,12},{24,0},{28,4},{1,25},{... | collective-permute-start | bytes 884744 | tf_op jit(solution)/shard_map/ppermute | solution.py:573
  56.3 8.6 %collective-permute-start.16 = (bf16[384,384]{1,0:T(8,128)(2,1)S(1)}, bf16[384,384]{1,0:T(8,128)(2,1)S(1)}, u32[]{:S(2)}, u32[]{:S(2)}) collective-permute-start(bf16[384,384]{1,0:T(8,128)(2,1)S(1)} %get-tuple-element.45.refs_0_), channel_id=1, source_target_pairs={{0,4},{4,0},{8,12},{12,8},{16,20},{20,16},{24,28},{28,24},{1,5},{5... | collective-permute-start | bytes 884744 | tf_op jit(solution)/shard_map/ppermute | solution.py:573
  56.4 14.8 %collective-permute-start.17 = (bf16[192,768]{1,0:T(8,128)(2,1)S(1)}, bf16[192,768]{1,0:T(8,128)(2,1)S(1)}, u32[]{:S(2)}, u32[]{:S(2)}) collective-permute-start(bf16[192,768]{1,0:T(8,128)(2,1)S(1)} %get-tuple-element.46.refs_3_), channel_id=1, source_target_pairs={{0,8},{4,12},{8,0},{12,4},{16,24},{20,28},{24,16},{28,20},{1,9},{5... | collective-permute-start | bytes 884744 | tf_op jit(solution)/shard_map/ppermute | solution.py:573
  58.6 15.2 %collective-permute-start.14 = (bf16[192,768]{1,0:T(8,128)(2,1)S(1)}, bf16[192,768]{1,0:T(8,128)(2,1)S(1)}, u32[]{:S(2)}, u32[]{:S(2)}) collective-permute-start(bf16[192,768]{1,0:T(8,128)(2,1)S(1)} %get-tuple-element.46.refs_3_), channel_id=1, source_target_pairs={{0,16},{4,20},{8,24},{12,28},{16,0},{20,4},{24,8},{28,12},{1,17},{... | collective-permute-start | bytes 884744 | tf_op jit(solution)/shard_map/ppermute | solution.py:573
  60.4 15.3 %collective-permute-start.15 = (bf16[192,768]{1,0:T(8,128)(2,1)S(1)}, bf16[192,768]{1,0:T(8,128)(2,1)S(1)}, u32[]{:S(2)}, u32[]{:S(2)}) collective-permute-start(bf16[192,768]{1,0:T(8,128)(2,1)S(1)} %get-tuple-element.46.refs_3_), channel_id=1, source_target_pairs={{0,24},{4,28},{8,16},{12,20},{16,8},{20,12},{24,0},{28,4},{1,25},{... | collective-permute-start | bytes 884744 | tf_op jit(solution)/shard_map/ppermute | solution.py:573
  81.6 9.5 %collective-permute-start.22 = (bf16[384,384]{1,0:T(8,128)(2,1)S(1)}, bf16[384,384]{1,0:T(8,128)(2,1)S(1)}, u32[]{:S(2)}, u32[]{:S(2)}) collective-permute-start(bf16[384,384]{1,0:T(8,128)(2,1)S(1)} %get-tuple-element.50), channel_id=1, source_target_pairs={{0,1},{1,0},{2,3},{3,2},{4,5},{5,4},{6,7},{7,6},{8,9},{9,8},{10,11... | collective-permute-start | bytes 884744 | tf_op jit(solution)/shard_map/ppermute | solution.py:141
  91.2 16.0 %collective-permute-start.23 = (bf16[384,384]{1,0:T(8,128)(2,1)S(1)}, bf16[384,384]{1,0:T(8,128)(2,1)S(1)}, u32[]{:S(2)}, u32[]{:S(2)}) collective-permute-start(bf16[384,384]{1,0:T(8,128)(2,1)S(1)} %add_convert_fusion.1), channel_id=1, source_target_pairs={{0,2},{1,3},{2,0},{3,1},{4,6},{5,7},{6,4},{7,5},{8,10},{9,11},{10,... | collective-permute-start | bytes 884744 | tf_op jit(solution)/shard_map/ppermute | solution.py:141
  91.9 15.3 %collective-permute-start.24 = (bf16[384,384]{1,0:T(8,128)(2,1)S(1)}, bf16[384,384]{1,0:T(8,128)(2,1)S(1)}, u32[]{:S(2)}, u32[]{:S(2)}) collective-permute-start(bf16[384,384]{1,0:T(8,128)(2,1)S(1)} %get-tuple-element.52), channel_id=1, source_target_pairs={{0,1},{1,0},{2,3},{3,2},{4,5},{5,4},{6,7},{7,6},{8,9},{9,8},{10,11... | collective-permute-start | bytes 884744 | tf_op jit(solution)/shard_map/ppermute | solution.py:141
  (8 other events, 75.7 us)
